TPU v7x, 512 devices: a whole 4x8x8 slice. The times are simulated.
512 devices in a mesh: space: 128 (over y_hi, x, z, core), filt: 4 (over y_lo).
Axes of the slice: x: 4, y: 8 (y_hi: 2, y_lo: 4; y = y_hi * 4 + y_lo), z: 8, core: 2. Of those that a mesh axis runs over, the one named last changes fastest.
Arguments:
- image: bfloat16 [96, 512, 1024], P(None, 'space', 'filt'), may hold values from -6 to 6
- cotangent: bfloat16 [96, 512, 1024], P(None, 'space', 'filt'), may hold values from -6 to 6
- kernel: float32 [96, 7, 7], replicated, may hold values from -0.875 to 0.875
- dw_bias: float32 [96], replicated, may hold values from -0.5 to 0.5
- layer_norm_gain: float32 [96], replicated, may hold values from 0.5 to 1.5
- layer_norm_bias: float32 [96], replicated, may hold values from -3 to 3
- w_expand: bfloat16 [384, 96], replicated, may hold values from -0.625 to 0.625
- b_expand: bfloat16 [384], replicated, may hold values from -3 to 3
- w_reduce: bfloat16 [384, 96], replicated, may hold values from -0.3125 to 0.3125
- b_reduce: float32 [96], replicated, may hold values from -3 to 3
- layer_scale: float32 [96], replicated, may hold values from 0.2 to 1
Outputs:
- output: bfloat16 [96, 512, 1024], P(None, 'space', 'filt')
- image_grad: bfloat16 [96, 512, 1024], P(None, 'space', 'filt')
- kernel_grad: float32 [96, 7, 7], replicated
- dw_bias_grad: float32 [96], replicated
- gain_grad: float32 [96], replicated
- ln_bias_grad: float32 [96], replicated
- expand_grad: float32 [384, 96], P('filt')
- expand_bias_grad: float32 [384], P('filt')
- reduce_grad: float32 [384, 96], P('filt')
- reduce_bias_grad: float32 [96], replicated
- scale_grad: float32 [96], replicated
All inputs are finite; a program needn't handle non-finite values.
Results may differ from a plain program's by a relative error of at most 0.011.
Values may be sent and summed in bfloat16 or wider, within the bound.
A program may use at most 64 MiB of HBM per device.

v0:
```python
import math

import jax
import jax.numpy as jnp
from jax import lax
from jax.sharding import PartitionSpec as P


def padded_2(x, sides, width):
    for axis, dim in sides:
        size, length = (lax.axis_size(axis), x.shape[dim])
        up = [(i, (i + 1) % size) for i in range(size - 1)]
        down = [(j, i) for i, j in up]
        last = lax.slice_in_dim(x, length - width, length, axis=dim)
        initial = lax.slice_in_dim(x, 0, width, axis=dim)
        before = lax.ppermute(last, axis, up)
        after = lax.ppermute(initial, axis, down)
        x = jnp.concatenate([before, x, after], axis=dim)
    return x


def depthwise(padded, kernel, row_count, col_count):
    total = jnp.zeros((padded.shape[0], row_count, col_count), jnp.float32)
    for shift_row in range(7):
        for shift_col in range(7):
            piece = padded[
                :, shift_row : shift_row + row_count, shift_col : shift_col + col_count
            ].astype(jnp.float32)
            total = total + kernel[:, shift_row, shift_col][:, None, None] * piece
    return total


def conv_back(padded, kernel, row_count, col_count):
    total = jnp.zeros((padded.shape[0], row_count, col_count), jnp.float32)
    for shift_row in range(7):
        for shift_col in range(7):
            piece = padded[
                :,
                6 - shift_row : 6 - shift_row + row_count,
                6 - shift_col : 6 - shift_col + col_count,
            ].astype(jnp.float32)
            total = total + kernel[:, shift_row, shift_col][:, None, None] * piece
    return total


def kernel_terms(padded, convolution_gradient, row_count, col_count):
    lines = []
    for shift_row in range(7):
        entries = []
        for shift_col in range(7):
            piece = padded[
                :, shift_row : shift_row + row_count, shift_col : shift_col + col_count
            ].astype(jnp.float32)
            entries.append(jnp.sum(piece * convolution_gradient, axis=(1, 2)))
        lines.append(jnp.stack(entries, axis=1))
    return jnp.stack(lines, axis=1)


def gelu_exact(value):
    return value * (1.0 + jax.scipy.special.erf(value / math.sqrt(2.0))) * 0.5


def gelu_slope(value):
    return (1.0 + jax.scipy.special.erf(value / math.sqrt(2.0))) * 0.5 + value * jnp.exp(
        -0.5 * value * value
    ) / math.sqrt(2.0 * math.pi)


def shards(
    image,
    cotangent,
    kernel,
    dw_bias,
    layer_norm_gain,
    layer_norm_bias,
    w_expand,
    b_expand,
    w_reduce,
    b_reduce,
    layer_scale,
):
    channels, row_count, col_count = image.shape
    panel_rows = w_expand.shape[0] // lax.axis_size("filt")
    tok_count = row_count * col_count
    padded = padded_2(image, (("space", 1), ("filt", 2)), 3)
    conv = depthwise(padded, kernel, row_count, col_count)
    conv = conv + dw_bias[:, None, None]
    flat = conv.reshape(channels, tok_count)
    average = jnp.mean(flat, axis=0, keepdims=True)
    mean_removed = flat - average
    inverse_deviation = lax.rsqrt(
        jnp.mean(mean_removed * mean_removed, axis=0, keepdims=True) + 1e-06
    )
    standardized_input = mean_removed * inverse_deviation
    normalized_input = (
        standardized_input * layer_norm_gain[:, None] + layer_norm_bias[:, None]
    ).astype(jnp.bfloat16)
    hidden = (
        jnp.dot(w_expand, normalized_input, preferred_element_type=jnp.float32)
        + b_expand.astype(jnp.float32)[:, None]
    )
    active = gelu_exact(hidden).astype(jnp.bfloat16)
    branch = (
        lax.dot_general(
            w_reduce, active, (((0,), (0,)), ((), ())), preferred_element_type=jnp.float32
        )
        + b_reduce[:, None]
    )
    resid = image.reshape(channels, tok_count).astype(jnp.float32)
    output = (
        (resid + layer_scale[:, None] * branch)
        .astype(jnp.bfloat16)
        .reshape(channels, row_count, col_count)
    )
    cot_flat = cotangent.reshape(channels, tok_count).astype(jnp.float32)
    scaled = layer_scale[:, None] * cot_flat
    g_scale = jnp.sum(cot_flat * branch, axis=1)
    g_rbias = jnp.sum(scaled, axis=1)
    d_branch = scaled.astype(jnp.bfloat16)
    g_reduce = lax.dot_general(
        active, d_branch, (((1,), (1,)), ((), ())), preferred_element_type=jnp.float32
    )
    d_active = jnp.dot(w_reduce, d_branch, preferred_element_type=jnp.float32)
    d_hidden = (d_active * gelu_slope(hidden)).astype(jnp.bfloat16)
    g_ebias = jnp.sum(d_hidden.astype(jnp.float32), axis=1)
    g_expand = lax.dot_general(
        d_hidden, normalized_input, (((1,), (1,)), ((), ())), preferred_element_type=jnp.float32
    )
    normalized_gradient = lax.dot_general(
        w_expand, d_hidden, (((0,), (0,)), ((), ())), preferred_element_type=jnp.float32
    )
    norm_gain_gradient = jnp.sum(normalized_gradient * standardized_input, axis=1)
    g_lbias = jnp.sum(normalized_gradient, axis=1)
    standardized_gradient = normalized_gradient * layer_norm_gain[:, None]
    convolution_gradient = inverse_deviation * (
        standardized_gradient
        - jnp.mean(standardized_gradient, axis=0, keepdims=True)
        - standardized_input
        * jnp.mean(standardized_gradient * standardized_input, axis=0, keepdims=True)
    )
    convolution_gradient = convolution_gradient.astype(jnp.bfloat16).reshape(
        channels, row_count, col_count
    )
    d_float = convolution_gradient.astype(jnp.float32)
    g_dbias = jnp.sum(d_float, axis=(1, 2))
    padded_grad = padded_2(convolution_gradient, (("space", 1), ("filt", 2)), 3)
    back = conv_back(padded_grad, kernel, row_count, col_count)
    image_grad = (cotangent.astype(jnp.float32) + back).astype(jnp.bfloat16)
    g_kernel = kernel_terms(padded, d_float, row_count, col_count)
    factor = 1.0 / math.sqrt(tok_count * lax.axis_size("space") * lax.axis_size("filt"))
    (
        g_reduce,
        g_expand,
        g_ebias,
        g_kernel,
        g_dbias,
        norm_gain_gradient,
        g_lbias,
        g_scale,
        g_rbias,
    ) = lax.psum(
        (
            g_reduce,
            g_expand,
            g_ebias,
            g_kernel,
            g_dbias,
            norm_gain_gradient,
            g_lbias,
            g_scale,
            g_rbias,
        ),
        ("space", "filt"),
    )
    start = lax.axis_index("filt") * panel_rows
    g_reduce = lax.dynamic_slice_in_dim(g_reduce, start, panel_rows, 0)
    g_expand = lax.dynamic_slice_in_dim(g_expand, start, panel_rows, 0)
    g_ebias = lax.dynamic_slice_in_dim(g_ebias, start, panel_rows, 0)
    return (
        output,
        image_grad,
        g_kernel * factor,
        g_dbias * factor,
        norm_gain_gradient * factor,
        g_lbias * factor,
        g_expand * factor,
        g_ebias * factor,
        g_reduce * factor,
        g_rbias * factor,
        g_scale * factor,
    )


def solution(mesh):
    in_specs = (
        P(None, "space", "filt"),
        P(None, "space", "filt"),
        P(),
        P(),
        P(),
        P(),
        P(),
        P(),
        P(),
        P(),
        P(),
    )
    out_specs = (
        P(None, "space", "filt"),
        P(None, "space", "filt"),
        P(),
        P(),
        P(),
        P(),
        P("filt", None),
        P("filt"),
        P("filt", None),
        P(),
        P(),
    )
    return jax.shard_map(shards, mesh=mesh, in_specs=in_specs, out_specs=out_specs, check_vma=False)
```

profile of v0, /device:TPU:56, one launch (start us, length us, event | category | flops | bytes accessed | tf_op | source)
XLA Modules:
  0.0 501.3 jit_solution(11829889516771855415)
XLA Ops:
  7.2 0.0 copy-start
  7.2 0.0 all-reduce.4.cloned.1.call-start
  7.2 1.2 fusion.139
  8.4 0.0 copy-start.8
  8.5 2.1 collective-permute-start
  10.5 14.8 %collective-permute-start.1 = (bf16[96,3,256]{2,1,0:T(4,128)(2,1)S(1)}, bf16[96,3,256]{2,1,0:T(4,128)(2,1)S(1)}, u32[]{:S(2)}, u32[]{:S(2)}) collective-permute-start(bf16[96,3,256]{2,1,0:T(4,128)(2,1)S(1)} %get-tuple-element.99), channel_id=1, source_target_pairs={{4,0},{8,4},{12,8},{16,12},{20,16},{24,20},{28,24},{32,28},{36,32}... | collective-permute-start | bytes 442376 | tf_op jit(solution)/shard_map/ppermute | solution.py:17
  25.4 1.0 slice_bitcast_fusion.48
  26.4 1.6 slice_bitcast_fusion.47
  28.1 1.5 slice_bitcast_fusion.46
  29.7 0.0 collective-permute-done.1
  29.7 1.5 pad_maximum_fusion.2
  31.2 0.2 fusion.137
  31.4 1.3 collective-permute-start.2
  32.7 6.6 %collective-permute-start.3 = (bf16[96,10,3]{2,1,0:T(8,128)(2,1)S(1)}, bf16[96,10,3]{2,1,0:T(8,128)(2,1)}, u32[]{:S(2)}, u32[]{:S(2)}) collective-permute-start(bf16[96,10,3]{2,1,0:T(8,128)(2,1)S(1)} %get-tuple-element.89), channel_id=1, source_target_pairs={{1,0},{2,1},{3,2},{5,4},{6,5},{7,6},{9,8},{10,9},{11,10},{13,12},{... | collective-permute-start | bytes 17288 | tf_op jit(solution)/shard_map/ppermute | solution.py:17
  39.4 2.0 multiply_reduce_fusion.1
  41.4 0.9 copy.22
  42.5 0.7 copy-done.10
  43.2 0.7 collective-permute-done.3
  43.9 3.4 maximum_maximum_fusion
  47.7 11.5 %fusion.134 = (f32[4,256]{1,0:T(4,128)S(1)}, f32[96,4,256]{2,1,0:T(4,128)S(1)}) fusion(f32[96]{0:T(128)S(1)} %copy-done.92, bf16[96,10,259]{2,1,0:T(8,128)(2,1)S(1)} %get-tuple-element.93, f32[96]{0:T(128)S(1)} %copy-done.82, f32[96]{0:T(128)S(1)} %copy-done.84, f32[96]{0:T(128)S(1)} %get-tuple-element.101, ...), kind=kLoop, calls=%fused_computation.346 | loop fusion | flops 16317440 | bytes 9165568 | tf_op jit(solution)/shard_map/reduce_sum | solution.py:89
  59.3 0.2 multiply_reduce_fusion.3
  59.4 0.1 copy.23
  59.6 1.5 fusion.9
  61.1 1.5 convert_reduce_fusion
  62.6 1.1 fusion.133
  63.7 1.0 fusion.120
  64.7 1.4 convert_reduce_fusion.1
  66.2 1.1 reshape.89
  67.2 7.8 %fusion.115 = (f32[96]{0:T(128)}, f32[96]{0:T(128)}, f32[96]{0:T(128)}, f32[96]{0:T(128)}, f32[96]{0:T(128)}, /*index=5*/f32[96]{0:T(128)}, f32[96]{0:T(128)}, f...) fusion(bf16[96,4,256]{2,1,0:T(4,128)(2,1)S(1)} %reshape.89, ...), kind=kLoop, calls=%fused_computation.241 | loop fusion | flops 5404992 | bytes 3742464 | tf_op jit(solution)/shard_map/reduce_sum | solution.py:54
  75.0 9.8 %fusion.119 = (f32[96]{0:T(128)}, f32[96]{0:T(128)}, f32[96]{0:T(128)}, f32[96]{0:T(128)}, f32[96]{0:T(128)}, /*index=5*/f32[96]{0:T(128)}, f32[96]{0:T(128)}, f...) fusion(bf16[96,4,256]{2,1,0:T(4,128)(2,1)S(1)} %reshape.89, ...), kind=kLoop, calls=%fused_computation.245 | loop fusion | flops 5404992 | bytes 3742464 | tf_op jit(solution)/shard_map/reduce_sum | solution.py:54
  84.8 2.8 fusion.73
  87.7 0.9 fusion.138
  88.5 1.1 fusion.132
  89.7 5.9 %fusion.118 = (f32[96]{0:T(128)}, f32[96]{0:T(128)}, f32[96]{0:T(128)}, f32[96]{0:T(128)}, f32[96]{0:T(128)}, /*index=5*/f32[96]{0:T(128)}, f32[96]{0:T(128)}, f32[96]{0:T(128)}, f32[96]{0:T(128)}, f32[96]{0:T(128)}) fusion(bf16[96,4,256]{2,1,0:T(4,128)(2,1)S(1)} %reshape.89, bf16[96,10,259]{2,1,0:T(8,128)(2,1)S(1)} %get-tuple-element.93, ...), kind=kLoop, calls=%fused_computation.244 | loop fusion | flops 4815936 | bytes 1281792 | tf_op jit(solution)/shard_map/reduce_sum | solution.py:54
  95.6 0.8 stack.199
  96.4 0.1 reduce_sum.586
  96.5 0.7 stack.208
  97.2 0.7 stack.217
  97.9 0.7 stack.226
  98.7 0.7 stack.235
  99.4 0.7 stack.244
  100.1 0.7 stack.253
  100.9 1.5 multiply_reduce_fusion
  102.4 101.1 %all-reduce = (f32[96,7,7]{0,2,1:T(8,128)S(1)}, f32[96]{0:T(128)S(1)}, f32[96]{0:T(128)S(1)}, f32[96]{0:T(128)S(1)}, f32[384]{0:T(512)S(1)}, /*index=5*/f32[96]{0:T(128)S(1)}, f32[96]{0:T(128)S(1)}) all-reduce(f32[96,7,7]{0,2,1:T(8,128)S(1)} %constant_dynamic-update-slice_fusion, ...), channel_id=1, replica_groups=mesh['space'=128,'filt'=4] {'space','filt'}, use_global_device_ids=true, to_apply=%region_53.0 | all-reduce | flops 5568 | bytes 44544 | tf_op jit(solution)/shard_map/psum | solution.py:161
  203.5 0.6 broadcast_multiply_fusion
  204.1 0.5 broadcast_multiply_fusion.4
  204.6 0.5 broadcast_multiply_fusion.5
  205.1 0.5 broadcast_multiply_fusion.6
  205.6 0.5 broadcast_multiply_fusion.7
  206.1 1.9 collective-permute-start.4
  208.1 11.8 %collective-permute-start.5 = (bf16[96,3,256]{2,1,0:T(4,128)(2,1)S(1)}, bf16[96,3,256]{2,1,0:T(4,128)(2,1)S(1)}, u32[]{:S(2)}, u32[]{:S(2)}) collective-permute-start(bf16[96,3,256]{2,1,0:T(4,128)(2,1)S(1)} %copy-done.11), channel_id=1, source_target_pairs={{4,0},{8,4},{12,8},{16,12},{20,16},{24,20},{28,24},{32,28},{36,32}... | collective-permute-start | bytes 442376 | tf_op jit(solution)/shard_map/ppermute | solution.py:17
  219.8 0.5 broadcast_multiply_fusion.8
  220.4 0.8 reshape.88
  221.2 0.0 all-reduce.4.cloned.1.call-update
  221.2 0.6 dynamic-slice_multiply_fusion.2
  221.8 3.3 collective-permute-done.5
  225.1 0.5 pad_maximum_fusion.3
  225.6 0.2 fusion.136
  225.8 3.3 collective-permute-start.6
  229.1 1.3 collective-permute-start.7
  230.4 247.9 %all-reduce.4.cloned.1.call-done = (f32[384,96]{1,0:T(8,128)}, f32[384,96]{1,0:T(8,128)}) async-done(((f32[384,96]{1,0:T(8,128)}, f32[384,96]{1,0:T(8,128)}), (f32[384,96]{1,0:T(8,128)}, f32[384,96]{1,0:T(8,128)})) %all-reduce.4.cloned.1.call-update) | async-done | bytes 294928 | tf_op jit(solution)/shard_map/psum | solution.py:161
  478.3 1.5 dynamic-slice_multiply_fusion
  480.1 2.3 pad_maximum_fusion.1
  482.8 11.7 %add_convert_fusion = bf16[96,4,256]{2,1,0:T(4,128)(2,1)} fusion(bf16[96,4,256]{2,1,0:T(4,128)(2,1)S(1)} %reshape.89, bf16[96,3,256]{2,1,0:T(4,128)(2,1)S(1)} %collective-permute-done.4, bf16[96,3,256]{2,1,0:T(4,128)(2,1)S(1)} %collective-permute-done.5, bf16[96,10,259]{2,1,0:T(8,128)(2,1)S(1)} %get-tuple-element.91, ...), kind=kLoop, calls=%fused_computation.252 | loop fusion | flops 16416768 | bytes 9161088 | tf_op jit(solution)/shard_map/convert_element_type | solution.py:148
  (202 shorter events, 0.5 us)
Async XLA Ops:
  7.2 52.4 %copy-start = (bf16[384,96]{0,1:T(8,128)(2,1)S(1)}, bf16[384,96]{0,1:T(8,128)(2,1)}, u32[]{:S(2)}) copy-start(bf16[384,96]{0,1:T(8,128)(2,1)} %param.17) | copy-start | bytes 221188
  7.2 471.1 %all-reduce.4.cloned.1.call-start = ((), (), s32[]{:S(2)}) async-start(), calls=%async_computation | async-start | bytes 786432 | tf_op jit(solution)/shard_map/psum | solution.py:161
  8.4 30.9 %copy-start.8 = (bf16[96,4,256]{2,1,0:T(4,128)(2,1)S(1)}, bf16[96,4,256]{2,1,0:T(4,128)(2,1)}, u32[]{:S(2)}) copy-start(bf16[96,4,256]{2,1,0:T(4,128)(2,1)} %param.12) | copy-start | bytes 589828
  8.4 30.9 %copy-start.15 = (f32[96]{0:T(128)S(1)}, f32[96]{0:T(128)}, u32[]{:S(2)}) copy-start(f32[96]{0:T(128)} %param.21) | copy-start | bytes 1156
  8.5 21.2 %collective-permute-start = (bf16[96,3,256]{2,1,0:T(4,128)(2,1)S(1)}, bf16[96,3,256]{2,1,0:T(4,128)(2,1)S(1)}, u32[]{:S(2)}, u32[]{:S(2)}) collective-permute-start(bf16[96,3,256]{2,1,0:T(4,128)(2,1)S(1)} %get-tuple-element.98), channel_id=1, source_target_pairs={{0,4},{4,8},{8,12},{12,16},{16,20},{20,24},{24,28},{28,32},{32,36}... | collective-permute-start | bytes 442376 | tf_op jit(solution)/shard_map/ppermute | solution.py:16
  10.5 19.2 %collective-permute-start.1 = (bf16[96,3,256]{2,1,0:T(4,128)(2,1)S(1)}, bf16[96,3,256]{2,1,0:T(4,128)(2,1)S(1)}, u32[]{:S(2)}, u32[]{:S(2)}) collective-permute-start(bf16[96,3,256]{2,1,0:T(4,128)(2,1)S(1)} %get-tuple-element.99), channel_id=1, source_target_pairs={{4,0},{8,4},{12,8},{16,12},{20,16},{24,20},{28,24},{32,28},{36,32}... | collective-permute-start | bytes 442376 | tf_op jit(solution)/shard_map/ppermute | solution.py:17
  26.3 21.0 %copy-start.16 = (f32[96]{0:T(128)}, f32[96]{0:T(128)S(1)}, u32[]{:S(2)}) copy-start(f32[96]{0:T(128)S(1)} %get-tuple-element.114) | copy-start | bytes 1156
  26.3 21.0 %copy-start.18 = (f32[96]{0:T(128)}, f32[96]{0:T(128)S(1)}, u32[]{:S(2)}) copy-start(f32[96]{0:T(128)S(1)} %get-tuple-element.115) | copy-start | bytes 1156
  26.3 21.0 %copy-start.20 = (f32[96]{0:T(128)}, f32[96]{0:T(128)S(1)}, u32[]{:S(2)}) copy-start(f32[96]{0:T(128)S(1)} %get-tuple-element.116) | copy-start | bytes 1156
  26.4 21.0 %copy-start.22 = (f32[96]{0:T(128)}, f32[96]{0:T(128)S(1)}, u32[]{:S(2)}) copy-start(f32[96]{0:T(128)S(1)} %get-tuple-element.117) | copy-start | bytes 1156
  26.4 21.0 %copy-start.24 = (f32[96]{0:T(128)}, f32[96]{0:T(128)S(1)}, u32[]{:S(2)}) copy-start(f32[96]{0:T(128)S(1)} %get-tuple-element.118) | copy-start | bytes 1156
  28.0 19.4 %copy-start.26 = (f32[96]{0:T(128)}, f32[96]{0:T(128)S(1)}, u32[]{:S(2)}) copy-start(f32[96]{0:T(128)S(1)} %get-tuple-element.119) | copy-start | bytes 1156
  28.0 19.4 %copy-start.28 = (f32[96]{0:T(128)}, f32[96]{0:T(128)S(1)}, u32[]{:S(2)}) copy-start(f32[96]{0:T(128)S(1)} %get-tuple-element.120) | copy-start | bytes 1156
  28.0 19.4 %copy-start.30 = (f32[96]{0:T(128)}, f32[96]{0:T(128)S(1)}, u32[]{:S(2)}) copy-start(f32[96]{0:T(128)S(1)} %get-tuple-element.121) | copy-start | bytes 1156
  28.0 19.4 %copy-start.32 = (f32[96]{0:T(128)}, f32[96]{0:T(128)S(1)}, u32[]{:S(2)}) copy-start(f32[96]{0:T(128)S(1)} %get-tuple-element.122) | copy-start | bytes 1156
  28.0 19.4 %copy-start.34 = (f32[96]{0:T(128)}, f32[96]{0:T(128)S(1)}, u32[]{:S(2)}) copy-start(f32[96]{0:T(128)S(1)} %get-tuple-element.123) | copy-start | bytes 1156
  28.0 19.4 %copy-start.36 = (f32[96]{0:T(128)}, f32[96]{0:T(128)S(1)}, u32[]{:S(2)}) copy-start(f32[96]{0:T(128)S(1)} %get-tuple-element.124) | copy-start | bytes 1156
  28.0 19.4 %copy-start.38 = (f32[96]{0:T(128)}, f32[96]{0:T(128)S(1)}, u32[]{:S(2)}) copy-start(f32[96]{0:T(128)S(1)} %get-tuple-element.125) | copy-start | bytes 1156
  28.1 19.4 %copy-start.40 = (f32[96]{0:T(128)}, f32[96]{0:T(128)S(1)}, u32[]{:S(2)}) copy-start(f32[96]{0:T(128)S(1)} %get-tuple-element.126) | copy-start | bytes 1156
  28.1 19.4 %copy-start.42 = (f32[96]{0:T(128)}, f32[96]{0:T(128)S(1)}, u32[]{:S(2)}) copy-start(f32[96]{0:T(128)S(1)} %get-tuple-element.127) | copy-start | bytes 1156
  28.1 19.4 %copy-start.44 = (f32[96]{0:T(128)}, f32[96]{0:T(128)S(1)}, u32[]{:S(2)}) copy-start(f32[96]{0:T(128)S(1)} %get-tuple-element.128) | copy-start | bytes 1156
  28.1 19.4 %copy-start.46 = (f32[96]{0:T(128)}, f32[96]{0:T(128)S(1)}, u32[]{:S(2)}) copy-start(f32[96]{0:T(128)S(1)} %get-tuple-element.129) | copy-start | bytes 1156
  28.1 19.4 %copy-start.48 = (f32[96]{0:T(128)}, f32[96]{0:T(128)S(1)}, u32[]{:S(2)}) copy-start(f32[96]{0:T(128)S(1)} %get-tuple-element.130) | copy-start | bytes 1156
  28.1 19.4 %copy-start.50 = (f32[96]{0:T(128)}, f32[96]{0:T(128)S(1)}, u32[]{:S(2)}) copy-start(f32[96]{0:T(128)S(1)} %get-tuple-element.131) | copy-start | bytes 1156
  29.6 11.7 %copy-start.91 = (bf16[384]{0:T(512)(128)(2,1)S(1)}, bf16[384]{0:T(512)(128)(2,1)}, u32[]{:S(2)}) copy-start(bf16[384]{0:T(512)(128)(2,1)} %param.18) | copy-start | bytes 2308
  29.6 11.8 %copy-start.1 = (bf16[96,4,256]{2,1,0:T(4,128)(2,1)S(1)}, bf16[96,4,256]{2,1,0:T(4,128)(2,1)}, u32[]{:S(2)}) copy-start(bf16[96,4,256]{2,1,0:T(4,128)(2,1)} %param.11) | copy-start | bytes 589828
  29.7 17.8 %copy-start.7 = (bf16[96,3,256]{2,1,0:T(4,128)(2,1)}, bf16[96,3,256]{2,1,0:T(4,128)(2,1)S(1)}, u32[]{:S(2)}) copy-start(bf16[96,3,256]{2,1,0:T(4,128)(2,1)S(1)} %collective-permute-done.1) | copy-start | bytes 442372
  31.4 11.0 %collective-permute-start.2 = (bf16[96,10,3]{2,1,0:T(8,128)(2,1)S(1)}, bf16[96,10,3]{2,1,0:T(8,128)(2,1)S(1)}, u32[]{:S(2)}, u32[]{:S(2)}) collective-permute-start(bf16[96,10,3]{2,1,0:T(8,128)(2,1)S(1)} %get-tuple-element.88), channel_id=1, source_target_pairs={{0,1},{1,2},{2,3},{4,5},{5,6},{6,7},{8,9},{9,10},{10,11},{12,13},{... | collective-permute-start | bytes 17288 | tf_op jit(solution)/shard_map/ppermute | solution.py:16
  32.7 11.2 %collective-permute-start.3 = (bf16[96,10,3]{2,1,0:T(8,128)(2,1)S(1)}, bf16[96,10,3]{2,1,0:T(8,128)(2,1)}, u32[]{:S(2)}, u32[]{:S(2)}) collective-permute-start(bf16[96,10,3]{2,1,0:T(8,128)(2,1)S(1)} %get-tuple-element.89), channel_id=1, source_target_pairs={{1,0},{2,1},{3,2},{5,4},{6,5},{7,6},{9,8},{10,9},{11,10},{13,12},{... | collective-permute-start | bytes 17288 | tf_op jit(solution)/shard_map/ppermute | solution.py:17
  41.4 19.7 %copy-start.4 = (f32[12,8,4,256]{3,1,2,0:T(8,128)}, f32[12,8,4,256]{3,1,2,0:T(8,128)S(1)}, u32[]{:S(2)}) copy-start(f32[12,8,4,256]{3,1,2,0:T(8,128)S(1)} %copy.26) | copy-start | bytes 1179652
  42.3 5.2 %copy-start.52 = (f32[96]{0:T(128)S(1)}, f32[96]{0:T(128)}, u32[]{:S(2)}) copy-start(f32[96]{0:T(128)} %get-tuple-element.132) | copy-start | bytes 1156
  42.3 5.2 %copy-start.54 = (f32[96]{0:T(128)S(1)}, f32[96]{0:T(128)}, u32[]{:S(2)}) copy-start(f32[96]{0:T(128)} %get-tuple-element.133) | copy-start | bytes 1156
  42.3 5.2 %copy-start.56 = (f32[96]{0:T(128)S(1)}, f32[96]{0:T(128)}, u32[]{:S(2)}) copy-start(f32[96]{0:T(128)} %get-tuple-element.134) | copy-start | bytes 1156
  42.3 5.2 %copy-start.58 = (f32[96]{0:T(128)S(1)}, f32[96]{0:T(128)}, u32[]{:S(2)}) copy-start(f32[96]{0:T(128)} %get-tuple-element.135) | copy-start | bytes 1156
  42.3 5.2 %copy-start.60 = (f32[96]{0:T(128)S(1)}, f32[96]{0:T(128)}, u32[]{:S(2)}) copy-start(f32[96]{0:T(128)} %get-tuple-element.136) | copy-start | bytes 1156
  42.3 5.2 %copy-start.62 = (f32[96]{0:T(128)S(1)}, f32[96]{0:T(128)}, u32[]{:S(2)}) copy-start(f32[96]{0:T(128)} %get-tuple-element.137) | copy-start | bytes 1156
  42.3 5.2 %copy-start.64 = (f32[96]{0:T(128)S(1)}, f32[96]{0:T(128)}, u32[]{:S(2)}) copy-start(f32[96]{0:T(128)} %get-tuple-element.138) | copy-start | bytes 1156
  42.3 5.2 %copy-start.66 = (f32[96]{0:T(128)S(1)}, f32[96]{0:T(128)}, u32[]{:S(2)}) copy-start(f32[96]{0:T(128)} %get-tuple-element.139) | copy-start | bytes 1156
  42.4 5.2 %copy-start.68 = (f32[96]{0:T(128)S(1)}, f32[96]{0:T(128)}, u32[]{:S(2)}) copy-start(f32[96]{0:T(128)} %get-tuple-element.140) | copy-start | bytes 1156
  42.4 5.2 %copy-start.70 = (f32[96]{0:T(128)S(1)}, f32[96]{0:T(128)}, u32[]{:S(2)}) copy-start(f32[96]{0:T(128)} %get-tuple-element.141) | copy-start | bytes 1156
  42.4 5.2 %copy-start.72 = (f32[96]{0:T(128)S(1)}, f32[96]{0:T(128)}, u32[]{:S(2)}) copy-start(f32[96]{0:T(128)} %get-tuple-element.142) | copy-start | bytes 1156
  42.4 5.2 %copy-start.74 = (f32[96]{0:T(128)S(1)}, f32[96]{0:T(128)}, u32[]{:S(2)}) copy-start(f32[96]{0:T(128)} %get-tuple-element.143) | copy-start | bytes 1156
  42.4 5.2 %copy-start.76 = (f32[96]{0:T(128)S(1)}, f32[96]{0:T(128)}, u32[]{:S(2)}) copy-start(f32[96]{0:T(128)} %get-tuple-element.144) | copy-start | bytes 1156
  42.4 5.2 %copy-start.78 = (f32[96]{0:T(128)S(1)}, f32[96]{0:T(128)}, u32[]{:S(2)}) copy-start(f32[96]{0:T(128)} %get-tuple-element.145) | copy-start | bytes 1156
  42.4 5.2 %copy-start.80 = (f32[96]{0:T(128)S(1)}, f32[96]{0:T(128)}, u32[]{:S(2)}) copy-start(f32[96]{0:T(128)} %get-tuple-element.146) | copy-start | bytes 1156
  42.4 5.2 %copy-start.82 = (f32[96]{0:T(128)S(1)}, f32[96]{0:T(128)}, u32[]{:S(2)}) copy-start(f32[96]{0:T(128)} %get-tuple-element.147) | copy-start | bytes 1156
  42.4 5.2 %copy-start.84 = (f32[96]{0:T(128)S(1)}, f32[96]{0:T(128)}, u32[]{:S(2)}) copy-start(f32[96]{0:T(128)} %get-tuple-element.148) | copy-start | bytes 1156
  42.4 5.2 %copy-start.92 = (f32[96]{0:T(128)S(1)}, f32[96]{0:T(128)}, u32[]{:S(2)}) copy-start(f32[96]{0:T(128)} %param.14) | copy-start | bytes 1156
  47.7 11.9 %copy-start.14 = (f32[96]{0:T(128)S(1)}, f32[96]{0:T(128)}, u32[]{:S(2)}) copy-start(f32[96]{0:T(128)} %param.15) | copy-start | bytes 1156
  47.7 11.9 %copy-start.86 = (f32[96]{0:T(128)S(1)}, f32[96]{0:T(128)}, u32[]{:S(2)}) copy-start(f32[96]{0:T(128)} %param.16) | copy-start | bytes 1156
  84.8 3.7 copy-start.2
  84.8 3.7 copy-start.5
  88.5 12.3 %copy-start.3 = (bf16[384,1024]{0,1:T(8,128)(2,1)S(1)}, bf16[384,1024]{0,1:T(8,128)(2,1)}, u32[]{:S(2)}) copy-start(bf16[384,1024]{0,1:T(8,128)(2,1)} %get-tuple-element.151) | copy-start | bytes 2359300
  88.5 12.3 %copy-start.6 = (f32[12,8,4,256]{3,1,2,0:T(8,128)S(1)}, f32[12,8,4,256]{3,1,2,0:T(8,128)}, u32[]{:S(2)}) copy-start(f32[12,8,4,256]{3,1,2,0:T(8,128)} %copy-done.4) | copy-start | bytes 1179652
  95.5 6.8 %copy-start.87 = (f32[96]{0:T(128)S(1)}, f32[96]{0:T(128)}, u32[]{:S(2)}) copy-start(f32[96]{0:T(128)} %multiply_reduce_fusion.1) | copy-start | bytes 1156
  95.5 6.8 %copy-start.88 = (f32[96]{0:T(128)S(1)}, f32[96]{0:T(128)}, u32[]{:S(2)}) copy-start(f32[96]{0:T(128)} %get-tuple-element.53) | copy-start | bytes 1156
  95.5 6.9 %copy-start.89 = (f32[96]{0:T(128)S(1)}, f32[96]{0:T(128)}, u32[]{:S(2)}) copy-start(f32[96]{0:T(128)} %get-tuple-element.82) | copy-start | bytes 1156
  95.5 6.9 %copy-start.90 = (f32[384]{0:T(512)S(1)}, f32[384]{0:T(512)}, u32[]{:S(2)}) copy-start(f32[384]{0:T(512)} %get-tuple-element.154) | copy-start | bytes 4612
  95.5 110.6 %copy-start.12 = (bf16[96,3,256]{2,1,0:T(4,128)(2,1)S(1)}, bf16[96,3,256]{2,1,0:T(4,128)(2,1)}, u32[]{:S(2)}) copy-start(bf16[96,3,256]{2,1,0:T(4,128)(2,1)} %get-tuple-element.97) | copy-start | bytes 442372
  95.5 112.5 %copy-start.11 = (bf16[96,3,256]{2,1,0:T(4,128)(2,1)S(1)}, bf16[96,3,256]{2,1,0:T(4,128)(2,1)}, u32[]{:S(2)}) copy-start(bf16[96,3,256]{2,1,0:T(4,128)(2,1)} %get-tuple-element.96) | copy-start | bytes 442372
  206.1 15.6 %collective-permute-start.4 = (bf16[96,3,256]{2,1,0:T(4,128)(2,1)S(1)}, bf16[96,3,256]{2,1,0:T(4,128)(2,1)S(1)}, u32[]{:S(2)}, u32[]{:S(2)}) collective-permute-start(bf16[96,3,256]{2,1,0:T(4,128)(2,1)S(1)} %copy-done.12), channel_id=1, source_target_pairs={{0,4},{4,8},{8,12},{12,16},{16,20},{20,24},{24,28},{28,32},{32,36}... | collective-permute-start | bytes 442376 | tf_op jit(solution)/shard_map/ppermute | solution.py:16
  208.1 17.0 %collective-permute-start.5 = (bf16[96,3,256]{2,1,0:T(4,128)(2,1)S(1)}, bf16[96,3,256]{2,1,0:T(4,128)(2,1)S(1)}, u32[]{:S(2)}, u32[]{:S(2)}) collective-permute-start(bf16[96,3,256]{2,1,0:T(4,128)(2,1)S(1)} %copy-done.11), channel_id=1, source_target_pairs={{4,0},{8,4},{12,8},{16,12},{20,16},{24,20},{28,24},{32,28},{36,32}... | collective-permute-start | bytes 442376 | tf_op jit(solution)/shard_map/ppermute | solution.py:17
  225.8 254.3 %collective-permute-start.6 = (bf16[96,10,3]{2,1,0:T(8,128)(2,1)S(1)}, bf16[96,10,3]{2,1,0:T(8,128)(2,1)S(1)}, u32[]{:S(2)}, u32[]{:S(2)}) collective-permute-start(bf16[96,10,3]{2,1,0:T(8,128)(2,1)S(1)} %get-tuple-element.86), channel_id=1, source_target_pairs={{1,0},{2,1},{3,2},{5,4},{6,5},{7,6},{9,8},{10,9},{11,10},{13,12},{... | collective-permute-start | bytes 17288 | tf_op jit(solution)/shard_map/ppermute | solution.py:17
  229.1 251.0 %collective-permute-start.7 = (bf16[96,10,3]{2,1,0:T(8,128)(2,1)S(1)}, bf16[96,10,3]{2,1,0:T(8,128)(2,1)S(1)}, u32[]{:S(2)}, u32[]{:S(2)}) collective-permute-start(bf16[96,10,3]{2,1,0:T(8,128)(2,1)S(1)} %get-tuple-element.87), channel_id=1, source_target_pairs={{0,1},{1,2},{2,3},{4,5},{5,6},{6,7},{8,9},{9,10},{10,11},{12,13},{... | collective-permute-start | bytes 17288 | tf_op jit(solution)/shard_map/ppermute | solution.py:16
  (38 other events, 98.8 us)
Sparse Core Ops, SparseCore 0:
  221.3 256.9 all-reduce.3
where the time goes:
time: 506 us; the launch traced here: 501 us
  waiting for transfers between devices  252 us (50%)
  blocking collectives  101 us (20%)
  other arithmetic  66.2 us (13%)
  starting transfers between devices  43.1 us (9%)
  local copies, waits for them, and re-layouts  15.7 us (3%)
  between operations  15.5 us (3%)
  matrix products  7.76 us (2%)
    psum x1, waiting for transfers between devices, shards(): lax.psum((g_reduce, g_expand, g_ebias, g_kernel, g_dbias, norm_gain_gradi...  248 us
    psum x1, blocking collectives, shards(): lax.psum((g_reduce, g_expand, g_ebias, g_kernel, g_dbias, norm_gain_gradi...  101 us
    ppermute x4, starting transfers between devices, padded_2(): after = lax.ppermute(initial, axis, down)  36.5 us
    reduce_sum x4, other arithmetic, kernel_terms(): entries.append(jnp.sum(piece * convolution_gradient, axis=(1, 2)))  26.3 us
    convert_element_type x1, other arithmetic, shards(): image_grad = (cotangent.astype(jnp.float32) + back).astype(jnp.bfloat16)  11.7 us
    reduce_sum x1, other arithmetic, shards(): average = jnp.mean(flat, axis=0, keepdims=True)  11.5 us
  transfers between devices with their start and end apart: 9, of which 3 were waited for; matrix products, arithmetic and copies ran while one was open for 2% of the time, Pallas kernels for 0%

commit v1 on v0

--- a/solution.py
+++ b/solution.py
@@ -148,47 +148,82 @@
     image_grad = (cotangent.astype(jnp.float32) + back).astype(jnp.bfloat16)
     g_kernel = kernel_terms(padded, d_float, row_count, col_count)
     factor = 1.0 / math.sqrt(tok_count * lax.axis_size("space") * lax.axis_size("filt"))
-    (
-        g_reduce,
-        g_expand,
-        g_ebias,
-        g_kernel,
-        g_dbias,
-        norm_gain_gradient,
-        g_lbias,
-        g_scale,
-        g_rbias,
-    ) = lax.psum(
-        (
-            g_reduce,
-            g_expand,
-            g_ebias,
-            g_kernel,
+    parts = lax.axis_size("filt")
+    panels = jnp.concatenate(
+        [
+            g_reduce.reshape(parts, panel_rows * channels),
+            g_expand.reshape(parts, panel_rows * channels),
+            g_ebias.reshape(parts, panel_rows),
+        ],
+        axis=1,
+    )
+    small = jnp.concatenate(
+        [
+            g_kernel.reshape(-1),
             g_dbias,
             norm_gain_gradient,
             g_lbias,
             g_scale,
             g_rbias,
-        ),
-        ("space", "filt"),
-    )
-    start = lax.axis_index("filt") * panel_rows
-    g_reduce = lax.dynamic_slice_in_dim(g_reduce, start, panel_rows, 0)
-    g_expand = lax.dynamic_slice_in_dim(g_expand, start, panel_rows, 0)
-    g_ebias = lax.dynamic_slice_in_dim(g_ebias, start, panel_rows, 0)
+        ]
+    )
+    panel, small = filt_reduce(panels, small)
+    total = space_butterfly(jnp.concatenate([panel, small]))
+    total = total * factor
+    cut = [panel_rows * channels, panel_rows * channels, panel_rows]
+    g_reduce = total[: cut[0]].reshape(panel_rows, channels)
+    g_expand = total[cut[0] : cut[0] + cut[1]].reshape(panel_rows, channels)
+    g_ebias = total[cut[0] + cut[1] : sum(cut)]
+    rest = total[sum(cut) :]
+    ksq = kernel.shape[1] * kernel.shape[2]
+    g_kernel = rest[: channels * ksq].reshape(kernel.shape)
+    g_dbias, norm_gain_gradient, g_lbias, g_scale, g_rbias = (
+        rest[channels * ksq + channels * i : channels * ksq + channels * (i + 1)]
+        for i in range(5)
+    )
     return (
         output,
         image_grad,
-        g_kernel * factor,
-        g_dbias * factor,
-        norm_gain_gradient * factor,
-        g_lbias * factor,
-        g_expand * factor,
-        g_ebias * factor,
-        g_reduce * factor,
-        g_rbias * factor,
-        g_scale * factor,
-    )
+        g_kernel,
+        g_dbias,
+        norm_gain_gradient,
+        g_lbias,
+        g_expand,
+        g_ebias,
+        g_reduce,
+        g_rbias,
+        g_scale,
+    )
+
+
+def filt_reduce(panels, small):
+    parts = lax.axis_size("filt")
+    me = lax.axis_index("filt")
+    width = panels.shape[1]
+    count = parts
+    bit = parts // 2
+    held = panels
+    while bit >= 1:
+        half = count // 2
+        upper = (me // bit) % 2
+        mine = lax.dynamic_slice_in_dim(held, upper * half, half, 0)
+        other = lax.dynamic_slice_in_dim(held, (1 - upper) * half, half, 0)
+        send = jnp.concatenate([other.reshape(-1), small])
+        got = lax.ppermute(send, "filt", [(i, i ^ bit) for i in range(parts)])
+        held = mine + got[: half * width].reshape(half, width)
+        small = small + got[half * width :]
+        count = half
+        bit //= 2
+    return held.reshape(-1), small
+
+
+def space_butterfly(buf):
+    size = lax.axis_size("space")
+    bit = 1
+    while bit < size:
+        buf = buf + lax.ppermute(buf, "space", [(i, i ^ bit) for i in range(size)])
+        bit *= 2
+    return buf
 
 
 def solution(mesh):

time: 506 us -> 201 us (0.40)
  the two profiles are of different devices: /device:TPU:56 before, /device:TPU:10 now
where the time goes in v1:
time: 201 us; the launch traced here: 200 us
  starting transfers between devices  78.7 us (39%)
  other arithmetic  61.8 us (31%)
  waiting for transfers between devices  25 us (12%)
  local copies, waits for them, and re-layouts  24.4 us (12%)
  matrix products  7.45 us (4%)
  between operations  2.56 us (1%)
    ppermute x7, starting transfers between devices, space_butterfly(): buf = buf + lax.ppermute(buf, 'space', [(i, i ^ bit) for i in range(size)])  39.9 us
    reduce_sum x4, other arithmetic, kernel_terms(): entries.append(jnp.sum(piece * convolution_gradient, axis=(1, 2)))  26.3 us
    ppermute x4, starting transfers between devices, padded_2(): after = lax.ppermute(initial, axis, down)  24.5 us
    convert_element_type x1, other arithmetic, shards(): image_grad = (cotangent.astype(jnp.float32) + back).astype(jnp.bfloat16)  11.7 us
    reduce_sum x1, other arithmetic, shards(): average = jnp.mean(flat, axis=0, keepdims=True)  11.5 us
    ppermute x2, waiting for transfers between devices, filt_reduce(): got = lax.ppermute(send, 'filt', [(i, i ^ bit) for i in range(parts)])  10.7 us
    ppermute x4, starting transfers between devices, padded_2(): before = lax.ppermute(last, axis, up)  9.38 us
    ppermute x7, waiting for transfers between devices, space_butterfly(): buf = buf + lax.ppermute(buf, 'space', [(i, i ^ bit) for i in range(size)])  9.36 us
  transfers between devices with their start and end apart: 17, of which 8 were waited for; matrix products, arithmetic and copies ran while one was open for 12% of the time, Pallas kernels for 0%

profile of v1, /device:TPU:10, one launch (start us, length us, event | category | flops | bytes accessed | tf_op | source)
XLA Modules:
  0.0 199.9 jit_solution(1928865893377018186)
XLA Ops:
  0.7 1.2 fusion.139
  1.9 2.1 %collective-permute-start = (bf16[96,3,256]{2,1,0:T(4,128)(2,1)S(1)}, bf16[96,3,256]{2,1,0:T(4,128)(2,1)S(1)}, u32[]{:S(2)}, u32[]{:S(2)}) collective-permute-start(bf16[96,3,256]{2,1,0:T(4,128)(2,1)S(1)} %get-tuple-element.100), channel_id=1, source_target_pairs={{0,4},{4,8},{8,12},{12,16},{16,20},{20,24},{24,28},{28,32},{32,36}... | collective-permute-start | bytes 442376 | tf_op jit(solution)/shard_map/ppermute | solution.py:16
  4.0 10.4 %collective-permute-start.1 = (bf16[96,3,256]{2,1,0:T(4,128)(2,1)S(1)}, bf16[96,3,256]{2,1,0:T(4,128)(2,1)S(1)}, u32[]{:S(2)}, u32[]{:S(2)}) collective-permute-start(bf16[96,3,256]{2,1,0:T(4,128)(2,1)S(1)} %get-tuple-element.101), channel_id=1, source_target_pairs={{4,0},{8,4},{12,8},{16,12},{20,16},{24,20},{28,24},{32,28},{36,32}... | collective-permute-start | bytes 442376 | tf_op jit(solution)/shard_map/ppermute | solution.py:17
  14.3 1.0 slice_bitcast_fusion.48
  15.4 1.6 slice_bitcast_fusion.47
  17.1 1.5 slice_bitcast_fusion.46
  18.7 1.6 pad_maximum_fusion.2
  20.4 3.5 %collective-permute-start.2 = (bf16[96,10,3]{2,1,0:T(8,128)(2,1)S(1)}, bf16[96,10,3]{2,1,0:T(8,128)(2,1)S(1)}, u32[]{:S(2)}, u32[]{:S(2)}) collective-permute-start(bf16[96,10,3]{2,1,0:T(8,128)(2,1)S(1)} %get-tuple-element.90), channel_id=1, source_target_pairs={{0,1},{1,2},{2,3},{4,5},{5,6},{6,7},{8,9},{9,10},{10,11},{12,13},{... | collective-permute-start | bytes 17288 | tf_op jit(solution)/shard_map/ppermute | solution.py:16
  23.9 2.4 %collective-permute-start.3 = (bf16[96,10,3]{2,1,0:T(8,128)(2,1)S(1)}, bf16[96,10,3]{2,1,0:T(8,128)(2,1)}, u32[]{:S(2)}, u32[]{:S(2)}) collective-permute-start(bf16[96,10,3]{2,1,0:T(8,128)(2,1)S(1)} %get-tuple-element.91), channel_id=1, source_target_pairs={{1,0},{2,1},{3,2},{5,4},{6,5},{7,6},{9,8},{10,9},{11,10},{13,12},{... | collective-permute-start | bytes 17288 | tf_op jit(solution)/shard_map/ppermute | solution.py:17
  26.3 1.4 multiply_reduce_fusion
  27.8 0.9 copy.28
  28.9 1.2 collective-permute-done.2
  30.1 0.7 copy-done.12
  30.8 2.9 %collective-permute-done.3 = bf16[96,10,3]{2,1,0:T(8,128)(2,1)} collective-permute-done((bf16[96,10,3]{2,1,0:T(8,128)(2,1)S(1)}, bf16[96,10,3]{2,1,0:T(8,128)(2,1)}, u32[]{:S(2)}, u32[]{:S(2)}) %collective-permute-start.3) | collective-permute-done | bytes 5792 | tf_op jit(solution)/shard_map/ppermute | solution.py:17
  33.7 3.4 %maximum_maximum_fusion = (bf16[96,10,259]{2,1,0:T(8,128)(2,1)S(1)}, bf16[96,10,259]{2,1,0:T(8,128)(2,1)S(1)}) fusion(bf16[96,3,256]{2,1,0:T(4,128)(2,1)S(1)} %collective-permute-done.1, bf16[96,4,256]{2,1,0:T(4,128)(2,1)S(1)} %copy-done.1, bf16[96,3,256]{2,1,0:T(4,128)(2,1)S(1)} %collective-permute-done, bf16[96,10,3]{2,1,0:T(8,128)(2,1)} %copy-done.12, ...), kind=kLoop, calls=%fused_computation.67 | loop fusion | flops 3978240 | bytes 1497600 | tf_op jit(solution)/shard_map/concatenate | solution.py:18
  37.5 11.5 %fusion.134 = (f32[4,256]{1,0:T(4,128)S(1)}, f32[96,4,256]{2,1,0:T(4,128)S(1)}) fusion(f32[96]{0:T(128)S(1)} %copy-done.94, bf16[96,10,259]{2,1,0:T(8,128)(2,1)S(1)} %get-tuple-element.95, f32[96]{0:T(128)S(1)} %copy-done.87, f32[96]{0:T(128)S(1)} %copy-done.89, f32[96]{0:T(128)S(1)} %get-tuple-element.111, ...), kind=kLoop, calls=%fused_computation.349 | loop fusion | flops 16317440 | bytes 9165568 | tf_op jit(solution)/shard_map/reduce_sum | solution.py:89
  49.3 1.5 fusion.9
  50.9 1.5 convert_reduce_fusion
  52.4 1.1 fusion.133
  54.0 0.9 convert_reduce_fusion.1
  54.9 1.1 reshape.137
  56.0 7.8 %fusion.115 = (f32[96]{0:T(128)}, f32[96]{0:T(128)}, f32[96]{0:T(128)}, f32[96]{0:T(128)}, f32[96]{0:T(128)}, /*index=5*/f32[96]{0:T(128)}, f32[96]{0:T(128)}, f...) fusion(bf16[96,4,256]{2,1,0:T(4,128)(2,1)S(1)} %reshape.137, ...), kind=kLoop, calls=%fused_computation.241 | loop fusion | flops 5404992 | bytes 3742464 | tf_op jit(solution)/shard_map/reduce_sum | solution.py:54
  63.8 9.8 %fusion.119 = (f32[96]{0:T(128)}, f32[96]{0:T(128)}, f32[96]{0:T(128)}, f32[96]{0:T(128)}, f32[96]{0:T(128)}, /*index=5*/f32[96]{0:T(128)}, f32[96]{0:T(128)}, f...) fusion(bf16[96,4,256]{2,1,0:T(4,128)(2,1)S(1)} %reshape.137, ...), kind=kLoop, calls=%fused_computation.245 | loop fusion | flops 5404992 | bytes 3742464 | tf_op jit(solution)/shard_map/reduce_sum | solution.py:54
  73.5 2.9 %fusion.73 = (f32[96]{0:T(128)}, f32[96]{0:T(128)}, f32[96]{0:T(128)}) fusion(bf16[96,4,256]{2,1,0:T(4,128)(2,1)S(1)} %reshape.137, bf16[96,10,259]{2,1,0:T(8,128)(2,1)S(1)} %get-tuple-element.94), kind=kLoop, calls=%fused_computation.199 | loop fusion | flops 982752 | bytes 787584 | tf_op jit(solution)/shard_map/reduce_sum | solution.py:54
  76.5 1.1 reshape.139
  77.6 1.7 fusion.132
  79.6 0.7 copy-done.9
  80.3 0.7 constant_dynamic-slice_fusion
  81.0 1.8 reshape.141
  82.9 5.9 %fusion.118 = (f32[96]{0:T(128)}, f32[96]{0:T(128)}, f32[96]{0:T(128)}, f32[96]{0:T(128)}, f32[96]{0:T(128)}, /*index=5*/f32[96]{0:T(128)}, f32[96]{0:T(128)}, f32[96]{0:T(128)}, f32[96]{0:T(128)}, f32[96]{0:T(128)}) fusion(bf16[96,4,256]{2,1,0:T(4,128)(2,1)S(1)} %reshape.137, bf16[96,10,259]{2,1,0:T(8,128)(2,1)S(1)} %get-tuple-element.95, ...), kind=kLoop, calls=%fused_computation.244 | loop fusion | flops 4815936 | bytes 1281792 | tf_op jit(solution)/shard_map/reduce_sum | solution.py:54
  88.7 0.8 stack.199
  89.5 0.7 stack.208
  90.2 0.7 stack.217
  90.9 0.7 stack.226
  91.7 0.7 stack.235
  92.4 0.7 stack.244
  93.1 0.7 stack.253
  94.5 1.1 multiply_reduce_fusion.1
  95.7 2.4 %collective-permute-start.8 = (f32[42240]{0:T(1024)S(1)}, f32[42240]{0:T(1024)S(1)}, u32[]{:S(2)}, u32[]{:S(2)}) collective-permute-start(f32[42240]{0:T(1024)S(1)} %concatenate.147), channel_id=1, source_target_pairs={{0,2},{1,3},{2,0},{3,1},{4,6},{5,7},{6,4},{7,5},{8,10},{9,11},{10,... | collective-permute-start | bytes 506888 | tf_op jit(solution)/shard_map/ppermute | solution.py:212
  98.2 6.8 %collective-permute-done.8 = f32[42240]{0:T(1024)S(1)} collective-permute-done((f32[42240]{0:T(1024)S(1)}, f32[42240]{0:T(1024)S(1)}, u32[]{:S(2)}, u32[]{:S(2)}) %collective-permute-start.8) | collective-permute-done | bytes 168992 | tf_op jit(solution)/shard_map/ppermute | solution.py:212
  105.6 2.5 %collective-permute-start.9 = (f32[23712]{0:T(1024)S(1)}, f32[23712]{0:T(1024)S(1)}, u32[]{:S(2)}, u32[]{:S(2)}) collective-permute-start(f32[23712]{0:T(1024)S(1)} %pad_maximum_fusion.8), channel_id=1, source_target_pairs={{0,1},{1,0},{2,3},{3,2},{4,5},{5,4},{6,7},{7,6},{8,9},{9,8},{10,11... | collective-permute-start | bytes 284552 | tf_op jit(solution)/shard_map/ppermute | solution.py:212
  108.2 4.0 %collective-permute-done.9 = f32[23712]{0:T(1024)S(1)} collective-permute-done((f32[23712]{0:T(1024)S(1)}, f32[23712]{0:T(1024)S(1)}, u32[]{:S(2)}, u32[]{:S(2)}) %collective-permute-start.9) | collective-permute-done | bytes 94880 | tf_op jit(solution)/shard_map/ppermute | solution.py:212
  112.5 1.9 collective-permute-start.10
  114.5 1.3 collective-permute-done.10
  115.8 3.6 %collective-permute-start.11 = (f32[23712]{0:T(1024)S(1)}, f32[23712]{0:T(1024)S(1)}, u32[]{:S(2)}, u32[]{:S(2)}) collective-permute-start(f32[23712]{0:T(1024)S(1)} %fusion.150), channel_id=1, source_target_pairs={{0,8},{4,12},{8,0},{12,4},{16,24},{20,28},{24,16},{28,20},{32,40},... | collective-permute-start | bytes 284552 | tf_op jit(solution)/shard_map/ppermute | solution.py:224
  119.6 1.9 collective-permute-start.4
  121.5 7.8 %collective-permute-start.5 = (bf16[96,3,256]{2,1,0:T(4,128)(2,1)S(1)}, bf16[96,3,256]{2,1,0:T(4,128)(2,1)S(1)}, u32[]{:S(2)}, u32[]{:S(2)}) collective-permute-start(bf16[96,3,256]{2,1,0:T(4,128)(2,1)S(1)} %get-tuple-element.98), channel_id=1, source_target_pairs={{4,0},{8,4},{12,8},{16,12},{20,16},{24,20},{28,24},{32,28},{36,32}... | collective-permute-start | bytes 442376 | tf_op jit(solution)/shard_map/ppermute | solution.py:17
  129.4 1.9 collective-permute-start.12
  131.3 5.5 %collective-permute-done.12 = f32[23712]{0:T(1024)S(1)} collective-permute-done((f32[23712]{0:T(1024)S(1)}, f32[23712]{0:T(1024)S(1)}, u32[]{:S(2)}, u32[]{:S(2)}) %collective-permute-start.12) | collective-permute-done | bytes 94880 | tf_op jit(solution)/shard_map/ppermute | solution.py:224
  136.8 8.1 %collective-permute-start.13 = (f32[23712]{0:T(1024)S(1)}, f32[23712]{0:T(1024)S(1)}, u32[]{:S(2)}, u32[]{:S(2)}) collective-permute-start(f32[23712]{0:T(1024)S(1)} %add.530), channel_id=1, source_target_pairs={{0,32},{4,36},{8,40},{12,44},{16,48},{20,52},{24,56},{28,60},{32,0... | collective-permute-start | bytes 284552 | tf_op jit(solution)/shard_map/ppermute | solution.py:224
  145.5 2.6 %collective-permute-done.13 = f32[23712]{0:T(1024)S(1)} collective-permute-done((f32[23712]{0:T(1024)S(1)}, f32[23712]{0:T(1024)S(1)}, u32[]{:S(2)}, u32[]{:S(2)}) %collective-permute-start.13) | collective-permute-done | bytes 94880 | tf_op jit(solution)/shard_map/ppermute | solution.py:224
  148.1 2.4 %collective-permute-start.14 = (f32[23712]{0:T(1024)S(1)}, f32[23712]{0:T(1024)S(1)}, u32[]{:S(2)}, u32[]{:S(2)}) collective-permute-start(f32[23712]{0:T(1024)S(1)} %add.531), channel_id=1, source_target_pairs={{0,64},{4,68},{8,72},{12,76},{16,80},{20,84},{24,88},{28,92},{32,9... | collective-permute-start | bytes 284552 | tf_op jit(solution)/shard_map/ppermute | solution.py:224
  150.7 3.9 %collective-permute-start.6 = (bf16[96,10,3]{2,1,0:T(8,128)(2,1)S(1)}, bf16[96,10,3]{2,1,0:T(8,128)(2,1)S(1)}, u32[]{:S(2)}, u32[]{:S(2)}) collective-permute-start(bf16[96,10,3]{2,1,0:T(8,128)(2,1)S(1)} %get-tuple-element.88), channel_id=1, source_target_pairs={{1,0},{2,1},{3,2},{5,4},{6,5},{7,6},{9,8},{10,9},{11,10},{13,12},{... | collective-permute-start | bytes 17288 | tf_op jit(solution)/shard_map/ppermute | solution.py:17
  154.7 1.9 collective-permute-start.7
  156.6 0.8 reshape.136
  157.8 5.0 %collective-permute-start.15 = (f32[23712]{0:T(1024)S(1)}, f32[23712]{0:T(1024)S(1)}, u32[]{:S(2)}, u32[]{:S(2)}) collective-permute-start(f32[23712]{0:T(1024)S(1)} %add.532), channel_id=1, source_target_pairs={{0,128},{4,132},{8,136},{12,140},{16,144},{20,148},{24,152},{28,15... | collective-permute-start | bytes 284552 | tf_op jit(solution)/shard_map/ppermute | solution.py:224
  162.9 0.7 copy-done.13
  163.6 0.8 collective-permute-done.7
  164.4 3.4 %pad_maximum_fusion.1 = (bf16[96,10,259]{2,1,0:T(8,128)(2,1)S(1)}, bf16[96,10,259]{2,1,0:T(8,128)(2,1)S(1)}) fusion(bf16[96,10,3]{2,1,0:T(8,128)(2,1)} %copy-done.13, bf16[96,3,256]{2,1,0:T(4,128)(2,1)S(1)} %collective-permute-done.5, bf16[96,4,256]{2,1,0:T(4,128)(2,1)S(1)} %reshape.137, bf16[96,3,256]{2,1,0:T(4,128)(2,1)S(1)} %collective-permute-done.4, ...), kind=kLoop, calls=%fused_computation.69 | loop fusion | flops 3978240 | bytes 1497600 | tf_op jit(solution)/shard_map/concatenate | solution.py:18
  167.9 16.8 %collective-permute-start.16 = (f32[23712]{0:T(1024)S(1)}, f32[23712]{0:T(1024)S(1)}, u32[]{:S(2)}, u32[]{:S(2)}) collective-permute-start(f32[23712]{0:T(1024)S(1)} %add.533), channel_id=1, source_target_pairs={{0,256},{4,260},{8,264},{12,268},{16,272},{20,276},{24,280},{28,28... | collective-permute-start | bytes 284552 | tf_op jit(solution)/shard_map/ppermute | solution.py:224
  185.1 11.7 %add_convert_fusion = bf16[96,4,256]{2,1,0:T(4,128)(2,1)} fusion(bf16[96,4,256]{2,1,0:T(4,128)(2,1)S(1)} %reshape.137, bf16[96,3,256]{2,1,0:T(4,128)(2,1)S(1)} %collective-permute-done.4, bf16[96,3,256]{2,1,0:T(4,128)(2,1)S(1)} %collective-permute-done.5, bf16[96,10,259]{2,1,0:T(8,128)(2,1)S(1)} %get-tuple-element.93, ...), kind=kLoop, calls=%fused_computation.252 | loop fusion | flops 16416768 | bytes 9161088 | tf_op jit(solution)/shard_map/convert_element_type | solution.py:148
  197.7 0.8 copy.25
  198.5 0.7 slice.880
  199.2 0.7 slice.883
  (248 shorter events, 5.4 us)
Async XLA Ops:
  0.6 48.7 %copy-start = (bf16[384,96]{0,1:T(8,128)(2,1)S(1)}, bf16[384,96]{0,1:T(8,128)(2,1)}, u32[]{:S(2)}) copy-start(bf16[384,96]{0,1:T(8,128)(2,1)} %param.17) | copy-start | bytes 221188
  1.9 24.4 %copy-start.6 = (bf16[96,4,256]{2,1,0:T(4,128)(2,1)S(1)}, bf16[96,4,256]{2,1,0:T(4,128)(2,1)}, u32[]{:S(2)}) copy-start(bf16[96,4,256]{2,1,0:T(4,128)(2,1)} %param.12) | copy-start | bytes 589828
  1.9 24.4 %copy-start.16 = (f32[96]{0:T(128)S(1)}, f32[96]{0:T(128)}, u32[]{:S(2)}) copy-start(f32[96]{0:T(128)} %param.21) | copy-start | bytes 1156
  1.9 16.7 %collective-permute-start = (bf16[96,3,256]{2,1,0:T(4,128)(2,1)S(1)}, bf16[96,3,256]{2,1,0:T(4,128)(2,1)S(1)}, u32[]{:S(2)}, u32[]{:S(2)}) collective-permute-start(bf16[96,3,256]{2,1,0:T(4,128)(2,1)S(1)} %get-tuple-element.100), channel_id=1, source_target_pairs={{0,4},{4,8},{8,12},{12,16},{16,20},{20,24},{24,28},{28,32},{32,36}... | collective-permute-start | bytes 442376 | tf_op jit(solution)/shard_map/ppermute | solution.py:16
  4.0 14.7 %collective-permute-start.1 = (bf16[96,3,256]{2,1,0:T(4,128)(2,1)S(1)}, bf16[96,3,256]{2,1,0:T(4,128)(2,1)S(1)}, u32[]{:S(2)}, u32[]{:S(2)}) collective-permute-start(bf16[96,3,256]{2,1,0:T(4,128)(2,1)S(1)} %get-tuple-element.101), channel_id=1, source_target_pairs={{4,0},{8,4},{12,8},{16,12},{20,16},{24,20},{28,24},{32,28},{36,32}... | collective-permute-start | bytes 442376 | tf_op jit(solution)/shard_map/ppermute | solution.py:17
  15.3 21.8 %copy-start.17 = (f32[96]{0:T(128)}, f32[96]{0:T(128)S(1)}, u32[]{:S(2)}) copy-start(f32[96]{0:T(128)S(1)} %get-tuple-element.122) | copy-start | bytes 1156
  15.3 21.8 %copy-start.19 = (f32[96]{0:T(128)}, f32[96]{0:T(128)S(1)}, u32[]{:S(2)}) copy-start(f32[96]{0:T(128)S(1)} %get-tuple-element.123) | copy-start | bytes 1156
  15.3 21.8 %copy-start.21 = (f32[96]{0:T(128)}, f32[96]{0:T(128)S(1)}, u32[]{:S(2)}) copy-start(f32[96]{0:T(128)S(1)} %get-tuple-element.124) | copy-start | bytes 1156
  15.3 21.8 %copy-start.23 = (f32[96]{0:T(128)}, f32[96]{0:T(128)S(1)}, u32[]{:S(2)}) copy-start(f32[96]{0:T(128)S(1)} %get-tuple-element.125) | copy-start | bytes 1156
  15.4 21.8 %copy-start.25 = (f32[96]{0:T(128)}, f32[96]{0:T(128)S(1)}, u32[]{:S(2)}) copy-start(f32[96]{0:T(128)S(1)} %get-tuple-element.126) | copy-start | bytes 1156
  20.4 9.7 %collective-permute-start.2 = (bf16[96,10,3]{2,1,0:T(8,128)(2,1)S(1)}, bf16[96,10,3]{2,1,0:T(8,128)(2,1)S(1)}, u32[]{:S(2)}, u32[]{:S(2)}) collective-permute-start(bf16[96,10,3]{2,1,0:T(8,128)(2,1)S(1)} %get-tuple-element.90), channel_id=1, source_target_pairs={{0,1},{1,2},{2,3},{4,5},{5,6},{6,7},{8,9},{9,10},{10,11},{12,13},{... | collective-permute-start | bytes 17288 | tf_op jit(solution)/shard_map/ppermute | solution.py:16
  23.9 9.8 %collective-permute-start.3 = (bf16[96,10,3]{2,1,0:T(8,128)(2,1)S(1)}, bf16[96,10,3]{2,1,0:T(8,128)(2,1)}, u32[]{:S(2)}, u32[]{:S(2)}) collective-permute-start(bf16[96,10,3]{2,1,0:T(8,128)(2,1)S(1)} %get-tuple-element.91), channel_id=1, source_target_pairs={{1,0},{2,1},{3,2},{5,4},{6,5},{7,6},{9,8},{10,9},{11,10},{13,12},{... | collective-permute-start | bytes 17288 | tf_op jit(solution)/shard_map/ppermute | solution.py:17
  27.8 23.1 %copy-start.3 = (f32[12,8,4,256]{3,1,2,0:T(8,128)}, f32[12,8,4,256]{3,1,2,0:T(8,128)S(1)}, u32[]{:S(2)}) copy-start(f32[12,8,4,256]{3,1,2,0:T(8,128)S(1)} %copy.32) | copy-start | bytes 1179652
  95.7 9.3 %collective-permute-start.8 = (f32[42240]{0:T(1024)S(1)}, f32[42240]{0:T(1024)S(1)}, u32[]{:S(2)}, u32[]{:S(2)}) collective-permute-start(f32[42240]{0:T(1024)S(1)} %concatenate.147), channel_id=1, source_target_pairs={{0,2},{1,3},{2,0},{3,1},{4,6},{5,7},{6,4},{7,5},{8,10},{9,11},{10,... | collective-permute-start | bytes 506888 | tf_op jit(solution)/shard_map/ppermute | solution.py:212
  105.6 6.5 %collective-permute-start.9 = (f32[23712]{0:T(1024)S(1)}, f32[23712]{0:T(1024)S(1)}, u32[]{:S(2)}, u32[]{:S(2)}) collective-permute-start(f32[23712]{0:T(1024)S(1)} %pad_maximum_fusion.8), channel_id=1, source_target_pairs={{0,1},{1,0},{2,3},{3,2},{4,5},{5,4},{6,7},{7,6},{8,9},{9,8},{10,11... | collective-permute-start | bytes 284552 | tf_op jit(solution)/shard_map/ppermute | solution.py:212
  112.5 3.2 %collective-permute-start.10 = (f32[23712]{0:T(1024)S(1)}, f32[23712]{0:T(1024)S(1)}, u32[]{:S(2)}, u32[]{:S(2)}) collective-permute-start(f32[23712]{0:T(1024)S(1)} %pad_maximum_fusion.9), channel_id=1, source_target_pairs={{0,4},{4,0},{8,12},{12,8},{16,20},{20,16},{24,28},{28,24},{32,36},... | collective-permute-start | bytes 284552 | tf_op jit(solution)/shard_map/ppermute | solution.py:224
  115.8 13.6 %collective-permute-start.11 = (f32[23712]{0:T(1024)S(1)}, f32[23712]{0:T(1024)S(1)}, u32[]{:S(2)}, u32[]{:S(2)}) collective-permute-start(f32[23712]{0:T(1024)S(1)} %fusion.150), channel_id=1, source_target_pairs={{0,8},{4,12},{8,0},{12,4},{16,24},{20,28},{24,16},{28,20},{32,40},... | collective-permute-start | bytes 284552 | tf_op jit(solution)/shard_map/ppermute | solution.py:224
  119.6 25.4 %collective-permute-start.4 = (bf16[96,3,256]{2,1,0:T(4,128)(2,1)S(1)}, bf16[96,3,256]{2,1,0:T(4,128)(2,1)S(1)}, u32[]{:S(2)}, u32[]{:S(2)}) collective-permute-start(bf16[96,3,256]{2,1,0:T(4,128)(2,1)S(1)} %get-tuple-element.99), channel_id=1, source_target_pairs={{0,4},{4,8},{8,12},{12,16},{16,20},{20,24},{24,28},{28,32},{32,36}... | collective-permute-start | bytes 442376 | tf_op jit(solution)/shard_map/ppermute | solution.py:16
  121.5 23.4 %collective-permute-start.5 = (bf16[96,3,256]{2,1,0:T(4,128)(2,1)S(1)}, bf16[96,3,256]{2,1,0:T(4,128)(2,1)S(1)}, u32[]{:S(2)}, u32[]{:S(2)}) collective-permute-start(bf16[96,3,256]{2,1,0:T(4,128)(2,1)S(1)} %get-tuple-element.98), channel_id=1, source_target_pairs={{4,0},{8,4},{12,8},{16,12},{20,16},{24,20},{28,24},{32,28},{36,32}... | collective-permute-start | bytes 442376 | tf_op jit(solution)/shard_map/ppermute | solution.py:17
  129.4 7.4 %collective-permute-start.12 = (f32[23712]{0:T(1024)S(1)}, f32[23712]{0:T(1024)S(1)}, u32[]{:S(2)}, u32[]{:S(2)}) collective-permute-start(f32[23712]{0:T(1024)S(1)} %add.529), channel_id=1, source_target_pairs={{0,16},{4,20},{8,24},{12,28},{16,0},{20,4},{24,8},{28,12},{32,48},... | collective-permute-start | bytes 284552 | tf_op jit(solution)/shard_map/ppermute | solution.py:224
  136.8 11.2 %collective-permute-start.13 = (f32[23712]{0:T(1024)S(1)}, f32[23712]{0:T(1024)S(1)}, u32[]{:S(2)}, u32[]{:S(2)}) collective-permute-start(f32[23712]{0:T(1024)S(1)} %add.530), channel_id=1, source_target_pairs={{0,32},{4,36},{8,40},{12,44},{16,48},{20,52},{24,56},{28,60},{32,0... | collective-permute-start | bytes 284552 | tf_op jit(solution)/shard_map/ppermute | solution.py:224
  148.1 9.3 %collective-permute-start.14 = (f32[23712]{0:T(1024)S(1)}, f32[23712]{0:T(1024)S(1)}, u32[]{:S(2)}, u32[]{:S(2)}) collective-permute-start(f32[23712]{0:T(1024)S(1)} %add.531), channel_id=1, source_target_pairs={{0,64},{4,68},{8,72},{12,76},{16,80},{20,84},{24,88},{28,92},{32,9... | collective-permute-start | bytes 284552 | tf_op jit(solution)/shard_map/ppermute | solution.py:224
  150.7 12.1 %collective-permute-start.6 = (bf16[96,10,3]{2,1,0:T(8,128)(2,1)S(1)}, bf16[96,10,3]{2,1,0:T(8,128)(2,1)S(1)}, u32[]{:S(2)}, u32[]{:S(2)}) collective-permute-start(bf16[96,10,3]{2,1,0:T(8,128)(2,1)S(1)} %get-tuple-element.88), channel_id=1, source_target_pairs={{1,0},{2,1},{3,2},{5,4},{6,5},{7,6},{9,8},{10,9},{11,10},{13,12},{... | collective-permute-start | bytes 17288 | tf_op jit(solution)/shard_map/ppermute | solution.py:17
  154.7 9.8 %collective-permute-start.7 = (bf16[96,10,3]{2,1,0:T(8,128)(2,1)S(1)}, bf16[96,10,3]{2,1,0:T(8,128)(2,1)}, u32[]{:S(2)}, u32[]{:S(2)}) collective-permute-start(bf16[96,10,3]{2,1,0:T(8,128)(2,1)S(1)} %get-tuple-element.89), channel_id=1, source_target_pairs={{0,1},{1,2},{2,3},{4,5},{5,6},{6,7},{8,9},{9,10},{10,11},{12,13},{... | collective-permute-start | bytes 17288 | tf_op jit(solution)/shard_map/ppermute | solution.py:16
  157.4 27.3 %copy-start.7 = (bf16[96,4,256]{2,1,0:T(4,128)(2,1)S(1)}, bf16[96,4,256]{2,1,0:T(4,128)(2,1)}, u32[]{:S(2)}) copy-start(bf16[96,4,256]{2,1,0:T(4,128)(2,1)} %param.12) | copy-start | bytes 589828
  157.4 27.3 %copy-start.18 = (f32[96]{0:T(128)S(1)}, f32[96]{0:T(128)}, u32[]{:S(2)}) copy-start(f32[96]{0:T(128)} %copy-done.17) | copy-start | bytes 1156
  157.5 27.3 %copy-start.20 = (f32[96]{0:T(128)S(1)}, f32[96]{0:T(128)}, u32[]{:S(2)}) copy-start(f32[96]{0:T(128)} %copy-done.19) | copy-start | bytes 1156
  157.5 27.3 %copy-start.22 = (f32[96]{0:T(128)S(1)}, f32[96]{0:T(128)}, u32[]{:S(2)}) copy-start(f32[96]{0:T(128)} %copy-done.21) | copy-start | bytes 1156
  157.5 27.3 %copy-start.24 = (f32[96]{0:T(128)S(1)}, f32[96]{0:T(128)}, u32[]{:S(2)}) copy-start(f32[96]{0:T(128)} %copy-done.23) | copy-start | bytes 1156
  157.5 27.3 %copy-start.26 = (f32[96]{0:T(128)S(1)}, f32[96]{0:T(128)}, u32[]{:S(2)}) copy-start(f32[96]{0:T(128)} %copy-done.25) | copy-start | bytes 1156
  157.5 27.3 %copy-start.28 = (f32[96]{0:T(128)S(1)}, f32[96]{0:T(128)}, u32[]{:S(2)}) copy-start(f32[96]{0:T(128)} %copy-done.27) | copy-start | bytes 1156
  157.5 27.3 %copy-start.30 = (f32[96]{0:T(128)S(1)}, f32[96]{0:T(128)}, u32[]{:S(2)}) copy-start(f32[96]{0:T(128)} %copy-done.29) | copy-start | bytes 1156
  157.5 27.3 %copy-start.32 = (f32[96]{0:T(128)S(1)}, f32[96]{0:T(128)}, u32[]{:S(2)}) copy-start(f32[96]{0:T(128)} %copy-done.31) | copy-start | bytes 1156
  157.5 27.3 %copy-start.34 = (f32[96]{0:T(128)S(1)}, f32[96]{0:T(128)}, u32[]{:S(2)}) copy-start(f32[96]{0:T(128)} %copy-done.33) | copy-start | bytes 1156
  157.5 27.3 %copy-start.36 = (f32[96]{0:T(128)S(1)}, f32[96]{0:T(128)}, u32[]{:S(2)}) copy-start(f32[96]{0:T(128)} %copy-done.35) | copy-start | bytes 1156
  157.5 27.3 %copy-start.38 = (f32[96]{0:T(128)S(1)}, f32[96]{0:T(128)}, u32[]{:S(2)}) copy-start(f32[96]{0:T(128)} %copy-done.37) | copy-start | bytes 1156
  157.6 27.3 %copy-start.40 = (f32[96]{0:T(128)S(1)}, f32[96]{0:T(128)}, u32[]{:S(2)}) copy-start(f32[96]{0:T(128)} %copy-done.39) | copy-start | bytes 1156
  157.6 27.3 %copy-start.42 = (f32[96]{0:T(128)S(1)}, f32[96]{0:T(128)}, u32[]{:S(2)}) copy-start(f32[96]{0:T(128)} %copy-done.41) | copy-start | bytes 1156
  157.6 27.3 %copy-start.44 = (f32[96]{0:T(128)S(1)}, f32[96]{0:T(128)}, u32[]{:S(2)}) copy-start(f32[96]{0:T(128)} %copy-done.43) | copy-start | bytes 1156
  157.6 27.3 %copy-start.46 = (f32[96]{0:T(128)S(1)}, f32[96]{0:T(128)}, u32[]{:S(2)}) copy-start(f32[96]{0:T(128)} %copy-done.45) | copy-start | bytes 1156
  157.6 27.3 %copy-start.48 = (f32[96]{0:T(128)S(1)}, f32[96]{0:T(128)}, u32[]{:S(2)}) copy-start(f32[96]{0:T(128)} %copy-done.47) | copy-start | bytes 1156
  157.6 27.3 %copy-start.50 = (f32[96]{0:T(128)S(1)}, f32[96]{0:T(128)}, u32[]{:S(2)}) copy-start(f32[96]{0:T(128)} %copy-done.49) | copy-start | bytes 1156
  157.6 27.3 %copy-start.52 = (f32[96]{0:T(128)S(1)}, f32[96]{0:T(128)}, u32[]{:S(2)}) copy-start(f32[96]{0:T(128)} %copy-done.51) | copy-start | bytes 1156
  157.6 27.3 %copy-start.54 = (f32[96]{0:T(128)S(1)}, f32[96]{0:T(128)}, u32[]{:S(2)}) copy-start(f32[96]{0:T(128)} %copy-done.53) | copy-start | bytes 1156
  157.6 27.3 %copy-start.56 = (f32[96]{0:T(128)S(1)}, f32[96]{0:T(128)}, u32[]{:S(2)}) copy-start(f32[96]{0:T(128)} %get-tuple-element.141) | copy-start | bytes 1156
  157.6 27.3 %copy-start.58 = (f32[96]{0:T(128)S(1)}, f32[96]{0:T(128)}, u32[]{:S(2)}) copy-start(f32[96]{0:T(128)} %get-tuple-element.142) | copy-start | bytes 1156
  157.7 27.3 %copy-start.60 = (f32[96]{0:T(128)S(1)}, f32[96]{0:T(128)}, u32[]{:S(2)}) copy-start(f32[96]{0:T(128)} %get-tuple-element.143) | copy-start | bytes 1156
  157.7 27.3 %copy-start.62 = (f32[96]{0:T(128)S(1)}, f32[96]{0:T(128)}, u32[]{:S(2)}) copy-start(f32[96]{0:T(128)} %get-tuple-element.144) | copy-start | bytes 1156
  157.7 27.3 %copy-start.64 = (f32[96]{0:T(128)S(1)}, f32[96]{0:T(128)}, u32[]{:S(2)}) copy-start(f32[96]{0:T(128)} %get-tuple-element.145) | copy-start | bytes 1156
  157.7 27.3 %copy-start.66 = (f32[96]{0:T(128)S(1)}, f32[96]{0:T(128)}, u32[]{:S(2)}) copy-start(f32[96]{0:T(128)} %get-tuple-element.146) | copy-start | bytes 1156
  157.7 27.3 %copy-start.68 = (f32[96]{0:T(128)S(1)}, f32[96]{0:T(128)}, u32[]{:S(2)}) copy-start(f32[96]{0:T(128)} %get-tuple-element.147) | copy-start | bytes 1156
  157.7 27.3 %copy-start.70 = (f32[96]{0:T(128)S(1)}, f32[96]{0:T(128)}, u32[]{:S(2)}) copy-start(f32[96]{0:T(128)} %get-tuple-element.148) | copy-start | bytes 1156
  157.7 27.3 %copy-start.72 = (f32[96]{0:T(128)S(1)}, f32[96]{0:T(128)}, u32[]{:S(2)}) copy-start(f32[96]{0:T(128)} %get-tuple-element.149) | copy-start | bytes 1156
  157.7 27.3 %copy-start.74 = (f32[96]{0:T(128)S(1)}, f32[96]{0:T(128)}, u32[]{:S(2)}) copy-start(f32[96]{0:T(128)} %get-tuple-element.150) | copy-start | bytes 1156
  157.7 27.3 %copy-start.76 = (f32[96]{0:T(128)S(1)}, f32[96]{0:T(128)}, u32[]{:S(2)}) copy-start(f32[96]{0:T(128)} %get-tuple-element.151) | copy-start | bytes 1156
  157.7 27.3 %copy-start.78 = (f32[96]{0:T(128)S(1)}, f32[96]{0:T(128)}, u32[]{:S(2)}) copy-start(f32[96]{0:T(128)} %get-tuple-element.152) | copy-start | bytes 1156
  157.8 27.3 %copy-start.80 = (f32[96]{0:T(128)S(1)}, f32[96]{0:T(128)}, u32[]{:S(2)}) copy-start(f32[96]{0:T(128)} %get-tuple-element.153) | copy-start | bytes 1156
  157.8 27.3 %copy-start.82 = (f32[96]{0:T(128)S(1)}, f32[96]{0:T(128)}, u32[]{:S(2)}) copy-start(f32[96]{0:T(128)} %get-tuple-element.154) | copy-start | bytes 1156
  157.8 27.3 %copy-start.84 = (f32[96]{0:T(128)S(1)}, f32[96]{0:T(128)}, u32[]{:S(2)}) copy-start(f32[96]{0:T(128)} %get-tuple-element.155) | copy-start | bytes 1156
  157.8 27.3 %copy-start.86 = (f32[96]{0:T(128)S(1)}, f32[96]{0:T(128)}, u32[]{:S(2)}) copy-start(f32[96]{0:T(128)} %get-tuple-element.156) | copy-start | bytes 1156
  157.8 27.3 %copy-start.88 = (f32[96]{0:T(128)S(1)}, f32[96]{0:T(128)}, u32[]{:S(2)}) copy-start(f32[96]{0:T(128)} %get-tuple-element.157) | copy-start | bytes 1156
  157.8 27.3 %copy-start.90 = (f32[96]{0:T(128)S(1)}, f32[96]{0:T(128)}, u32[]{:S(2)}) copy-start(f32[96]{0:T(128)} %get-tuple-element.158) | copy-start | bytes 1156
  157.8 10.0 %collective-permute-start.15 = (f32[23712]{0:T(1024)S(1)}, f32[23712]{0:T(1024)S(1)}, u32[]{:S(2)}, u32[]{:S(2)}) collective-permute-start(f32[23712]{0:T(1024)S(1)} %add.532), channel_id=1, source_target_pairs={{0,128},{4,132},{8,136},{12,140},{16,144},{20,148},{24,152},{28,15... | collective-permute-start | bytes 284552 | tf_op jit(solution)/shard_map/ppermute | solution.py:224
  167.9 28.9 %collective-permute-start.16 = (f32[23712]{0:T(1024)S(1)}, f32[23712]{0:T(1024)S(1)}, u32[]{:S(2)}, u32[]{:S(2)}) collective-permute-start(f32[23712]{0:T(1024)S(1)} %add.533), channel_id=1, source_target_pairs={{0,256},{4,260},{8,264},{12,268},{16,272},{20,276},{24,280},{28,28... | collective-permute-start | bytes 284552 | tf_op jit(solution)/shard_map/ppermute | solution.py:224
  (48 other events, 563.3 us)

commit v2 on v1

--- a/solution.py
+++ b/solution.py
@@ -1,9 +1,15 @@
+import functools
 import math
 
 import jax
 import jax.numpy as jnp
 from jax import lax
+from jax.experimental import pallas as pl
+from jax.experimental.pallas import tpu as pltpu
 from jax.sharding import PartitionSpec as P
+
+MESH = pl.DeviceIdType.MESH
+LANES = 128
 
 
 def padded_2(x, sides, width):
@@ -167,8 +173,8 @@
             g_rbias,
         ]
     )
-    panel, small = filt_reduce(panels, small)
-    total = space_butterfly(jnp.concatenate([panel, small]))
+    panel, small = grad_reduce(panels, small)
+    total = jnp.concatenate([panel, small])
     total = total * factor
     cut = [panel_rows * channels, panel_rows * channels, panel_rows]
     g_reduce = total[: cut[0]].reshape(panel_rows, channels)
@@ -196,34 +202,133 @@
     )
 
 
-def filt_reduce(panels, small):
-    parts = lax.axis_size("filt")
-    me = lax.axis_index("filt")
-    width = panels.shape[1]
-    count = parts
-    bit = parts // 2
-    held = panels
+def _rows(length):
+    return -(-length // (8 * LANES)) * 8
+
+
+def _flip(index, bit):
+    return index + bit - 2 * bit * ((index // bit) % 2)
+
+
+def reduce_kernel(nfilt, nspace, pr, sr, buf_ref, out_ref, *scratch):
+    levels = nfilt.bit_length() - 1
+    steps = nspace.bit_length() - 1
+    recvs = scratch[:levels]
+    stages = scratch[levels : 2 * levels]
+    recv_s, send_sem, recv_sem = scratch[2 * levels :]
+    s = lax.axis_index("space")
+    f = lax.axis_index("filt")
+
+    peers = []
+    bit = nfilt // 2
     while bit >= 1:
+        peers.append((s, _flip(f, bit)))
+        bit //= 2
+    for k in range(steps):
+        peers.append((_flip(s, 1 << k), f))
+    barrier = pltpu.get_barrier_semaphore()
+    for peer in peers:
+        pl.semaphore_signal(barrier, inc=1, device_id=peer, device_id_type=MESH)
+    pl.semaphore_wait(barrier, len(peers))
+
+    held = buf_ref
+    count = nfilt
+    bit = nfilt // 2
+    sem = 0
+    for level in range(levels):
         half = count // 2
-        upper = (me // bit) % 2
-        mine = lax.dynamic_slice_in_dim(held, upper * half, half, 0)
-        other = lax.dynamic_slice_in_dim(held, (1 - upper) * half, half, 0)
-        send = jnp.concatenate([other.reshape(-1), small])
-        got = lax.ppermute(send, "filt", [(i, i ^ bit) for i in range(parts)])
-        held = mine + got[: half * width].reshape(half, width)
-        small = small + got[half * width :]
+        upper = (f // bit) % 2
+        rows = half * pr
+        peer = peers[level]
+        send_panels = pltpu.make_async_remote_copy(
+            src_ref=held.at[pl.ds(pl.multiple_of((1 - upper) * rows, 8), rows)],
+            dst_ref=recvs[level].at[pl.ds(0, rows)],
+            send_sem=send_sem.at[sem],
+            recv_sem=recv_sem.at[sem],
+            device_id=peer,
+            device_id_type=MESH,
+        )
+        send_small = pltpu.make_async_remote_copy(
+            src_ref=held.at[pl.ds(count * pr, sr)],
+            dst_ref=recvs[level].at[pl.ds(rows, sr)],
+            send_sem=send_sem.at[sem + 1],
+            recv_sem=recv_sem.at[sem + 1],
+            device_id=peer,
+            device_id_type=MESH,
+        )
+        send_panels.start()
+        send_small.start()
+        send_panels.wait()
+        send_small.wait()
+        sem += 2
+        stage = stages[level]
+        stage[pl.ds(0, rows)] = (
+            held[pl.ds(pl.multiple_of(upper * rows, 8), rows)] + recvs[level][pl.ds(0, rows)]
+        )
+        stage[pl.ds(rows, sr)] = held[pl.ds(count * pr, sr)] + recvs[level][pl.ds(rows, sr)]
+        held = stage
         count = half
         bit //= 2
-    return held.reshape(-1), small
-
-
-def space_butterfly(buf):
-    size = lax.axis_size("space")
-    bit = 1
-    while bit < size:
-        buf = buf + lax.ppermute(buf, "space", [(i, i ^ bit) for i in range(size)])
-        bit *= 2
-    return buf
+
+    if levels == 0:
+        out_ref[...] = buf_ref[...]
+    else:
+        out_ref[...] = held[...]
+    for k in range(steps):
+        copy = pltpu.make_async_remote_copy(
+            src_ref=out_ref,
+            dst_ref=recv_s.at[k],
+            send_sem=send_sem.at[sem],
+            recv_sem=recv_sem.at[sem],
+            device_id=peers[levels + k],
+            device_id_type=MESH,
+        )
+        copy.start()
+        copy.wait()
+        sem += 1
+        out_ref[...] = out_ref[...] + recv_s[k]
+
+
+def grad_reduce(panels, small):
+    nfilt = lax.axis_size("filt")
+    nspace = lax.axis_size("space")
+    width = panels.shape[1]
+    pr = _rows(width)
+    sr = _rows(small.shape[0])
+    buf = jnp.concatenate(
+        [
+            jnp.pad(panels, ((0, 0), (0, pr * LANES - width))).reshape(nfilt * pr, LANES),
+            jnp.pad(small, (0, sr * LANES - small.shape[0])).reshape(sr, LANES),
+        ]
+    )
+    levels = nfilt.bit_length() - 1
+    steps = nspace.bit_length() - 1
+    scratch = []
+    count = nfilt
+    for _ in range(levels):
+        count //= 2
+        scratch.append(pltpu.VMEM((count * pr + sr, LANES), jnp.float32))
+    count = nfilt
+    for _ in range(levels):
+        count //= 2
+        scratch.append(pltpu.VMEM((count * pr + sr, LANES), jnp.float32))
+    ncopies = 2 * levels + steps
+    scratch += [
+        pltpu.VMEM((max(steps, 1), pr + sr, LANES), jnp.float32),
+        pltpu.SemaphoreType.DMA((ncopies,)),
+        pltpu.SemaphoreType.DMA((ncopies,)),
+    ]
+    out = pl.pallas_call(
+        functools.partial(reduce_kernel, nfilt, nspace, pr, sr),
+        out_shape=jax.ShapeDtypeStruct((pr + sr, LANES), jnp.float32),
+        in_specs=[pl.BlockSpec(memory_space=pltpu.VMEM)],
+        out_specs=pl.BlockSpec(memory_space=pltpu.VMEM),
+        scratch_shapes=scratch,
+        compiler_params=pltpu.CompilerParams(collective_id=0, has_side_effects=True),
+    )(buf)
+    panel = out[:pr].reshape(-1)[:width]
+    small = out[pr:].reshape(-1)[: small.shape[0]]
+    return panel, small
 
 
 def solution(mesh):

time: 201 us -> 207 us (1.030)
  the two profiles are of different devices: /device:TPU:10 before, /device:TPU:56 now
where the time goes in v2:
time: 207 us
  other arithmetic  60.6 us (29%)
  Pallas kernels  57.4 us (28%)
  starting transfers between devices  46.2 us (22%)
  local copies, waits for them, and re-layouts  21.1 us (10%)
  waiting for transfers between devices  11.3 us (5%)
  matrix products  7.96 us (4%)
  between operations  2.19 us (1%)
    pallas_call x1, Pallas kernels, grad_reduce(): pl.pallas_call(functools.partial(reduce_kernel, nfilt, nspace, pr, sr), o...  57.4 us
    ppermute x4, starting transfers between devices, padded_2(): after = lax.ppermute(initial, axis, down)  39.6 us
    reduce_sum x4, other arithmetic, kernel_terms(): entries.append(jnp.sum(piece * convolution_gradient, axis=(1, 2)))  26.3 us
    convert_element_type x1, other arithmetic, shards(): image_grad = (cotangent.astype(jnp.float32) + back).astype(jnp.bfloat16)  11.7 us
    reduce_sum x1, other arithmetic, shards(): average = jnp.mean(flat, axis=0, keepdims=True)  11.5 us
    ppermute x4, starting transfers between devices, padded_2(): before = lax.ppermute(last, axis, up)  6.56 us
    concatenate x4, other arithmetic, padded_2(): x = jnp.concatenate([before, x, after], axis=dim)  6.53 us
    ppermute x4, waiting for transfers between devices, padded_2(): before = lax.ppermute(last, axis, up)  6.51 us
  transfers between devices with their start and end apart: 8, of which 6 were waited for; matrix products, arithmetic and copies ran while one was open for 5% of the time, Pallas kernels for 0%

profile of v2, /device:TPU:56, one launch (start us, length us, event | category | flops | bytes accessed | tf_op | source)
XLA Modules:
  0.0 206.6 jit_solution(5138667370807455925)
XLA Ops:
  0.7 1.2 fusion.139
  1.9 2.1 collective-permute-start
  4.0 14.8 %collective-permute-start.1 = (bf16[96,3,256]{2,1,0:T(4,128)(2,1)S(1)}, bf16[96,3,256]{2,1,0:T(4,128)(2,1)S(1)}, u32[]{:S(2)}, u32[]{:S(2)}) collective-permute-start(bf16[96,3,256]{2,1,0:T(4,128)(2,1)S(1)} %get-tuple-element.101), channel_id=1, source_target_pairs={{4,0},{8,4},{12,8},{16,12},{20,16},{24,20},{28,24},{32,28},{36,32}... | collective-permute-start | bytes 442376 | tf_op jit(solution)/shard_map/ppermute | solution.py:23
  18.8 1.0 slice_bitcast_fusion.50
  19.8 1.0 slice_bitcast_fusion.49
  21.0 0.9 slice_bitcast_fusion.48
  22.1 1.1 collective-permute-done.1
  23.2 1.5 pad_maximum_fusion.2
  24.6 0.2 fusion.137
  24.8 1.3 collective-permute-start.2
  26.1 5.9 %collective-permute-start.3 = (bf16[96,10,3]{2,1,0:T(8,128)(2,1)S(1)}, bf16[96,10,3]{2,1,0:T(8,128)(2,1)S(1)}, u32[]{:S(2)}, u32[]{:S(2)}) collective-permute-start(bf16[96,10,3]{2,1,0:T(8,128)(2,1)S(1)} %get-tuple-element.91), channel_id=1, source_target_pairs={{1,0},{2,1},{3,2},{5,4},{6,5},{7,6},{9,8},{10,9},{11,10},{13,12},{... | collective-permute-start | bytes 17288 | tf_op jit(solution)/shard_map/ppermute | solution.py:23
  32.1 1.9 multiply_reduce_fusion
  34.1 0.9 copy.28
  35.0 0.9 collective-permute-done.2
  35.9 1.5 collective-permute-done.3
  37.3 2.3 %maximum_maximum_fusion = (bf16[96,10,259]{2,1,0:T(8,128)(2,1)S(1)}, bf16[96,10,259]{2,1,0:T(8,128)(2,1)S(1)}) fusion(bf16[96,3,256]{2,1,0:T(4,128)(2,1)S(1)} %collective-permute-done.1, bf16[96,4,256]{2,1,0:T(4,128)(2,1)S(1)} %copy-done.1, bf16[96,3,256]{2,1,0:T(4,128)(2,1)S(1)} %collective-permute-done, bf16[96,10,3]{2,1,0:T(8,128)(2,1)S(1)} %collective-permute-done.2, ...), kind=kLoop, calls=%fused_computation.67 | loop fusion | flops 3978240 | bytes 1497600 | tf_op jit(solution)/shard_map/concatenate | solution.py:24
  40.0 11.5 %fusion.134 = (f32[4,256]{1,0:T(4,128)S(1)}, f32[96,4,256]{2,1,0:T(4,128)S(1)}) fusion(f32[96]{0:T(128)S(1)} %copy-done.86, bf16[96,10,259]{2,1,0:T(8,128)(2,1)S(1)} %get-tuple-element.95, f32[96]{0:T(128)S(1)} %get-tuple-element.157, f32[96]{0:T(128)S(1)} %get-tuple-element.158, f32[96]{0:T(128)S(1)} %get-tuple-element.111, ...), kind=kLoop, calls=%fused_computation.345 | loop fusion | flops 16317440 | bytes 9165568 | tf_op jit(solution)/shard_map/reduce_sum | solution.py:95
  51.6 0.2 multiply_reduce_fusion.3
  51.9 1.5 fusion.9
  53.4 1.5 convert_reduce_fusion
  54.9 1.1 fusion.133
  56.0 1.0 fusion.120
  57.0 1.4 convert_reduce_fusion.1
  58.5 1.1 reshape.126
  59.5 7.8 %fusion.115 = (f32[96]{0:T(128)}, f32[96]{0:T(128)}, f32[96]{0:T(128)}, f32[96]{0:T(128)}, f32[96]{0:T(128)}, /*index=5*/f32[96]{0:T(128)}, f32[96]{0:T(128)}, f...) fusion(bf16[96,4,256]{2,1,0:T(4,128)(2,1)S(1)} %reshape.126, ...), kind=kLoop, calls=%fused_computation.241 | loop fusion | flops 5404992 | bytes 3742464 | tf_op jit(solution)/shard_map/reduce_sum | solution.py:60
  67.3 9.8 %fusion.119 = (f32[96]{0:T(128)}, f32[96]{0:T(128)}, f32[96]{0:T(128)}, f32[96]{0:T(128)}, f32[96]{0:T(128)}, /*index=5*/f32[96]{0:T(128)}, f32[96]{0:T(128)}, f...) fusion(bf16[96,4,256]{2,1,0:T(4,128)(2,1)S(1)} %reshape.126, ...), kind=kLoop, calls=%fused_computation.245 | loop fusion | flops 5404992 | bytes 3742464 | tf_op jit(solution)/shard_map/reduce_sum | solution.py:60
  77.1 2.8 %fusion.73 = (f32[96]{0:T(128)}, f32[96]{0:T(128)}, f32[96]{0:T(128)}) fusion(bf16[96,4,256]{2,1,0:T(4,128)(2,1)S(1)} %reshape.126, bf16[96,10,259]{2,1,0:T(8,128)(2,1)S(1)} %get-tuple-element.94), kind=kLoop, calls=%fused_computation.199 | loop fusion | flops 982752 | bytes 787584 | tf_op jit(solution)/shard_map/reduce_sum | solution.py:60
  79.9 1.1 reshape.128
  81.0 0.8 reshape.129
  81.8 1.7 fusion.132
  83.5 0.2 reshape.127
  83.8 0.8 reshape.130
  84.6 5.9 %fusion.118 = (f32[96]{0:T(128)}, f32[96]{0:T(128)}, f32[96]{0:T(128)}, f32[96]{0:T(128)}, f32[96]{0:T(128)}, /*index=5*/f32[96]{0:T(128)}, f32[96]{0:T(128)}, f32[96]{0:T(128)}, f32[96]{0:T(128)}, f32[96]{0:T(128)}) fusion(bf16[96,4,256]{2,1,0:T(4,128)(2,1)S(1)} %reshape.126, bf16[96,10,259]{2,1,0:T(8,128)(2,1)S(1)} %get-tuple-element.95, ...), kind=kLoop, calls=%fused_computation.244 | loop fusion | flops 4815936 | bytes 1281792 | tf_op jit(solution)/shard_map/reduce_sum | solution.py:60
  90.5 0.8 stack.199
  91.3 0.7 stack.208
  92.0 0.7 stack.217
  92.7 0.7 stack.226
  93.4 0.7 stack.235
  94.2 0.7 stack.244
  94.9 0.7 stack.253
  95.7 0.2 copy.24
  95.9 0.2 reshape.131
  96.2 1.1 multiply_reduce_fusion.1
  97.5 0.7 pad_maximum_fusion.4.buf_ref
  98.2 57.4 %shard_map.194 = f32[200,128]{1,0:T(8,128)} custom-call(f32[656,128]{1,0:T(8,128)} %pad_maximum_fusion.4.buf_ref), custom_call_target="tpu_custom_call" | custom-call | tf_op jit(solution)/shard_map/pallas_call | solution.py:321
  155.6 0.9 slice_bitcast_fusion
  156.5 0.7 slice_bitcast_fusion.1
  157.4 1.9 collective-permute-start.4
  159.4 11.8 %collective-permute-start.5 = (bf16[96,3,256]{2,1,0:T(4,128)(2,1)S(1)}, bf16[96,3,256]{2,1,0:T(4,128)(2,1)S(1)}, u32[]{:S(2)}, u32[]{:S(2)}) collective-permute-start(bf16[96,3,256]{2,1,0:T(4,128)(2,1)S(1)} %get-tuple-element.98), channel_id=1, source_target_pairs={{4,0},{8,4},{12,8},{16,12},{20,16},{24,20},{28,24},{32,28},{36,32}... | collective-permute-start | bytes 442376 | tf_op jit(solution)/shard_map/ppermute | solution.py:23
  171.2 1.4 collective-permute-done.4
  172.6 2.2 %collective-permute-done.5 = bf16[96,3,256]{2,1,0:T(4,128)(2,1)S(1)} collective-permute-done((bf16[96,3,256]{2,1,0:T(4,128)(2,1)S(1)}, bf16[96,3,256]{2,1,0:T(4,128)(2,1)S(1)}, u32[]{:S(2)}, u32[]{:S(2)}) %collective-permute-start.5) | collective-permute-done | bytes 147488 | tf_op jit(solution)/shard_map/ppermute | solution.py:23
  174.9 0.5 pad_maximum_fusion.3
  175.4 0.2 fusion.136
  175.6 7.1 %collective-permute-start.6 = (bf16[96,10,3]{2,1,0:T(8,128)(2,1)S(1)}, bf16[96,10,3]{2,1,0:T(8,128)(2,1)S(1)}, u32[]{:S(2)}, u32[]{:S(2)}) collective-permute-start(bf16[96,10,3]{2,1,0:T(8,128)(2,1)S(1)} %get-tuple-element.88), channel_id=1, source_target_pairs={{1,0},{2,1},{3,2},{5,4},{6,5},{7,6},{9,8},{10,9},{11,10},{13,12},{... | collective-permute-start | bytes 17288 | tf_op jit(solution)/shard_map/ppermute | solution.py:23
  182.6 1.3 collective-permute-start.7
  183.9 0.6 fusion.140
  184.6 0.2 reshape.135
  184.8 0.8 copy.25
  185.6 0.7 slice.868
  186.3 0.7 slice.871
  187.0 0.8 reshape.125
  188.1 4.2 %collective-permute-done.7 = bf16[96,10,3]{2,1,0:T(8,128)(2,1)S(1)} collective-permute-done((bf16[96,10,3]{2,1,0:T(8,128)(2,1)S(1)}, bf16[96,10,3]{2,1,0:T(8,128)(2,1)S(1)}, u32[]{:S(2)}, u32[]{:S(2)}) %collective-permute-start.7) | collective-permute-done | bytes 5792 | tf_op jit(solution)/shard_map/ppermute | solution.py:22
  192.3 2.3 %pad_maximum_fusion.1 = (bf16[96,10,259]{2,1,0:T(8,128)(2,1)S(1)}, bf16[96,10,259]{2,1,0:T(8,128)(2,1)S(1)}) fusion(bf16[96,10,3]{2,1,0:T(8,128)(2,1)S(1)} %collective-permute-done.6, bf16[96,3,256]{2,1,0:T(4,128)(2,1)S(1)} %collective-permute-done.5, bf16[96,4,256]{2,1,0:T(4,128)(2,1)S(1)} %reshape.126, bf16[96,3,256]{2,1,0:T(4,128)(2,1)S(1)} %collective-permute-done.4, ...), kind=kLoop, calls=%fused_computation.69 | loop fusion | flops 3978240 | bytes 1497600 | tf_op jit(solution)/shard_map/concatenate | solution.py:24
  195.0 11.7 %add_convert_fusion = bf16[96,4,256]{2,1,0:T(4,128)(2,1)} fusion(bf16[96,4,256]{2,1,0:T(4,128)(2,1)S(1)} %reshape.126, bf16[96,3,256]{2,1,0:T(4,128)(2,1)S(1)} %collective-permute-done.4, bf16[96,3,256]{2,1,0:T(4,128)(2,1)S(1)} %collective-permute-done.5, bf16[96,10,259]{2,1,0:T(8,128)(2,1)S(1)} %get-tuple-element.93, ...), kind=kLoop, calls=%fused_computation.252 | loop fusion | flops 16416768 | bytes 9161088 | tf_op jit(solution)/shard_map/convert_element_type | solution.py:154
  (199 shorter events, 1.1 us)
Async XLA Ops:
  0.6 51.2 %copy-start = (bf16[384,96]{0,1:T(8,128)(2,1)S(1)}, bf16[384,96]{0,1:T(8,128)(2,1)}, u32[]{:S(2)}) copy-start(bf16[384,96]{0,1:T(8,128)(2,1)} %param.17) | copy-start | bytes 221188
  1.9 30.2 %copy-start.6 = (bf16[96,4,256]{2,1,0:T(4,128)(2,1)S(1)}, bf16[96,4,256]{2,1,0:T(4,128)(2,1)}, u32[]{:S(2)}) copy-start(bf16[96,4,256]{2,1,0:T(4,128)(2,1)} %param.12) | copy-start | bytes 589828
  1.9 30.2 %copy-start.12 = (f32[96]{0:T(128)S(1)}, f32[96]{0:T(128)}, u32[]{:S(2)}) copy-start(f32[96]{0:T(128)} %param.21) | copy-start | bytes 1156
  1.9 20.1 %collective-permute-start = (bf16[96,3,256]{2,1,0:T(4,128)(2,1)S(1)}, bf16[96,3,256]{2,1,0:T(4,128)(2,1)S(1)}, u32[]{:S(2)}, u32[]{:S(2)}) collective-permute-start(bf16[96,3,256]{2,1,0:T(4,128)(2,1)S(1)} %get-tuple-element.100), channel_id=1, source_target_pairs={{0,4},{4,8},{8,12},{12,16},{16,20},{20,24},{24,28},{28,32},{32,36}... | collective-permute-start | bytes 442376 | tf_op jit(solution)/shard_map/ppermute | solution.py:22
  4.0 19.2 %collective-permute-start.1 = (bf16[96,3,256]{2,1,0:T(4,128)(2,1)S(1)}, bf16[96,3,256]{2,1,0:T(4,128)(2,1)S(1)}, u32[]{:S(2)}, u32[]{:S(2)}) collective-permute-start(bf16[96,3,256]{2,1,0:T(4,128)(2,1)S(1)} %get-tuple-element.101), channel_id=1, source_target_pairs={{4,0},{8,4},{12,8},{16,12},{20,16},{24,20},{28,24},{32,28},{36,32}... | collective-permute-start | bytes 442376 | tf_op jit(solution)/shard_map/ppermute | solution.py:23
  19.8 19.8 %copy-start.13 = (f32[96]{0:T(128)}, f32[96]{0:T(128)S(1)}, u32[]{:S(2)}) copy-start(f32[96]{0:T(128)S(1)} %get-tuple-element.125) | copy-start | bytes 1156
  19.8 19.8 %copy-start.15 = (f32[96]{0:T(128)}, f32[96]{0:T(128)S(1)}, u32[]{:S(2)}) copy-start(f32[96]{0:T(128)S(1)} %get-tuple-element.126) | copy-start | bytes 1156
  19.8 19.8 %copy-start.17 = (f32[96]{0:T(128)}, f32[96]{0:T(128)S(1)}, u32[]{:S(2)}) copy-start(f32[96]{0:T(128)S(1)} %get-tuple-element.127) | copy-start | bytes 1156
  19.8 19.8 %copy-start.19 = (f32[96]{0:T(128)}, f32[96]{0:T(128)S(1)}, u32[]{:S(2)}) copy-start(f32[96]{0:T(128)S(1)} %get-tuple-element.128) | copy-start | bytes 1156
  20.8 18.8 %copy-start.21 = (f32[96]{0:T(128)}, f32[96]{0:T(128)S(1)}, u32[]{:S(2)}) copy-start(f32[96]{0:T(128)S(1)} %get-tuple-element.129) | copy-start | bytes 1156
  20.8 18.8 %copy-start.23 = (f32[96]{0:T(128)}, f32[96]{0:T(128)S(1)}, u32[]{:S(2)}) copy-start(f32[96]{0:T(128)S(1)} %get-tuple-element.130) | copy-start | bytes 1156
  20.9 18.8 %copy-start.25 = (f32[96]{0:T(128)}, f32[96]{0:T(128)S(1)}, u32[]{:S(2)}) copy-start(f32[96]{0:T(128)S(1)} %get-tuple-element.131) | copy-start | bytes 1156
  20.9 18.8 %copy-start.27 = (f32[96]{0:T(128)}, f32[96]{0:T(128)S(1)}, u32[]{:S(2)}) copy-start(f32[96]{0:T(128)S(1)} %get-tuple-element.132) | copy-start | bytes 1156
  20.9 18.8 %copy-start.29 = (f32[96]{0:T(128)}, f32[96]{0:T(128)S(1)}, u32[]{:S(2)}) copy-start(f32[96]{0:T(128)S(1)} %get-tuple-element.133) | copy-start | bytes 1156
  20.9 18.8 %copy-start.31 = (f32[96]{0:T(128)}, f32[96]{0:T(128)S(1)}, u32[]{:S(2)}) copy-start(f32[96]{0:T(128)S(1)} %get-tuple-element.134) | copy-start | bytes 1156
  20.9 18.8 %copy-start.33 = (f32[96]{0:T(128)}, f32[96]{0:T(128)S(1)}, u32[]{:S(2)}) copy-start(f32[96]{0:T(128)S(1)} %get-tuple-element.135) | copy-start | bytes 1156
  20.9 18.8 %copy-start.35 = (f32[96]{0:T(128)}, f32[96]{0:T(128)S(1)}, u32[]{:S(2)}) copy-start(f32[96]{0:T(128)S(1)} %get-tuple-element.136) | copy-start | bytes 1156
  20.9 18.8 %copy-start.37 = (f32[96]{0:T(128)}, f32[96]{0:T(128)S(1)}, u32[]{:S(2)}) copy-start(f32[96]{0:T(128)S(1)} %get-tuple-element.137) | copy-start | bytes 1156
  20.9 18.8 %copy-start.39 = (f32[96]{0:T(128)}, f32[96]{0:T(128)S(1)}, u32[]{:S(2)}) copy-start(f32[96]{0:T(128)S(1)} %get-tuple-element.138) | copy-start | bytes 1156
  20.9 18.8 %copy-start.41 = (f32[96]{0:T(128)}, f32[96]{0:T(128)S(1)}, u32[]{:S(2)}) copy-start(f32[96]{0:T(128)S(1)} %get-tuple-element.139) | copy-start | bytes 1156
  20.9 18.8 %copy-start.43 = (f32[96]{0:T(128)}, f32[96]{0:T(128)S(1)}, u32[]{:S(2)}) copy-start(f32[96]{0:T(128)S(1)} %get-tuple-element.140) | copy-start | bytes 1156
  21.0 18.8 %copy-start.45 = (f32[96]{0:T(128)}, f32[96]{0:T(128)S(1)}, u32[]{:S(2)}) copy-start(f32[96]{0:T(128)S(1)} %get-tuple-element.141) | copy-start | bytes 1156
  21.0 18.8 %copy-start.47 = (f32[96]{0:T(128)}, f32[96]{0:T(128)S(1)}, u32[]{:S(2)}) copy-start(f32[96]{0:T(128)S(1)} %get-tuple-element.142) | copy-start | bytes 1156
  21.0 18.8 %copy-start.49 = (f32[96]{0:T(128)}, f32[96]{0:T(128)S(1)}, u32[]{:S(2)}) copy-start(f32[96]{0:T(128)S(1)} %get-tuple-element.143) | copy-start | bytes 1156
  21.0 18.8 %copy-start.51 = (f32[96]{0:T(128)}, f32[96]{0:T(128)S(1)}, u32[]{:S(2)}) copy-start(f32[96]{0:T(128)S(1)} %get-tuple-element.144) | copy-start | bytes 1156
  21.0 18.8 %copy-start.53 = (f32[96]{0:T(128)}, f32[96]{0:T(128)S(1)}, u32[]{:S(2)}) copy-start(f32[96]{0:T(128)S(1)} %get-tuple-element.145) | copy-start | bytes 1156
  21.0 18.8 %copy-start.55 = (f32[96]{0:T(128)}, f32[96]{0:T(128)S(1)}, u32[]{:S(2)}) copy-start(f32[96]{0:T(128)S(1)} %get-tuple-element.146) | copy-start | bytes 1156
  21.0 18.8 %copy-start.57 = (f32[96]{0:T(128)}, f32[96]{0:T(128)S(1)}, u32[]{:S(2)}) copy-start(f32[96]{0:T(128)S(1)} %get-tuple-element.147) | copy-start | bytes 1156
  21.9 17.9 %copy-start.59 = (f32[96]{0:T(128)}, f32[96]{0:T(128)S(1)}, u32[]{:S(2)}) copy-start(f32[96]{0:T(128)S(1)} %get-tuple-element.148) | copy-start | bytes 1156
  21.9 17.9 %copy-start.61 = (f32[96]{0:T(128)}, f32[96]{0:T(128)S(1)}, u32[]{:S(2)}) copy-start(f32[96]{0:T(128)S(1)} %get-tuple-element.149) | copy-start | bytes 1156
  21.9 17.9 %copy-start.63 = (f32[96]{0:T(128)}, f32[96]{0:T(128)S(1)}, u32[]{:S(2)}) copy-start(f32[96]{0:T(128)S(1)} %get-tuple-element.150) | copy-start | bytes 1156
  21.9 17.9 %copy-start.65 = (f32[96]{0:T(128)}, f32[96]{0:T(128)S(1)}, u32[]{:S(2)}) copy-start(f32[96]{0:T(128)S(1)} %get-tuple-element.151) | copy-start | bytes 1156
  22.0 17.9 %copy-start.67 = (f32[96]{0:T(128)}, f32[96]{0:T(128)S(1)}, u32[]{:S(2)}) copy-start(f32[96]{0:T(128)S(1)} %get-tuple-element.152) | copy-start | bytes 1156
  22.0 17.9 %copy-start.69 = (f32[96]{0:T(128)}, f32[96]{0:T(128)S(1)}, u32[]{:S(2)}) copy-start(f32[96]{0:T(128)S(1)} %get-tuple-element.153) | copy-start | bytes 1156
  22.0 17.9 %copy-start.71 = (f32[96]{0:T(128)}, f32[96]{0:T(128)S(1)}, u32[]{:S(2)}) copy-start(f32[96]{0:T(128)S(1)} %get-tuple-element.154) | copy-start | bytes 1156
  22.0 17.9 %copy-start.73 = (f32[96]{0:T(128)}, f32[96]{0:T(128)S(1)}, u32[]{:S(2)}) copy-start(f32[96]{0:T(128)S(1)} %get-tuple-element.155) | copy-start | bytes 1156
  22.0 17.9 %copy-start.75 = (f32[96]{0:T(128)}, f32[96]{0:T(128)S(1)}, u32[]{:S(2)}) copy-start(f32[96]{0:T(128)S(1)} %get-tuple-element.156) | copy-start | bytes 1156
  22.0 17.9 %copy-start.77 = (f32[96]{0:T(128)}, f32[96]{0:T(128)S(1)}, u32[]{:S(2)}) copy-start(f32[96]{0:T(128)S(1)} %get-tuple-element.157) | copy-start | bytes 1156
  22.0 17.9 %copy-start.79 = (f32[96]{0:T(128)}, f32[96]{0:T(128)S(1)}, u32[]{:S(2)}) copy-start(f32[96]{0:T(128)S(1)} %get-tuple-element.158) | copy-start | bytes 1156
  22.0 12.0 %copy-start.85 = (bf16[384]{0:T(512)(128)(2,1)S(1)}, bf16[384]{0:T(512)(128)(2,1)}, u32[]{:S(2)}) copy-start(bf16[384]{0:T(512)(128)(2,1)} %param.18) | copy-start | bytes 2308
  22.0 12.0 %copy-start.1 = (bf16[96,4,256]{2,1,0:T(4,128)(2,1)S(1)}, bf16[96,4,256]{2,1,0:T(4,128)(2,1)}, u32[]{:S(2)}) copy-start(bf16[96,4,256]{2,1,0:T(4,128)(2,1)} %param.11) | copy-start | bytes 589828
  23.1 16.8 %copy-start.5 = (bf16[96,3,256]{2,1,0:T(4,128)(2,1)}, bf16[96,3,256]{2,1,0:T(4,128)(2,1)S(1)}, u32[]{:S(2)}) copy-start(bf16[96,3,256]{2,1,0:T(4,128)(2,1)S(1)} %collective-permute-done.1) | copy-start | bytes 442372
  24.8 11.0 %collective-permute-start.2 = (bf16[96,10,3]{2,1,0:T(8,128)(2,1)S(1)}, bf16[96,10,3]{2,1,0:T(8,128)(2,1)S(1)}, u32[]{:S(2)}, u32[]{:S(2)}) collective-permute-start(bf16[96,10,3]{2,1,0:T(8,128)(2,1)S(1)} %get-tuple-element.90), channel_id=1, source_target_pairs={{0,1},{1,2},{2,3},{4,5},{5,6},{6,7},{8,9},{9,10},{10,11},{12,13},{... | collective-permute-start | bytes 17288 | tf_op jit(solution)/shard_map/ppermute | solution.py:22
  26.1 11.2 %collective-permute-start.3 = (bf16[96,10,3]{2,1,0:T(8,128)(2,1)S(1)}, bf16[96,10,3]{2,1,0:T(8,128)(2,1)S(1)}, u32[]{:S(2)}, u32[]{:S(2)}) collective-permute-start(bf16[96,10,3]{2,1,0:T(8,128)(2,1)S(1)} %get-tuple-element.91), channel_id=1, source_target_pairs={{1,0},{2,1},{3,2},{5,4},{6,5},{7,6},{9,8},{10,9},{11,10},{13,12},{... | collective-permute-start | bytes 17288 | tf_op jit(solution)/shard_map/ppermute | solution.py:23
  34.1 19.3 %copy-start.3 = (f32[12,8,4,256]{3,1,2,0:T(8,128)}, f32[12,8,4,256]{3,1,2,0:T(8,128)S(1)}, u32[]{:S(2)}) copy-start(f32[12,8,4,256]{3,1,2,0:T(8,128)S(1)} %copy.32) | copy-start | bytes 1179652
  40.0 11.9 %copy-start.11 = (f32[96]{0:T(128)S(1)}, f32[96]{0:T(128)}, u32[]{:S(2)}) copy-start(f32[96]{0:T(128)} %param.15) | copy-start | bytes 1156
  40.0 11.9 %copy-start.81 = (f32[96]{0:T(128)S(1)}, f32[96]{0:T(128)}, u32[]{:S(2)}) copy-start(f32[96]{0:T(128)} %param.16) | copy-start | bytes 1156
  84.6 11.6 %copy-start.2 = (bf16[384,1024]{0,1:T(8,128)(2,1)S(1)}, bf16[384,1024]{0,1:T(8,128)(2,1)}, u32[]{:S(2)}) copy-start(bf16[384,1024]{0,1:T(8,128)(2,1)} %get-tuple-element.161) | copy-start | bytes 2359300
  84.6 11.6 %copy-start.4 = (f32[12,8,4,256]{3,1,2,0:T(8,128)S(1)}, f32[12,8,4,256]{3,1,2,0:T(8,128)}, u32[]{:S(2)}) copy-start(f32[12,8,4,256]{3,1,2,0:T(8,128)} %copy-done.3) | copy-start | bytes 1179652
  157.4 15.2 %collective-permute-start.4 = (bf16[96,3,256]{2,1,0:T(4,128)(2,1)S(1)}, bf16[96,3,256]{2,1,0:T(4,128)(2,1)S(1)}, u32[]{:S(2)}, u32[]{:S(2)}) collective-permute-start(bf16[96,3,256]{2,1,0:T(4,128)(2,1)S(1)} %get-tuple-element.99), channel_id=1, source_target_pairs={{0,4},{4,8},{8,12},{12,16},{16,20},{20,24},{24,28},{28,32},{32,36}... | collective-permute-start | bytes 442376 | tf_op jit(solution)/shard_map/ppermute | solution.py:22
  159.4 15.5 %collective-permute-start.5 = (bf16[96,3,256]{2,1,0:T(4,128)(2,1)S(1)}, bf16[96,3,256]{2,1,0:T(4,128)(2,1)S(1)}, u32[]{:S(2)}, u32[]{:S(2)}) collective-permute-start(bf16[96,3,256]{2,1,0:T(4,128)(2,1)S(1)} %get-tuple-element.98), channel_id=1, source_target_pairs={{4,0},{8,4},{12,8},{16,12},{20,16},{24,20},{28,24},{32,28},{36,32}... | collective-permute-start | bytes 442376 | tf_op jit(solution)/shard_map/ppermute | solution.py:23
  175.6 12.6 %collective-permute-start.6 = (bf16[96,10,3]{2,1,0:T(8,128)(2,1)S(1)}, bf16[96,10,3]{2,1,0:T(8,128)(2,1)S(1)}, u32[]{:S(2)}, u32[]{:S(2)}) collective-permute-start(bf16[96,10,3]{2,1,0:T(8,128)(2,1)S(1)} %get-tuple-element.88), channel_id=1, source_target_pairs={{1,0},{2,1},{3,2},{5,4},{6,5},{7,6},{9,8},{10,9},{11,10},{13,12},{... | collective-permute-start | bytes 17288 | tf_op jit(solution)/shard_map/ppermute | solution.py:23
  182.6 9.7 %collective-permute-start.7 = (bf16[96,10,3]{2,1,0:T(8,128)(2,1)S(1)}, bf16[96,10,3]{2,1,0:T(8,128)(2,1)S(1)}, u32[]{:S(2)}, u32[]{:S(2)}) collective-permute-start(bf16[96,10,3]{2,1,0:T(8,128)(2,1)S(1)} %get-tuple-element.89), channel_id=1, source_target_pairs={{0,1},{1,2},{2,3},{4,5},{5,6},{6,7},{8,9},{9,10},{10,11},{12,13},{... | collective-permute-start | bytes 17288 | tf_op jit(solution)/shard_map/ppermute | solution.py:22
  187.8 6.8 %copy-start.20 = (f32[96]{0:T(128)S(1)}, f32[96]{0:T(128)}, u32[]{:S(2)}) copy-start(f32[96]{0:T(128)} %copy-done.19) | copy-start | bytes 1156
  187.8 6.8 %copy-start.22 = (f32[96]{0:T(128)S(1)}, f32[96]{0:T(128)}, u32[]{:S(2)}) copy-start(f32[96]{0:T(128)} %copy-done.21) | copy-start | bytes 1156
  187.8 6.8 %copy-start.24 = (f32[96]{0:T(128)S(1)}, f32[96]{0:T(128)}, u32[]{:S(2)}) copy-start(f32[96]{0:T(128)} %copy-done.23) | copy-start | bytes 1156
  187.9 6.8 %copy-start.26 = (f32[96]{0:T(128)S(1)}, f32[96]{0:T(128)}, u32[]{:S(2)}) copy-start(f32[96]{0:T(128)} %copy-done.25) | copy-start | bytes 1156
  187.9 6.8 %copy-start.28 = (f32[96]{0:T(128)S(1)}, f32[96]{0:T(128)}, u32[]{:S(2)}) copy-start(f32[96]{0:T(128)} %copy-done.27) | copy-start | bytes 1156
  187.9 6.8 %copy-start.30 = (f32[96]{0:T(128)S(1)}, f32[96]{0:T(128)}, u32[]{:S(2)}) copy-start(f32[96]{0:T(128)} %copy-done.29) | copy-start | bytes 1156
  187.9 6.8 %copy-start.32 = (f32[96]{0:T(128)S(1)}, f32[96]{0:T(128)}, u32[]{:S(2)}) copy-start(f32[96]{0:T(128)} %copy-done.31) | copy-start | bytes 1156
  187.9 6.8 %copy-start.34 = (f32[96]{0:T(128)S(1)}, f32[96]{0:T(128)}, u32[]{:S(2)}) copy-start(f32[96]{0:T(128)} %copy-done.33) | copy-start | bytes 1156
  187.9 6.8 %copy-start.36 = (f32[96]{0:T(128)S(1)}, f32[96]{0:T(128)}, u32[]{:S(2)}) copy-start(f32[96]{0:T(128)} %copy-done.35) | copy-start | bytes 1156
  187.9 6.8 %copy-start.38 = (f32[96]{0:T(128)S(1)}, f32[96]{0:T(128)}, u32[]{:S(2)}) copy-start(f32[96]{0:T(128)} %copy-done.37) | copy-start | bytes 1156
  187.9 6.8 %copy-start.40 = (f32[96]{0:T(128)S(1)}, f32[96]{0:T(128)}, u32[]{:S(2)}) copy-start(f32[96]{0:T(128)} %copy-done.39) | copy-start | bytes 1156
  (31 other events, 187.8 us)

commit v3 on v2

--- a/solution.py
+++ b/solution.py
@@ -150,8 +150,6 @@
     d_float = convolution_gradient.astype(jnp.float32)
     g_dbias = jnp.sum(d_float, axis=(1, 2))
     padded_grad = padded_2(convolution_gradient, (("space", 1), ("filt", 2)), 3)
-    back = conv_back(padded_grad, kernel, row_count, col_count)
-    image_grad = (cotangent.astype(jnp.float32) + back).astype(jnp.bfloat16)
     g_kernel = kernel_terms(padded, d_float, row_count, col_count)
     factor = 1.0 / math.sqrt(tok_count * lax.axis_size("space") * lax.axis_size("filt"))
     parts = lax.axis_size("filt")
@@ -173,6 +171,9 @@
             g_rbias,
         ]
     )
+    panels, small, padded_grad = lax.optimization_barrier((panels, small, padded_grad))
+    back = conv_back(padded_grad, kernel, row_count, col_count)
+    image_grad = (cotangent.astype(jnp.float32) + back).astype(jnp.bfloat16)
     panel, small = grad_reduce(panels, small)
     total = jnp.concatenate([panel, small])
     total = total * factor
@@ -325,6 +326,9 @@
         out_specs=pl.BlockSpec(memory_space=pltpu.VMEM),
         scratch_shapes=scratch,
         compiler_params=pltpu.CompilerParams(collective_id=0, has_side_effects=True),
+        cost_estimate=pl.CostEstimate(
+            flops=0, transcendentals=0, bytes_accessed=200 * 1024 * 1024
+        ),
     )(buf)
     panel = out[:pr].reshape(-1)[:width]
     small = out[pr:].reshape(-1)[: small.shape[0]]

time: 207 us -> 207 us (level); the launches traced: 207 us -> 204 us
  waiting for transfers between devices: 11.3 us -> 29.1 us
  Pallas kernels: 57.4 us -> 45.6 us
  starting transfers between devices: 46.2 us -> 36.3 us
    ppermute x4, waiting for transfers between devices: 6.51 us -> 25.1 us  [padded_2(): before = lax.ppermute(last, axis, up)]
    pallas_call x1, Pallas kernels: 57.4 us -> 45.6 us  [grad_reduce(): pl.pallas_call(functools.partial(reduce_kernel, nfilt, nspace, pr, sr), o...]
    ppermute x4, starting transfers between devices: 39.6 us -> 29.1 us  [padded_2(): after = lax.ppermute(initial, axis, down)]
    another operation x7, local copies, waits for them, and re-layouts: 5.07 us -> 2.12 us  [kernel_terms(): lines.append(jnp.stack(entries, axis=1))]
    reduce_sum x4, other arithmetic: 26.3 us -> 24.1 us  [kernel_terms(): entries.append(jnp.sum(piece * convolution_gradient, axis=(1, 2)))]
  transfers between devices with their start and end apart: 8 -> 8, of which waited for: 6 -> 6; matrix products, arithmetic and copies ran while one was open for 5% -> 6% of each run, Pallas kernels for 0% -> 0%
where the time goes in v3:
time: 207 us; the launch traced here: 204 us
  other arithmetic  62 us (30%)
  Pallas kernels  45.6 us (22%)
  starting transfers between devices  36.3 us (18%)
  waiting for transfers between devices  29.1 us (14%)
  local copies, waits for them, and re-layouts  20.4 us (10%)
  matrix products  7.36 us (4%)
  between operations  2.87 us (1%)
    pallas_call x1, Pallas kernels, grad_reduce(): pl.pallas_call(functools.partial(reduce_kernel, nfilt, nspace, pr, sr), o...  45.6 us
    ppermute x4, starting transfers between devices, padded_2(): after = lax.ppermute(initial, axis, down)  29.1 us
    ppermute x4, waiting for transfers between devices, padded_2(): before = lax.ppermute(last, axis, up)  25.1 us
    reduce_sum x4, other arithmetic, kernel_terms(): entries.append(jnp.sum(piece * convolution_gradient, axis=(1, 2)))  24.1 us
    convert_element_type x1, other arithmetic, shards(): image_grad = (cotangent.astype(jnp.float32) + back).astype(jnp.bfloat16)  13.5 us
    reduce_sum x1, other arithmetic, shards(): average = jnp.mean(flat, axis=0, keepdims=True)  12.7 us
    ppermute x4, starting transfers between devices, padded_2(): before = lax.ppermute(last, axis, up)  7.17 us
    concatenate x4, other arithmetic, padded_2(): x = jnp.concatenate([before, x, after], axis=dim)  7.16 us
  transfers between devices with their start and end apart: 8, of which 6 were waited for; matrix products, arithmetic and copies ran while one was open for 6% of the time, Pallas kernels for 0%

profile of v3, /device:TPU:56, one launch (start us, length us, event | category | flops | bytes accessed | tf_op | source)
XLA Modules:
  0.0 203.6 jit_solution(11576289924872893158)
XLA Ops:
  0.7 1.2 fusion.123
  1.9 15.0 %collective-permute-start.1 = (bf16[96,3,256]{2,1,0:T(4,128)(2,1)S(1)}, bf16[96,3,256]{2,1,0:T(4,128)(2,1)S(1)}, u32[]{:S(2)}, u32[]{:S(2)}) collective-permute-start(bf16[96,3,256]{2,1,0:T(4,128)(2,1)S(1)} %get-tuple-element.101), channel_id=1, source_target_pairs={{4,0},{8,4},{12,8},{16,12},{20,16},{24,20},{28,24},{32,28},{36,32}... | collective-permute-start | bytes 442376 | tf_op jit(solution)/shard_map/ppermute | solution.py:23
  16.9 1.9 collective-permute-start
  18.8 1.0 slice_bitcast_fusion.50
  19.9 1.0 slice_bitcast_fusion.49
  21.1 1.4 slice_bitcast_fusion.48
  22.6 9.5 %collective-permute-done = bf16[96,3,256]{2,1,0:T(4,128)(2,1)S(1)} collective-permute-done((bf16[96,3,256]{2,1,0:T(4,128)(2,1)S(1)}, bf16[96,3,256]{2,1,0:T(4,128)(2,1)S(1)}, u32[]{:S(2)}, u32[]{:S(2)}) %collective-permute-start) | collective-permute-done | bytes 147488 | tf_op jit(solution)/shard_map/ppermute | solution.py:22
  32.1 1.5 pad_maximum_fusion.2
  33.6 0.2 fusion.121
  33.8 1.3 collective-permute-start.2
  35.1 6.8 %collective-permute-start.3 = (bf16[96,10,3]{2,1,0:T(8,128)(2,1)S(1)}, bf16[96,10,3]{2,1,0:T(8,128)(2,1)S(1)}, u32[]{:S(2)}, u32[]{:S(2)}) collective-permute-start(bf16[96,10,3]{2,1,0:T(8,128)(2,1)S(1)} %get-tuple-element.93), channel_id=1, source_target_pairs={{1,0},{2,1},{3,2},{5,4},{6,5},{7,6},{9,8},{10,9},{11,10},{13,12},{... | collective-permute-start | bytes 17288 | tf_op jit(solution)/shard_map/ppermute | solution.py:23
  41.9 1.9 multiply_reduce_fusion
  43.9 0.9 copy.28
  44.8 0.9 collective-permute-done.2
  45.7 1.5 collective-permute-done.3
  47.2 2.3 %maximum_maximum_fusion = (bf16[96,10,259]{2,1,0:T(8,128)(2,1)S(1)}, bf16[96,10,259]{2,1,0:T(8,128)(2,1)S(1)}) fusion(bf16[96,3,256]{2,1,0:T(4,128)(2,1)S(1)} %collective-permute-done.1, bf16[96,4,256]{2,1,0:T(4,128)(2,1)S(1)} %copy-done.1, bf16[96,3,256]{2,1,0:T(4,128)(2,1)S(1)} %collective-permute-done, bf16[96,10,3]{2,1,0:T(8,128)(2,1)S(1)} %collective-permute-done.2, ...), kind=kLoop, calls=%fused_computation.66 | loop fusion | flops 3978240 | bytes 1497600 | tf_op jit(solution)/shard_map/concatenate | solution.py:24
  49.9 12.7 %fusion.118 = (f32[4,256]{1,0:T(4,128)S(1)}, f32[96,4,256]{2,1,0:T(4,128)S(1)}) fusion(f32[96]{0:T(128)S(1)} %copy-done.135, bf16[96,10,259]{2,1,0:T(8,128)(2,1)S(1)} %get-tuple-element.95, f32[96]{0:T(128)} %get-tuple-element.157, f32[96]{0:T(128)} %get-tuple-element.158, f32[96]{0:T(128)S(1)} %get-tuple-element.111, ...), kind=kLoop, calls=%fused_computation.315 | loop fusion | flops 16317440 | bytes 9165568 | tf_op jit(solution)/shard_map/reduce_sum | solution.py:95
  62.7 0.2 multiply_reduce_fusion.3
  62.9 1.5 fusion.9
  64.4 0.9 convert_reduce_fusion
  65.4 1.1 fusion.117
  66.5 1.0 fusion.108
  67.5 1.4 convert_reduce_fusion.1
  68.9 1.1 reshape.129
  70.0 2.9 %fusion.106 = (f32[96]{0:T(128)}, f32[96]{0:T(128)}, f32[96]{0:T(128)}, f32[96]{0:T(128)S(1)}, f32[96]{0:T(128)}, /*index=5*/f32[96]{0:T(128)}) fusion(bf16[96,4,256]{2,1,0:T(4,128)(2,1)S(1)} %reshape.129, bf16[96,10,259]{2,1,0:T(8,128)(2,1)S(1)} %get-tuple-element.95, bf16[96,10,259]{2,1,0:T(8,128)(2,1)S(1)} %get-tuple-element.94), kind=kLoop, calls=%fused_computation.222 | loop fusion | flops 1867200 | bytes 1378560 | tf_op jit(solution)/shard_map/reduce_sum | solution.py:60
  72.9 8.1 %fusion.103 = (f32[96]{0:T(128)}, f32[96]{0:T(128)S(1)}, f32[96]{0:T(128)S(1)}, f32[96]{0:T(128)}, f32[96]{0:T(128)}, /*index=5*/f32[96]{0:T(128)}, f32[96]{0:T(...) fusion(bf16[96,4,256]{2,1,0:T(4,128)(2,1)S(1)} %reshape.129, ...), kind=kLoop, calls=%fused_computation.219 | loop fusion | flops 5404992 | bytes 3742464 | tf_op jit(solution)/shard_map/reduce_sum | solution.py:60
  81.0 9.8 %fusion.107 = (f32[96]{0:T(128)}, f32[96]{0:T(128)S(1)}, f32[96]{0:T(128)S(1)}, f32[96]{0:T(128)S(1)}, f32[96]{0:T(128)}, /*index=5*/f32[96]{0:T(128)}, f32[96]{...) fusion(bf16[96,4,256]{2,1,0:T(4,128)(2,1)S(1)} %reshape.129, ...), kind=kLoop, calls=%fused_computation.223 | loop fusion | flops 5404992 | bytes 3742464 | tf_op jit(solution)/shard_map/reduce_sum | solution.py:60
  90.9 0.9 fusion.122
  91.7 0.1 reshape.128
  91.8 1.8 reshape.127
  93.6 0.4 fusion.116
  94.3 0.8 reshape.126
  95.2 3.2 %fusion.104 = (f32[96]{0:T(128)}, f32[96]{0:T(128)}, f32[96]{0:T(128)}, f32[96]{0:T(128)}, f32[96]{0:T(128)S(1)}, /*index=5*/f32[96]{0:T(128)}, f32[96]{0:T(128)}) fusion(bf16[96,4,256]{2,1,0:T(4,128)(2,1)S(1)} %reshape.129, bf16[96,3,256]{2,1,0:T(4,128)(2,1)S(1)} %collective-permute-done.1, bf16[96,4,256]{2,1,0:T(4,128)(2,1)S(1)} %copy-done.1, ...), kind=kLoop, calls=%fused_computation.220 | loop fusion | flops 3931488 | bytes 690816 | tf_op jit(solution)/shard_map/reduce_sum | solution.py:60
  98.6 1.9 collective-permute-start.5
  100.5 2.4 %collective-permute-start.4 = (bf16[96,3,256]{2,1,0:T(4,128)(2,1)}, bf16[96,3,256]{2,1,0:T(4,128)(2,1)S(1)}, u32[]{:S(2)}, u32[]{:S(2)}) collective-permute-start(bf16[96,3,256]{2,1,0:T(4,128)(2,1)} %get-tuple-element.98), channel_id=1, source_target_pairs={{0,4},{4,8},{8,12},{12,16},{16,20},{20,24},{24,28},{28,32},{32,36}... | collective-permute-start | bytes 442376 | tf_op jit(solution)/shard_map/ppermute | solution.py:22
  102.9 2.3 %multiply_reduce_fusion.1 = (f32[96]{0:T(128)}, bf16[96,1024]{1,0:T(8,128)(2,1)}) fusion(f32[96,1024]{1,0:T(8,128)S(1)} %bitcast.230, f32[96,1024]{1,0:T(8,128)S(1)} %bitcast.233, f32[96]{0:T(128)S(1)} %copy-done.17, f32[96]{0:T(128)} %param.20, bf16[384,1024]{0,1:T(8,128)(2,1)S(1)} %copy-done.2, bf16[384,96]{0,1:T(8,128)(2,1)S(1)} %copy-done.15), kind=kOutput, calls=%fused_computation.229 | convolution fusion | flops 76087200 | bytes 1844352 | tf_op jit(solution)/shard_map/dot_general | solution.py:110
  105.3 0.7 stack.208
  106.0 0.7 stack.217
  106.8 0.6 stack.226
  107.9 10.1 %collective-permute-done.4 = bf16[96,3,256]{2,1,0:T(4,128)(2,1)S(1)} collective-permute-done((bf16[96,3,256]{2,1,0:T(4,128)(2,1)}, bf16[96,3,256]{2,1,0:T(4,128)(2,1)S(1)}, u32[]{:S(2)}, u32[]{:S(2)}) %collective-permute-start.4) | collective-permute-done | bytes 147488 | tf_op jit(solution)/shard_map/ppermute | solution.py:22
  117.9 0.5 pad_maximum_fusion.3
  118.5 1.1 fusion.120
  119.5 5.4 %collective-permute-start.7 = (bf16[96,10,3]{2,1,0:T(8,128)(2,1)}, bf16[96,10,3]{2,1,0:T(8,128)(2,1)S(1)}, u32[]{:S(2)}, u32[]{:S(2)}) collective-permute-start(bf16[96,10,3]{2,1,0:T(8,128)(2,1)} %get-tuple-element.91), channel_id=1, source_target_pairs={{1,0},{2,1},{3,2},{5,4},{6,5},{7,6},{9,8},{10,9},{11,10},{13,12},{... | collective-permute-start | bytes 17288 | tf_op jit(solution)/shard_map/ppermute | solution.py:23
  125.0 1.6 collective-permute-start.6
  126.5 0.8 reshape.125
  127.4 0.2 copy.24
  127.6 0.2 reshape.130
  127.8 0.1 reduce_sum.587
  127.9 0.1 concatenate.84
  128.0 2.5 %collective-permute-done.7 = bf16[96,10,3]{2,1,0:T(8,128)(2,1)S(1)} collective-permute-done((bf16[96,10,3]{2,1,0:T(8,128)(2,1)}, bf16[96,10,3]{2,1,0:T(8,128)(2,1)S(1)}, u32[]{:S(2)}, u32[]{:S(2)}) %collective-permute-start.7) | collective-permute-done | bytes 5792 | tf_op jit(solution)/shard_map/ppermute | solution.py:23
  130.5 4.6 %collective-permute-done.6 = bf16[96,10,3]{2,1,0:T(8,128)(2,1)S(1)} collective-permute-done((bf16[96,10,3]{2,1,0:T(8,128)(2,1)}, bf16[96,10,3]{2,1,0:T(8,128)(2,1)S(1)}, u32[]{:S(2)}, u32[]{:S(2)}) %collective-permute-start.6) | collective-permute-done | bytes 5792 | tf_op jit(solution)/shard_map/ppermute | solution.py:22
  135.2 2.9 %pad_maximum_fusion.1 = bf16[96,10,262]{2,1,0:T(8,128)(2,1)S(1)} fusion(bf16[96,10,3]{2,1,0:T(8,128)(2,1)S(1)} %collective-permute-done.7, bf16[96,3,256]{2,1,0:T(4,128)(2,1)} %copy-done.10, bf16[96,4,256]{2,1,0:T(4,128)(2,1)S(1)} %reshape.129, bf16[96,3,256]{2,1,0:T(4,128)(2,1)} %copy-done.11, bf16[96,10,3]{2,1,0:T(8,128)(2,1)S(1)} %collective-permute-done.6), kind=kLoop, calls=%fused_computation.68 | loop fusion | flops 2515200 | bytes 1006080 | tf_op jit(solution)/shard_map/concatenate | solution.py:24
  138.5 0.1 reshape.131
  138.7 0.7 pad_maximum_fusion.4.buf_ref
  139.4 45.6 %shard_map.194 = f32[200,128]{1,0:T(8,128)} custom-call(f32[656,128]{1,0:T(8,128)} %pad_maximum_fusion.4.buf_ref), custom_call_target="tpu_custom_call" | custom-call | bytes 209715200 | tf_op jit(solution)/shard_map/pallas_call | solution.py:322
  185.0 0.7 slice_bitcast_fusion.1
  185.7 0.9 slice_bitcast_fusion
  186.6 0.1 maximum_multiply_fusion
  186.8 0.6 fusion.124
  187.8 13.5 %add_convert_fusion = bf16[96,4,256]{2,1,0:T(4,128)(2,1)} fusion(bf16[96,10,262]{2,1,0:T(8,128)(2,1)S(1)} %pad_maximum_fusion.1, bf16[96,4,256]{2,1,0:T(4,128)(2,1)S(1)} %copy-done.8, f32[96]{0:T(128)} %get-tuple-element.157, f32[96]{0:T(128)} %get-tuple-element.158, f32[96]{0:T(128)S(1)} %get-tuple-element.111, f32[96]{0:T(128)S(1)} %get-tuple-element.112, ...), kind=kLoop, calls=%fused_computation.227 | loop fusion | flops 14647296 | bytes 10045824 | tf_op jit(solution)/shard_map/convert_element_type | solution.py:176
  201.3 0.2 reshape.135
  201.5 0.8 copy.25
  202.2 0.7 slice.824
  202.9 0.7 slice.827
  (298 shorter events, 1.1 us)
Async XLA Ops:
  0.6 62.2 %copy-start = (bf16[384,96]{0,1:T(8,128)(2,1)S(1)}, bf16[384,96]{0,1:T(8,128)(2,1)}, u32[]{:S(2)}) copy-start(bf16[384,96]{0,1:T(8,128)(2,1)} %param.17) | copy-start | bytes 221188
  1.9 40.0 %copy-start.7 = (bf16[96,4,256]{2,1,0:T(4,128)(2,1)S(1)}, bf16[96,4,256]{2,1,0:T(4,128)(2,1)}, u32[]{:S(2)}) copy-start(bf16[96,4,256]{2,1,0:T(4,128)(2,1)} %param.12) | copy-start | bytes 589828
  1.9 40.0 %copy-start.17 = (f32[96]{0:T(128)S(1)}, f32[96]{0:T(128)}, u32[]{:S(2)}) copy-start(f32[96]{0:T(128)} %param.21) | copy-start | bytes 1156
  1.9 20.7 %collective-permute-start.1 = (bf16[96,3,256]{2,1,0:T(4,128)(2,1)S(1)}, bf16[96,3,256]{2,1,0:T(4,128)(2,1)S(1)}, u32[]{:S(2)}, u32[]{:S(2)}) collective-permute-start(bf16[96,3,256]{2,1,0:T(4,128)(2,1)S(1)} %get-tuple-element.101), channel_id=1, source_target_pairs={{4,0},{8,4},{12,8},{16,12},{20,16},{24,20},{28,24},{32,28},{36,32}... | collective-permute-start | bytes 442376 | tf_op jit(solution)/shard_map/ppermute | solution.py:23
  16.9 15.2 %collective-permute-start = (bf16[96,3,256]{2,1,0:T(4,128)(2,1)S(1)}, bf16[96,3,256]{2,1,0:T(4,128)(2,1)S(1)}, u32[]{:S(2)}, u32[]{:S(2)}) collective-permute-start(bf16[96,3,256]{2,1,0:T(4,128)(2,1)S(1)} %get-tuple-element.100), channel_id=1, source_target_pairs={{0,4},{4,8},{8,12},{12,16},{16,20},{20,24},{24,28},{28,32},{32,36}... | collective-permute-start | bytes 442376 | tf_op jit(solution)/shard_map/ppermute | solution.py:22
  19.8 29.7 %copy-start.18 = (f32[96]{0:T(128)}, f32[96]{0:T(128)S(1)}, u32[]{:S(2)}) copy-start(f32[96]{0:T(128)S(1)} %get-tuple-element.118) | copy-start | bytes 1156
  19.8 29.7 %copy-start.20 = (f32[96]{0:T(128)}, f32[96]{0:T(128)S(1)}, u32[]{:S(2)}) copy-start(f32[96]{0:T(128)S(1)} %get-tuple-element.119) | copy-start | bytes 1156
  19.8 29.7 %copy-start.22 = (f32[96]{0:T(128)}, f32[96]{0:T(128)S(1)}, u32[]{:S(2)}) copy-start(f32[96]{0:T(128)S(1)} %get-tuple-element.120) | copy-start | bytes 1156
  19.8 29.7 %copy-start.24 = (f32[96]{0:T(128)}, f32[96]{0:T(128)S(1)}, u32[]{:S(2)}) copy-start(f32[96]{0:T(128)S(1)} %get-tuple-element.121) | copy-start | bytes 1156
  19.8 29.7 %copy-start.26 = (f32[96]{0:T(128)}, f32[96]{0:T(128)S(1)}, u32[]{:S(2)}) copy-start(f32[96]{0:T(128)S(1)} %get-tuple-element.122) | copy-start | bytes 1156
  19.8 29.7 %copy-start.28 = (f32[96]{0:T(128)}, f32[96]{0:T(128)S(1)}, u32[]{:S(2)}) copy-start(f32[96]{0:T(128)S(1)} %get-tuple-element.123) | copy-start | bytes 1156
  19.8 29.7 %copy-start.30 = (f32[96]{0:T(128)}, f32[96]{0:T(128)S(1)}, u32[]{:S(2)}) copy-start(f32[96]{0:T(128)S(1)} %get-tuple-element.124) | copy-start | bytes 1156
  19.8 29.7 %copy-start.32 = (f32[96]{0:T(128)}, f32[96]{0:T(128)S(1)}, u32[]{:S(2)}) copy-start(f32[96]{0:T(128)S(1)} %get-tuple-element.125) | copy-start | bytes 1156
  19.9 29.7 %copy-start.34 = (f32[96]{0:T(128)}, f32[96]{0:T(128)S(1)}, u32[]{:S(2)}) copy-start(f32[96]{0:T(128)S(1)} %get-tuple-element.126) | copy-start | bytes 1156
  19.9 29.7 %copy-start.36 = (f32[96]{0:T(128)}, f32[96]{0:T(128)S(1)}, u32[]{:S(2)}) copy-start(f32[96]{0:T(128)S(1)} %get-tuple-element.127) | copy-start | bytes 1156
  19.9 29.7 %copy-start.38 = (f32[96]{0:T(128)}, f32[96]{0:T(128)S(1)}, u32[]{:S(2)}) copy-start(f32[96]{0:T(128)S(1)} %get-tuple-element.128) | copy-start | bytes 1156
  20.9 28.7 %copy-start.40 = (f32[96]{0:T(128)}, f32[96]{0:T(128)S(1)}, u32[]{:S(2)}) copy-start(f32[96]{0:T(128)S(1)} %get-tuple-element.129) | copy-start | bytes 1156
  20.9 28.7 %copy-start.42 = (f32[96]{0:T(128)}, f32[96]{0:T(128)S(1)}, u32[]{:S(2)}) copy-start(f32[96]{0:T(128)S(1)} %get-tuple-element.130) | copy-start | bytes 1156
  20.9 28.7 %copy-start.44 = (f32[96]{0:T(128)}, f32[96]{0:T(128)S(1)}, u32[]{:S(2)}) copy-start(f32[96]{0:T(128)S(1)} %get-tuple-element.131) | copy-start | bytes 1156
  20.9 28.7 %copy-start.46 = (f32[96]{0:T(128)}, f32[96]{0:T(128)S(1)}, u32[]{:S(2)}) copy-start(f32[96]{0:T(128)S(1)} %get-tuple-element.132) | copy-start | bytes 1156
  33.8 11.9 %collective-permute-start.2 = (bf16[96,10,3]{2,1,0:T(8,128)(2,1)S(1)}, bf16[96,10,3]{2,1,0:T(8,128)(2,1)S(1)}, u32[]{:S(2)}, u32[]{:S(2)}) collective-permute-start(bf16[96,10,3]{2,1,0:T(8,128)(2,1)S(1)} %get-tuple-element.92), channel_id=1, source_target_pairs={{0,1},{1,2},{2,3},{4,5},{5,6},{6,7},{8,9},{9,10},{10,11},{12,13},{... | collective-permute-start | bytes 17288 | tf_op jit(solution)/shard_map/ppermute | solution.py:22
  35.1 12.1 %collective-permute-start.3 = (bf16[96,10,3]{2,1,0:T(8,128)(2,1)S(1)}, bf16[96,10,3]{2,1,0:T(8,128)(2,1)S(1)}, u32[]{:S(2)}, u32[]{:S(2)}) collective-permute-start(bf16[96,10,3]{2,1,0:T(8,128)(2,1)S(1)} %get-tuple-element.93), channel_id=1, source_target_pairs={{1,0},{2,1},{3,2},{5,4},{6,5},{7,6},{9,8},{10,9},{11,10},{13,12},{... | collective-permute-start | bytes 17288 | tf_op jit(solution)/shard_map/ppermute | solution.py:23
  98.6 9.3 %collective-permute-start.5 = (bf16[96,3,256]{2,1,0:T(4,128)(2,1)}, bf16[96,3,256]{2,1,0:T(4,128)(2,1)S(1)}, u32[]{:S(2)}, u32[]{:S(2)}) collective-permute-start(bf16[96,3,256]{2,1,0:T(4,128)(2,1)} %get-tuple-element.99), channel_id=1, source_target_pairs={{4,0},{8,4},{12,8},{16,12},{20,16},{24,20},{28,24},{32,28},{36,32}... | collective-permute-start | bytes 442376 | tf_op jit(solution)/shard_map/ppermute | solution.py:23
  100.5 17.4 %collective-permute-start.4 = (bf16[96,3,256]{2,1,0:T(4,128)(2,1)}, bf16[96,3,256]{2,1,0:T(4,128)(2,1)S(1)}, u32[]{:S(2)}, u32[]{:S(2)}) collective-permute-start(bf16[96,3,256]{2,1,0:T(4,128)(2,1)} %get-tuple-element.98), channel_id=1, source_target_pairs={{0,4},{4,8},{8,12},{12,16},{16,20},{20,24},{24,28},{28,32},{32,36}... | collective-permute-start | bytes 442376 | tf_op jit(solution)/shard_map/ppermute | solution.py:22
  119.5 11.0 %collective-permute-start.7 = (bf16[96,10,3]{2,1,0:T(8,128)(2,1)}, bf16[96,10,3]{2,1,0:T(8,128)(2,1)S(1)}, u32[]{:S(2)}, u32[]{:S(2)}) collective-permute-start(bf16[96,10,3]{2,1,0:T(8,128)(2,1)} %get-tuple-element.91), channel_id=1, source_target_pairs={{1,0},{2,1},{3,2},{5,4},{6,5},{7,6},{9,8},{10,9},{11,10},{13,12},{... | collective-permute-start | bytes 17288 | tf_op jit(solution)/shard_map/ppermute | solution.py:23
  125.0 10.2 %collective-permute-start.6 = (bf16[96,10,3]{2,1,0:T(8,128)(2,1)}, bf16[96,10,3]{2,1,0:T(8,128)(2,1)S(1)}, u32[]{:S(2)}, u32[]{:S(2)}) collective-permute-start(bf16[96,10,3]{2,1,0:T(8,128)(2,1)} %get-tuple-element.90), channel_id=1, source_target_pairs={{0,1},{1,2},{2,3},{4,5},{5,6},{6,7},{8,9},{9,10},{10,11},{12,13},{... | collective-permute-start | bytes 17288 | tf_op jit(solution)/shard_map/ppermute | solution.py:22
  138.1 49.3 %copy-start.8 = (bf16[96,4,256]{2,1,0:T(4,128)(2,1)S(1)}, bf16[96,4,256]{2,1,0:T(4,128)(2,1)}, u32[]{:S(2)}) copy-start(bf16[96,4,256]{2,1,0:T(4,128)(2,1)} %param.12) | copy-start | bytes 589828
  138.1 49.3 %copy-start.19 = (f32[96]{0:T(128)S(1)}, f32[96]{0:T(128)}, u32[]{:S(2)}) copy-start(f32[96]{0:T(128)} %copy-done.18) | copy-start | bytes 1156
  138.1 49.3 %copy-start.21 = (f32[96]{0:T(128)S(1)}, f32[96]{0:T(128)}, u32[]{:S(2)}) copy-start(f32[96]{0:T(128)} %copy-done.20) | copy-start | bytes 1156
  138.1 49.3 %copy-start.23 = (f32[96]{0:T(128)S(1)}, f32[96]{0:T(128)}, u32[]{:S(2)}) copy-start(f32[96]{0:T(128)} %copy-done.22) | copy-start | bytes 1156
  138.1 49.3 %copy-start.25 = (f32[96]{0:T(128)S(1)}, f32[96]{0:T(128)}, u32[]{:S(2)}) copy-start(f32[96]{0:T(128)} %copy-done.24) | copy-start | bytes 1156
  138.1 49.3 %copy-start.27 = (f32[96]{0:T(128)S(1)}, f32[96]{0:T(128)}, u32[]{:S(2)}) copy-start(f32[96]{0:T(128)} %copy-done.26) | copy-start | bytes 1156
  138.1 49.3 %copy-start.29 = (f32[96]{0:T(128)S(1)}, f32[96]{0:T(128)}, u32[]{:S(2)}) copy-start(f32[96]{0:T(128)} %copy-done.28) | copy-start | bytes 1156
  138.1 49.3 %copy-start.31 = (f32[96]{0:T(128)S(1)}, f32[96]{0:T(128)}, u32[]{:S(2)}) copy-start(f32[96]{0:T(128)} %copy-done.30) | copy-start | bytes 1156
  138.2 49.3 %copy-start.33 = (f32[96]{0:T(128)S(1)}, f32[96]{0:T(128)}, u32[]{:S(2)}) copy-start(f32[96]{0:T(128)} %copy-done.32) | copy-start | bytes 1156
  138.2 49.3 %copy-start.35 = (f32[96]{0:T(128)S(1)}, f32[96]{0:T(128)}, u32[]{:S(2)}) copy-start(f32[96]{0:T(128)} %copy-done.34) | copy-start | bytes 1156
  138.2 49.3 %copy-start.37 = (f32[96]{0:T(128)S(1)}, f32[96]{0:T(128)}, u32[]{:S(2)}) copy-start(f32[96]{0:T(128)} %copy-done.36) | copy-start | bytes 1156
  138.2 49.3 %copy-start.39 = (f32[96]{0:T(128)S(1)}, f32[96]{0:T(128)}, u32[]{:S(2)}) copy-start(f32[96]{0:T(128)} %copy-done.38) | copy-start | bytes 1156
  138.2 49.3 %copy-start.41 = (f32[96]{0:T(128)S(1)}, f32[96]{0:T(128)}, u32[]{:S(2)}) copy-start(f32[96]{0:T(128)} %copy-done.40) | copy-start | bytes 1156
  138.2 49.3 %copy-start.43 = (f32[96]{0:T(128)S(1)}, f32[96]{0:T(128)}, u32[]{:S(2)}) copy-start(f32[96]{0:T(128)} %copy-done.42) | copy-start | bytes 1156
  138.2 49.3 %copy-start.45 = (f32[96]{0:T(128)S(1)}, f32[96]{0:T(128)}, u32[]{:S(2)}) copy-start(f32[96]{0:T(128)} %copy-done.44) | copy-start | bytes 1156
  138.2 49.3 %copy-start.47 = (f32[96]{0:T(128)S(1)}, f32[96]{0:T(128)}, u32[]{:S(2)}) copy-start(f32[96]{0:T(128)} %copy-done.46) | copy-start | bytes 1156
  138.2 49.3 %copy-start.49 = (f32[96]{0:T(128)S(1)}, f32[96]{0:T(128)}, u32[]{:S(2)}) copy-start(f32[96]{0:T(128)} %copy-done.48) | copy-start | bytes 1156
  138.2 49.3 %copy-start.51 = (f32[96]{0:T(128)S(1)}, f32[96]{0:T(128)}, u32[]{:S(2)}) copy-start(f32[96]{0:T(128)} %copy-done.50) | copy-start | bytes 1156
  138.3 49.3 %copy-start.53 = (f32[96]{0:T(128)S(1)}, f32[96]{0:T(128)}, u32[]{:S(2)}) copy-start(f32[96]{0:T(128)} %copy-done.52) | copy-start | bytes 1156
  138.3 49.3 %copy-start.55 = (f32[96]{0:T(128)S(1)}, f32[96]{0:T(128)}, u32[]{:S(2)}) copy-start(f32[96]{0:T(128)} %copy-done.54) | copy-start | bytes 1156
  138.3 49.3 %copy-start.57 = (f32[96]{0:T(128)S(1)}, f32[96]{0:T(128)}, u32[]{:S(2)}) copy-start(f32[96]{0:T(128)} %copy-done.56) | copy-start | bytes 1156
  138.3 49.3 %copy-start.59 = (f32[96]{0:T(128)S(1)}, f32[96]{0:T(128)}, u32[]{:S(2)}) copy-start(f32[96]{0:T(128)} %copy-done.58) | copy-start | bytes 1156
  138.3 49.3 %copy-start.61 = (f32[96]{0:T(128)S(1)}, f32[96]{0:T(128)}, u32[]{:S(2)}) copy-start(f32[96]{0:T(128)} %copy-done.60) | copy-start | bytes 1156
  138.3 49.3 %copy-start.63 = (f32[96]{0:T(128)S(1)}, f32[96]{0:T(128)}, u32[]{:S(2)}) copy-start(f32[96]{0:T(128)} %copy-done.62) | copy-start | bytes 1156
  138.3 49.3 %copy-start.65 = (f32[96]{0:T(128)S(1)}, f32[96]{0:T(128)}, u32[]{:S(2)}) copy-start(f32[96]{0:T(128)} %copy-done.64) | copy-start | bytes 1156
  138.3 49.3 %copy-start.67 = (f32[96]{0:T(128)S(1)}, f32[96]{0:T(128)}, u32[]{:S(2)}) copy-start(f32[96]{0:T(128)} %copy-done.66) | copy-start | bytes 1156
  138.3 49.3 %copy-start.69 = (f32[96]{0:T(128)S(1)}, f32[96]{0:T(128)}, u32[]{:S(2)}) copy-start(f32[96]{0:T(128)} %copy-done.68) | copy-start | bytes 1156
  138.3 49.3 %copy-start.71 = (f32[96]{0:T(128)S(1)}, f32[96]{0:T(128)}, u32[]{:S(2)}) copy-start(f32[96]{0:T(128)} %copy-done.70) | copy-start | bytes 1156
  138.4 49.3 %copy-start.73 = (f32[96]{0:T(128)S(1)}, f32[96]{0:T(128)}, u32[]{:S(2)}) copy-start(f32[96]{0:T(128)} %copy-done.72) | copy-start | bytes 1156
  138.4 49.3 %copy-start.75 = (f32[96]{0:T(128)S(1)}, f32[96]{0:T(128)}, u32[]{:S(2)}) copy-start(f32[96]{0:T(128)} %copy-done.74) | copy-start | bytes 1156
  138.4 49.3 %copy-start.77 = (f32[96]{0:T(128)S(1)}, f32[96]{0:T(128)}, u32[]{:S(2)}) copy-start(f32[96]{0:T(128)} %copy-done.76) | copy-start | bytes 1156
  138.4 49.3 %copy-start.79 = (f32[96]{0:T(128)S(1)}, f32[96]{0:T(128)}, u32[]{:S(2)}) copy-start(f32[96]{0:T(128)} %copy-done.78) | copy-start | bytes 1156
  138.4 49.3 %copy-start.81 = (f32[96]{0:T(128)S(1)}, f32[96]{0:T(128)}, u32[]{:S(2)}) copy-start(f32[96]{0:T(128)} %copy-done.80) | copy-start | bytes 1156
  138.4 49.3 %copy-start.83 = (f32[96]{0:T(128)S(1)}, f32[96]{0:T(128)}, u32[]{:S(2)}) copy-start(f32[96]{0:T(128)} %copy-done.82) | copy-start | bytes 1156
  138.4 49.3 %copy-start.85 = (f32[96]{0:T(128)S(1)}, f32[96]{0:T(128)}, u32[]{:S(2)}) copy-start(f32[96]{0:T(128)} %copy-done.84) | copy-start | bytes 1156
  138.4 49.3 %copy-start.87 = (f32[96]{0:T(128)S(1)}, f32[96]{0:T(128)}, u32[]{:S(2)}) copy-start(f32[96]{0:T(128)} %copy-done.86) | copy-start | bytes 1156
  138.4 49.3 %copy-start.89 = (f32[96]{0:T(128)S(1)}, f32[96]{0:T(128)}, u32[]{:S(2)}) copy-start(f32[96]{0:T(128)} %copy-done.88) | copy-start | bytes 1156
  138.4 49.3 %copy-start.91 = (f32[96]{0:T(128)S(1)}, f32[96]{0:T(128)}, u32[]{:S(2)}) copy-start(f32[96]{0:T(128)} %copy-done.90) | copy-start | bytes 1156
  (80 other events, 1284.4 us)

commit v4 on v3

--- a/solution.py
+++ b/solution.py
@@ -50,16 +50,20 @@
 
 
 def kernel_terms(padded, convolution_gradient, row_count, col_count):
-    lines = []
-    for shift_row in range(7):
-        entries = []
-        for shift_col in range(7):
-            piece = padded[
-                :, shift_row : shift_row + row_count, shift_col : shift_col + col_count
-            ].astype(jnp.float32)
-            entries.append(jnp.sum(piece * convolution_gradient, axis=(1, 2)))
-        lines.append(jnp.stack(entries, axis=1))
-    return jnp.stack(lines, axis=1)
+    ksize = 7
+    columns = []
+    for shift_col in range(ksize):
+        corr = jnp.einsum(
+            "crj,cij->cri",
+            padded[:, :, shift_col : shift_col + col_count],
+            convolution_gradient,
+            preferred_element_type=jnp.float32,
+        )
+        total = corr[:, 0:ksize, 0]
+        for row in range(1, row_count):
+            total = total + corr[:, row : row + ksize, row]
+        columns.append(total)
+    return jnp.stack(columns, axis=2)
 
 
 def gelu_exact(value):
@@ -150,7 +154,7 @@
     d_float = convolution_gradient.astype(jnp.float32)
     g_dbias = jnp.sum(d_float, axis=(1, 2))
     padded_grad = padded_2(convolution_gradient, (("space", 1), ("filt", 2)), 3)
-    g_kernel = kernel_terms(padded, d_float, row_count, col_count)
+    g_kernel = kernel_terms(padded, convolution_gradient, row_count, col_count)
     factor = 1.0 / math.sqrt(tok_count * lax.axis_size("space") * lax.axis_size("filt"))
     parts = lax.axis_size("filt")
     panels = jnp.concatenate(

time: 207 us -> 190 us (0.918)
  other arithmetic: 62 us -> 38.8 us
  matrix products: 7.36 us -> 11.8 us
  starting transfers between devices: 36.3 us -> 38.4 us
    reduce_sum x4 -> x0, other arithmetic: 24.1 us -> none  [kernel_terms(): entries.append(jnp.sum(piece * convolution_gradient, axis=(1, 2)))]
    dot_general x0 -> x7, matrix products: none -> 5.4 us  [kernel_terms(): jnp.einsum('crj,cij->cri', padded[:, :, shift_col:shift_col + col_count],...]
    slice x0 -> x35, local copies, waits for them, and re-layouts: none -> 4.86 us  [the longest x28 4.3 us: kernel_terms(): total = total + corr[:, row:row + ksize, row]]
    ppermute x4, starting transfers between devices: 29.1 us -> 31.2 us  [padded_2(): after = lax.ppermute(initial, axis, down)]
    another operation x9 -> x2, local copies, waits for them, and re-layouts: 2.34 us -> 0.27 us  [kernel_terms(): return jnp.stack(columns, axis=2)]
  transfers between devices with their start and end apart: 8 -> 8, of which waited for: 6 -> 6; matrix products, arithmetic and copies ran while one was open for 6% -> 5% of each run, Pallas kernels for 0% -> 0%
where the time goes in v4:
time: 190 us; the launch traced here: 188 us
  Pallas kernels  45.2 us (24%)
  other arithmetic  38.8 us (20%)
  starting transfers between devices  38.4 us (20%)
  waiting for transfers between devices  30.6 us (16%)
  local copies, waits for them, and re-layouts  20.7 us (11%)
  matrix products  11.8 us (6%)
  between operations  2.45 us (1%)
    pallas_call x1, Pallas kernels, grad_reduce(): pl.pallas_call(functools.partial(reduce_kernel, nfilt, nspace, pr, sr), o...  45.2 us
    ppermute x4, starting transfers between devices, padded_2(): after = lax.ppermute(initial, axis, down)  31.2 us
    ppermute x4, waiting for transfers between devices, padded_2(): before = lax.ppermute(last, axis, up)  26.7 us
    convert_element_type x1, other arithmetic, shards(): image_grad = (cotangent.astype(jnp.float32) + back).astype(jnp.bfloat16)  14 us
    reduce_sum x1, other arithmetic, shards(): average = jnp.mean(flat, axis=0, keepdims=True)  13.2 us
    ppermute x4, starting transfers between devices, padded_2(): before = lax.ppermute(last, axis, up)  7.13 us
    concatenate x4, other arithmetic, padded_2(): x = jnp.concatenate([before, x, after], axis=dim)  7.02 us
    dot_general x7, matrix products, kernel_terms(): jnp.einsum('crj,cij->cri', padded[:, :, shift_col:shift_col + col_count],...  5.4 us
  transfers between devices with their start and end apart: 8, of which 6 were waited for; matrix products, arithmetic and copies ran while one was open for 5% of the time, Pallas kernels for 0%

profile of v4, /device:TPU:56, one launch (start us, length us, event | category | flops | bytes accessed | tf_op | source)
XLA Modules:
  0.0 188.0 jit_solution(11205198445199776060)
XLA Ops:
  0.7 1.2 fusion.43
  1.9 15.0 %collective-permute-start.1 = (bf16[96,3,256]{2,1,0:T(4,128)(2,1)S(1)}, bf16[96,3,256]{2,1,0:T(4,128)(2,1)S(1)}, u32[]{:S(2)}, u32[]{:S(2)}) collective-permute-start(bf16[96,3,256]{2,1,0:T(4,128)(2,1)S(1)} %get-tuple-element.85), channel_id=1, source_target_pairs={{4,0},{8,4},{12,8},{16,12},{20,16},{24,20},{28,24},{32,28},{36,32}... | collective-permute-start | bytes 442376 | tf_op jit(solution)/shard_map/ppermute | solution.py:23
  16.9 1.9 %collective-permute-start = (bf16[96,3,256]{2,1,0:T(4,128)(2,1)S(1)}, bf16[96,3,256]{2,1,0:T(4,128)(2,1)S(1)}, u32[]{:S(2)}, u32[]{:S(2)}) collective-permute-start(bf16[96,3,256]{2,1,0:T(4,128)(2,1)S(1)} %get-tuple-element.84), channel_id=1, source_target_pairs={{0,4},{4,8},{8,12},{12,16},{16,20},{20,24},{24,28},{28,32},{32,36}... | collective-permute-start | bytes 442376 | tf_op jit(solution)/shard_map/ppermute | solution.py:22
  18.8 1.0 slice_bitcast_fusion.50
  20.0 1.0 slice_bitcast_fusion.49
  21.2 1.5 slice_bitcast_fusion.48
  22.7 9.4 %collective-permute-done = bf16[96,3,256]{2,1,0:T(4,128)(2,1)S(1)} collective-permute-done((bf16[96,3,256]{2,1,0:T(4,128)(2,1)S(1)}, bf16[96,3,256]{2,1,0:T(4,128)(2,1)S(1)}, u32[]{:S(2)}, u32[]{:S(2)}) %collective-permute-start) | collective-permute-done | bytes 147488 | tf_op jit(solution)/shard_map/ppermute | solution.py:22
  32.1 1.4 pad_maximum_fusion.2
  33.5 0.2 fusion.34
  33.7 1.3 collective-permute-start.2
  35.0 6.8 %collective-permute-start.3 = (bf16[96,10,3]{2,1,0:T(8,128)(2,1)S(1)}, bf16[96,10,3]{2,1,0:T(8,128)(2,1)S(1)}, u32[]{:S(2)}, u32[]{:S(2)}) collective-permute-start(bf16[96,10,3]{2,1,0:T(8,128)(2,1)S(1)} %get-tuple-element.49), channel_id=1, source_target_pairs={{1,0},{2,1},{3,2},{5,4},{6,5},{7,6},{9,8},{10,9},{11,10},{13,12},{... | collective-permute-start | bytes 17288 | tf_op jit(solution)/shard_map/ppermute | solution.py:23
  41.8 1.9 %multiply_reduce_fusion = f32[96]{0:T(128)} fusion(f32[96]{0:T(128)S(1)} %copy-done.18, bf16[96,4,256]{2,1,0:T(4,128)(2,1)S(1)} %copy-done.7), kind=kLoop, calls=%fused_computation.46 | loop fusion | flops 294816 | bytes 197376 | tf_op jit(solution)/shard_map/reduce_sum | solution.py:128
  43.8 0.8 copy.60
  44.7 0.9 collective-permute-done.2
  45.6 1.5 collective-permute-done.3
  47.1 2.2 %maximum_maximum_fusion = (bf16[96,10,259]{2,1,0:T(8,128)(2,1)S(1)}, bf16[96,10,259]{2,1,0:T(8,128)(2,1)S(1)}) fusion(bf16[96,3,256]{2,1,0:T(4,128)(2,1)S(1)} %collective-permute-done.1, bf16[96,4,256]{2,1,0:T(4,128)(2,1)S(1)} %copy-done.2, bf16[96,3,256]{2,1,0:T(4,128)(2,1)S(1)} %collective-permute-done, bf16[96,10,3]{2,1,0:T(8,128)(2,1)S(1)} %collective-permute-done.2, ...), kind=kLoop, calls=%fused_computation.17 | loop fusion | flops 3978240 | bytes 1497600 | tf_op jit(solution)/shard_map/concatenate | solution.py:24
  49.7 13.2 %fusion.32 = (f32[4,256]{1,0:T(4,128)S(1)}, f32[96,4,256]{2,1,0:T(4,128)S(1)}) fusion(f32[96]{0:T(128)S(1)} %copy-done.100, bf16[96,10,259]{2,1,0:T(8,128)(2,1)S(1)} %get-tuple-element.51, f32[96]{0:T(128)} %get-tuple-element.141, f32[96]{0:T(128)} %get-tuple-element.142, f32[96]{0:T(128)S(1)} %get-tuple-element.95, ...), kind=kLoop, calls=%fused_computation.133 | loop fusion | flops 16317440 | bytes 9165568 | tf_op jit(solution)/shard_map/reduce_sum | solution.py:99
  63.2 1.5 fusion.9
  64.8 0.9 convert_reduce_fusion
  65.7 1.1 fusion.31
  66.8 1.0 fusion.23
  67.8 1.4 convert_reduce_fusion.1
  69.3 1.1 reshape.129
  70.4 1.0 fusion.21
  71.3 1.1 fusion.19
  72.4 1.1 fusion.17
  73.5 1.0 fusion.46
  74.5 0.4 fusion.15
  74.9 0.4 fusion.13
  75.4 0.4 fusion.11
  75.8 0.9 fusion.35
  77.0 0.4 fusion.30
  77.4 0.2 reshape.126
  77.6 0.4 fusion.42
  78.3 0.4 fusion.41
  79.0 0.4 fusion.40
  79.7 0.4 fusion.39
  80.4 0.4 fusion.38
  81.1 0.4 fusion.37
  81.8 0.4 fusion.36
  82.5 1.9 %collective-permute-start.5 = (bf16[96,3,256]{2,1,0:T(4,128)(2,1)}, bf16[96,3,256]{2,1,0:T(4,128)(2,1)S(1)}, u32[]{:S(2)}, u32[]{:S(2)}) collective-permute-start(bf16[96,3,256]{2,1,0:T(4,128)(2,1)} %get-tuple-element.55), channel_id=1, source_target_pairs={{4,0},{8,4},{12,8},{16,12},{20,16},{24,20},{28,24},{32,28},{36,32}... | collective-permute-start | bytes 442376 | tf_op jit(solution)/shard_map/ppermute | solution.py:23
  84.5 2.4 %collective-permute-start.4 = (bf16[96,3,256]{2,1,0:T(4,128)(2,1)S(1)}, bf16[96,3,256]{2,1,0:T(4,128)(2,1)S(1)}, u32[]{:S(2)}, u32[]{:S(2)}) collective-permute-start(bf16[96,3,256]{2,1,0:T(4,128)(2,1)S(1)} %copy-done.15), channel_id=1, source_target_pairs={{0,4},{4,8},{8,12},{12,16},{16,20},{20,24},{24,28},{28,32},{32,36}... | collective-permute-start | bytes 442376 | tf_op jit(solution)/shard_map/ppermute | solution.py:22
  86.9 1.4 multiply_reduce_fusion.1
  88.5 12.1 %collective-permute-done.4 = bf16[96,3,256]{2,1,0:T(4,128)(2,1)S(1)} collective-permute-done((bf16[96,3,256]{2,1,0:T(4,128)(2,1)S(1)}, bf16[96,3,256]{2,1,0:T(4,128)(2,1)S(1)}, u32[]{:S(2)}, u32[]{:S(2)}) %collective-permute-start.4) | collective-permute-done | bytes 147488 | tf_op jit(solution)/shard_map/ppermute | solution.py:22
  100.6 0.5 pad_maximum_fusion.3
  101.1 0.9 fusion.33
  102.1 7.6 %collective-permute-start.7 = (bf16[96,10,3]{2,1,0:T(8,128)(2,1)}, bf16[96,10,3]{2,1,0:T(8,128)(2,1)S(1)}, u32[]{:S(2)}, u32[]{:S(2)}) collective-permute-start(bf16[96,10,3]{2,1,0:T(8,128)(2,1)} %get-tuple-element.47), channel_id=1, source_target_pairs={{1,0},{2,1},{3,2},{5,4},{6,5},{7,6},{9,8},{10,9},{11,10},{13,12},{... | collective-permute-start | bytes 17288 | tf_op jit(solution)/shard_map/ppermute | solution.py:23
  109.6 1.5 collective-permute-start.6
  111.2 0.8 reshape.125
  112.0 0.2 copy.56
  112.3 0.2 reshape.130
  112.7 2.5 %collective-permute-done.7 = bf16[96,10,3]{2,1,0:T(8,128)(2,1)S(1)} collective-permute-done((bf16[96,10,3]{2,1,0:T(8,128)(2,1)}, bf16[96,10,3]{2,1,0:T(8,128)(2,1)S(1)}, u32[]{:S(2)}, u32[]{:S(2)}) %collective-permute-start.7) | collective-permute-done | bytes 5792 | tf_op jit(solution)/shard_map/ppermute | solution.py:23
  115.2 4.2 %collective-permute-done.6 = bf16[96,10,3]{2,1,0:T(8,128)(2,1)} collective-permute-done((bf16[96,10,3]{2,1,0:T(8,128)(2,1)S(1)}, bf16[96,10,3]{2,1,0:T(8,128)(2,1)}, u32[]{:S(2)}, u32[]{:S(2)}) %collective-permute-start.6) | collective-permute-done | bytes 5792 | tf_op jit(solution)/shard_map/ppermute | solution.py:22
  119.4 2.9 %pad_maximum_fusion.1 = bf16[96,10,262]{2,1,0:T(8,128)(2,1)S(1)} fusion(bf16[96,10,3]{2,1,0:T(8,128)(2,1)S(1)} %collective-permute-done.7, bf16[96,3,256]{2,1,0:T(4,128)(2,1)S(1)} %collective-permute-done.5, bf16[96,4,256]{2,1,0:T(4,128)(2,1)S(1)} %reshape.129, bf16[96,3,256]{2,1,0:T(4,128)(2,1)S(1)} %collective-permute-done.4, ...), kind=kLoop, calls=%fused_computation.19 | loop fusion | flops 2515200 | bytes 1006080 | tf_op jit(solution)/shard_map/concatenate | solution.py:24
  122.9 0.8 pad_maximum_fusion.4.buf_ref
  123.7 45.2 %shard_map.194 = f32[200,128]{1,0:T(8,128)} custom-call(f32[656,128]{1,0:T(8,128)} %pad_maximum_fusion.4.buf_ref), custom_call_target="tpu_custom_call" | custom-call | bytes 209715200 | tf_op jit(solution)/shard_map/pallas_call | solution.py:326
  168.9 0.7 slice_bitcast_fusion.1
  169.6 0.9 slice_bitcast_fusion
  170.7 0.6 fusion.44
  171.7 14.0 %add_convert_fusion = bf16[96,4,256]{2,1,0:T(4,128)(2,1)} fusion(bf16[96,10,262]{2,1,0:T(8,128)(2,1)S(1)} %pad_maximum_fusion.1, bf16[96,4,256]{2,1,0:T(4,128)(2,1)S(1)} %copy-done.8, f32[96]{0:T(128)} %get-tuple-element.141, f32[96]{0:T(128)} %get-tuple-element.142, f32[96]{0:T(128)S(1)} %copy-done.22, f32[96]{0:T(128)S(1)} %copy-done.24, ...), kind=kLoop, calls=%fused_computation.45 | loop fusion | flops 14647296 | bytes 10045824 | tf_op jit(solution)/shard_map/convert_element_type | solution.py:180
  185.6 0.2 reshape.135
  185.8 0.8 copy.57
  186.6 0.7 slice.918
  187.3 0.7 slice.921
  (260 shorter events, 3.9 us)
Async XLA Ops:
  0.6 62.6 %copy-start = (bf16[384,96]{0,1:T(8,128)(2,1)S(1)}, bf16[384,96]{0,1:T(8,128)(2,1)}, u32[]{:S(2)}) copy-start(bf16[384,96]{0,1:T(8,128)(2,1)} %param.17) | copy-start | bytes 221188
  1.9 39.9 %copy-start.7 = (bf16[96,4,256]{2,1,0:T(4,128)(2,1)S(1)}, bf16[96,4,256]{2,1,0:T(4,128)(2,1)}, u32[]{:S(2)}) copy-start(bf16[96,4,256]{2,1,0:T(4,128)(2,1)} %param.12) | copy-start | bytes 589828
  1.9 39.9 %copy-start.18 = (f32[96]{0:T(128)S(1)}, f32[96]{0:T(128)}, u32[]{:S(2)}) copy-start(f32[96]{0:T(128)} %param.21) | copy-start | bytes 1156
  1.9 20.8 %collective-permute-start.1 = (bf16[96,3,256]{2,1,0:T(4,128)(2,1)S(1)}, bf16[96,3,256]{2,1,0:T(4,128)(2,1)S(1)}, u32[]{:S(2)}, u32[]{:S(2)}) collective-permute-start(bf16[96,3,256]{2,1,0:T(4,128)(2,1)S(1)} %get-tuple-element.85), channel_id=1, source_target_pairs={{4,0},{8,4},{12,8},{16,12},{20,16},{24,20},{28,24},{32,28},{36,32}... | collective-permute-start | bytes 442376 | tf_op jit(solution)/shard_map/ppermute | solution.py:23
  16.9 15.2 %collective-permute-start = (bf16[96,3,256]{2,1,0:T(4,128)(2,1)S(1)}, bf16[96,3,256]{2,1,0:T(4,128)(2,1)S(1)}, u32[]{:S(2)}, u32[]{:S(2)}) collective-permute-start(bf16[96,3,256]{2,1,0:T(4,128)(2,1)S(1)} %get-tuple-element.84), channel_id=1, source_target_pairs={{0,4},{4,8},{8,12},{12,16},{16,20},{20,24},{24,28},{28,32},{32,36}... | collective-permute-start | bytes 442376 | tf_op jit(solution)/shard_map/ppermute | solution.py:22
  19.8 29.5 %copy-start.19 = (f32[96]{0:T(128)}, f32[96]{0:T(128)S(1)}, u32[]{:S(2)}) copy-start(f32[96]{0:T(128)S(1)} %get-tuple-element.94) | copy-start | bytes 1156
  19.8 29.5 %copy-start.21 = (f32[96]{0:T(128)}, f32[96]{0:T(128)S(1)}, u32[]{:S(2)}) copy-start(f32[96]{0:T(128)S(1)} %get-tuple-element.95) | copy-start | bytes 1156
  19.8 29.5 %copy-start.23 = (f32[96]{0:T(128)}, f32[96]{0:T(128)S(1)}, u32[]{:S(2)}) copy-start(f32[96]{0:T(128)S(1)} %get-tuple-element.96) | copy-start | bytes 1156
  19.8 29.5 %copy-start.25 = (f32[96]{0:T(128)}, f32[96]{0:T(128)S(1)}, u32[]{:S(2)}) copy-start(f32[96]{0:T(128)S(1)} %get-tuple-element.97) | copy-start | bytes 1156
  19.8 29.5 %copy-start.27 = (f32[96]{0:T(128)}, f32[96]{0:T(128)S(1)}, u32[]{:S(2)}) copy-start(f32[96]{0:T(128)S(1)} %get-tuple-element.98) | copy-start | bytes 1156
  19.8 29.5 %copy-start.29 = (f32[96]{0:T(128)}, f32[96]{0:T(128)S(1)}, u32[]{:S(2)}) copy-start(f32[96]{0:T(128)S(1)} %get-tuple-element.99) | copy-start | bytes 1156
  19.8 29.5 %copy-start.31 = (f32[96]{0:T(128)}, f32[96]{0:T(128)S(1)}, u32[]{:S(2)}) copy-start(f32[96]{0:T(128)S(1)} %get-tuple-element.100) | copy-start | bytes 1156
  19.8 29.5 %copy-start.33 = (f32[96]{0:T(128)}, f32[96]{0:T(128)S(1)}, u32[]{:S(2)}) copy-start(f32[96]{0:T(128)S(1)} %get-tuple-element.101) | copy-start | bytes 1156
  19.9 29.5 %copy-start.35 = (f32[96]{0:T(128)}, f32[96]{0:T(128)S(1)}, u32[]{:S(2)}) copy-start(f32[96]{0:T(128)S(1)} %get-tuple-element.102) | copy-start | bytes 1156
  19.9 29.5 %copy-start.37 = (f32[96]{0:T(128)}, f32[96]{0:T(128)S(1)}, u32[]{:S(2)}) copy-start(f32[96]{0:T(128)S(1)} %get-tuple-element.103) | copy-start | bytes 1156
  19.9 29.5 %copy-start.39 = (f32[96]{0:T(128)}, f32[96]{0:T(128)S(1)}, u32[]{:S(2)}) copy-start(f32[96]{0:T(128)S(1)} %get-tuple-element.104) | copy-start | bytes 1156
  19.9 29.5 %copy-start.41 = (f32[96]{0:T(128)}, f32[96]{0:T(128)S(1)}, u32[]{:S(2)}) copy-start(f32[96]{0:T(128)S(1)} %get-tuple-element.105) | copy-start | bytes 1156
  19.9 29.5 %copy-start.43 = (f32[96]{0:T(128)}, f32[96]{0:T(128)S(1)}, u32[]{:S(2)}) copy-start(f32[96]{0:T(128)S(1)} %get-tuple-element.106) | copy-start | bytes 1156
  19.9 29.5 %copy-start.45 = (f32[96]{0:T(128)}, f32[96]{0:T(128)S(1)}, u32[]{:S(2)}) copy-start(f32[96]{0:T(128)S(1)} %get-tuple-element.107) | copy-start | bytes 1156
  33.7 11.9 %collective-permute-start.2 = (bf16[96,10,3]{2,1,0:T(8,128)(2,1)S(1)}, bf16[96,10,3]{2,1,0:T(8,128)(2,1)S(1)}, u32[]{:S(2)}, u32[]{:S(2)}) collective-permute-start(bf16[96,10,3]{2,1,0:T(8,128)(2,1)S(1)} %get-tuple-element.48), channel_id=1, source_target_pairs={{0,1},{1,2},{2,3},{4,5},{5,6},{6,7},{8,9},{9,10},{10,11},{12,13},{... | collective-permute-start | bytes 17288 | tf_op jit(solution)/shard_map/ppermute | solution.py:22
  35.0 12.0 %collective-permute-start.3 = (bf16[96,10,3]{2,1,0:T(8,128)(2,1)S(1)}, bf16[96,10,3]{2,1,0:T(8,128)(2,1)S(1)}, u32[]{:S(2)}, u32[]{:S(2)}) collective-permute-start(bf16[96,10,3]{2,1,0:T(8,128)(2,1)S(1)} %get-tuple-element.49), channel_id=1, source_target_pairs={{1,0},{2,1},{3,2},{5,4},{6,5},{7,6},{9,8},{10,9},{11,10},{13,12},{... | collective-permute-start | bytes 17288 | tf_op jit(solution)/shard_map/ppermute | solution.py:23
  82.5 6.0 %collective-permute-start.5 = (bf16[96,3,256]{2,1,0:T(4,128)(2,1)}, bf16[96,3,256]{2,1,0:T(4,128)(2,1)S(1)}, u32[]{:S(2)}, u32[]{:S(2)}) collective-permute-start(bf16[96,3,256]{2,1,0:T(4,128)(2,1)} %get-tuple-element.55), channel_id=1, source_target_pairs={{4,0},{8,4},{12,8},{16,12},{20,16},{24,20},{28,24},{32,28},{36,32}... | collective-permute-start | bytes 442376 | tf_op jit(solution)/shard_map/ppermute | solution.py:23
  84.5 16.1 %collective-permute-start.4 = (bf16[96,3,256]{2,1,0:T(4,128)(2,1)S(1)}, bf16[96,3,256]{2,1,0:T(4,128)(2,1)S(1)}, u32[]{:S(2)}, u32[]{:S(2)}) collective-permute-start(bf16[96,3,256]{2,1,0:T(4,128)(2,1)S(1)} %copy-done.15), channel_id=1, source_target_pairs={{0,4},{4,8},{8,12},{12,16},{16,20},{20,24},{24,28},{28,32},{32,36}... | collective-permute-start | bytes 442376 | tf_op jit(solution)/shard_map/ppermute | solution.py:22
  102.1 13.2 %collective-permute-start.7 = (bf16[96,10,3]{2,1,0:T(8,128)(2,1)}, bf16[96,10,3]{2,1,0:T(8,128)(2,1)S(1)}, u32[]{:S(2)}, u32[]{:S(2)}) collective-permute-start(bf16[96,10,3]{2,1,0:T(8,128)(2,1)} %get-tuple-element.47), channel_id=1, source_target_pairs={{1,0},{2,1},{3,2},{5,4},{6,5},{7,6},{9,8},{10,9},{11,10},{13,12},{... | collective-permute-start | bytes 17288 | tf_op jit(solution)/shard_map/ppermute | solution.py:23
  109.6 9.8 %collective-permute-start.6 = (bf16[96,10,3]{2,1,0:T(8,128)(2,1)S(1)}, bf16[96,10,3]{2,1,0:T(8,128)(2,1)}, u32[]{:S(2)}, u32[]{:S(2)}) collective-permute-start(bf16[96,10,3]{2,1,0:T(8,128)(2,1)S(1)} %get-tuple-element.46), channel_id=1, source_target_pairs={{0,1},{1,2},{2,3},{4,5},{5,6},{6,7},{8,9},{9,10},{10,11},{12,13},{... | collective-permute-start | bytes 17288 | tf_op jit(solution)/shard_map/ppermute | solution.py:22
  122.3 49.0 %copy-start.8 = (bf16[96,4,256]{2,1,0:T(4,128)(2,1)S(1)}, bf16[96,4,256]{2,1,0:T(4,128)(2,1)}, u32[]{:S(2)}) copy-start(bf16[96,4,256]{2,1,0:T(4,128)(2,1)} %param.12) | copy-start | bytes 589828
  122.3 49.0 %copy-start.20 = (f32[96]{0:T(128)S(1)}, f32[96]{0:T(128)}, u32[]{:S(2)}) copy-start(f32[96]{0:T(128)} %copy-done.19) | copy-start | bytes 1156
  122.3 49.0 %copy-start.22 = (f32[96]{0:T(128)S(1)}, f32[96]{0:T(128)}, u32[]{:S(2)}) copy-start(f32[96]{0:T(128)} %copy-done.21) | copy-start | bytes 1156
  122.3 49.0 %copy-start.24 = (f32[96]{0:T(128)S(1)}, f32[96]{0:T(128)}, u32[]{:S(2)}) copy-start(f32[96]{0:T(128)} %copy-done.23) | copy-start | bytes 1156
  122.4 49.0 %copy-start.26 = (f32[96]{0:T(128)S(1)}, f32[96]{0:T(128)}, u32[]{:S(2)}) copy-start(f32[96]{0:T(128)} %copy-done.25) | copy-start | bytes 1156
  122.4 49.0 %copy-start.28 = (f32[96]{0:T(128)S(1)}, f32[96]{0:T(128)}, u32[]{:S(2)}) copy-start(f32[96]{0:T(128)} %copy-done.27) | copy-start | bytes 1156
  122.4 49.0 %copy-start.30 = (f32[96]{0:T(128)S(1)}, f32[96]{0:T(128)}, u32[]{:S(2)}) copy-start(f32[96]{0:T(128)} %copy-done.29) | copy-start | bytes 1156
  122.4 49.0 %copy-start.32 = (f32[96]{0:T(128)S(1)}, f32[96]{0:T(128)}, u32[]{:S(2)}) copy-start(f32[96]{0:T(128)} %copy-done.31) | copy-start | bytes 1156
  122.4 49.0 %copy-start.34 = (f32[96]{0:T(128)S(1)}, f32[96]{0:T(128)}, u32[]{:S(2)}) copy-start(f32[96]{0:T(128)} %copy-done.33) | copy-start | bytes 1156
  122.4 49.0 %copy-start.36 = (f32[96]{0:T(128)S(1)}, f32[96]{0:T(128)}, u32[]{:S(2)}) copy-start(f32[96]{0:T(128)} %copy-done.35) | copy-start | bytes 1156
  122.4 49.0 %copy-start.38 = (f32[96]{0:T(128)S(1)}, f32[96]{0:T(128)}, u32[]{:S(2)}) copy-start(f32[96]{0:T(128)} %copy-done.37) | copy-start | bytes 1156
  122.4 49.0 %copy-start.40 = (f32[96]{0:T(128)S(1)}, f32[96]{0:T(128)}, u32[]{:S(2)}) copy-start(f32[96]{0:T(128)} %copy-done.39) | copy-start | bytes 1156
  122.4 49.0 %copy-start.42 = (f32[96]{0:T(128)S(1)}, f32[96]{0:T(128)}, u32[]{:S(2)}) copy-start(f32[96]{0:T(128)} %copy-done.41) | copy-start | bytes 1156
  122.4 49.0 %copy-start.44 = (f32[96]{0:T(128)S(1)}, f32[96]{0:T(128)}, u32[]{:S(2)}) copy-start(f32[96]{0:T(128)} %copy-done.43) | copy-start | bytes 1156
  122.5 49.0 %copy-start.46 = (f32[96]{0:T(128)S(1)}, f32[96]{0:T(128)}, u32[]{:S(2)}) copy-start(f32[96]{0:T(128)} %copy-done.45) | copy-start | bytes 1156
  122.5 49.0 %copy-start.48 = (f32[96]{0:T(128)S(1)}, f32[96]{0:T(128)}, u32[]{:S(2)}) copy-start(f32[96]{0:T(128)} %copy-done.47) | copy-start | bytes 1156
  122.5 49.0 %copy-start.50 = (f32[96]{0:T(128)S(1)}, f32[96]{0:T(128)}, u32[]{:S(2)}) copy-start(f32[96]{0:T(128)} %copy-done.49) | copy-start | bytes 1156
  122.5 49.0 %copy-start.52 = (f32[96]{0:T(128)S(1)}, f32[96]{0:T(128)}, u32[]{:S(2)}) copy-start(f32[96]{0:T(128)} %copy-done.51) | copy-start | bytes 1156
  122.5 49.0 %copy-start.54 = (f32[96]{0:T(128)S(1)}, f32[96]{0:T(128)}, u32[]{:S(2)}) copy-start(f32[96]{0:T(128)} %copy-done.53) | copy-start | bytes 1156
  122.5 49.0 %copy-start.56 = (f32[96]{0:T(128)S(1)}, f32[96]{0:T(128)}, u32[]{:S(2)}) copy-start(f32[96]{0:T(128)} %copy-done.55) | copy-start | bytes 1156
  122.5 49.0 %copy-start.58 = (f32[96]{0:T(128)S(1)}, f32[96]{0:T(128)}, u32[]{:S(2)}) copy-start(f32[96]{0:T(128)} %copy-done.57) | copy-start | bytes 1156
  122.5 49.0 %copy-start.60 = (f32[96]{0:T(128)S(1)}, f32[96]{0:T(128)}, u32[]{:S(2)}) copy-start(f32[96]{0:T(128)} %copy-done.59) | copy-start | bytes 1156
  122.5 49.0 %copy-start.62 = (f32[96]{0:T(128)S(1)}, f32[96]{0:T(128)}, u32[]{:S(2)}) copy-start(f32[96]{0:T(128)} %copy-done.61) | copy-start | bytes 1156
  122.5 49.0 %copy-start.64 = (f32[96]{0:T(128)S(1)}, f32[96]{0:T(128)}, u32[]{:S(2)}) copy-start(f32[96]{0:T(128)} %copy-done.63) | copy-start | bytes 1156
  122.6 49.0 %copy-start.66 = (f32[96]{0:T(128)S(1)}, f32[96]{0:T(128)}, u32[]{:S(2)}) copy-start(f32[96]{0:T(128)} %copy-done.65) | copy-start | bytes 1156
  122.6 49.0 %copy-start.68 = (f32[96]{0:T(128)S(1)}, f32[96]{0:T(128)}, u32[]{:S(2)}) copy-start(f32[96]{0:T(128)} %copy-done.67) | copy-start | bytes 1156
  122.6 49.0 %copy-start.70 = (f32[96]{0:T(128)S(1)}, f32[96]{0:T(128)}, u32[]{:S(2)}) copy-start(f32[96]{0:T(128)} %copy-done.69) | copy-start | bytes 1156
  122.6 49.0 %copy-start.72 = (f32[96]{0:T(128)S(1)}, f32[96]{0:T(128)}, u32[]{:S(2)}) copy-start(f32[96]{0:T(128)} %copy-done.71) | copy-start | bytes 1156
  122.6 49.0 %copy-start.74 = (f32[96]{0:T(128)S(1)}, f32[96]{0:T(128)}, u32[]{:S(2)}) copy-start(f32[96]{0:T(128)} %copy-done.73) | copy-start | bytes 1156
  122.6 49.0 %copy-start.76 = (f32[96]{0:T(128)S(1)}, f32[96]{0:T(128)}, u32[]{:S(2)}) copy-start(f32[96]{0:T(128)} %copy-done.75) | copy-start | bytes 1156
  122.6 49.0 %copy-start.78 = (f32[96]{0:T(128)S(1)}, f32[96]{0:T(128)}, u32[]{:S(2)}) copy-start(f32[96]{0:T(128)} %copy-done.77) | copy-start | bytes 1156
  122.6 49.0 %copy-start.80 = (f32[96]{0:T(128)S(1)}, f32[96]{0:T(128)}, u32[]{:S(2)}) copy-start(f32[96]{0:T(128)} %copy-done.79) | copy-start | bytes 1156
  122.6 49.0 %copy-start.82 = (f32[96]{0:T(128)S(1)}, f32[96]{0:T(128)}, u32[]{:S(2)}) copy-start(f32[96]{0:T(128)} %copy-done.81) | copy-start | bytes 1156
  122.6 49.0 %copy-start.84 = (f32[96]{0:T(128)S(1)}, f32[96]{0:T(128)}, u32[]{:S(2)}) copy-start(f32[96]{0:T(128)} %copy-done.83) | copy-start | bytes 1156
  122.7 49.0 %copy-start.86 = (f32[96]{0:T(128)S(1)}, f32[96]{0:T(128)}, u32[]{:S(2)}) copy-start(f32[96]{0:T(128)} %copy-done.85) | copy-start | bytes 1156
  122.7 49.0 %copy-start.88 = (f32[96]{0:T(128)S(1)}, f32[96]{0:T(128)}, u32[]{:S(2)}) copy-start(f32[96]{0:T(128)} %copy-done.87) | copy-start | bytes 1156
  122.7 49.0 %copy-start.90 = (f32[96]{0:T(128)S(1)}, f32[96]{0:T(128)}, u32[]{:S(2)}) copy-start(f32[96]{0:T(128)} %copy-done.89) | copy-start | bytes 1156
  122.7 49.0 %copy-start.92 = (f32[96]{0:T(128)S(1)}, f32[96]{0:T(128)}, u32[]{:S(2)}) copy-start(f32[96]{0:T(128)} %copy-done.91) | copy-start | bytes 1156
  122.7 49.0 %copy-start.94 = (f32[96]{0:T(128)S(1)}, f32[96]{0:T(128)}, u32[]{:S(2)}) copy-start(f32[96]{0:T(128)} %copy-done.93) | copy-start | bytes 1156
  (45 other events, 851.9 us)

commit v5 on v4

--- a/solution.py
+++ b/solution.py
@@ -12,17 +12,39 @@
 LANES = 128
 
 
+def _pairs(ds, df):
+    ns, nf = lax.axis_size("space"), lax.axis_size("filt")
+    pairs = []
+    for s in range(ns):
+        for f in range(nf):
+            t, g = s + ds, f + df
+            if 0 <= t < ns and 0 <= g < nf:
+                pairs.append((s * nf + f, t * nf + g))
+    return pairs
+
+
 def padded_2(x, sides, width):
-    for axis, dim in sides:
-        size, length = (lax.axis_size(axis), x.shape[dim])
-        up = [(i, (i + 1) % size) for i in range(size - 1)]
-        down = [(j, i) for i, j in up]
-        last = lax.slice_in_dim(x, length - width, length, axis=dim)
-        initial = lax.slice_in_dim(x, 0, width, axis=dim)
-        before = lax.ppermute(last, axis, up)
-        after = lax.ppermute(initial, axis, down)
-        x = jnp.concatenate([before, x, after], axis=dim)
-    return x
+    del sides
+    axes = ("space", "filt")
+    rows, cols = x.shape[1], x.shape[2]
+    lo_r, hi_r = slice(0, width), slice(rows - width, rows)
+    lo_c, hi_c = slice(0, width), slice(cols - width, cols)
+    above = lax.ppermute(x[:, hi_r, :], axes, _pairs(1, 0))
+    below = lax.ppermute(x[:, lo_r, :], axes, _pairs(-1, 0))
+    left = lax.ppermute(x[:, :, hi_c], axes, _pairs(0, 1))
+    right = lax.ppermute(x[:, :, lo_c], axes, _pairs(0, -1))
+    top_left = lax.ppermute(x[:, hi_r, hi_c], axes, _pairs(1, 1))
+    top_right = lax.ppermute(x[:, hi_r, lo_c], axes, _pairs(1, -1))
+    bottom_left = lax.ppermute(x[:, lo_r, hi_c], axes, _pairs(-1, 1))
+    bottom_right = lax.ppermute(x[:, lo_r, lo_c], axes, _pairs(-1, -1))
+    return jnp.concatenate(
+        [
+            jnp.concatenate([top_left, above, top_right], axis=2),
+            jnp.concatenate([left, x, right], axis=2),
+            jnp.concatenate([bottom_left, below, bottom_right], axis=2),
+        ],
+        axis=1,
+    )
 
 
 def depthwise(padded, kernel, row_count, col_count):

time: 190 us -> 219 us (1.15)
  the two profiles are of different devices: /device:TPU:56 before, /device:TPU:8 now
where the time goes in v5:
time: 219 us; the launch traced here: 218 us
  Pallas kernels  77.8 us (36%)
  starting transfers between devices  45.7 us (21%)
  other arithmetic  43 us (20%)
  local copies, waits for them, and re-layouts  31 us (14%)
  matrix products  12.3 us (6%)
  waiting for transfers between devices  5.9 us (3%)
  between operations  2.51 us (1%)
    pallas_call x1, Pallas kernels, grad_reduce(): pl.pallas_call(functools.partial(reduce_kernel, nfilt, nspace, pr, sr), o...  77.8 us
    convert_element_type x1, other arithmetic, shards(): image_grad = (cotangent.astype(jnp.float32) + back).astype(jnp.bfloat16)  14 us
    reduce_sum x1, other arithmetic, shards(): average = jnp.mean(flat, axis=0, keepdims=True)  13.9 us
    slice x28, local copies, waits for them, and re-layouts, kernel_terms(): total = total + corr[:, row:row + ksize, row]  12.8 us
    ppermute x2, starting transfers between devices, padded_2(): left = lax.ppermute(x[:, :, hi_c], axes, _pairs(0, 1))  10.2 us
    ppermute x2, starting transfers between devices, padded_2(): right = lax.ppermute(x[:, :, lo_c], axes, _pairs(0, -1))  10.1 us
    concatenate x3, other arithmetic, padded_2(): jnp.concatenate([jnp.concatenate([top_left, above, top_right], axis=2), j...  8.38 us
    dot_general x7, matrix products, kernel_terms(): jnp.einsum('crj,cij->cri', padded[:, :, shift_col:shift_col + col_count],...  6.9 us
  transfers between devices with their start and end apart: 16, of which 3 were waited for; matrix products, arithmetic and copies ran while one was open for 5% of the time, Pallas kernels for 0%

profile of v5, /device:TPU:8, one launch (start us, length us, event | category | flops | bytes accessed | tf_op | source)
XLA Modules:
  0.0 218.2 jit_solution(3645080977700977269)
XLA Ops:
  0.7 1.1 fusion.45
  1.9 7.7 %collective-permute-start.4 = (bf16[96,4,3]{2,1,0:T(4,128)(2,1)S(1)}, bf16[96,4,3]{2,1,0:T(4,128)(2,1)S(1)}, u32[]{:S(2)}, u32[]{:S(2)}) collective-permute-start(bf16[96,4,3]{2,1,0:T(4,128)(2,1)S(1)} %get-tuple-element.93), channel_id=1, source_target_pairs={{1,0},{2,1},{3,2},{5,4},{6,5},{7,6},{9,8},{10,9},{11,10},{13,12},{... | collective-permute-start | bytes 6920 | tf_op jit(solution)/shard_map/ppermute | solution.py:35
  9.6 1.3 fusion.43
  10.9 1.3 collective-permute-start.2
  12.2 1.2 fusion.44
  13.4 1.3 collective-permute-start.1
  14.7 1.4 collective-permute-start
  16.1 1.3 collective-permute-start.6
  18.5 1.9 multiply_reduce_fusion
  20.6 3.4 %collective-permute-start.3 = (bf16[96,4,3]{2,1,0:T(4,128)(2,1)S(1)}, bf16[96,4,3]{2,1,0:T(4,128)(2,1)S(1)}, u32[]{:S(2)}, u32[]{:S(2)}) collective-permute-start(bf16[96,4,3]{2,1,0:T(4,128)(2,1)S(1)} %get-tuple-element.92), channel_id=1, source_target_pairs={{0,1},{1,2},{2,3},{4,5},{5,6},{6,7},{8,9},{9,10},{10,11},{12,13},{... | collective-permute-start | bytes 6920 | tf_op jit(solution)/shard_map/ppermute | solution.py:34
  24.0 1.3 collective-permute-start.7
  25.3 1.3 collective-permute-start.5
  26.7 4.1 %collective-permute-done.7 = bf16[96,3,3]{2,1,0:T(4,128)(2,1)S(1)} collective-permute-done((bf16[96,3,3]{2,1,0:T(4,128)(2,1)S(1)}, bf16[96,3,3]{2,1,0:T(4,128)(2,1)S(1)}, u32[]{:S(2)}, u32[]{:S(2)}) %collective-permute-start.7) | collective-permute-done | bytes 1760 | tf_op jit(solution)/shard_map/ppermute | solution.py:39
  30.7 0.8 collective-permute-done.5
  31.6 1.8 maximum_maximum_fusion.2
  33.8 13.9 %fusion.32 = (f32[4,256]{1,0:T(4,128)S(1)}, f32[96,4,256]{2,1,0:T(4,128)S(1)}) fusion(f32[96]{0:T(128)S(1)} %copy-done.95, bf16[96,7,262]{2,1,0:T(8,128)(2,1)S(1)} %get-tuple-element.49, f32[96]{0:T(128)S(1)} %get-tuple-element.149, f32[96]{0:T(128)S(1)} %get-tuple-element.150, f32[96]{0:T(128)S(1)} %get-tuple-element.103, f32[96]{0:T(128)S(1)} %get-tuple-element.104, ...), kind=kLoop, calls=%fused_computation.129 | loop fusion | flops 15432704 | bytes 9462784 | tf_op jit(solution)/shard_map/reduce_sum | solution.py:121
  48.7 1.0 convert_reduce_fusion
  50.1 1.0 fusion.25
  51.1 1.4 convert_reduce_fusion.1
  52.5 1.1 reshape.129
  53.6 3.4 %maximum_maximum_fusion = bf16[96,10,262]{2,1,0:T(8,128)(2,1)S(1)} fusion(bf16[96,3,3]{2,1,0:T(4,128)(2,1)} %copy-done.4, bf16[96,3,256]{2,1,0:T(4,128)(2,1)S(1)} %collective-permute-done.6, bf16[96,3,3]{2,1,0:T(4,128)(2,1)} %copy-done.5, bf16[96,4,3]{2,1,0:T(4,128)(2,1)S(1)} %collective-permute-done.4, bf16[96,4,256]{2,1,0:T(4,128)(2,1)S(1)} %copy-done.1, ...), kind=kLoop, calls=%fused_computation.17 | loop fusion | flops 4527360 | bytes 1006080 | tf_op jit(solution)/shard_map/concatenate | solution.py:40
  56.9 1.0 fusion.23
  57.9 1.1 fusion.21
  59.0 1.1 fusion.19
  60.1 1.1 fusion.17
  61.2 1.1 fusion.15
  62.3 1.1 fusion.13
  63.8 0.9 fusion.33
  64.7 0.9 fusion.34
  65.6 0.8 fusion.35
  66.4 0.7 reshape.128
  67.9 1.7 fusion.42
  69.9 1.6 fusion.41
  71.8 1.6 fusion.40
  73.8 1.6 fusion.39
  75.7 1.6 fusion.38
  77.4 0.7 copy.44
  78.1 0.7 copy.45
  79.1 0.7 copy.51
  80.5 0.7 copy.48
  81.1 0.7 copy.49
  82.5 1.4 collective-permute-start.15
  83.9 1.3 collective-permute-start.14
  85.2 1.3 collective-permute-start.13
  86.5 2.4 %collective-permute-start.12 = (bf16[96,4,3]{2,1,0:T(4,128)(2,1)}, bf16[96,4,3]{2,1,0:T(4,128)(2,1)}, u32[]{:S(2)}, u32[]{:S(2)}) collective-permute-start(bf16[96,4,3]{2,1,0:T(4,128)(2,1)} %get-tuple-element.57), channel_id=1, source_target_pairs={{1,0},{2,1},{3,2},{5,4},{6,5},{7,6},{9,8},{10,9},{11,10},{13,12},{... | collective-permute-start | bytes 6920 | tf_op jit(solution)/shard_map/ppermute | solution.py:35
  88.9 4.9 %collective-permute-start.10 = (bf16[96,3,3]{2,1,0:T(4,128)(2,1)}, bf16[96,3,3]{2,1,0:T(4,128)(2,1)S(1)}, u32[]{:S(2)}, u32[]{:S(2)}) collective-permute-start(bf16[96,3,3]{2,1,0:T(4,128)(2,1)} %get-tuple-element.53), channel_id=1, source_target_pairs={{1,4},{2,5},{3,6},{5,8},{6,9},{7,10},{9,12},{10,13},{11,14},{13,16... | collective-permute-start | bytes 5192 | tf_op jit(solution)/shard_map/ppermute | solution.py:37
  93.8 1.9 multiply_reduce_fusion.1
  95.8 0.8 pad_maximum_fusion.1
  96.6 0.7 add_add_fusion.3
  97.4 0.7 add_add_fusion.2
  98.1 6.8 %collective-permute-start.11 = (bf16[96,4,3]{2,1,0:T(4,128)(2,1)}, bf16[96,4,3]{2,1,0:T(4,128)(2,1)S(1)}, u32[]{:S(2)}, u32[]{:S(2)}) collective-permute-start(bf16[96,4,3]{2,1,0:T(4,128)(2,1)} %get-tuple-element.56), channel_id=1, source_target_pairs={{0,1},{1,2},{2,3},{4,5},{5,6},{6,7},{8,9},{9,10},{10,11},{12,13},{... | collective-permute-start | bytes 6920 | tf_op jit(solution)/shard_map/ppermute | solution.py:34
  104.9 4.7 %collective-permute-start.9 = (bf16[96,3,256]{2,1,0:T(4,128)(2,1)S(1)}, bf16[96,3,256]{2,1,0:T(4,128)(2,1)S(1)}, u32[]{:S(2)}, u32[]{:S(2)}) collective-permute-start(bf16[96,3,256]{2,1,0:T(4,128)(2,1)S(1)} %copy-done.7), channel_id=1, source_target_pairs={{0,4},{1,5},{2,6},{3,7},{4,8},{5,9},{6,10},{7,11},{8,12},{9,13},{1... | collective-permute-start | bytes 442376 | tf_op jit(solution)/shard_map/ppermute | solution.py:32
  110.2 3.9 %collective-permute-start.8 = (bf16[96,3,3]{2,1,0:T(4,128)(2,1)}, bf16[96,3,3]{2,1,0:T(4,128)(2,1)S(1)}, u32[]{:S(2)}, u32[]{:S(2)}) collective-permute-start(bf16[96,3,3]{2,1,0:T(4,128)(2,1)} %get-tuple-element.50), channel_id=1, source_target_pairs={{0,5},{1,6},{2,7},{4,9},{5,10},{6,11},{8,13},{9,14},{10,15},{12,17... | collective-permute-start | bytes 5192 | tf_op jit(solution)/shard_map/ppermute | solution.py:36
  114.2 0.8 reshape.125
  115.7 1.0 collective-permute-done.8
  116.7 3.3 %maximum_maximum_fusion.1 = bf16[96,10,262]{2,1,0:T(8,128)(2,1)S(1)} fusion(bf16[96,3,3]{2,1,0:T(4,128)(2,1)S(1)} %collective-permute-done.15, bf16[96,3,256]{2,1,0:T(4,128)(2,1)S(1)} %collective-permute-done.14, bf16[96,3,3]{2,1,0:T(4,128)(2,1)S(1)} %copy-done.9, bf16[96,4,3]{2,1,0:T(4,128)(2,1)} %collective-permute-done.12, ...), kind=kLoop, calls=%fused_computation.18 | loop fusion | flops 4527360 | bytes 1006080 | tf_op jit(solution)/shard_map/concatenate | solution.py:40
  120.6 0.7 pad_maximum_fusion.buf_ref
  121.3 77.8 %shard_map.194 = f32[200,128]{1,0:T(8,128)} custom-call(f32[656,128]{1,0:T(8,128)} %pad_maximum_fusion.buf_ref), custom_call_target="tpu_custom_call" | custom-call | bytes 209715200 | tf_op jit(solution)/shard_map/pallas_call | solution.py:348
  199.1 0.7 slice_bitcast_fusion.1
  199.8 0.9 slice_bitcast_fusion
  201.9 14.0 %add_convert_fusion = bf16[96,4,256]{2,1,0:T(4,128)(2,1)} fusion(bf16[96,10,262]{2,1,0:T(8,128)(2,1)S(1)} %maximum_maximum_fusion.1, bf16[96,4,256]{2,1,0:T(4,128)(2,1)S(1)} %copy-done.2, f32[96]{0:T(128)S(1)} %copy-done.35, f32[96]{0:T(128)S(1)} %copy-done.37, f32[96]{0:T(128)S(1)} %copy-done.41, f32[96]{0:T(128)S(1)} %copy-done.43, f32[96]{0:T(128)S(1)} %copy-done.45, ...), kind=kLoop, calls=%fused_computation.38 | loop fusion | flops 14647296 | bytes 10045824 | tf_op jit(solution)/shard_map/convert_element_type | solution.py:202
  216.0 0.8 copy.57
  216.8 0.7 slice.948
  217.5 0.7 slice.951
  (269 shorter events, 9.5 us)
Async XLA Ops:
  0.6 47.3 %copy-start = (bf16[384,96]{0,1:T(8,128)(2,1)S(1)}, bf16[384,96]{0,1:T(8,128)(2,1)}, u32[]{:S(2)}) copy-start(bf16[384,96]{0,1:T(8,128)(2,1)} %param.17) | copy-start | bytes 221188
  0.7 19.7 %copy-start.1 = (bf16[96,4,256]{2,1,0:T(4,128)(2,1)S(1)}, bf16[96,4,256]{2,1,0:T(4,128)(2,1)}, u32[]{:S(2)}) copy-start(bf16[96,4,256]{2,1,0:T(4,128)(2,1)} %param.11) | copy-start | bytes 589828
  0.7 17.7 %copy-start.2 = (bf16[96,4,256]{2,1,0:T(4,128)(2,1)S(1)}, bf16[96,4,256]{2,1,0:T(4,128)(2,1)}, u32[]{:S(2)}) copy-start(bf16[96,4,256]{2,1,0:T(4,128)(2,1)} %param.12) | copy-start | bytes 589828
  0.7 17.7 %copy-start.88 = (f32[96]{0:T(128)S(1)}, f32[96]{0:T(128)}, u32[]{:S(2)}) copy-start(f32[96]{0:T(128)} %param.21) | copy-start | bytes 1156
  1.8 18.7 %copy-start.94 = (bf16[384]{0:T(512)(128)(2,1)S(1)}, bf16[384]{0:T(512)(128)(2,1)}, u32[]{:S(2)}) copy-start(bf16[384]{0:T(512)(128)(2,1)} %param.18) | copy-start | bytes 2308
  1.9 23.4 %collective-permute-start.4 = (bf16[96,4,3]{2,1,0:T(4,128)(2,1)S(1)}, bf16[96,4,3]{2,1,0:T(4,128)(2,1)S(1)}, u32[]{:S(2)}, u32[]{:S(2)}) collective-permute-start(bf16[96,4,3]{2,1,0:T(4,128)(2,1)S(1)} %get-tuple-element.93), channel_id=1, source_target_pairs={{1,0},{2,1},{3,2},{5,4},{6,5},{7,6},{9,8},{10,9},{11,10},{13,12},{... | collective-permute-start | bytes 6920 | tf_op jit(solution)/shard_map/ppermute | solution.py:35
  10.9 9.7 %collective-permute-start.2 = (bf16[96,3,3]{2,1,0:T(4,128)(2,1)S(1)}, bf16[96,3,3]{2,1,0:T(4,128)(2,1)S(1)}, u32[]{:S(2)}, u32[]{:S(2)}) collective-permute-start(bf16[96,3,3]{2,1,0:T(4,128)(2,1)S(1)} %get-tuple-element.88), channel_id=1, source_target_pairs={{1,4},{2,5},{3,6},{5,8},{6,9},{7,10},{9,12},{10,13},{11,14},{13,16... | collective-permute-start | bytes 5192 | tf_op jit(solution)/shard_map/ppermute | solution.py:37
  13.4 18.2 %collective-permute-start.1 = (bf16[96,3,256]{2,1,0:T(4,128)(2,1)S(1)}, bf16[96,3,256]{2,1,0:T(4,128)(2,1)S(1)}, u32[]{:S(2)}, u32[]{:S(2)}) collective-permute-start(bf16[96,3,256]{2,1,0:T(4,128)(2,1)S(1)} %get-tuple-element.90), channel_id=1, source_target_pairs={{0,4},{1,5},{2,6},{3,7},{4,8},{5,9},{6,10},{7,11},{8,12},{9,13},{1... | collective-permute-start | bytes 442376 | tf_op jit(solution)/shard_map/ppermute | solution.py:32
  14.7 9.3 %collective-permute-start = (bf16[96,3,3]{2,1,0:T(4,128)(2,1)S(1)}, bf16[96,3,3]{2,1,0:T(4,128)(2,1)S(1)}, u32[]{:S(2)}, u32[]{:S(2)}) collective-permute-start(bf16[96,3,3]{2,1,0:T(4,128)(2,1)S(1)} %get-tuple-element.86), channel_id=1, source_target_pairs={{0,5},{1,6},{2,7},{4,9},{5,10},{6,11},{8,13},{9,14},{10,15},{12,17... | collective-permute-start | bytes 5192 | tf_op jit(solution)/shard_map/ppermute | solution.py:36
  16.1 15.5 %collective-permute-start.6 = (bf16[96,3,256]{2,1,0:T(4,128)(2,1)S(1)}, bf16[96,3,256]{2,1,0:T(4,128)(2,1)S(1)}, u32[]{:S(2)}, u32[]{:S(2)}) collective-permute-start(bf16[96,3,256]{2,1,0:T(4,128)(2,1)S(1)} %get-tuple-element.91), channel_id=1, source_target_pairs={{4,0},{5,1},{6,2},{7,3},{8,4},{9,5},{10,6},{11,7},{12,8},{13,9},{1... | collective-permute-start | bytes 442376 | tf_op jit(solution)/shard_map/ppermute | solution.py:33
  20.6 11.0 %collective-permute-start.3 = (bf16[96,4,3]{2,1,0:T(4,128)(2,1)S(1)}, bf16[96,4,3]{2,1,0:T(4,128)(2,1)S(1)}, u32[]{:S(2)}, u32[]{:S(2)}) collective-permute-start(bf16[96,4,3]{2,1,0:T(4,128)(2,1)S(1)} %get-tuple-element.92), channel_id=1, source_target_pairs={{0,1},{1,2},{2,3},{4,5},{5,6},{6,7},{8,9},{9,10},{10,11},{12,13},{... | collective-permute-start | bytes 6920 | tf_op jit(solution)/shard_map/ppermute | solution.py:34
  24.0 23.7 %copy-start.3 = (bf16[96,3,3]{2,1,0:T(4,128)(2,1)}, bf16[96,3,3]{2,1,0:T(4,128)(2,1)S(1)}, u32[]{:S(2)}) copy-start(bf16[96,3,3]{2,1,0:T(4,128)(2,1)S(1)} %collective-permute-done) | copy-start | bytes 5188
  24.0 6.8 %collective-permute-start.7 = (bf16[96,3,3]{2,1,0:T(4,128)(2,1)S(1)}, bf16[96,3,3]{2,1,0:T(4,128)(2,1)S(1)}, u32[]{:S(2)}, u32[]{:S(2)}) collective-permute-start(bf16[96,3,3]{2,1,0:T(4,128)(2,1)S(1)} %get-tuple-element.89), channel_id=1, source_target_pairs={{5,0},{6,1},{7,2},{9,4},{10,5},{11,6},{13,8},{14,9},{15,10},{17,12... | collective-permute-start | bytes 5192 | tf_op jit(solution)/shard_map/ppermute | solution.py:39
  25.3 6.3 %collective-permute-start.5 = (bf16[96,3,3]{2,1,0:T(4,128)(2,1)S(1)}, bf16[96,3,3]{2,1,0:T(4,128)(2,1)S(1)}, u32[]{:S(2)}, u32[]{:S(2)}) collective-permute-start(bf16[96,3,3]{2,1,0:T(4,128)(2,1)S(1)} %get-tuple-element.87), channel_id=1, source_target_pairs={{4,1},{5,2},{6,3},{8,5},{9,6},{10,7},{12,9},{13,10},{14,11},{16,13... | collective-permute-start | bytes 5192 | tf_op jit(solution)/shard_map/ppermute | solution.py:38
  30.7 16.9 %copy-start.4 = (bf16[96,3,3]{2,1,0:T(4,128)(2,1)}, bf16[96,3,3]{2,1,0:T(4,128)(2,1)S(1)}, u32[]{:S(2)}) copy-start(bf16[96,3,3]{2,1,0:T(4,128)(2,1)S(1)} %collective-permute-done.7) | copy-start | bytes 5188
  82.2 22.8 %copy-start.7 = (bf16[96,3,256]{2,1,0:T(4,128)(2,1)S(1)}, bf16[96,3,256]{2,1,0:T(4,128)(2,1)}, u32[]{:S(2)}) copy-start(bf16[96,3,256]{2,1,0:T(4,128)(2,1)} %get-tuple-element.54) | copy-start | bytes 442372
  82.5 15.6 %collective-permute-start.15 = (bf16[96,3,3]{2,1,0:T(4,128)(2,1)}, bf16[96,3,3]{2,1,0:T(4,128)(2,1)S(1)}, u32[]{:S(2)}, u32[]{:S(2)}) collective-permute-start(bf16[96,3,3]{2,1,0:T(4,128)(2,1)} %get-tuple-element.51), channel_id=1, source_target_pairs={{5,0},{6,1},{7,2},{9,4},{10,5},{11,6},{13,8},{14,9},{15,10},{17,12... | collective-permute-start | bytes 5192 | tf_op jit(solution)/shard_map/ppermute | solution.py:39
  83.9 32.8 %collective-permute-start.14 = (bf16[96,3,256]{2,1,0:T(4,128)(2,1)}, bf16[96,3,256]{2,1,0:T(4,128)(2,1)S(1)}, u32[]{:S(2)}, u32[]{:S(2)}) collective-permute-start(bf16[96,3,256]{2,1,0:T(4,128)(2,1)} %get-tuple-element.55), channel_id=1, source_target_pairs={{4,0},{5,1},{6,2},{7,3},{8,4},{9,5},{10,6},{11,7},{12,8},{13,9},{1... | collective-permute-start | bytes 442376 | tf_op jit(solution)/shard_map/ppermute | solution.py:33
  85.2 19.7 %collective-permute-start.13 = (bf16[96,3,3]{2,1,0:T(4,128)(2,1)}, bf16[96,3,3]{2,1,0:T(4,128)(2,1)S(1)}, u32[]{:S(2)}, u32[]{:S(2)}) collective-permute-start(bf16[96,3,3]{2,1,0:T(4,128)(2,1)} %get-tuple-element.52), channel_id=1, source_target_pairs={{4,1},{5,2},{6,3},{8,5},{9,6},{10,7},{12,9},{13,10},{14,11},{16,13... | collective-permute-start | bytes 5192 | tf_op jit(solution)/shard_map/ppermute | solution.py:38
  86.5 30.2 %collective-permute-start.12 = (bf16[96,4,3]{2,1,0:T(4,128)(2,1)}, bf16[96,4,3]{2,1,0:T(4,128)(2,1)}, u32[]{:S(2)}, u32[]{:S(2)}) collective-permute-start(bf16[96,4,3]{2,1,0:T(4,128)(2,1)} %get-tuple-element.57), channel_id=1, source_target_pairs={{1,0},{2,1},{3,2},{5,4},{6,5},{7,6},{9,8},{10,9},{11,10},{13,12},{... | collective-permute-start | bytes 6920 | tf_op jit(solution)/shard_map/ppermute | solution.py:35
  88.9 20.7 %collective-permute-start.10 = (bf16[96,3,3]{2,1,0:T(4,128)(2,1)}, bf16[96,3,3]{2,1,0:T(4,128)(2,1)S(1)}, u32[]{:S(2)}, u32[]{:S(2)}) collective-permute-start(bf16[96,3,3]{2,1,0:T(4,128)(2,1)} %get-tuple-element.53), channel_id=1, source_target_pairs={{1,4},{2,5},{3,6},{5,8},{6,9},{7,10},{9,12},{10,13},{11,14},{13,16... | collective-permute-start | bytes 5192 | tf_op jit(solution)/shard_map/ppermute | solution.py:37
  95.8 19.8 %copy-start.90 = (f32[96]{0:T(128)S(1)}, f32[96]{0:T(128)}, u32[]{:S(2)}) copy-start(f32[96]{0:T(128)} %multiply_reduce_fusion) | copy-start | bytes 1156
  95.8 19.9 %copy-start.91 = (f32[96]{0:T(128)S(1)}, f32[96]{0:T(128)}, u32[]{:S(2)}) copy-start(f32[96]{0:T(128)} %get-tuple-element.39) | copy-start | bytes 1156
  95.8 19.9 %copy-start.92 = (f32[96]{0:T(128)S(1)}, f32[96]{0:T(128)}, u32[]{:S(2)}) copy-start(f32[96]{0:T(128)} %get-tuple-element.42) | copy-start | bytes 1156
  95.8 19.9 %copy-start.93 = (f32[96]{0:T(128)S(1)}, f32[96]{0:T(128)}, u32[]{:S(2)}) copy-start(f32[96]{0:T(128)} %get-tuple-element.46) | copy-start | bytes 1156
  98.1 18.6 %collective-permute-start.11 = (bf16[96,4,3]{2,1,0:T(4,128)(2,1)}, bf16[96,4,3]{2,1,0:T(4,128)(2,1)S(1)}, u32[]{:S(2)}, u32[]{:S(2)}) collective-permute-start(bf16[96,4,3]{2,1,0:T(4,128)(2,1)} %get-tuple-element.56), channel_id=1, source_target_pairs={{0,1},{1,2},{2,3},{4,5},{5,6},{6,7},{8,9},{9,10},{10,11},{12,13},{... | collective-permute-start | bytes 6920 | tf_op jit(solution)/shard_map/ppermute | solution.py:34
  104.9 11.8 %collective-permute-start.9 = (bf16[96,3,256]{2,1,0:T(4,128)(2,1)S(1)}, bf16[96,3,256]{2,1,0:T(4,128)(2,1)S(1)}, u32[]{:S(2)}, u32[]{:S(2)}) collective-permute-start(bf16[96,3,256]{2,1,0:T(4,128)(2,1)S(1)} %copy-done.7), channel_id=1, source_target_pairs={{0,4},{1,5},{2,6},{3,7},{4,8},{5,9},{6,10},{7,11},{8,12},{9,13},{1... | collective-permute-start | bytes 442376 | tf_op jit(solution)/shard_map/ppermute | solution.py:32
  110.2 6.4 %collective-permute-start.8 = (bf16[96,3,3]{2,1,0:T(4,128)(2,1)}, bf16[96,3,3]{2,1,0:T(4,128)(2,1)S(1)}, u32[]{:S(2)}, u32[]{:S(2)}) collective-permute-start(bf16[96,3,3]{2,1,0:T(4,128)(2,1)} %get-tuple-element.50), channel_id=1, source_target_pairs={{0,5},{1,6},{2,7},{4,9},{5,10},{6,11},{8,13},{9,14},{10,15},{12,17... | collective-permute-start | bytes 5192 | tf_op jit(solution)/shard_map/ppermute | solution.py:36
  120.0 81.5 %copy-start.17 = (f32[96]{0:T(128)S(1)}, f32[96]{0:T(128)}, u32[]{:S(2)}) copy-start(f32[96]{0:T(128)} %copy-done.16) | copy-start | bytes 1156
  120.0 81.5 %copy-start.19 = (f32[96]{0:T(128)S(1)}, f32[96]{0:T(128)}, u32[]{:S(2)}) copy-start(f32[96]{0:T(128)} %copy-done.18) | copy-start | bytes 1156
  120.0 81.5 %copy-start.21 = (f32[96]{0:T(128)S(1)}, f32[96]{0:T(128)}, u32[]{:S(2)}) copy-start(f32[96]{0:T(128)} %copy-done.20) | copy-start | bytes 1156
  120.0 81.5 %copy-start.23 = (f32[96]{0:T(128)S(1)}, f32[96]{0:T(128)}, u32[]{:S(2)}) copy-start(f32[96]{0:T(128)} %copy-done.22) | copy-start | bytes 1156
  120.0 81.5 %copy-start.25 = (f32[96]{0:T(128)S(1)}, f32[96]{0:T(128)}, u32[]{:S(2)}) copy-start(f32[96]{0:T(128)} %copy-done.24) | copy-start | bytes 1156
  120.0 81.5 %copy-start.27 = (f32[96]{0:T(128)S(1)}, f32[96]{0:T(128)}, u32[]{:S(2)}) copy-start(f32[96]{0:T(128)} %copy-done.26) | copy-start | bytes 1156
  120.0 81.5 %copy-start.29 = (f32[96]{0:T(128)S(1)}, f32[96]{0:T(128)}, u32[]{:S(2)}) copy-start(f32[96]{0:T(128)} %copy-done.28) | copy-start | bytes 1156
  120.1 81.5 %copy-start.31 = (f32[96]{0:T(128)S(1)}, f32[96]{0:T(128)}, u32[]{:S(2)}) copy-start(f32[96]{0:T(128)} %copy-done.30) | copy-start | bytes 1156
  120.1 81.5 %copy-start.33 = (f32[96]{0:T(128)S(1)}, f32[96]{0:T(128)}, u32[]{:S(2)}) copy-start(f32[96]{0:T(128)} %copy-done.32) | copy-start | bytes 1156
  120.1 81.5 %copy-start.35 = (f32[96]{0:T(128)S(1)}, f32[96]{0:T(128)}, u32[]{:S(2)}) copy-start(f32[96]{0:T(128)} %copy-done.34) | copy-start | bytes 1156
  120.1 81.5 %copy-start.37 = (f32[96]{0:T(128)S(1)}, f32[96]{0:T(128)}, u32[]{:S(2)}) copy-start(f32[96]{0:T(128)} %copy-done.36) | copy-start | bytes 1156
  120.1 81.5 %copy-start.39 = (f32[96]{0:T(128)S(1)}, f32[96]{0:T(128)}, u32[]{:S(2)}) copy-start(f32[96]{0:T(128)} %copy-done.38) | copy-start | bytes 1156
  120.1 81.5 %copy-start.41 = (f32[96]{0:T(128)S(1)}, f32[96]{0:T(128)}, u32[]{:S(2)}) copy-start(f32[96]{0:T(128)} %copy-done.40) | copy-start | bytes 1156
  120.1 81.5 %copy-start.43 = (f32[96]{0:T(128)S(1)}, f32[96]{0:T(128)}, u32[]{:S(2)}) copy-start(f32[96]{0:T(128)} %copy-done.42) | copy-start | bytes 1156
  120.1 81.5 %copy-start.45 = (f32[96]{0:T(128)S(1)}, f32[96]{0:T(128)}, u32[]{:S(2)}) copy-start(f32[96]{0:T(128)} %copy-done.44) | copy-start | bytes 1156
  120.1 81.5 %copy-start.47 = (f32[96]{0:T(128)S(1)}, f32[96]{0:T(128)}, u32[]{:S(2)}) copy-start(f32[96]{0:T(128)} %copy-done.46) | copy-start | bytes 1156
  120.1 81.5 %copy-start.49 = (f32[96]{0:T(128)S(1)}, f32[96]{0:T(128)}, u32[]{:S(2)}) copy-start(f32[96]{0:T(128)} %copy-done.48) | copy-start | bytes 1156
  120.2 81.5 %copy-start.51 = (f32[96]{0:T(128)S(1)}, f32[96]{0:T(128)}, u32[]{:S(2)}) copy-start(f32[96]{0:T(128)} %copy-done.50) | copy-start | bytes 1156
  120.2 81.5 %copy-start.53 = (f32[96]{0:T(128)S(1)}, f32[96]{0:T(128)}, u32[]{:S(2)}) copy-start(f32[96]{0:T(128)} %copy-done.52) | copy-start | bytes 1156
  120.2 81.5 %copy-start.55 = (f32[96]{0:T(128)S(1)}, f32[96]{0:T(128)}, u32[]{:S(2)}) copy-start(f32[96]{0:T(128)} %copy-done.54) | copy-start | bytes 1156
  120.2 81.5 %copy-start.57 = (f32[96]{0:T(128)S(1)}, f32[96]{0:T(128)}, u32[]{:S(2)}) copy-start(f32[96]{0:T(128)} %copy-done.56) | copy-start | bytes 1156
  120.2 81.5 %copy-start.59 = (f32[96]{0:T(128)S(1)}, f32[96]{0:T(128)}, u32[]{:S(2)}) copy-start(f32[96]{0:T(128)} %copy-done.58) | copy-start | bytes 1156
  120.2 81.5 %copy-start.61 = (f32[96]{0:T(128)S(1)}, f32[96]{0:T(128)}, u32[]{:S(2)}) copy-start(f32[96]{0:T(128)} %copy-done.60) | copy-start | bytes 1156
  120.2 81.5 %copy-start.63 = (f32[96]{0:T(128)S(1)}, f32[96]{0:T(128)}, u32[]{:S(2)}) copy-start(f32[96]{0:T(128)} %copy-done.62) | copy-start | bytes 1156
  120.2 81.5 %copy-start.65 = (f32[96]{0:T(128)S(1)}, f32[96]{0:T(128)}, u32[]{:S(2)}) copy-start(f32[96]{0:T(128)} %copy-done.64) | copy-start | bytes 1156
  120.2 81.5 %copy-start.67 = (f32[96]{0:T(128)S(1)}, f32[96]{0:T(128)}, u32[]{:S(2)}) copy-start(f32[96]{0:T(128)} %copy-done.66) | copy-start | bytes 1156
  120.2 81.5 %copy-start.69 = (f32[96]{0:T(128)S(1)}, f32[96]{0:T(128)}, u32[]{:S(2)}) copy-start(f32[96]{0:T(128)} %copy-done.68) | copy-start | bytes 1156
  120.3 81.5 %copy-start.71 = (f32[96]{0:T(128)S(1)}, f32[96]{0:T(128)}, u32[]{:S(2)}) copy-start(f32[96]{0:T(128)} %copy-done.70) | copy-start | bytes 1156
  120.3 81.5 %copy-start.73 = (f32[96]{0:T(128)S(1)}, f32[96]{0:T(128)}, u32[]{:S(2)}) copy-start(f32[96]{0:T(128)} %copy-done.72) | copy-start | bytes 1156
  120.3 81.5 %copy-start.75 = (f32[96]{0:T(128)S(1)}, f32[96]{0:T(128)}, u32[]{:S(2)}) copy-start(f32[96]{0:T(128)} %copy-done.74) | copy-start | bytes 1156
  120.3 81.5 %copy-start.77 = (f32[96]{0:T(128)S(1)}, f32[96]{0:T(128)}, u32[]{:S(2)}) copy-start(f32[96]{0:T(128)} %copy-done.76) | copy-start | bytes 1156
  120.3 81.5 %copy-start.79 = (f32[96]{0:T(128)S(1)}, f32[96]{0:T(128)}, u32[]{:S(2)}) copy-start(f32[96]{0:T(128)} %copy-done.78) | copy-start | bytes 1156
  120.3 81.5 %copy-start.81 = (f32[96]{0:T(128)S(1)}, f32[96]{0:T(128)}, u32[]{:S(2)}) copy-start(f32[96]{0:T(128)} %copy-done.80) | copy-start | bytes 1156
  120.3 81.5 %copy-start.83 = (f32[96]{0:T(128)S(1)}, f32[96]{0:T(128)}, u32[]{:S(2)}) copy-start(f32[96]{0:T(128)} %copy-done.82) | copy-start | bytes 1156
  120.3 81.5 %copy-start.85 = (f32[96]{0:T(128)S(1)}, f32[96]{0:T(128)}, u32[]{:S(2)}) copy-start(f32[96]{0:T(128)} %copy-done.84) | copy-start | bytes 1156
  120.3 81.5 %copy-start.87 = (f32[96]{0:T(128)S(1)}, f32[96]{0:T(128)}, u32[]{:S(2)}) copy-start(f32[96]{0:T(128)} %copy-done.86) | copy-start | bytes 1156
  (48 other events, 688.7 us)

commit v6 on v4

--- a/solution.py
+++ b/solution.py
@@ -12,17 +12,113 @@
 LANES = 128
 
 
-def padded_2(x, sides, width):
-    for axis, dim in sides:
-        size, length = (lax.axis_size(axis), x.shape[dim])
-        up = [(i, (i + 1) % size) for i in range(size - 1)]
-        down = [(j, i) for i, j in up]
-        last = lax.slice_in_dim(x, length - width, length, axis=dim)
-        initial = lax.slice_in_dim(x, 0, width, axis=dim)
-        before = lax.ppermute(last, axis, up)
-        after = lax.ppermute(initial, axis, down)
-        x = jnp.concatenate([before, x, after], axis=dim)
-    return x
+_DIRS = [(-1, 0), (1, 0), (0, -1), (0, 1), (-1, -1), (-1, 1), (1, -1), (1, 1)]
+
+
+def _lanes(df, cols):
+    if df == 0:
+        return slice(0, cols)
+    if df > 0:
+        return slice(cols - LANES, cols)
+    return slice(0, LANES)
+
+
+def halo_kernel(ns, nf, cols, x_ref, *refs):
+    outs = refs[:8]
+    slots = refs[8:16]
+    send_sem, recv_sem = refs[16:]
+    s = lax.axis_index("space")
+    f = lax.axis_index("filt")
+
+    def exists(d):
+        t, g = s + d[0], f + d[1]
+        return (t >= 0) & (t < ns) & (g >= 0) & (g < nf)
+
+    def desc(k):
+        d = _DIRS[k]
+        back = _DIRS.index((-d[0], -d[1]))
+        return pltpu.make_async_remote_copy(
+            src_ref=x_ref.at[:, :, _lanes(d[1], cols)],
+            dst_ref=slots[back],
+            send_sem=send_sem.at[k],
+            recv_sem=recv_sem.at[back],
+            device_id=(s + d[0], f + d[1]),
+            device_id_type=MESH,
+        )
+
+    barrier = pltpu.get_barrier_semaphore()
+    for k, d in enumerate(_DIRS):
+
+        @pl.when(exists(d))
+        def _():
+            pl.semaphore_signal(
+                barrier, inc=1, device_id=(s + d[0], f + d[1]), device_id_type=MESH
+            )
+
+    count = exists(_DIRS[0]).astype(jnp.int32)
+    for d in _DIRS[1:]:
+        count = count + exists(d).astype(jnp.int32)
+    pl.semaphore_wait(barrier, count)
+
+    for k, d in enumerate(_DIRS):
+
+        @pl.when(exists(d))
+        def _():
+            desc(k).start()
+
+    for k, d in enumerate(_DIRS):
+        back = _DIRS.index((-d[0], -d[1]))
+
+        @pl.when(exists(d))
+        def _():
+            desc(k).wait_send()
+            desc(back).wait_recv()
+            outs[k][...] = slots[k][...]
+
+        @pl.when(jnp.logical_not(exists(d)))
+        def _():
+            outs[k][...] = jnp.zeros(outs[k].shape, outs[k].dtype)
+
+
+def padded_2(x, sides, width, collective_id):
+    del sides
+    ns, nf = lax.axis_size("space"), lax.axis_size("filt")
+    channels, rows, cols = x.shape
+    shapes = [
+        jax.ShapeDtypeStruct((channels, rows, _lanes(d[1], cols).stop - _lanes(d[1], cols).start), x.dtype)
+        for d in _DIRS
+    ]
+    got = pl.pallas_call(
+        functools.partial(halo_kernel, ns, nf, cols),
+        out_shape=shapes,
+        in_specs=[pl.BlockSpec(memory_space=pltpu.VMEM)],
+        out_specs=[pl.BlockSpec(memory_space=pltpu.VMEM)] * 8,
+        scratch_shapes=[pltpu.VMEM(sh.shape, sh.dtype) for sh in shapes]
+        + [pltpu.SemaphoreType.DMA((8,)), pltpu.SemaphoreType.DMA((8,))],
+        compiler_params=pltpu.CompilerParams(
+            collective_id=collective_id, has_side_effects=True
+        ),
+    )(x)
+    piece = dict(zip(_DIRS, got))
+    hi_r, lo_r = slice(rows - width, rows), slice(0, width)
+
+    above = piece[(-1, 0)][:, hi_r, :]
+    below = piece[(1, 0)][:, lo_r, :]
+    lw = piece[(0, -1)].shape[2]
+    left = piece[(0, -1)][:, :, lw - width : lw]
+    right = piece[(0, 1)][:, :, 0:width]
+    top_left = piece[(-1, -1)][:, hi_r, lw - width : lw]
+    top_right = piece[(-1, 1)][:, hi_r, 0:width]
+    bottom_left = piece[(1, -1)][:, lo_r, lw - width : lw]
+    bottom_right = piece[(1, 1)][:, lo_r, 0:width]
+    return jnp.concatenate(
+        [
+            jnp.concatenate([top_left, above, top_right], axis=2),
+            jnp.concatenate([left, x, right], axis=2),
+            jnp.concatenate([bottom_left, below, bottom_right], axis=2),
+        ],
+        axis=1,
+    )
 
 
 def depthwise(padded, kernel, row_count, col_count):
@@ -92,7 +188,7 @@
     channels, row_count, col_count = image.shape
     panel_rows = w_expand.shape[0] // lax.axis_size("filt")
     tok_count = row_count * col_count
-    padded = padded_2(image, (("space", 1), ("filt", 2)), 3)
+    padded = padded_2(image, (("space", 1), ("filt", 2)), 3, 1)
     conv = depthwise(padded, kernel, row_count, col_count)
     conv = conv + dw_bias[:, None, None]
     flat = conv.reshape(channels, tok_count)
@@ -153,7 +249,7 @@
     )
     d_float = convolution_gradient.astype(jnp.float32)
     g_dbias = jnp.sum(d_float, axis=(1, 2))
-    padded_grad = padded_2(convolution_gradient, (("space", 1), ("filt", 2)), 3)
+    padded_grad = padded_2(convolution_gradient, (("space", 1), ("filt", 2)), 3, 2)
     g_kernel = kernel_terms(padded, convolution_gradient, row_count, col_count)
     factor = 1.0 / math.sqrt(tok_count * lax.axis_size("space") * lax.axis_size("filt"))
     parts = lax.axis_size("filt")

time: 190 us -> 182 us (0.958)
  the two profiles are of different devices: /device:TPU:56 before, /device:TPU:8 now
where the time goes in v6:
time: 182 us; the launch traced here: 181 us
  Pallas kernels  101 us (55%)
  other arithmetic  40.8 us (22%)
  local copies, waits for them, and re-layouts  25.7 us (14%)
  matrix products  10.6 us (6%)
  between operations  2.36 us (1%)
    pallas_call x1, Pallas kernels, grad_reduce(): pl.pallas_call(functools.partial(reduce_kernel, nfilt, nspace, pr, sr), o...  76.7 us
    pallas_call x2, Pallas kernels, padded_2(): pl.pallas_call(functools.partial(halo_kernel, ns, nf, cols), out_shape=sh...  24.7 us
    reduce_sum x1, other arithmetic, shards(): average = jnp.mean(flat, axis=0, keepdims=True)  13.4 us
    convert_element_type x1, other arithmetic, shards(): image_grad = (cotangent.astype(jnp.float32) + back).astype(jnp.bfloat16)  13.2 us
    concatenate x3, other arithmetic, padded_2(): jnp.concatenate([jnp.concatenate([top_left, above, top_right], axis=2), j...  9.58 us
    slice x28, local copies, waits for them, and re-layouts, kernel_terms(): total = total + corr[:, row:row + ksize, row]  4.21 us

profile of v6, /device:TPU:8, one launch (start us, length us, event | category | flops | bytes accessed | tf_op | source)
XLA Modules:
  0.0 180.8 jit_solution(15688511642924664188)
XLA Ops:
  0.7 1.0 copy.64
  1.7 1.0 copy.60
  2.7 0.7 convert_element_type.397
  3.3 13.9 %shard_map.194 = (bf16[96,4,256]{2,1,0:T(4,128)(2,1)}, bf16[96,4,256]{2,1,0:T(4,128)(2,1)}, bf16[96,4,128]{2,1,0:T(4,128)(2,1)}, bf16[96,4,128]{2,1,0:T(4,128)(2...) custom-call(bf16[96,4,256]{2,1,0:T(4,128)(2,1)} %x_ref.1), custom_call_target="tpu_custom_call" | custom-call | tf_op jit(solution)/shard_map/pallas_call | solution.py:91
  17.3 1.0 slice.746
  18.3 0.9 slice.745
  19.3 1.1 slice.744
  20.4 1.0 slice.743
  21.4 1.0 slice.803
  22.4 2.9 %maximum_maximum_fusion.2 = (bf16[96,7,262]{2,1,0:T(8,128)(2,1)S(1)}, bf16[96,7,262]{2,1,0:T(8,128)(2,1)S(1)}) fusion(bf16[96,4,3]{2,1,0:T(4,128)(2,1)} %bitcast.184, bf16[96,4,256]{2,1,0:T(4,128)(2,1)S(1)} %copy-done.1, bf16[96,4,3]{2,1,0:T(4,128)(2,1)S(1)} %slice.746, bf16[96,3,3]{2,1,0:T(4,128)(2,1)S(1)} %slice.745, bf16[96,3,256]{2,1,0:T(4,128)(2,1)S(1)} %slice.744, ...), kind=kLoop, calls=%fused_computation.33 | loop fusion | flops 4225536 | bytes 1207296 | tf_op jit(solution)/shard_map/concatenate | solution.py:114
  25.6 0.5 slice_bitcast_fusion.49
  26.3 13.4 %fusion.34 = (f32[4,256]{1,0:T(4,128)S(1)}, f32[96,4,256]{2,1,0:T(4,128)S(1)}) fusion(f32[96]{0:T(128)S(1)} %copy-done.92, bf16[96,7,262]{2,1,0:T(8,128)(2,1)S(1)} %get-tuple-element.81, f32[96]{0:T(128)S(1)} %get-tuple-element.165, f32[96]{0:T(128)S(1)} %get-tuple-element.166, f32[96]{0:T(128)S(1)} %get-tuple-element.119, f32[96]{0:T(128)S(1)} %get-tuple-element.120, ...), kind=kLoop, calls=%fused_computation.134 | loop fusion | flops 16317440 | bytes 8875264 | tf_op jit(solution)/shard_map/reduce_sum | solution.py:195
  40.3 0.2 multiply_reduce_fusion.3
  40.5 1.8 fusion.9
  42.2 1.0 multiply_reduce_fusion.1
  43.2 0.8 reshape.125
  44.0 2.3 %convert_reduce_fusion = (f32[384]{0:T(512)S(1)}, bf16[384,1024]{0,1:T(8,128)(2,1)S(1)}) fusion(f32[1024,384]{1,0:T(8,128)} %get-tuple-element.170, bf16[384,96]{0,1:T(8,128)(2,1)S(1)} %copy-done.7, f32[96,1024]{1,0:T(8,128)S(1)} %bitcast.180, f32[96]{0:T(128)S(1)} %copy-done.88), kind=kOutput, calls=%fused_computation.13 | convolution fusion | flops 80412288 | bytes 2828160 | tf_op jit(solution)/shard_map/dot_general | solution.py:229
  46.4 0.1 reshape.128
  46.5 1.1 fusion.33
  47.6 0.8 reshape.127
  48.4 1.1 fusion.32
  49.5 0.2 reshape.126
  49.7 1.0 pad_maximum_fusion.1
  50.7 0.5 fusion.25
  51.2 0.2 convert_reduce_fusion.1
  51.4 0.1 reshape.129.x_ref
  51.6 3.3 %maximum_maximum_fusion = bf16[96,10,262]{2,1,0:T(8,128)(2,1)S(1)} fusion(bf16[96,3,3]{2,1,0:T(4,128)(2,1)} %bitcast.190, bf16[96,3,256]{2,1,0:T(4,128)(2,1)S(1)} %bitcast.188, bf16[96,3,3]{2,1,0:T(4,128)(2,1)S(1)} %slice.803, bf16[96,4,3]{2,1,0:T(4,128)(2,1)S(1)} %bitcast.186, bf16[96,4,256]{2,1,0:T(4,128)(2,1)S(1)} %copy-done.1, ...), kind=kLoop, calls=%fused_computation.17 | loop fusion | flops 4527360 | bytes 1006080 | tf_op jit(solution)/shard_map/concatenate | solution.py:114
  54.9 0.3 fusion.23
  55.2 0.4 fusion.41
  56.0 0.4 fusion.21
  56.4 0.4 fusion.40
  57.1 0.4 fusion.19
  57.5 0.4 fusion.39
  58.2 0.4 fusion.17
  58.7 0.4 fusion.38
  59.4 0.4 fusion.15
  59.8 0.4 fusion.37
  60.5 0.4 fusion.13
  60.9 0.4 fusion.36
  61.7 0.4 fusion.11
  62.1 0.4 fusion.35
  62.9 0.2 copy.56
  63.1 0.4 reshape.130
  63.5 0.1 reduce_sum.97
  63.7 1.4 multiply_reduce_fusion
  65.1 0.1 concatenate.101
  65.2 10.7 %shard_map.195 = (bf16[96,4,256]{2,1,0:T(4,128)(2,1)}, bf16[96,4,256]{2,1,0:T(4,128)(2,1)}, bf16[96,4,128]{2,1,0:T(4,128)(2,1)}, bf16[96,4,128]{2,1,0:T(4,128)(2...) custom-call(bf16[96,4,256]{2,1,0:T(4,128)(2,1)} %copy-done.2), custom_call_target="tpu_custom_call" | custom-call | tf_op jit(solution)/shard_map/pallas_call | solution.py:91
  75.9 1.0 slice.887
  76.9 1.0 slice.885
  78.3 0.9 slice.884
  79.3 1.0 slice.883
  80.3 1.0 slice.882
  81.4 3.4 %maximum_maximum_fusion.1 = bf16[96,10,262]{2,1,0:T(8,128)(2,1)S(1)} fusion(bf16[96,3,3]{2,1,0:T(4,128)(2,1)} %bitcast.202, bf16[96,3,256]{2,1,0:T(4,128)(2,1)} %bitcast.192, bf16[96,3,3]{2,1,0:T(4,128)(2,1)S(1)} %slice.887, bf16[96,4,3]{2,1,0:T(4,128)(2,1)} %bitcast.201, bf16[96,4,256]{2,1,0:T(4,128)(2,1)S(1)} %copy-done.3, ...), kind=kLoop, calls=%fused_computation.18 | loop fusion | flops 4527360 | bytes 1006080 | tf_op jit(solution)/shard_map/concatenate | solution.py:114
  85.1 13.2 %add_convert_fusion = bf16[96,4,256]{2,1,0:T(4,128)(2,1)} fusion(bf16[96,10,262]{2,1,0:T(8,128)(2,1)S(1)} %maximum_maximum_fusion.1, bf16[96,4,256]{2,1,0:T(4,128)(2,1)S(1)} %copy-done.4, f32[96]{0:T(128)S(1)} %copy-done.17, f32[96]{0:T(128)S(1)} %copy-done.19, f32[96]{0:T(128)S(1)} %copy-done.23, f32[96]{0:T(128)S(1)} %copy-done.25, f32[96]{0:T(128)S(1)} %copy-done.27, ...), kind=kLoop, calls=%fused_computation.38 | loop fusion | flops 14647296 | bytes 10045824 | tf_op jit(solution)/shard_map/convert_element_type | solution.py:276
  98.4 0.1 reshape.131
  98.6 0.8 pad_maximum_fusion.buf_ref
  99.3 76.7 %shard_map.196 = f32[200,128]{1,0:T(8,128)} custom-call(f32[656,128]{1,0:T(8,128)} %pad_maximum_fusion.buf_ref), custom_call_target="tpu_custom_call" | custom-call | bytes 209715200 | tf_op jit(solution)/shard_map/pallas_call | solution.py:422
  176.0 0.7 slice_bitcast_fusion.1
  176.8 0.9 slice_bitcast_fusion
  177.8 0.2 reshape.135
  178.0 0.8 copy.57
  178.8 0.6 fusion.42
  179.4 0.7 slice.948
  180.1 0.7 slice.951
  (237 shorter events, 3.2 us)
Async XLA Ops:
  0.6 39.8 %copy-start = (bf16[384,96]{0,1:T(8,128)(2,1)S(1)}, bf16[384,96]{0,1:T(8,128)(2,1)}, u32[]{:S(2)}) copy-start(bf16[384,96]{0,1:T(8,128)(2,1)} %param.17) | copy-start | bytes 221188
  0.7 21.8 %copy-start.1 = (bf16[96,4,256]{2,1,0:T(4,128)(2,1)S(1)}, bf16[96,4,256]{2,1,0:T(4,128)(2,1)}, u32[]{:S(2)}) copy-start(bf16[96,4,256]{2,1,0:T(4,128)(2,1)} %x_ref.1) | copy-start | bytes 589828
  19.3 7.0 %copy-start.5 = (bf16[96,4,128]{2,1,0:T(4,128)(2,1)S(1)}, bf16[96,4,128]{2,1,0:T(4,128)(2,1)}, u32[]{:S(2)}) copy-start(bf16[96,4,128]{2,1,0:T(4,128)(2,1)} %get-tuple-element.34) | copy-start | bytes 294916
  19.3 7.0 %copy-start.92 = (f32[96]{0:T(128)S(1)}, f32[96]{0:T(128)}, u32[]{:S(2)}) copy-start(f32[96]{0:T(128)} %param.14) | copy-start | bytes 1156
  25.3 14.4 %copy-start.10 = (f32[96]{0:T(128)}, f32[96]{0:T(128)S(1)}, u32[]{:S(2)}) copy-start(f32[96]{0:T(128)S(1)} %get-tuple-element.162) | copy-start | bytes 1156
  25.3 14.4 %copy-start.12 = (f32[96]{0:T(128)}, f32[96]{0:T(128)S(1)}, u32[]{:S(2)}) copy-start(f32[96]{0:T(128)S(1)} %get-tuple-element.163) | copy-start | bytes 1156
  25.3 14.4 %copy-start.14 = (f32[96]{0:T(128)}, f32[96]{0:T(128)S(1)}, u32[]{:S(2)}) copy-start(f32[96]{0:T(128)S(1)} %get-tuple-element.164) | copy-start | bytes 1156
  25.4 14.4 %copy-start.16 = (f32[96]{0:T(128)}, f32[96]{0:T(128)S(1)}, u32[]{:S(2)}) copy-start(f32[96]{0:T(128)S(1)} %get-tuple-element.165) | copy-start | bytes 1156
  25.4 14.4 %copy-start.18 = (f32[96]{0:T(128)}, f32[96]{0:T(128)S(1)}, u32[]{:S(2)}) copy-start(f32[96]{0:T(128)S(1)} %get-tuple-element.166) | copy-start | bytes 1156
  25.4 14.4 %copy-start.20 = (f32[96]{0:T(128)}, f32[96]{0:T(128)S(1)}, u32[]{:S(2)}) copy-start(f32[96]{0:T(128)S(1)} %get-tuple-element.118) | copy-start | bytes 1156
  25.4 14.4 %copy-start.22 = (f32[96]{0:T(128)}, f32[96]{0:T(128)S(1)}, u32[]{:S(2)}) copy-start(f32[96]{0:T(128)S(1)} %get-tuple-element.119) | copy-start | bytes 1156
  25.4 14.4 %copy-start.24 = (f32[96]{0:T(128)}, f32[96]{0:T(128)S(1)}, u32[]{:S(2)}) copy-start(f32[96]{0:T(128)S(1)} %get-tuple-element.120) | copy-start | bytes 1156
  25.4 14.4 %copy-start.26 = (f32[96]{0:T(128)}, f32[96]{0:T(128)S(1)}, u32[]{:S(2)}) copy-start(f32[96]{0:T(128)S(1)} %get-tuple-element.121) | copy-start | bytes 1156
  25.4 14.4 %copy-start.28 = (f32[96]{0:T(128)}, f32[96]{0:T(128)S(1)}, u32[]{:S(2)}) copy-start(f32[96]{0:T(128)S(1)} %get-tuple-element.122) | copy-start | bytes 1156
  25.5 14.4 %copy-start.30 = (f32[96]{0:T(128)}, f32[96]{0:T(128)S(1)}, u32[]{:S(2)}) copy-start(f32[96]{0:T(128)S(1)} %get-tuple-element.123) | copy-start | bytes 1156
  25.5 14.4 %copy-start.32 = (f32[96]{0:T(128)}, f32[96]{0:T(128)S(1)}, u32[]{:S(2)}) copy-start(f32[96]{0:T(128)S(1)} %get-tuple-element.124) | copy-start | bytes 1156
  25.5 14.4 %copy-start.34 = (f32[96]{0:T(128)}, f32[96]{0:T(128)S(1)}, u32[]{:S(2)}) copy-start(f32[96]{0:T(128)S(1)} %get-tuple-element.125) | copy-start | bytes 1156
  25.5 14.4 %copy-start.36 = (f32[96]{0:T(128)}, f32[96]{0:T(128)S(1)}, u32[]{:S(2)}) copy-start(f32[96]{0:T(128)S(1)} %get-tuple-element.126) | copy-start | bytes 1156
  25.5 14.4 %copy-start.38 = (f32[96]{0:T(128)}, f32[96]{0:T(128)S(1)}, u32[]{:S(2)}) copy-start(f32[96]{0:T(128)S(1)} %get-tuple-element.127) | copy-start | bytes 1156
  25.5 14.4 %copy-start.40 = (f32[96]{0:T(128)}, f32[96]{0:T(128)S(1)}, u32[]{:S(2)}) copy-start(f32[96]{0:T(128)S(1)} %get-tuple-element.128) | copy-start | bytes 1156
  25.5 14.4 %copy-start.42 = (f32[96]{0:T(128)}, f32[96]{0:T(128)S(1)}, u32[]{:S(2)}) copy-start(f32[96]{0:T(128)S(1)} %get-tuple-element.129) | copy-start | bytes 1156
  25.5 14.4 %copy-start.44 = (f32[96]{0:T(128)}, f32[96]{0:T(128)S(1)}, u32[]{:S(2)}) copy-start(f32[96]{0:T(128)S(1)} %get-tuple-element.130) | copy-start | bytes 1156
  25.5 14.4 %copy-start.46 = (f32[96]{0:T(128)}, f32[96]{0:T(128)S(1)}, u32[]{:S(2)}) copy-start(f32[96]{0:T(128)S(1)} %get-tuple-element.131) | copy-start | bytes 1156
  25.5 14.4 %copy-start.48 = (f32[96]{0:T(128)}, f32[96]{0:T(128)S(1)}, u32[]{:S(2)}) copy-start(f32[96]{0:T(128)S(1)} %get-tuple-element.132) | copy-start | bytes 1156
  25.6 14.4 %copy-start.50 = (f32[96]{0:T(128)}, f32[96]{0:T(128)S(1)}, u32[]{:S(2)}) copy-start(f32[96]{0:T(128)S(1)} %get-tuple-element.133) | copy-start | bytes 1156
  25.6 14.4 %copy-start.52 = (f32[96]{0:T(128)}, f32[96]{0:T(128)S(1)}, u32[]{:S(2)}) copy-start(f32[96]{0:T(128)S(1)} %get-tuple-element.134) | copy-start | bytes 1156
  25.6 14.4 %copy-start.54 = (f32[96]{0:T(128)}, f32[96]{0:T(128)S(1)}, u32[]{:S(2)}) copy-start(f32[96]{0:T(128)S(1)} %get-tuple-element.135) | copy-start | bytes 1156
  25.6 14.4 %copy-start.56 = (f32[96]{0:T(128)}, f32[96]{0:T(128)S(1)}, u32[]{:S(2)}) copy-start(f32[96]{0:T(128)S(1)} %get-tuple-element.136) | copy-start | bytes 1156
  26.1 13.8 %copy-start.58 = (f32[96]{0:T(128)}, f32[96]{0:T(128)S(1)}, u32[]{:S(2)}) copy-start(f32[96]{0:T(128)S(1)} %get-tuple-element.137) | copy-start | bytes 1156
  26.1 13.9 %copy-start.60 = (f32[96]{0:T(128)}, f32[96]{0:T(128)S(1)}, u32[]{:S(2)}) copy-start(f32[96]{0:T(128)S(1)} %get-tuple-element.138) | copy-start | bytes 1156
  26.1 13.9 %copy-start.62 = (f32[96]{0:T(128)}, f32[96]{0:T(128)S(1)}, u32[]{:S(2)}) copy-start(f32[96]{0:T(128)S(1)} %get-tuple-element.139) | copy-start | bytes 1156
  26.1 13.9 %copy-start.64 = (f32[96]{0:T(128)}, f32[96]{0:T(128)S(1)}, u32[]{:S(2)}) copy-start(f32[96]{0:T(128)S(1)} %get-tuple-element.140) | copy-start | bytes 1156
  26.1 13.9 %copy-start.66 = (f32[96]{0:T(128)}, f32[96]{0:T(128)S(1)}, u32[]{:S(2)}) copy-start(f32[96]{0:T(128)S(1)} %get-tuple-element.141) | copy-start | bytes 1156
  26.2 13.9 %copy-start.68 = (f32[96]{0:T(128)}, f32[96]{0:T(128)S(1)}, u32[]{:S(2)}) copy-start(f32[96]{0:T(128)S(1)} %get-tuple-element.142) | copy-start | bytes 1156
  26.2 13.9 %copy-start.70 = (f32[96]{0:T(128)}, f32[96]{0:T(128)S(1)}, u32[]{:S(2)}) copy-start(f32[96]{0:T(128)S(1)} %get-tuple-element.143) | copy-start | bytes 1156
  26.2 13.9 %copy-start.72 = (f32[96]{0:T(128)}, f32[96]{0:T(128)S(1)}, u32[]{:S(2)}) copy-start(f32[96]{0:T(128)S(1)} %get-tuple-element.144) | copy-start | bytes 1156
  26.2 13.9 %copy-start.74 = (f32[96]{0:T(128)}, f32[96]{0:T(128)S(1)}, u32[]{:S(2)}) copy-start(f32[96]{0:T(128)S(1)} %get-tuple-element.145) | copy-start | bytes 1156
  26.2 13.9 %copy-start.76 = (f32[96]{0:T(128)}, f32[96]{0:T(128)S(1)}, u32[]{:S(2)}) copy-start(f32[96]{0:T(128)S(1)} %get-tuple-element.146) | copy-start | bytes 1156
  26.2 13.9 %copy-start.78 = (f32[96]{0:T(128)}, f32[96]{0:T(128)S(1)}, u32[]{:S(2)}) copy-start(f32[96]{0:T(128)S(1)} %get-tuple-element.147) | copy-start | bytes 1156
  26.2 13.9 %copy-start.80 = (f32[96]{0:T(128)}, f32[96]{0:T(128)S(1)}, u32[]{:S(2)}) copy-start(f32[96]{0:T(128)S(1)} %get-tuple-element.148) | copy-start | bytes 1156
  26.2 13.9 %copy-start.82 = (f32[96]{0:T(128)}, f32[96]{0:T(128)S(1)}, u32[]{:S(2)}) copy-start(f32[96]{0:T(128)S(1)} %get-tuple-element.149) | copy-start | bytes 1156
  26.2 13.9 %copy-start.84 = (f32[96]{0:T(128)}, f32[96]{0:T(128)S(1)}, u32[]{:S(2)}) copy-start(f32[96]{0:T(128)S(1)} %get-tuple-element.150) | copy-start | bytes 1156
  26.2 13.9 %copy-start.86 = (f32[96]{0:T(128)}, f32[96]{0:T(128)S(1)}, u32[]{:S(2)}) copy-start(f32[96]{0:T(128)S(1)} %get-tuple-element.151) | copy-start | bytes 1156
  26.3 14.2 %copy-start.9 = (f32[96]{0:T(128)S(1)}, f32[96]{0:T(128)}, u32[]{:S(2)}) copy-start(f32[96]{0:T(128)} %param.15) | copy-start | bytes 1156
  26.3 14.2 %copy-start.90 = (f32[96]{0:T(128)S(1)}, f32[96]{0:T(128)}, u32[]{:S(2)}) copy-start(f32[96]{0:T(128)} %param.16) | copy-start | bytes 1156
  51.6 10.0 %copy-start.2 = (bf16[96,4,256]{2,1,0:T(4,128)(2,1)}, bf16[96,4,256]{2,1,0:T(4,128)(2,1)S(1)}, u32[]{:S(2)}) copy-start(bf16[96,4,256]{2,1,0:T(4,128)(2,1)S(1)} %reshape.129.x_ref) | copy-start | bytes 589828
  62.5 18.9 %copy-start.3 = (bf16[96,4,256]{2,1,0:T(4,128)(2,1)S(1)}, bf16[96,4,256]{2,1,0:T(4,128)(2,1)}, u32[]{:S(2)}) copy-start(bf16[96,4,256]{2,1,0:T(4,128)(2,1)} %copy-done.2) | copy-start | bytes 589828
  77.9 6.8 %copy-start.11 = (f32[96]{0:T(128)S(1)}, f32[96]{0:T(128)}, u32[]{:S(2)}) copy-start(f32[96]{0:T(128)} %copy-done.10) | copy-start | bytes 1156
  77.9 6.8 %copy-start.13 = (f32[96]{0:T(128)S(1)}, f32[96]{0:T(128)}, u32[]{:S(2)}) copy-start(f32[96]{0:T(128)} %copy-done.12) | copy-start | bytes 1156
  77.9 6.8 %copy-start.15 = (f32[96]{0:T(128)S(1)}, f32[96]{0:T(128)}, u32[]{:S(2)}) copy-start(f32[96]{0:T(128)} %copy-done.14) | copy-start | bytes 1156
  78.0 6.8 %copy-start.17 = (f32[96]{0:T(128)S(1)}, f32[96]{0:T(128)}, u32[]{:S(2)}) copy-start(f32[96]{0:T(128)} %copy-done.16) | copy-start | bytes 1156
  78.0 6.8 %copy-start.19 = (f32[96]{0:T(128)S(1)}, f32[96]{0:T(128)}, u32[]{:S(2)}) copy-start(f32[96]{0:T(128)} %copy-done.18) | copy-start | bytes 1156
  78.0 6.8 %copy-start.21 = (f32[96]{0:T(128)S(1)}, f32[96]{0:T(128)}, u32[]{:S(2)}) copy-start(f32[96]{0:T(128)} %copy-done.20) | copy-start | bytes 1156
  78.0 6.8 %copy-start.23 = (f32[96]{0:T(128)S(1)}, f32[96]{0:T(128)}, u32[]{:S(2)}) copy-start(f32[96]{0:T(128)} %copy-done.22) | copy-start | bytes 1156
  78.0 6.8 %copy-start.25 = (f32[96]{0:T(128)S(1)}, f32[96]{0:T(128)}, u32[]{:S(2)}) copy-start(f32[96]{0:T(128)} %copy-done.24) | copy-start | bytes 1156
  78.0 6.8 %copy-start.27 = (f32[96]{0:T(128)S(1)}, f32[96]{0:T(128)}, u32[]{:S(2)}) copy-start(f32[96]{0:T(128)} %copy-done.26) | copy-start | bytes 1156
  78.0 6.8 %copy-start.29 = (f32[96]{0:T(128)S(1)}, f32[96]{0:T(128)}, u32[]{:S(2)}) copy-start(f32[96]{0:T(128)} %copy-done.28) | copy-start | bytes 1156
  78.0 6.8 %copy-start.31 = (f32[96]{0:T(128)S(1)}, f32[96]{0:T(128)}, u32[]{:S(2)}) copy-start(f32[96]{0:T(128)} %copy-done.30) | copy-start | bytes 1156
  78.0 6.8 %copy-start.33 = (f32[96]{0:T(128)S(1)}, f32[96]{0:T(128)}, u32[]{:S(2)}) copy-start(f32[96]{0:T(128)} %copy-done.32) | copy-start | bytes 1156
  78.1 6.8 %copy-start.35 = (f32[96]{0:T(128)S(1)}, f32[96]{0:T(128)}, u32[]{:S(2)}) copy-start(f32[96]{0:T(128)} %copy-done.34) | copy-start | bytes 1156
  78.1 6.8 %copy-start.37 = (f32[96]{0:T(128)S(1)}, f32[96]{0:T(128)}, u32[]{:S(2)}) copy-start(f32[96]{0:T(128)} %copy-done.36) | copy-start | bytes 1156
  78.1 6.8 %copy-start.39 = (f32[96]{0:T(128)S(1)}, f32[96]{0:T(128)}, u32[]{:S(2)}) copy-start(f32[96]{0:T(128)} %copy-done.38) | copy-start | bytes 1156
  78.1 6.8 %copy-start.41 = (f32[96]{0:T(128)S(1)}, f32[96]{0:T(128)}, u32[]{:S(2)}) copy-start(f32[96]{0:T(128)} %copy-done.40) | copy-start | bytes 1156
  78.1 6.8 %copy-start.43 = (f32[96]{0:T(128)S(1)}, f32[96]{0:T(128)}, u32[]{:S(2)}) copy-start(f32[96]{0:T(128)} %copy-done.42) | copy-start | bytes 1156
  (30 other events, 170.4 us)

commit v7 on v6

--- a/solution.py
+++ b/solution.py
@@ -23,10 +23,7 @@
     return slice(0, LANES)
 
 
-def halo_kernel(ns, nf, cols, x_ref, *refs):
-    outs = refs[:8]
-    slots = refs[8:16]
-    send_sem, recv_sem = refs[16:]
+def _halo_ops(ns, nf, cols, x_ref, outs, slots, send_sem, recv_sem):
     s = lax.axis_index("space")
     f = lax.axis_index("filt")
 
@@ -46,62 +43,63 @@
             device_id_type=MESH,
         )
 
+    def signal(barrier):
+        count = 0
+        for d in _DIRS:
+
+            @pl.when(exists(d))
+            def _():
+                pl.semaphore_signal(
+                    barrier, inc=1, device_id=(s + d[0], f + d[1]), device_id_type=MESH
+                )
+
+            count = count + exists(d).astype(jnp.int32)
+        return count
+
+    def start():
+        for k, d in enumerate(_DIRS):
+
+            @pl.when(exists(d))
+            def _():
+                desc(k).start()
+
+    def finish():
+        for k, d in enumerate(_DIRS):
+            back = _DIRS.index((-d[0], -d[1]))
+
+            @pl.when(exists(d))
+            def _():
+                desc(k).wait_send()
+                desc(back).wait_recv()
+                outs[k][...] = slots[k][...]
+
+            @pl.when(jnp.logical_not(exists(d)))
+            def _():
+                outs[k][...] = jnp.zeros(outs[k].shape, outs[k].dtype)
+
+    return signal, start, finish
+
+
+def halo_kernel(ns, nf, cols, x_ref, *refs):
+    signal, start, finish = _halo_ops(ns, nf, cols, x_ref, refs[:8], refs[8:16], *refs[16:])
     barrier = pltpu.get_barrier_semaphore()
-    for k, d in enumerate(_DIRS):
-
-        @pl.when(exists(d))
-        def _():
-            pl.semaphore_signal(
-                barrier, inc=1, device_id=(s + d[0], f + d[1]), device_id_type=MESH
-            )
-
-    count = exists(_DIRS[0]).astype(jnp.int32)
-    for d in _DIRS[1:]:
-        count = count + exists(d).astype(jnp.int32)
-    pl.semaphore_wait(barrier, count)
-
-    for k, d in enumerate(_DIRS):
-
-        @pl.when(exists(d))
-        def _():
-            desc(k).start()
-
-    for k, d in enumerate(_DIRS):
-        back = _DIRS.index((-d[0], -d[1]))
-
-        @pl.when(exists(d))
-        def _():
-            desc(k).wait_send()
-            desc(back).wait_recv()
-            outs[k][...] = slots[k][...]
-
-        @pl.when(jnp.logical_not(exists(d)))
-        def _():
-            outs[k][...] = jnp.zeros(outs[k].shape, outs[k].dtype)
-
-
-def padded_2(x, sides, width, collective_id):
-    del sides
-    ns, nf = lax.axis_size("space"), lax.axis_size("filt")
+    pl.semaphore_wait(barrier, signal(barrier))
+    start()
+    finish()
+
+
+def _halo_shapes(x):
     channels, rows, cols = x.shape
-    shapes = [
+    return [
         jax.ShapeDtypeStruct((channels, rows, _lanes(d[1], cols).stop - _lanes(d[1], cols).start), x.dtype)
         for d in _DIRS
     ]
-    got = pl.pallas_call(
-        functools.partial(halo_kernel, ns, nf, cols),
-        out_shape=shapes,
-        in_specs=[pl.BlockSpec(memory_space=pltpu.VMEM)],
-        out_specs=[pl.BlockSpec(memory_space=pltpu.VMEM)] * 8,
-        scratch_shapes=[pltpu.VMEM(sh.shape, sh.dtype) for sh in shapes]
-        + [pltpu.SemaphoreType.DMA((8,)), pltpu.SemaphoreType.DMA((8,))],
-        compiler_params=pltpu.CompilerParams(
-            collective_id=collective_id, has_side_effects=True
-        ),
-    )(x)
+
+
+def _assemble(x, got, width):
+    rows = x.shape[1]
     piece = dict(zip(_DIRS, got))
     hi_r, lo_r = slice(rows - width, rows), slice(0, width)
-
     above = piece[(-1, 0)][:, hi_r, :]
     below = piece[(1, 0)][:, lo_r, :]
     lw = piece[(0, -1)].shape[2]
@@ -119,6 +117,24 @@
         ],
         axis=1,
     )
+
+
+def padded_2(x, sides, width, collective_id):
+    del sides
+    ns, nf = lax.axis_size("space"), lax.axis_size("filt")
+    shapes = _halo_shapes(x)
+    got = pl.pallas_call(
+        functools.partial(halo_kernel, ns, nf, x.shape[2]),
+        out_shape=shapes,
+        in_specs=[pl.BlockSpec(memory_space=pltpu.VMEM)],
+        out_specs=[pl.BlockSpec(memory_space=pltpu.VMEM)] * 8,
+        scratch_shapes=[pltpu.VMEM(sh.shape, sh.dtype) for sh in shapes]
+        + [pltpu.SemaphoreType.DMA((8,)), pltpu.SemaphoreType.DMA((8,))],
+        compiler_params=pltpu.CompilerParams(
+            collective_id=collective_id, has_side_effects=True
+        ),
+    )(x)
+    return _assemble(x, got, width)
 
 
 def depthwise(padded, kernel, row_count, col_count):
@@ -249,7 +265,6 @@
     )
     d_float = convolution_gradient.astype(jnp.float32)
     g_dbias = jnp.sum(d_float, axis=(1, 2))
-    padded_grad = padded_2(convolution_gradient, (("space", 1), ("filt", 2)), 3, 2)
     g_kernel = kernel_terms(padded, convolution_gradient, row_count, col_count)
     factor = 1.0 / math.sqrt(tok_count * lax.axis_size("space") * lax.axis_size("filt"))
     parts = lax.axis_size("filt")
@@ -271,10 +286,10 @@
             g_rbias,
         ]
     )
-    panels, small, padded_grad = lax.optimization_barrier((panels, small, padded_grad))
+    panel, small, got = grad_reduce(panels, small, convolution_gradient)
+    padded_grad = _assemble(convolution_gradient, got, 3)
     back = conv_back(padded_grad, kernel, row_count, col_count)
     image_grad = (cotangent.astype(jnp.float32) + back).astype(jnp.bfloat16)
-    panel, small = grad_reduce(panels, small)
     total = jnp.concatenate([panel, small])
     total = total * factor
     cut = [panel_rows * channels, panel_rows * channels, panel_rows]
@@ -311,12 +326,18 @@
     return index + bit - 2 * bit * ((index // bit) % 2)
 
 
-def reduce_kernel(nfilt, nspace, pr, sr, buf_ref, out_ref, *scratch):
+def reduce_kernel(nfilt, nspace, pr, sr, cols, buf_ref, x_ref, out_ref, *refs):
     levels = nfilt.bit_length() - 1
     steps = nspace.bit_length() - 1
+    halo_outs = refs[:8]
+    scratch = refs[8:]
     recvs = scratch[:levels]
     stages = scratch[levels : 2 * levels]
-    recv_s, send_sem, recv_sem = scratch[2 * levels :]
+    recv_s, send_sem, recv_sem = scratch[2 * levels : 2 * levels + 3]
+    halo = scratch[2 * levels + 3 :]
+    halo_signal, halo_start, halo_finish = _halo_ops(
+        nspace, nfilt, cols, x_ref, halo_outs, halo[:8], halo[8], halo[9]
+    )
     s = lax.axis_index("space")
     f = lax.axis_index("filt")
 
@@ -330,7 +351,9 @@
     barrier = pltpu.get_barrier_semaphore()
     for peer in peers:
         pl.semaphore_signal(barrier, inc=1, device_id=peer, device_id_type=MESH)
-    pl.semaphore_wait(barrier, len(peers))
+    count = halo_signal(barrier)
+    pl.semaphore_wait(barrier, count + len(peers))
+    halo_start()
 
     held = buf_ref
     count = nfilt
@@ -388,9 +411,10 @@
         copy.wait()
         sem += 1
         out_ref[...] = out_ref[...] + recv_s[k]
-
-
-def grad_reduce(panels, small):
+    halo_finish()
+
+
+def grad_reduce(panels, small, x):
     nfilt = lax.axis_size("filt")
     nspace = lax.axis_size("space")
     width = panels.shape[1]
@@ -419,20 +443,23 @@
         pltpu.SemaphoreType.DMA((ncopies,)),
         pltpu.SemaphoreType.DMA((ncopies,)),
     ]
-    out = pl.pallas_call(
-        functools.partial(reduce_kernel, nfilt, nspace, pr, sr),
-        out_shape=jax.ShapeDtypeStruct((pr + sr, LANES), jnp.float32),
-        in_specs=[pl.BlockSpec(memory_space=pltpu.VMEM)],
-        out_specs=pl.BlockSpec(memory_space=pltpu.VMEM),
+    shapes = _halo_shapes(x)
+    scratch += [pltpu.VMEM(sh.shape, sh.dtype) for sh in shapes]
+    scratch += [pltpu.SemaphoreType.DMA((8,)), pltpu.SemaphoreType.DMA((8,))]
+    out, *got = pl.pallas_call(
+        functools.partial(reduce_kernel, nfilt, nspace, pr, sr, x.shape[2]),
+        out_shape=[jax.ShapeDtypeStruct((pr + sr, LANES), jnp.float32)] + shapes,
+        in_specs=[pl.BlockSpec(memory_space=pltpu.VMEM)] * 2,
+        out_specs=[pl.BlockSpec(memory_space=pltpu.VMEM)] * 9,
         scratch_shapes=scratch,
         compiler_params=pltpu.CompilerParams(collective_id=0, has_side_effects=True),
         cost_estimate=pl.CostEstimate(
             flops=0, transcendentals=0, bytes_accessed=200 * 1024 * 1024
         ),
-    )(buf)
+    )(buf, x)
     panel = out[:pr].reshape(-1)[:width]
     small = out[pr:].reshape(-1)[: small.shape[0]]
-    return panel, small
+    return panel, small, got
 
 
 def solution(mesh):

time: 182 us -> 171 us (0.940)
  the two profiles are of different devices: /device:TPU:8 before, /device:TPU:56 now
where the time goes in v7:
time: 171 us; the launch traced here: 168 us
  Pallas kernels  89.4 us (52%)
  other arithmetic  39.8 us (23%)
  local copies, waits for them, and re-layouts  22.4 us (13%)
  matrix products  14.2 us (8%)
  between operations  2.5 us (1%)
    pallas_call x1, Pallas kernels, grad_reduce(): pl.pallas_call(functools.partial(reduce_kernel, nfilt, nspace, pr, sr, x....  63.2 us
    pallas_call x1, Pallas kernels, padded_2(): pl.pallas_call(functools.partial(halo_kernel, ns, nf, x.shape[2]), out_sh...  26.2 us
    convert_element_type x1, other arithmetic, shards(): image_grad = (cotangent.astype(jnp.float32) + back).astype(jnp.bfloat16)  14.4 us
    reduce_sum x1, other arithmetic, shards(): average = jnp.mean(flat, axis=0, keepdims=True)  13.8 us
    dot_general x7, matrix products, kernel_terms(): jnp.einsum('crj,cij->cri', padded[:, :, shift_col:shift_col + col_count],...  10.3 us
    concatenate x3, other arithmetic, _assemble(): jnp.concatenate([jnp.concatenate([top_left, above, top_right], axis=2), j...  6.89 us
    slice x28, local copies, waits for them, and re-layouts, kernel_terms(): total = total + corr[:, row:row + ksize, row]  4.29 us

profile of v7, /device:TPU:56, one launch (start us, length us, event | category | flops | bytes accessed | tf_op | source)
XLA Modules:
  0.0 168.4 jit_solution(12282593401795811891)
XLA Ops:
  0.7 26.2 %shard_map.194 = (bf16[96,4,256]{2,1,0:T(4,128)(2,1)}, bf16[96,4,256]{2,1,0:T(4,128)(2,1)}, bf16[96,4,128]{2,1,0:T(4,128)(2,1)}, bf16[96,4,128]{2,1,0:T(4,128)(2...) custom-call(bf16[96,4,256]{2,1,0:T(4,128)(2,1)} %x_ref.1), custom_call_target="tpu_custom_call" | custom-call | tf_op jit(solution)/shard_map/pallas_call | solution.py:126
  26.9 1.1 slice.791
  28.0 1.0 slice.789
  29.0 1.0 slice.788
  30.0 1.0 slice.790
  31.0 1.0 slice.848
  32.2 1.8 %maximum_maximum_fusion.1 = (bf16[96,7,262]{2,1,0:T(8,128)(2,1)S(1)}, bf16[96,7,262]{2,1,0:T(8,128)(2,1)S(1)}) fusion(bf16[96,4,3]{2,1,0:T(4,128)(2,1)S(1)} %bitcast.184, bf16[96,4,256]{2,1,0:T(4,128)(2,1)S(1)} %copy-done.1, bf16[96,4,3]{2,1,0:T(4,128)(2,1)S(1)} %slice.791, bf16[96,3,3]{2,1,0:T(4,128)(2,1)S(1)} %slice.790, ...), kind=kLoop, calls=%fused_computation.32 | loop fusion | flops 4225536 | bytes 1207296 | tf_op jit(solution)/shard_map/concatenate | solution.py:112
  34.3 0.6 slice_bitcast_fusion.48
  35.0 13.8 %fusion.38 = (f32[4,256]{1,0:T(4,128)S(1)}, f32[96,4,256]{2,1,0:T(4,128)S(1)}) fusion(f32[96]{0:T(128)S(1)} %copy-done.110, bf16[96,7,262]{2,1,0:T(8,128)(2,1)S(1)} %get-tuple-element.79, f32[96]{0:T(128)} %get-tuple-element.163, f32[96]{0:T(128)} %get-tuple-element.164, f32[96]{0:T(128)S(1)} %get-tuple-element.117, f32[96]{0:T(128)S(1)} %get-tuple-element.118, ...), kind=kLoop, calls=%fused_computation.151 | loop fusion | flops 16317440 | bytes 8875264 | tf_op jit(solution)/shard_map/reduce_sum | solution.py:211
  49.2 0.2 multiply_reduce_fusion.3
  49.5 0.4 copy-done.109
  49.9 0.6 fusion.9
  50.6 0.3 copy-done.4
  50.9 0.9 convert_reduce_fusion
  51.8 0.4 fusion.37
  52.3 0.8 reshape.127
  53.1 0.1 reshape.128
  53.2 0.4 fusion.36
  53.7 0.8 reshape.126
  54.5 1.0 select_maximum_fusion
  55.6 0.9 reshape.129
  56.4 1.0 fusion.25
  57.5 0.8 convert_reduce_fusion.1
  58.2 0.1 reshape.130.x_ref
  58.5 3.3 %maximum_maximum_fusion = bf16[96,10,262]{2,1,0:T(8,128)(2,1)S(1)} fusion(bf16[96,3,3]{2,1,0:T(4,128)(2,1)} %bitcast.191, bf16[96,3,256]{2,1,0:T(4,128)(2,1)S(1)} %bitcast.188, bf16[96,3,3]{2,1,0:T(4,128)(2,1)S(1)} %copy-done.14, bf16[96,4,3]{2,1,0:T(4,128)(2,1)S(1)} %bitcast.186, bf16[96,4,256]{2,1,0:T(4,128)(2,1)S(1)} %copy-done.1, ...), kind=kLoop, calls=%fused_computation.17 | loop fusion | flops 4527360 | bytes 1006080 | tf_op jit(solution)/shard_map/concatenate | solution.py:112
  61.9 1.0 copy-done.6
  62.9 0.4 fusion.11
  63.3 0.4 fusion.39
  63.9 0.1 copy.55
  64.0 1.7 %fusion.13 = f32[96,10,4]{1,2,0:T(4,128)S(1)} fusion(bf16[96,4,256]{2,1,0:T(4,128)(2,1)S(1)} %reshape.130.x_ref, bf16[96,10,262]{2,1,0:T(8,128)(2,1)} %copy-done.6), kind=kOutput, calls=%fused_computation.20 | convolution fusion | flops 1966080 | bytes 998400 | tf_op jit(solution)/shard_map/crj,cij->cri/dot_general | solution.py:168
  65.7 0.4 fusion.40
  66.2 0.1 copy.49
  66.4 1.7 %fusion.15 = f32[96,10,4]{1,2,0:T(4,128)S(1)} fusion(bf16[96,4,256]{2,1,0:T(4,128)(2,1)S(1)} %reshape.130.x_ref, bf16[96,10,262]{2,1,0:T(8,128)(2,1)} %copy-done.6), kind=kOutput, calls=%fused_computation.22 | convolution fusion | flops 1966080 | bytes 998400 | tf_op jit(solution)/shard_map/crj,cij->cri/dot_general | solution.py:168
  68.1 0.4 fusion.41
  68.8 1.7 %fusion.17 = f32[96,10,4]{1,2,0:T(4,128)S(1)} fusion(bf16[96,4,256]{2,1,0:T(4,128)(2,1)S(1)} %reshape.130.x_ref, bf16[96,10,262]{2,1,0:T(8,128)(2,1)} %copy-done.6), kind=kOutput, calls=%fused_computation.24 | convolution fusion | flops 1966080 | bytes 998400 | tf_op jit(solution)/shard_map/crj,cij->cri/dot_general | solution.py:168
  70.5 0.4 fusion.42
  71.2 1.7 %fusion.19 = f32[96,10,4]{1,2,0:T(4,128)S(1)} fusion(bf16[96,4,256]{2,1,0:T(4,128)(2,1)S(1)} %reshape.130.x_ref, bf16[96,10,262]{2,1,0:T(8,128)(2,1)} %copy-done.6), kind=kOutput, calls=%fused_computation.26 | convolution fusion | flops 1966080 | bytes 998400 | tf_op jit(solution)/shard_map/crj,cij->cri/dot_general | solution.py:168
  72.9 0.4 fusion.43
  73.6 1.7 %fusion.21 = f32[96,10,4]{1,2,0:T(4,128)S(1)} fusion(bf16[96,4,256]{2,1,0:T(4,128)(2,1)S(1)} %reshape.130.x_ref, bf16[96,10,262]{2,1,0:T(8,128)(2,1)} %copy-done.6), kind=kOutput, calls=%fused_computation.28 | convolution fusion | flops 1966080 | bytes 998400 | tf_op jit(solution)/shard_map/crj,cij->cri/dot_general | solution.py:168
  75.3 0.4 fusion.44
  76.1 1.4 fusion.23
  77.5 0.4 fusion.45
  78.3 0.2 copy.56
  78.5 0.2 reshape.131
  78.7 0.3 reduce_sum.97
  79.1 0.5 multiply_reduce_fusion.1
  79.6 1.4 multiply_reduce_fusion
  81.0 0.1 concatenate.155
  81.1 0.8 pad_maximum_fusion.buf_ref
  81.9 63.2 %shard_map.195 = (f32[200,128]{1,0:T(8,128)}, bf16[96,4,256]{2,1,0:T(4,128)(2,1)}, bf16[96,4,256]{2,1,0:T(4,128)(2,1)}, bf16[96,4,128]{2,1,0:T(4,128)(2,1)}, bf1...) custom-call(f32[656,128]{1,0:T(8,128)} %pad_maximum_fusion.buf_ref, ...), custom_call_target="tpu_custom_call" | custom-call | bytes 209715200 | tf_op jit(solution)/shard_map/pallas_call | solution.py:449
  145.2 0.9 slice_bitcast_fusion
  146.1 0.7 slice_bitcast_fusion.1
  147.0 0.2 reshape.135
  147.2 0.8 copy.57
  148.0 0.7 slice.992
  148.7 0.7 slice.995
  149.4 0.6 fusion.46
  150.0 0.1 slice.960
  150.1 0.1 slice.927
  150.3 0.1 slice.929
  150.4 0.1 slice.959
  151.0 1.8 %maximum_maximum_fusion.3 = (bf16[96,7,262]{2,1,0:T(8,128)(2,1)S(1)}, bf16[96,7,262]{2,1,0:T(8,128)(2,1)S(1)}) fusion(bf16[96,3,3]{2,1,0:T(4,128)(2,1)S(1)} %bitcast.203, bf16[96,3,256]{2,1,0:T(4,128)(2,1)S(1)} %bitcast.194, bf16[96,3,3]{2,1,0:T(4,128)(2,1)S(1)} %slice.929, bf16[96,4,3]{2,1,0:T(4,128)(2,1)S(1)} %bitcast.189, ...), kind=kLoop, calls=%fused_computation.34 | loop fusion | flops 4225536 | bytes 1207296 | tf_op jit(solution)/shard_map/concatenate | solution.py:112
  153.2 14.4 %add_convert_fusion = bf16[96,4,256]{2,1,0:T(4,128)(2,1)} fusion(bf16[96,4,256]{2,1,0:T(4,128)(2,1)S(1)} %copy-done.3, bf16[96,4,3]{2,1,0:T(4,128)(2,1)S(1)} %slice.927, bf16[96,4,3]{2,1,0:T(4,128)(2,1)S(1)} %bitcast.190, bf16[96,7,262]{2,1,0:T(8,128)(2,1)S(1)} %get-tuple-element.75, bf16[96,7,262]{2,1,0:T(8,128)(2,1)S(1)} %get-tuple-element.74, ...), kind=kLoop, calls=%fused_computation.39 | loop fusion | flops 16416768 | bytes 8870784 | tf_op jit(solution)/shard_map/convert_element_type | solution.py:292
  167.6 0.8 reshape.125
  (271 shorter events, 3.3 us)
Async XLA Ops:
  0.6 49.2 %copy-start = (bf16[384,96]{0,1:T(8,128)(2,1)S(1)}, bf16[384,96]{0,1:T(8,128)(2,1)}, u32[]{:S(2)}) copy-start(bf16[384,96]{0,1:T(8,128)(2,1)} %param.17) | copy-start | bytes 221188
  0.7 31.4 %copy-start.1 = (bf16[96,4,256]{2,1,0:T(4,128)(2,1)S(1)}, bf16[96,4,256]{2,1,0:T(4,128)(2,1)}, u32[]{:S(2)}) copy-start(bf16[96,4,256]{2,1,0:T(4,128)(2,1)} %x_ref.1) | copy-start | bytes 589828
  26.9 5.2 %copy-start.7 = (bf16[96,4,128]{2,1,0:T(4,128)(2,1)S(1)}, bf16[96,4,128]{2,1,0:T(4,128)(2,1)}, u32[]{:S(2)}) copy-start(bf16[96,4,128]{2,1,0:T(4,128)(2,1)} %get-tuple-element.32) | copy-start | bytes 294916
  26.9 5.2 %copy-start.15 = (bf16[96,4,256]{2,1,0:T(4,128)(2,1)S(1)}, bf16[96,4,256]{2,1,0:T(4,128)(2,1)}, u32[]{:S(2)}) copy-start(bf16[96,4,256]{2,1,0:T(4,128)(2,1)} %get-tuple-element.34) | copy-start | bytes 589828
  26.9 5.2 %copy-start.18 = (bf16[96,4,128]{2,1,0:T(4,128)(2,1)S(1)}, bf16[96,4,128]{2,1,0:T(4,128)(2,1)}, u32[]{:S(2)}) copy-start(bf16[96,4,128]{2,1,0:T(4,128)(2,1)} %get-tuple-element.35) | copy-start | bytes 294916
  30.0 3.9 %copy-start.9 = (bf16[96,3,3]{2,1,0:T(4,128)(2,1)}, bf16[96,3,3]{2,1,0:T(4,128)(2,1)S(1)}, u32[]{:S(2)}) copy-start(bf16[96,3,3]{2,1,0:T(4,128)(2,1)S(1)} %slice.788) | copy-start | bytes 5188
  31.0 2.9 %copy-start.11 = (bf16[96,3,3]{2,1,0:T(4,128)(2,1)}, bf16[96,3,3]{2,1,0:T(4,128)(2,1)S(1)}, u32[]{:S(2)}) copy-start(bf16[96,3,3]{2,1,0:T(4,128)(2,1)S(1)} %slice.790) | copy-start | bytes 5188
  32.2 2.8 %copy-start.110 = (f32[96]{0:T(128)S(1)}, f32[96]{0:T(128)}, u32[]{:S(2)}) copy-start(f32[96]{0:T(128)} %param.14) | copy-start | bytes 1156
  34.0 14.8 %copy-start.31 = (f32[96]{0:T(128)}, f32[96]{0:T(128)S(1)}, u32[]{:S(2)}) copy-start(f32[96]{0:T(128)S(1)} %get-tuple-element.122) | copy-start | bytes 1156
  34.0 14.8 %copy-start.33 = (f32[96]{0:T(128)}, f32[96]{0:T(128)S(1)}, u32[]{:S(2)}) copy-start(f32[96]{0:T(128)S(1)} %get-tuple-element.123) | copy-start | bytes 1156
  34.0 14.8 %copy-start.35 = (f32[96]{0:T(128)}, f32[96]{0:T(128)S(1)}, u32[]{:S(2)}) copy-start(f32[96]{0:T(128)S(1)} %get-tuple-element.124) | copy-start | bytes 1156
  34.0 14.8 %copy-start.37 = (f32[96]{0:T(128)}, f32[96]{0:T(128)S(1)}, u32[]{:S(2)}) copy-start(f32[96]{0:T(128)S(1)} %get-tuple-element.125) | copy-start | bytes 1156
  34.0 14.8 %copy-start.39 = (f32[96]{0:T(128)}, f32[96]{0:T(128)S(1)}, u32[]{:S(2)}) copy-start(f32[96]{0:T(128)S(1)} %get-tuple-element.126) | copy-start | bytes 1156
  34.0 14.8 %copy-start.41 = (f32[96]{0:T(128)}, f32[96]{0:T(128)S(1)}, u32[]{:S(2)}) copy-start(f32[96]{0:T(128)S(1)} %get-tuple-element.127) | copy-start | bytes 1156
  34.1 14.8 %copy-start.43 = (f32[96]{0:T(128)}, f32[96]{0:T(128)S(1)}, u32[]{:S(2)}) copy-start(f32[96]{0:T(128)S(1)} %get-tuple-element.128) | copy-start | bytes 1156
  34.1 14.8 %copy-start.45 = (f32[96]{0:T(128)}, f32[96]{0:T(128)S(1)}, u32[]{:S(2)}) copy-start(f32[96]{0:T(128)S(1)} %get-tuple-element.129) | copy-start | bytes 1156
  34.1 14.8 %copy-start.47 = (f32[96]{0:T(128)}, f32[96]{0:T(128)S(1)}, u32[]{:S(2)}) copy-start(f32[96]{0:T(128)S(1)} %get-tuple-element.130) | copy-start | bytes 1156
  34.1 14.8 %copy-start.49 = (f32[96]{0:T(128)}, f32[96]{0:T(128)S(1)}, u32[]{:S(2)}) copy-start(f32[96]{0:T(128)S(1)} %get-tuple-element.131) | copy-start | bytes 1156
  34.1 14.8 %copy-start.51 = (f32[96]{0:T(128)}, f32[96]{0:T(128)S(1)}, u32[]{:S(2)}) copy-start(f32[96]{0:T(128)S(1)} %get-tuple-element.132) | copy-start | bytes 1156
  34.1 14.8 %copy-start.53 = (f32[96]{0:T(128)}, f32[96]{0:T(128)S(1)}, u32[]{:S(2)}) copy-start(f32[96]{0:T(128)S(1)} %get-tuple-element.133) | copy-start | bytes 1156
  34.1 14.8 %copy-start.55 = (f32[96]{0:T(128)}, f32[96]{0:T(128)S(1)}, u32[]{:S(2)}) copy-start(f32[96]{0:T(128)S(1)} %get-tuple-element.134) | copy-start | bytes 1156
  34.1 14.8 %copy-start.57 = (f32[96]{0:T(128)}, f32[96]{0:T(128)S(1)}, u32[]{:S(2)}) copy-start(f32[96]{0:T(128)S(1)} %get-tuple-element.135) | copy-start | bytes 1156
  34.2 14.8 %copy-start.59 = (f32[96]{0:T(128)}, f32[96]{0:T(128)S(1)}, u32[]{:S(2)}) copy-start(f32[96]{0:T(128)S(1)} %get-tuple-element.136) | copy-start | bytes 1156
  34.2 14.8 %copy-start.61 = (f32[96]{0:T(128)}, f32[96]{0:T(128)S(1)}, u32[]{:S(2)}) copy-start(f32[96]{0:T(128)S(1)} %get-tuple-element.137) | copy-start | bytes 1156
  34.2 14.8 %copy-start.63 = (f32[96]{0:T(128)}, f32[96]{0:T(128)S(1)}, u32[]{:S(2)}) copy-start(f32[96]{0:T(128)S(1)} %get-tuple-element.138) | copy-start | bytes 1156
  34.2 14.8 %copy-start.65 = (f32[96]{0:T(128)}, f32[96]{0:T(128)S(1)}, u32[]{:S(2)}) copy-start(f32[96]{0:T(128)S(1)} %get-tuple-element.139) | copy-start | bytes 1156
  34.2 14.8 %copy-start.67 = (f32[96]{0:T(128)}, f32[96]{0:T(128)S(1)}, u32[]{:S(2)}) copy-start(f32[96]{0:T(128)S(1)} %get-tuple-element.140) | copy-start | bytes 1156
  34.2 14.8 %copy-start.69 = (f32[96]{0:T(128)}, f32[96]{0:T(128)S(1)}, u32[]{:S(2)}) copy-start(f32[96]{0:T(128)S(1)} %get-tuple-element.141) | copy-start | bytes 1156
  34.2 14.8 %copy-start.71 = (f32[96]{0:T(128)}, f32[96]{0:T(128)S(1)}, u32[]{:S(2)}) copy-start(f32[96]{0:T(128)S(1)} %get-tuple-element.142) | copy-start | bytes 1156
  34.2 14.8 %copy-start.73 = (f32[96]{0:T(128)}, f32[96]{0:T(128)S(1)}, u32[]{:S(2)}) copy-start(f32[96]{0:T(128)S(1)} %get-tuple-element.143) | copy-start | bytes 1156
  34.2 14.8 %copy-start.75 = (f32[96]{0:T(128)}, f32[96]{0:T(128)S(1)}, u32[]{:S(2)}) copy-start(f32[96]{0:T(128)S(1)} %get-tuple-element.144) | copy-start | bytes 1156
  34.2 14.8 %copy-start.77 = (f32[96]{0:T(128)}, f32[96]{0:T(128)S(1)}, u32[]{:S(2)}) copy-start(f32[96]{0:T(128)S(1)} %get-tuple-element.145) | copy-start | bytes 1156
  34.3 14.8 %copy-start.79 = (f32[96]{0:T(128)}, f32[96]{0:T(128)S(1)}, u32[]{:S(2)}) copy-start(f32[96]{0:T(128)S(1)} %get-tuple-element.146) | copy-start | bytes 1156
  34.3 14.8 %copy-start.81 = (f32[96]{0:T(128)}, f32[96]{0:T(128)S(1)}, u32[]{:S(2)}) copy-start(f32[96]{0:T(128)S(1)} %get-tuple-element.147) | copy-start | bytes 1156
  34.3 14.8 %copy-start.83 = (f32[96]{0:T(128)}, f32[96]{0:T(128)S(1)}, u32[]{:S(2)}) copy-start(f32[96]{0:T(128)S(1)} %get-tuple-element.148) | copy-start | bytes 1156
  34.3 14.8 %copy-start.85 = (f32[96]{0:T(128)}, f32[96]{0:T(128)S(1)}, u32[]{:S(2)}) copy-start(f32[96]{0:T(128)S(1)} %get-tuple-element.149) | copy-start | bytes 1156
  34.3 14.8 %copy-start.87 = (f32[96]{0:T(128)}, f32[96]{0:T(128)S(1)}, u32[]{:S(2)}) copy-start(f32[96]{0:T(128)S(1)} %get-tuple-element.150) | copy-start | bytes 1156
  34.3 14.8 %copy-start.89 = (f32[96]{0:T(128)}, f32[96]{0:T(128)S(1)}, u32[]{:S(2)}) copy-start(f32[96]{0:T(128)S(1)} %get-tuple-element.151) | copy-start | bytes 1156
  34.3 14.8 %copy-start.91 = (f32[96]{0:T(128)}, f32[96]{0:T(128)S(1)}, u32[]{:S(2)}) copy-start(f32[96]{0:T(128)S(1)} %get-tuple-element.152) | copy-start | bytes 1156
  34.3 14.8 %copy-start.93 = (f32[96]{0:T(128)}, f32[96]{0:T(128)S(1)}, u32[]{:S(2)}) copy-start(f32[96]{0:T(128)S(1)} %get-tuple-element.153) | copy-start | bytes 1156
  34.9 14.2 %copy-start.95 = (f32[96]{0:T(128)}, f32[96]{0:T(128)S(1)}, u32[]{:S(2)}) copy-start(f32[96]{0:T(128)S(1)} %get-tuple-element.154) | copy-start | bytes 1156
  34.9 14.2 %copy-start.97 = (f32[96]{0:T(128)}, f32[96]{0:T(128)S(1)}, u32[]{:S(2)}) copy-start(f32[96]{0:T(128)S(1)} %get-tuple-element.155) | copy-start | bytes 1156
  34.9 14.2 %copy-start.99 = (f32[96]{0:T(128)}, f32[96]{0:T(128)S(1)}, u32[]{:S(2)}) copy-start(f32[96]{0:T(128)S(1)} %get-tuple-element.156) | copy-start | bytes 1156
  34.9 14.2 %copy-start.101 = (f32[96]{0:T(128)}, f32[96]{0:T(128)S(1)}, u32[]{:S(2)}) copy-start(f32[96]{0:T(128)S(1)} %get-tuple-element.157) | copy-start | bytes 1156
  34.9 14.2 %copy-start.103 = (f32[96]{0:T(128)}, f32[96]{0:T(128)S(1)}, u32[]{:S(2)}) copy-start(f32[96]{0:T(128)S(1)} %get-tuple-element.158) | copy-start | bytes 1156
  35.0 14.2 %copy-start.104 = (f32[96]{0:T(128)}, f32[96]{0:T(128)S(1)}, u32[]{:S(2)}) copy-start(f32[96]{0:T(128)S(1)} %get-tuple-element.159) | copy-start | bytes 1156
  35.0 14.2 %copy-start.105 = (f32[96]{0:T(128)}, f32[96]{0:T(128)S(1)}, u32[]{:S(2)}) copy-start(f32[96]{0:T(128)S(1)} %get-tuple-element.160) | copy-start | bytes 1156
  58.5 17.5 %copy-start.2 = (bf16[96,4,256]{2,1,0:T(4,128)(2,1)}, bf16[96,4,256]{2,1,0:T(4,128)(2,1)S(1)}, u32[]{:S(2)}) copy-start(bf16[96,4,256]{2,1,0:T(4,128)(2,1)S(1)} %reshape.130.x_ref) | copy-start | bytes 589828
  145.1 4.9 %copy-start.20 = (bf16[96,4,256]{2,1,0:T(4,128)(2,1)S(1)}, bf16[96,4,256]{2,1,0:T(4,128)(2,1)}, u32[]{:S(2)}) copy-start(bf16[96,4,256]{2,1,0:T(4,128)(2,1)} %get-tuple-element.42) | copy-start | bytes 589828
  145.1 5.0 %copy-start.25 = (bf16[96,4,128]{2,1,0:T(4,128)(2,1)S(1)}, bf16[96,4,128]{2,1,0:T(4,128)(2,1)}, u32[]{:S(2)}) copy-start(bf16[96,4,128]{2,1,0:T(4,128)(2,1)} %get-tuple-element.36) | copy-start | bytes 294916
  145.1 5.1 %copy-start.24 = (bf16[96,4,128]{2,1,0:T(4,128)(2,1)S(1)}, bf16[96,4,128]{2,1,0:T(4,128)(2,1)}, u32[]{:S(2)}) copy-start(bf16[96,4,128]{2,1,0:T(4,128)(2,1)} %get-tuple-element.38) | copy-start | bytes 294916
  145.2 5.3 %copy-start.23 = (bf16[96,4,128]{2,1,0:T(4,128)(2,1)S(1)}, bf16[96,4,128]{2,1,0:T(4,128)(2,1)}, u32[]{:S(2)}) copy-start(bf16[96,4,128]{2,1,0:T(4,128)(2,1)} %get-tuple-element.41) | copy-start | bytes 294916
  146.9 3.7 %copy-start.22 = (bf16[96,4,128]{2,1,0:T(4,128)(2,1)S(1)}, bf16[96,4,128]{2,1,0:T(4,128)(2,1)}, u32[]{:S(2)}) copy-start(bf16[96,4,128]{2,1,0:T(4,128)(2,1)} %get-tuple-element.43) | copy-start | bytes 294916
  147.0 3.6 %copy-start.3 = (bf16[96,4,256]{2,1,0:T(4,128)(2,1)S(1)}, bf16[96,4,256]{2,1,0:T(4,128)(2,1)}, u32[]{:S(2)}) copy-start(bf16[96,4,256]{2,1,0:T(4,128)(2,1)} %copy-done.2) | copy-start | bytes 589828
  147.0 3.6 %copy-start.17 = (bf16[96,4,128]{2,1,0:T(4,128)(2,1)S(1)}, bf16[96,4,128]{2,1,0:T(4,128)(2,1)}, u32[]{:S(2)}) copy-start(bf16[96,4,128]{2,1,0:T(4,128)(2,1)} %get-tuple-element.37) | copy-start | bytes 294916
  147.0 3.6 %copy-start.19 = (bf16[96,4,256]{2,1,0:T(4,128)(2,1)S(1)}, bf16[96,4,256]{2,1,0:T(4,128)(2,1)}, u32[]{:S(2)}) copy-start(bf16[96,4,256]{2,1,0:T(4,128)(2,1)} %get-tuple-element.39) | copy-start | bytes 589828
  147.0 3.6 %copy-start.21 = (bf16[96,4,128]{2,1,0:T(4,128)(2,1)S(1)}, bf16[96,4,128]{2,1,0:T(4,128)(2,1)}, u32[]{:S(2)}) copy-start(bf16[96,4,128]{2,1,0:T(4,128)(2,1)} %get-tuple-element.40) | copy-start | bytes 294916
  150.7 2.2 %copy-start.32 = (f32[96]{0:T(128)S(1)}, f32[96]{0:T(128)}, u32[]{:S(2)}) copy-start(f32[96]{0:T(128)} %copy-done.31) | copy-start | bytes 1156
  150.7 2.2 %copy-start.34 = (f32[96]{0:T(128)S(1)}, f32[96]{0:T(128)}, u32[]{:S(2)}) copy-start(f32[96]{0:T(128)} %copy-done.33) | copy-start | bytes 1156
  150.7 2.2 %copy-start.36 = (f32[96]{0:T(128)S(1)}, f32[96]{0:T(128)}, u32[]{:S(2)}) copy-start(f32[96]{0:T(128)} %copy-done.35) | copy-start | bytes 1156
  150.7 2.2 %copy-start.38 = (f32[96]{0:T(128)S(1)}, f32[96]{0:T(128)}, u32[]{:S(2)}) copy-start(f32[96]{0:T(128)} %copy-done.37) | copy-start | bytes 1156
  150.7 2.2 %copy-start.40 = (f32[96]{0:T(128)S(1)}, f32[96]{0:T(128)}, u32[]{:S(2)}) copy-start(f32[96]{0:T(128)} %copy-done.39) | copy-start | bytes 1156
  150.7 2.2 %copy-start.42 = (f32[96]{0:T(128)S(1)}, f32[96]{0:T(128)}, u32[]{:S(2)}) copy-start(f32[96]{0:T(128)} %copy-done.41) | copy-start | bytes 1156
  150.7 2.2 %copy-start.44 = (f32[96]{0:T(128)S(1)}, f32[96]{0:T(128)}, u32[]{:S(2)}) copy-start(f32[96]{0:T(128)} %copy-done.43) | copy-start | bytes 1156
  (48 other events, 86.5 us)

commit v8 on v7

--- a/solution.py
+++ b/solution.py
@@ -137,28 +137,50 @@
     return _assemble(x, got, width)
 
 
+def dw_kernel(flip, cb, x_ref, k_ref, o_ref):
+    rows, channels, cols = o_ref.shape
+    wide = x_ref.shape[2]
+
+    def block(i, carry):
+        ch = pl.ds(pl.multiple_of(i * cb, cb), cb)
+        x = x_ref[:, ch, :]
+        acc = jnp.zeros((rows, cb, cols), jnp.float32)
+        for shift_col in range(7):
+            c0 = 6 - shift_col if flip else shift_col
+            xb = pltpu.roll(x, shift=wide - c0, axis=2) if c0 else x
+            xb = xb[:, :, :cols]
+            for shift_row in range(7):
+                r0 = 6 - shift_row if flip else shift_row
+                kv = k_ref[shift_row * 7 + shift_col, ch, :]
+                acc = acc + kv[None] * xb[r0 : r0 + rows]
+        o_ref[:, ch, :] = acc
+        return carry
+
+    lax.fori_loop(0, channels // cb, block, 0)
+
+
+def _dw(padded, kernel, row_count, col_count, flip):
+    channels = padded.shape[0]
+    wide = -(-padded.shape[2] // LANES) * LANES
+    x = jnp.transpose(padded, (1, 0, 2)).astype(jnp.float32)
+    x = jnp.pad(x, ((0, 0), (0, 0), (0, wide - padded.shape[2])))
+    taps = jnp.transpose(kernel.reshape(channels, 49), (1, 0))[:, :, None]
+    cb = 8
+    out = pl.pallas_call(
+        functools.partial(dw_kernel, flip, cb),
+        out_shape=jax.ShapeDtypeStruct((row_count, channels, col_count), jnp.float32),
+        in_specs=[pl.BlockSpec(memory_space=pltpu.VMEM)] * 2,
+        out_specs=pl.BlockSpec(memory_space=pltpu.VMEM),
+    )(x, taps)
+    return jnp.transpose(out, (1, 0, 2))
+
+
 def depthwise(padded, kernel, row_count, col_count):
-    total = jnp.zeros((padded.shape[0], row_count, col_count), jnp.float32)
-    for shift_row in range(7):
-        for shift_col in range(7):
-            piece = padded[
-                :, shift_row : shift_row + row_count, shift_col : shift_col + col_count
-            ].astype(jnp.float32)
-            total = total + kernel[:, shift_row, shift_col][:, None, None] * piece
-    return total
+    return _dw(padded, kernel, row_count, col_count, False)
 
 
 def conv_back(padded, kernel, row_count, col_count):
-    total = jnp.zeros((padded.shape[0], row_count, col_count), jnp.float32)
-    for shift_row in range(7):
-        for shift_col in range(7):
-            piece = padded[
-                :,
-                6 - shift_row : 6 - shift_row + row_count,
-                6 - shift_col : 6 - shift_col + col_count,
-            ].astype(jnp.float32)
-            total = total + kernel[:, shift_row, shift_col][:, None, None] * piece
-    return total
+    return _dw(padded, kernel, row_count, col_count, True)
 
 
 def kernel_terms(padded, convolution_gradient, row_count, col_count):

time: 171 us -> 153 us (0.89)
  other arithmetic: 39.8 us -> 12.5 us
  Pallas kernels: 89.4 us -> 103 us
  matrix products: 14.2 us -> 7.41 us
  local copies, waits for them, and re-layouts: 22.4 us -> 26.8 us
    pallas_call x0 -> x2, Pallas kernels: none -> 13.5 us  [_dw(): pl.pallas_call(functools.partial(dw_kernel, flip, cb), out_shape=jax.Shap...]
    convert_element_type x1, other arithmetic: 14.4 us -> 1.04 us  [shards(): image_grad = (cotangent.astype(jnp.float32) + back).astype(jnp.bfloat16)]
    reduce_sum x1, other arithmetic: 13.8 us -> 1.13 us  [shards(): average = jnp.mean(flat, axis=0, keepdims=True)]
    pallas_call x0 -> x16, local copies, waits for them, and re-layouts: none -> 6.65 us  [the longest x8 4.66 us: padded_2(): pl.pallas_call(functools.partial(halo_kernel, ns, nf, x.shape[2]), out_sh...]
    concatenate x3 -> x1, other arithmetic: 6.89 us -> 0.45 us  [_assemble(): jnp.concatenate([jnp.concatenate([top_left, above, top_right], axis=2), j...]
    dot_general x7, matrix products: 10.3 us -> 3.99 us  [kernel_terms(): jnp.einsum('crj,cij->cri', padded[:, :, shift_col:shift_col + col_count],...]
    pad x0 -> x2, other arithmetic: none -> 2.45 us  [_dw(): x = jnp.pad(x, ((0, 0), (0, 0), (0, wide - padded.shape[2])))]
    broadcast_in_dim x0 -> x1, local copies, waits for them, and re-layouts: none -> 2.2 us  [_dw(): taps = jnp.transpose(kernel.reshape(channels, 49), (1, 0))[:, :, None]]
where the time goes in v8:
time: 153 us; the launch traced here: 151 us
  Pallas kernels  103 us (67%)
  local copies, waits for them, and re-layouts  26.8 us (18%)
  other arithmetic  12.5 us (8%)
  matrix products  7.41 us (5%)
    pallas_call x1, Pallas kernels, grad_reduce(): pl.pallas_call(functools.partial(reduce_kernel, nfilt, nspace, pr, sr, x....  63.2 us
    pallas_call x1, Pallas kernels, padded_2(): pl.pallas_call(functools.partial(halo_kernel, ns, nf, x.shape[2]), out_sh...  26.1 us
    pallas_call x2, Pallas kernels, _dw(): pl.pallas_call(functools.partial(dw_kernel, flip, cb), out_shape=jax.Shap...  13.5 us
    pallas_call x8, local copies, waits for them, and re-layouts, padded_2(): pl.pallas_call(functools.partial(halo_kernel, ns, nf, x.shape[2]), out_sh...  4.66 us
    slice x28, local copies, waits for them, and re-layouts, kernel_terms(): total = total + corr[:, row:row + ksize, row]  4.22 us
    dot_general x7, matrix products, kernel_terms(): jnp.einsum('crj,cij->cri', padded[:, :, shift_col:shift_col + col_count],...  3.99 us
    unnamed x44, local copies, waits for them, and re-layouts  3.77 us

profile of v8, /device:TPU:56, one launch (start us, length us, event | category | flops | bytes accessed | tf_op | source)
XLA Modules:
  0.0 150.8 jit_solution(17430328062435586918)
XLA Ops:
  0.7 1.2 fusion.25
  1.8 0.7 convert_element_type.66
  2.5 0.8 reshape.128
  3.3 0.9 copy.96
  4.2 1.0 copy.159
  5.2 1.0 convert_bitcast_fusion
  6.2 26.1 %shard_map.194 = (bf16[96,4,256]{2,1,0:T(4,128)(2,1)}, bf16[96,4,256]{2,1,0:T(4,128)(2,1)}, bf16[96,4,128]{2,1,0:T(4,128)(2,1)}, bf16[96,4,128]{2,1,0:T(4,128)(2...) custom-call(bf16[96,4,256]{2,1,0:T(4,128)(2,1)} %x_ref.1), custom_call_target="tpu_custom_call" | custom-call | tf_op jit(solution)/shard_map/pallas_call | solution.py:126
  32.3 1.0 copy.91
  33.4 0.9 copy.93
  34.3 0.9 copy.94
  35.3 0.9 copy.95
  36.2 0.9 copy.97
  37.4 0.5 fusion.59
  37.8 0.5 maximum_maximum_fusion
  38.3 1.2 pad_convert_fusion.1.x_ref
  39.5 2.2 %copy.100.k_ref = f32[49,96,1]{2,1,0:T(8,128)} copy(f32[49,96,1]{1,0,2:T(8,128)S(1)} %bitcast.109) | data formatting | bytes 37632 | tf_op jit(solution)/shard_map/broadcast_in_dim | solution.py:167
  41.7 6.7 %shard_map.195 = f32[4,96,256]{2,1,0:T(8,128)} custom-call(f32[10,96,384]{2,1,0:T(8,128)} %pad_convert_fusion.1.x_ref, f32[49,96,1]{2,1,0:T(8,128)} %copy.100.k_ref), custom_call_target="tpu_custom_call" | custom-call | tf_op jit(solution)/shard_map/pallas_call | solution.py:169
  48.4 1.1 bitcast_reduce_fusion
  49.6 1.1 fusion.29
  50.7 1.1 add_bitcast_fusion
  51.9 0.6 fusion.9
  52.6 0.2 copy-done.13
  52.7 0.5 multiply_reduce_fusion
  53.2 0.9 convert_reduce_fusion
  54.2 0.4 fusion.32
  54.6 0.2 reshape.131
  54.9 0.8 reshape.130
  55.7 0.4 fusion.33
  56.1 0.5 fusion.27
  56.6 0.2 reshape.132
  56.9 0.2 convert_reduce_fusion.1
  57.6 2.0 %fusion.34 = (bf16[96,10,256]{2,0,1:T(8,128)(2,1)S(1)}, bf16[96,10,256]{2,0,1:T(8,128)(2,1)}, bf16[96,10,256]{2,0,1:T(8,128)(2,1)}, bf16[96,10,256]{2,0,1:T(8,12...) fusion(bf16[96,10,262]{2,0,1:T(8,128)(2,1)S(1)} %maximum_maximu, ...), kind=kLoop, calls=%fused_computation.80 | loop fusion | bytes 6881280 | tf_op jit(solution)/shard_map/slice | solution.py:192
  59.5 0.4 fusion.11
  59.9 0.4 fusion.35
  60.7 1.5 fusion.13
  62.1 0.4 fusion.36
  62.8 0.4 fusion.15
  63.3 0.4 fusion.37
  64.0 0.4 fusion.17
  64.4 0.4 fusion.38
  65.1 0.4 fusion.19
  65.6 0.4 fusion.39
  66.3 0.4 fusion.21
  66.7 0.4 fusion.40
  67.4 0.4 fusion.23
  67.8 0.4 fusion.41
  68.6 0.2 copy.141
  68.8 0.2 reshape.136
  69.1 0.8 pad_maximum_fusion.buf_ref
  69.9 63.2 %shard_map.196 = (f32[200,128]{1,0:T(8,128)}, bf16[96,4,256]{2,1,0:T(4,128)(2,1)}, bf16[96,4,256]{2,1,0:T(4,128)(2,1)}, bf16[96,4,128]{2,1,0:T(4,128)(2,1)}, bf1...) custom-call(f32[656,128]{1,0:T(8,128)} %pad_maximum_fusion.buf_ref, ...), custom_call_target="tpu_custom_call" | custom-call | bytes 209715200 | tf_op jit(solution)/shard_map/pallas_call | solution.py:471
  133.2 1.0 copy.142
  134.2 0.7 slice_bitcast_fusion.1
  135.0 0.9 slice_bitcast_fusion
  135.9 0.6 fusion.42
  136.6 0.7 slice.270
  137.3 0.7 slice.267
  138.0 0.9 copy.144
  139.4 0.5 maximum_bitcast_fusion
  139.9 0.2 reshape.140
  140.1 0.8 copy.153
  140.9 1.2 pad_convert_fusion.x_ref
  142.1 6.8 %shard_map.197 = f32[4,96,256]{2,1,0:T(8,128)} custom-call(f32[10,96,384]{2,1,0:T(8,128)} %pad_convert_fusion.x_ref, f32[49,96,1]{2,1,0:T(8,128)} %copy.100.k_ref), custom_call_target="tpu_custom_call" | custom-call | tf_op jit(solution)/shard_map/pallas_call | solution.py:169
  148.9 1.0 fusion.26
  149.9 0.8 copy.152
  (114 shorter events, 4.1 us)
Async XLA Ops:
  0.6 51.3 %copy-start = (bf16[384,96]{0,1:T(8,128)(2,1)S(1)}, bf16[384,96]{0,1:T(8,128)(2,1)}, u32[]{:S(2)}) copy-start(bf16[384,96]{0,1:T(8,128)(2,1)} %param.17) | copy-start | bytes 221188
  32.3 4.9 %copy-start.12 = (bf16[96,4,128]{2,1,0:T(4,128)(2,1)S(1)}, bf16[96,4,128]{2,1,0:T(4,128)(2,1)}, u32[]{:S(2)}) copy-start(bf16[96,4,128]{2,1,0:T(4,128)(2,1)} %get-tuple-element.35) | copy-start | bytes 294916
  32.3 5.0 %copy-start.7 = (bf16[96,4,256]{2,1,0:T(4,128)(2,1)S(1)}, bf16[96,4,256]{2,1,0:T(4,128)(2,1)}, u32[]{:S(2)}) copy-start(bf16[96,4,256]{2,1,0:T(4,128)(2,1)} %get-tuple-element.29) | copy-start | bytes 589828
  32.3 5.0 %copy-start.6 = (bf16[96,4,256]{2,1,0:T(4,128)(2,1)S(1)}, bf16[96,4,256]{2,1,0:T(4,128)(2,1)}, u32[]{:S(2)}) copy-start(bf16[96,4,256]{2,1,0:T(4,128)(2,1)} %get-tuple-element.34) | copy-start | bytes 589828
  41.7 6.7 %copy-start.15 = (f32[96]{0:T(128)S(1)}, f32[96]{0:T(128)}, u32[]{:S(2)}) copy-start(f32[96]{0:T(128)} %param.14) | copy-start | bytes 1156
  48.4 3.5 %copy-start.14 = (f32[96]{0:T(128)S(1)}, f32[96]{0:T(128)}, u32[]{:S(2)}) copy-start(f32[96]{0:T(128)} %param.15) | copy-start | bytes 1156
  48.4 3.5 %copy-start.17 = (f32[96]{0:T(128)S(1)}, f32[96]{0:T(128)}, u32[]{:S(2)}) copy-start(f32[96]{0:T(128)} %param.16) | copy-start | bytes 1156
  51.8 0.9 copy-start.13
  51.9 0.9 copy-start.16
  51.9 0.9 copy-start.18
  57.5 9.9 %copy-start.2 = (bf16[96,4,256]{2,1,0:T(4,128)(2,1)}, bf16[96,4,256]{2,1,0:T(4,128)(2,1)S(1)}, u32[]{:S(2)}) copy-start(bf16[96,4,256]{2,1,0:T(4,128)(2,1)S(1)} %reshape.135.x_ref) | copy-start | bytes 589828
  59.9 2.9 %copy-start.3 = (bf16[96,10,256]{2,0,1:T(8,128)(2,1)S(1)}, bf16[96,10,256]{2,0,1:T(8,128)(2,1)}, u32[]{:S(2)}) copy-start(bf16[96,10,256]{2,0,1:T(8,128)(2,1)} %get-tuple-element.85) | copy-start | bytes 1474564
  133.1 5.8 %copy-start.11 = (bf16[96,4,128]{2,1,0:T(4,128)(2,1)S(1)}, bf16[96,4,128]{2,1,0:T(4,128)(2,1)}, u32[]{:S(2)}) copy-start(bf16[96,4,128]{2,1,0:T(4,128)(2,1)} %get-tuple-element.39) | copy-start | bytes 294916
  133.1 6.0 %copy-start.10 = (bf16[96,4,128]{2,1,0:T(4,128)(2,1)S(1)}, bf16[96,4,128]{2,1,0:T(4,128)(2,1)}, u32[]{:S(2)}) copy-start(bf16[96,4,128]{2,1,0:T(4,128)(2,1)} %get-tuple-element.40) | copy-start | bytes 294916
  133.1 6.0 %copy-start.9 = (bf16[96,4,128]{2,1,0:T(4,128)(2,1)S(1)}, bf16[96,4,128]{2,1,0:T(4,128)(2,1)}, u32[]{:S(2)}) copy-start(bf16[96,4,128]{2,1,0:T(4,128)(2,1)} %get-tuple-element.41) | copy-start | bytes 294916
  133.1 6.1 %copy-start.8 = (bf16[96,4,128]{2,1,0:T(4,128)(2,1)S(1)}, bf16[96,4,128]{2,1,0:T(4,128)(2,1)}, u32[]{:S(2)}) copy-start(bf16[96,4,128]{2,1,0:T(4,128)(2,1)} %get-tuple-element.43) | copy-start | bytes 294916
  133.1 6.2 %copy-start.5 = (bf16[96,4,256]{2,1,0:T(4,128)(2,1)S(1)}, bf16[96,4,256]{2,1,0:T(4,128)(2,1)}, u32[]{:S(2)}) copy-start(bf16[96,4,256]{2,1,0:T(4,128)(2,1)} %get-tuple-element.37) | copy-start | bytes 589828
  135.9 3.5 %copy-start.4 = (bf16[96,4,256]{2,1,0:T(4,128)(2,1)S(1)}, bf16[96,4,256]{2,1,0:T(4,128)(2,1)}, u32[]{:S(2)}) copy-start(bf16[96,4,256]{2,1,0:T(4,128)(2,1)} %get-tuple-element.42) | copy-start | bytes 589828
  142.1 6.8 %copy-start.1 = (bf16[96,4,256]{2,1,0:T(4,128)(2,1)S(1)}, bf16[96,4,256]{2,1,0:T(4,128)(2,1)}, u32[]{:S(2)}) copy-start(bf16[96,4,256]{2,1,0:T(4,128)(2,1)} %param.12) | copy-start | bytes 589828

commit v9 on v8

--- a/solution.py
+++ b/solution.py
@@ -151,7 +151,7 @@
             xb = xb[:, :, :cols]
             for shift_row in range(7):
                 r0 = 6 - shift_row if flip else shift_row
-                kv = k_ref[shift_row * 7 + shift_col, ch, :]
+                kv = k_ref[ch, pl.ds(shift_row * 7 + shift_col, 1)]
                 acc = acc + kv[None] * xb[r0 : r0 + rows]
         o_ref[:, ch, :] = acc
         return carry
@@ -164,7 +164,7 @@
     wide = -(-padded.shape[2] // LANES) * LANES
     x = jnp.transpose(padded, (1, 0, 2)).astype(jnp.float32)
     x = jnp.pad(x, ((0, 0), (0, 0), (0, wide - padded.shape[2])))
-    taps = jnp.transpose(kernel.reshape(channels, 49), (1, 0))[:, :, None]
+    taps = kernel.reshape(channels, 49)
     cb = 8
     out = pl.pallas_call(
         functools.partial(dw_kernel, flip, cb),

time: 153 us -> 150 us (0.980)
    broadcast_in_dim x1 -> x0, local copies, waits for them, and re-layouts: 2.2 us -> none  [_dw(): taps = jnp.transpose(kernel.reshape(channels, 49), (1, 0))[:, :, None]]
    unnamed x44 -> x46, local copies, waits for them, and re-layouts: 3.77 us -> 3.77 us
where the time goes in v9:
time: 150 us; the launch traced here: 148 us
  Pallas kernels  102 us (68%)
  local copies, waits for them, and re-layouts  25.3 us (17%)
  other arithmetic  12.5 us (8%)
  matrix products  6.38 us (4%)
    pallas_call x1, Pallas kernels, grad_reduce(): pl.pallas_call(functools.partial(reduce_kernel, nfilt, nspace, pr, sr, x....  63.2 us
    pallas_call x1, Pallas kernels, padded_2(): pl.pallas_call(functools.partial(halo_kernel, ns, nf, x.shape[2]), out_sh...  26.1 us
    pallas_call x2, Pallas kernels, _dw(): pl.pallas_call(functools.partial(dw_kernel, flip, cb), out_shape=jax.Shap...  13.1 us
    pallas_call x8, local copies, waits for them, and re-layouts, padded_2(): pl.pallas_call(functools.partial(halo_kernel, ns, nf, x.shape[2]), out_sh...  4.66 us
    slice x28, local copies, waits for them, and re-layouts, kernel_terms(): total = total + corr[:, row:row + ksize, row]  4.22 us
    unnamed x46, local copies, waits for them, and re-layouts  3.77 us

profile of v9, /device:TPU:56, one launch (start us, length us, event | category | flops | bytes accessed | tf_op | source)
XLA Modules:
  0.0 147.9 jit_solution(1382661469080931641)
XLA Ops:
  0.7 1.2 fusion.25
  1.8 0.7 convert_element_type.66
  2.5 0.8 reshape.128
  3.3 0.7 copy.101.k_ref
  4.0 0.9 copy.97
  5.0 1.0 copy.160
  5.9 1.0 convert_bitcast_fusion
  6.9 26.1 %shard_map.194 = (bf16[96,4,256]{2,1,0:T(4,128)(2,1)}, bf16[96,4,256]{2,1,0:T(4,128)(2,1)}, bf16[96,4,128]{2,1,0:T(4,128)(2,1)}, bf16[96,4,128]{2,1,0:T(4,128)(2...) custom-call(bf16[96,4,256]{2,1,0:T(4,128)(2,1)} %x_ref.1), custom_call_target="tpu_custom_call" | custom-call | tf_op jit(solution)/shard_map/pallas_call | solution.py:126
  33.0 1.0 copy.92
  34.1 0.9 copy.94
  35.0 0.9 copy.95
  36.0 0.9 copy.96
  36.9 0.9 copy.98
  38.1 0.5 fusion.59
  38.6 0.5 maximum_maximum_fusion
  39.0 1.3 pad_convert_fusion.1.x_ref
  40.3 6.5 %shard_map.195 = f32[4,96,256]{2,1,0:T(8,128)} custom-call(f32[10,96,384]{2,1,0:T(8,128)} %pad_convert_fusion.1.x_ref, f32[96,49]{1,0:T(8,128)} %copy.101.k_ref), custom_call_target="tpu_custom_call" | custom-call | tf_op jit(solution)/shard_map/pallas_call | solution.py:169
  46.8 1.1 bitcast_reduce_fusion
  48.0 1.1 fusion.29
  49.1 1.1 add_bitcast_fusion
  50.3 0.6 fusion.9
  51.0 0.2 copy-done.14
  51.1 0.5 multiply_reduce_fusion
  51.6 0.9 convert_reduce_fusion
  52.6 0.4 fusion.32
  53.0 0.2 reshape.131
  53.3 0.8 reshape.130
  54.1 0.4 fusion.33
  54.5 0.5 fusion.27
  55.0 0.2 reshape.132
  55.3 0.2 convert_reduce_fusion.1
  56.0 1.9 %fusion.34 = (bf16[96,10,256]{2,0,1:T(8,128)(2,1)S(1)}, bf16[96,10,256]{2,0,1:T(8,128)(2,1)}, bf16[96,10,256]{2,0,1:T(8,128)(2,1)S(1)}, bf16[96,10,256]{2,0,1:T(...) fusion(bf16[96,10,262]{2,0,1:T(8,128)(2,1)S(1)} %maximum_maximu, ...), kind=kLoop, calls=%fused_computation.80 | loop fusion | bytes 6881280 | tf_op jit(solution)/shard_map/slice | solution.py:192
  57.9 0.4 fusion.11
  58.3 0.4 fusion.35
  59.1 0.4 fusion.13
  59.5 0.4 fusion.36
  60.2 0.4 fusion.15
  60.6 0.4 fusion.37
  61.4 0.4 fusion.17
  61.8 0.4 fusion.38
  62.5 0.4 fusion.19
  62.9 0.4 fusion.39
  63.6 0.4 fusion.21
  64.1 0.4 fusion.40
  64.8 0.4 fusion.23
  65.2 0.4 fusion.41
  66.0 0.2 copy.142
  66.2 0.2 reshape.136
  66.5 0.8 pad_maximum_fusion.buf_ref
  67.3 63.2 %shard_map.196 = (f32[200,128]{1,0:T(8,128)}, bf16[96,4,256]{2,1,0:T(4,128)(2,1)}, bf16[96,4,256]{2,1,0:T(4,128)(2,1)}, bf16[96,4,128]{2,1,0:T(4,128)(2,1)}, bf1...) custom-call(f32[656,128]{1,0:T(8,128)} %pad_maximum_fusion.buf_ref, ...), custom_call_target="tpu_custom_call" | custom-call | bytes 209715200 | tf_op jit(solution)/shard_map/pallas_call | solution.py:471
  130.5 1.0 copy.143
  131.6 0.7 slice_bitcast_fusion.1
  132.3 0.9 slice_bitcast_fusion
  133.3 0.6 fusion.42
  134.0 0.7 slice.270
  134.7 0.7 slice.267
  135.4 0.9 copy.145
  136.8 0.5 maximum_bitcast_fusion
  137.2 0.2 reshape.140
  137.4 0.8 copy.154
  138.2 1.3 pad_convert_fusion.x_ref
  139.5 6.5 %shard_map.197 = f32[4,96,256]{2,1,0:T(8,128)} custom-call(f32[10,96,384]{2,1,0:T(8,128)} %pad_convert_fusion.x_ref, f32[96,49]{1,0:T(8,128)} %copy.101.k_ref), custom_call_target="tpu_custom_call" | custom-call | tf_op jit(solution)/shard_map/pallas_call | solution.py:169
  146.0 1.0 fusion.26
  147.1 0.8 copy.153
  (116 shorter events, 4.1 us)
Async XLA Ops:
  0.6 49.7 %copy-start = (bf16[384,96]{0,1:T(8,128)(2,1)S(1)}, bf16[384,96]{0,1:T(8,128)(2,1)}, u32[]{:S(2)}) copy-start(bf16[384,96]{0,1:T(8,128)(2,1)} %param.17) | copy-start | bytes 221188
  33.0 4.9 %copy-start.13 = (bf16[96,4,128]{2,1,0:T(4,128)(2,1)S(1)}, bf16[96,4,128]{2,1,0:T(4,128)(2,1)}, u32[]{:S(2)}) copy-start(bf16[96,4,128]{2,1,0:T(4,128)(2,1)} %get-tuple-element.35) | copy-start | bytes 294916
  33.0 5.0 %copy-start.8 = (bf16[96,4,256]{2,1,0:T(4,128)(2,1)S(1)}, bf16[96,4,256]{2,1,0:T(4,128)(2,1)}, u32[]{:S(2)}) copy-start(bf16[96,4,256]{2,1,0:T(4,128)(2,1)} %get-tuple-element.29) | copy-start | bytes 589828
  33.0 5.0 %copy-start.7 = (bf16[96,4,256]{2,1,0:T(4,128)(2,1)S(1)}, bf16[96,4,256]{2,1,0:T(4,128)(2,1)}, u32[]{:S(2)}) copy-start(bf16[96,4,256]{2,1,0:T(4,128)(2,1)} %get-tuple-element.34) | copy-start | bytes 589828
  40.3 6.6 %copy-start.16 = (f32[96]{0:T(128)S(1)}, f32[96]{0:T(128)}, u32[]{:S(2)}) copy-start(f32[96]{0:T(128)} %param.14) | copy-start | bytes 1156
  46.8 3.5 %copy-start.15 = (f32[96]{0:T(128)S(1)}, f32[96]{0:T(128)}, u32[]{:S(2)}) copy-start(f32[96]{0:T(128)} %param.15) | copy-start | bytes 1156
  46.8 3.5 %copy-start.18 = (f32[96]{0:T(128)S(1)}, f32[96]{0:T(128)}, u32[]{:S(2)}) copy-start(f32[96]{0:T(128)} %param.16) | copy-start | bytes 1156
  50.2 0.9 copy-start.14
  50.3 0.9 copy-start.17
  50.3 0.9 copy-start.19
  55.9 8.9 %copy-start.2 = (bf16[96,4,256]{2,1,0:T(4,128)(2,1)}, bf16[96,4,256]{2,1,0:T(4,128)(2,1)S(1)}, u32[]{:S(2)}) copy-start(bf16[96,4,256]{2,1,0:T(4,128)(2,1)S(1)} %reshape.135.x_ref) | copy-start | bytes 589828
  57.9 1.1 copy-start.4
  59.5 1.9 %copy-start.3 = (bf16[96,10,256]{2,0,1:T(8,128)(2,1)S(1)}, bf16[96,10,256]{2,0,1:T(8,128)(2,1)}, u32[]{:S(2)}) copy-start(bf16[96,10,256]{2,0,1:T(8,128)(2,1)} %get-tuple-element.86) | copy-start | bytes 1474564
  130.5 5.8 %copy-start.12 = (bf16[96,4,128]{2,1,0:T(4,128)(2,1)S(1)}, bf16[96,4,128]{2,1,0:T(4,128)(2,1)}, u32[]{:S(2)}) copy-start(bf16[96,4,128]{2,1,0:T(4,128)(2,1)} %get-tuple-element.39) | copy-start | bytes 294916
  130.5 6.0 %copy-start.11 = (bf16[96,4,128]{2,1,0:T(4,128)(2,1)S(1)}, bf16[96,4,128]{2,1,0:T(4,128)(2,1)}, u32[]{:S(2)}) copy-start(bf16[96,4,128]{2,1,0:T(4,128)(2,1)} %get-tuple-element.40) | copy-start | bytes 294916
  130.5 6.0 %copy-start.10 = (bf16[96,4,128]{2,1,0:T(4,128)(2,1)S(1)}, bf16[96,4,128]{2,1,0:T(4,128)(2,1)}, u32[]{:S(2)}) copy-start(bf16[96,4,128]{2,1,0:T(4,128)(2,1)} %get-tuple-element.41) | copy-start | bytes 294916
  130.5 6.1 %copy-start.9 = (bf16[96,4,128]{2,1,0:T(4,128)(2,1)S(1)}, bf16[96,4,128]{2,1,0:T(4,128)(2,1)}, u32[]{:S(2)}) copy-start(bf16[96,4,128]{2,1,0:T(4,128)(2,1)} %get-tuple-element.43) | copy-start | bytes 294916
  130.5 6.2 %copy-start.6 = (bf16[96,4,256]{2,1,0:T(4,128)(2,1)S(1)}, bf16[96,4,256]{2,1,0:T(4,128)(2,1)}, u32[]{:S(2)}) copy-start(bf16[96,4,256]{2,1,0:T(4,128)(2,1)} %get-tuple-element.37) | copy-start | bytes 589828
  133.2 3.5 %copy-start.5 = (bf16[96,4,256]{2,1,0:T(4,128)(2,1)S(1)}, bf16[96,4,256]{2,1,0:T(4,128)(2,1)}, u32[]{:S(2)}) copy-start(bf16[96,4,256]{2,1,0:T(4,128)(2,1)} %get-tuple-element.42) | copy-start | bytes 589828
  139.5 6.5 %copy-start.1 = (bf16[96,4,256]{2,1,0:T(4,128)(2,1)S(1)}, bf16[96,4,256]{2,1,0:T(4,128)(2,1)}, u32[]{:S(2)}) copy-start(bf16[96,4,256]{2,1,0:T(4,128)(2,1)} %param.12) | copy-start | bytes 589828

commit v10 on v9

--- a/solution.py
+++ b/solution.py
@@ -156,7 +156,7 @@
         o_ref[:, ch, :] = acc
         return carry
 
-    lax.fori_loop(0, channels // cb, block, 0)
+    lax.fori_loop(0, channels // cb, block, 0, unroll=True)
 
 
 def _dw(padded, kernel, row_count, col_count, flip):

time: 150 us -> 150 us (level)
  no operation moved by 1% of the time
where the time goes in v10:
time: 150 us; the launch traced here: 148 us
  Pallas kernels  102 us (68%)
  local copies, waits for them, and re-layouts  25.5 us (17%)
  other arithmetic  12.5 us (8%)
  matrix products  6.37 us (4%)
    pallas_call x1, Pallas kernels, grad_reduce(): pl.pallas_call(functools.partial(reduce_kernel, nfilt, nspace, pr, sr, x....  63.2 us
    pallas_call x1, Pallas kernels, padded_2(): pl.pallas_call(functools.partial(halo_kernel, ns, nf, x.shape[2]), out_sh...  26.1 us
    pallas_call x2, Pallas kernels, _dw(): pl.pallas_call(functools.partial(dw_kernel, flip, cb), out_shape=jax.Shap...  12.9 us
    pallas_call x8, local copies, waits for them, and re-layouts, padded_2(): pl.pallas_call(functools.partial(halo_kernel, ns, nf, x.shape[2]), out_sh...  4.66 us
    slice x28, local copies, waits for them, and re-layouts, kernel_terms(): total = total + corr[:, row:row + ksize, row]  4.39 us
    unnamed x46, local copies, waits for them, and re-layouts  3.77 us

profile of v10, /device:TPU:56, one launch (start us, length us, event | category | flops | bytes accessed | tf_op | source)
XLA Modules:
  0.0 147.9 jit_solution(16037970805958909554)
XLA Ops:
  0.7 1.2 fusion.25
  1.8 0.7 convert_element_type.66
  2.5 0.8 reshape.128
  3.3 0.7 copy.101.k_ref
  4.0 0.9 copy.97
  5.0 1.0 copy.160
  5.9 1.0 convert_bitcast_fusion
  6.9 26.1 %shard_map.194 = (bf16[96,4,256]{2,1,0:T(4,128)(2,1)}, bf16[96,4,256]{2,1,0:T(4,128)(2,1)}, bf16[96,4,128]{2,1,0:T(4,128)(2,1)}, bf16[96,4,128]{2,1,0:T(4,128)(2...) custom-call(bf16[96,4,256]{2,1,0:T(4,128)(2,1)} %x_ref.1), custom_call_target="tpu_custom_call" | custom-call | tf_op jit(solution)/shard_map/pallas_call | solution.py:126
  33.0 1.0 copy.92
  34.1 0.9 copy.94
  35.0 0.9 copy.95
  36.0 0.9 copy.96
  36.9 0.9 copy.98
  38.1 0.5 fusion.59
  38.6 0.5 maximum_maximum_fusion
  39.0 1.3 pad_convert_fusion.1.x_ref
  40.3 6.5 %shard_map.195 = f32[4,96,256]{2,1,0:T(8,128)} custom-call(f32[10,96,384]{2,1,0:T(8,128)} %pad_convert_fusion.1.x_ref, f32[96,49]{1,0:T(8,128)} %copy.101.k_ref), custom_call_target="tpu_custom_call" | custom-call | tf_op jit(solution)/shard_map/pallas_call | solution.py:169
  46.7 1.1 bitcast_reduce_fusion
  47.9 1.1 fusion.29
  49.0 1.1 add_bitcast_fusion
  50.3 0.6 fusion.9
  50.9 0.2 copy-done.14
  51.1 0.5 multiply_reduce_fusion
  51.5 0.9 convert_reduce_fusion
  52.5 0.4 fusion.32
  52.9 0.2 reshape.131
  53.2 0.8 reshape.130
  54.0 0.4 fusion.33
  54.4 0.5 fusion.27
  54.9 0.2 reshape.132
  55.3 0.2 convert_reduce_fusion.1
  55.9 1.9 %fusion.34 = (bf16[96,10,256]{2,0,1:T(8,128)(2,1)S(1)}, bf16[96,10,256]{2,0,1:T(8,128)(2,1)}, bf16[96,10,256]{2,0,1:T(8,128)(2,1)S(1)}, bf16[96,10,256]{2,0,1:T(...) fusion(bf16[96,10,262]{2,0,1:T(8,128)(2,1)S(1)} %maximum_maximu, ...), kind=kLoop, calls=%fused_computation.80 | loop fusion | bytes 6881280 | tf_op jit(solution)/shard_map/slice | solution.py:192
  57.8 0.4 fusion.11
  58.2 0.4 fusion.35
  59.0 0.4 fusion.13
  59.4 0.5 fusion.36
  60.3 0.4 fusion.15
  60.7 0.4 fusion.37
  61.4 0.4 fusion.17
  61.9 0.4 fusion.38
  62.6 0.4 fusion.19
  63.0 0.4 fusion.39
  63.7 0.4 fusion.21
  64.1 0.4 fusion.40
  64.9 0.4 fusion.23
  65.3 0.4 fusion.41
  66.1 0.2 copy.142
  66.3 0.2 reshape.136
  66.6 0.8 pad_maximum_fusion.buf_ref
  67.4 63.2 %shard_map.196 = (f32[200,128]{1,0:T(8,128)}, bf16[96,4,256]{2,1,0:T(4,128)(2,1)}, bf16[96,4,256]{2,1,0:T(4,128)(2,1)}, bf16[96,4,128]{2,1,0:T(4,128)(2,1)}, bf1...) custom-call(f32[656,128]{1,0:T(8,128)} %pad_maximum_fusion.buf_ref, ...), custom_call_target="tpu_custom_call" | custom-call | bytes 209715200 | tf_op jit(solution)/shard_map/pallas_call | solution.py:471
  130.6 1.0 copy.143
  131.7 0.7 slice_bitcast_fusion.1
  132.4 0.9 slice_bitcast_fusion
  133.4 0.6 fusion.42
  134.1 0.7 slice.270
  134.8 0.7 slice.267
  135.5 0.9 copy.145
  136.9 0.5 maximum_bitcast_fusion
  137.3 0.2 reshape.140
  137.5 0.8 copy.154
  138.3 1.3 pad_convert_fusion.x_ref
  139.6 6.4 %shard_map.197 = f32[4,96,256]{2,1,0:T(8,128)} custom-call(f32[10,96,384]{2,1,0:T(8,128)} %pad_convert_fusion.x_ref, f32[96,49]{1,0:T(8,128)} %copy.101.k_ref), custom_call_target="tpu_custom_call" | custom-call | tf_op jit(solution)/shard_map/pallas_call | solution.py:169
  146.0 1.0 fusion.26
  147.1 0.8 copy.153
  (116 shorter events, 4.1 us)
Async XLA Ops:
  0.6 49.6 %copy-start = (bf16[384,96]{0,1:T(8,128)(2,1)S(1)}, bf16[384,96]{0,1:T(8,128)(2,1)}, u32[]{:S(2)}) copy-start(bf16[384,96]{0,1:T(8,128)(2,1)} %param.17) | copy-start | bytes 221188
  33.0 4.9 %copy-start.13 = (bf16[96,4,128]{2,1,0:T(4,128)(2,1)S(1)}, bf16[96,4,128]{2,1,0:T(4,128)(2,1)}, u32[]{:S(2)}) copy-start(bf16[96,4,128]{2,1,0:T(4,128)(2,1)} %get-tuple-element.35) | copy-start | bytes 294916
  33.0 5.0 %copy-start.8 = (bf16[96,4,256]{2,1,0:T(4,128)(2,1)S(1)}, bf16[96,4,256]{2,1,0:T(4,128)(2,1)}, u32[]{:S(2)}) copy-start(bf16[96,4,256]{2,1,0:T(4,128)(2,1)} %get-tuple-element.29) | copy-start | bytes 589828
  33.0 5.0 %copy-start.7 = (bf16[96,4,256]{2,1,0:T(4,128)(2,1)S(1)}, bf16[96,4,256]{2,1,0:T(4,128)(2,1)}, u32[]{:S(2)}) copy-start(bf16[96,4,256]{2,1,0:T(4,128)(2,1)} %get-tuple-element.34) | copy-start | bytes 589828
  40.3 6.5 %copy-start.16 = (f32[96]{0:T(128)S(1)}, f32[96]{0:T(128)}, u32[]{:S(2)}) copy-start(f32[96]{0:T(128)} %param.14) | copy-start | bytes 1156
  46.7 3.5 %copy-start.15 = (f32[96]{0:T(128)S(1)}, f32[96]{0:T(128)}, u32[]{:S(2)}) copy-start(f32[96]{0:T(128)} %param.15) | copy-start | bytes 1156
  46.7 3.5 %copy-start.18 = (f32[96]{0:T(128)S(1)}, f32[96]{0:T(128)}, u32[]{:S(2)}) copy-start(f32[96]{0:T(128)} %param.16) | copy-start | bytes 1156
  50.2 0.9 copy-start.14
  50.2 0.9 copy-start.17
  50.2 0.9 copy-start.19
  55.8 9.0 %copy-start.2 = (bf16[96,4,256]{2,1,0:T(4,128)(2,1)}, bf16[96,4,256]{2,1,0:T(4,128)(2,1)S(1)}, u32[]{:S(2)}) copy-start(bf16[96,4,256]{2,1,0:T(4,128)(2,1)S(1)} %reshape.135.x_ref) | copy-start | bytes 589828
  57.8 1.1 copy-start.4
  59.4 2.0 %copy-start.3 = (bf16[96,10,256]{2,0,1:T(8,128)(2,1)S(1)}, bf16[96,10,256]{2,0,1:T(8,128)(2,1)}, u32[]{:S(2)}) copy-start(bf16[96,10,256]{2,0,1:T(8,128)(2,1)} %get-tuple-element.86) | copy-start | bytes 1474564
  130.6 5.8 %copy-start.12 = (bf16[96,4,128]{2,1,0:T(4,128)(2,1)S(1)}, bf16[96,4,128]{2,1,0:T(4,128)(2,1)}, u32[]{:S(2)}) copy-start(bf16[96,4,128]{2,1,0:T(4,128)(2,1)} %get-tuple-element.39) | copy-start | bytes 294916
  130.6 6.0 %copy-start.11 = (bf16[96,4,128]{2,1,0:T(4,128)(2,1)S(1)}, bf16[96,4,128]{2,1,0:T(4,128)(2,1)}, u32[]{:S(2)}) copy-start(bf16[96,4,128]{2,1,0:T(4,128)(2,1)} %get-tuple-element.40) | copy-start | bytes 294916
  130.6 6.0 %copy-start.10 = (bf16[96,4,128]{2,1,0:T(4,128)(2,1)S(1)}, bf16[96,4,128]{2,1,0:T(4,128)(2,1)}, u32[]{:S(2)}) copy-start(bf16[96,4,128]{2,1,0:T(4,128)(2,1)} %get-tuple-element.41) | copy-start | bytes 294916
  130.6 6.1 %copy-start.9 = (bf16[96,4,128]{2,1,0:T(4,128)(2,1)S(1)}, bf16[96,4,128]{2,1,0:T(4,128)(2,1)}, u32[]{:S(2)}) copy-start(bf16[96,4,128]{2,1,0:T(4,128)(2,1)} %get-tuple-element.43) | copy-start | bytes 294916
  130.6 6.2 %copy-start.6 = (bf16[96,4,256]{2,1,0:T(4,128)(2,1)S(1)}, bf16[96,4,256]{2,1,0:T(4,128)(2,1)}, u32[]{:S(2)}) copy-start(bf16[96,4,256]{2,1,0:T(4,128)(2,1)} %get-tuple-element.37) | copy-start | bytes 589828
  133.3 3.5 %copy-start.5 = (bf16[96,4,256]{2,1,0:T(4,128)(2,1)S(1)}, bf16[96,4,256]{2,1,0:T(4,128)(2,1)}, u32[]{:S(2)}) copy-start(bf16[96,4,256]{2,1,0:T(4,128)(2,1)} %get-tuple-element.42) | copy-start | bytes 589828
  139.6 6.4 %copy-start.1 = (bf16[96,4,256]{2,1,0:T(4,128)(2,1)S(1)}, bf16[96,4,256]{2,1,0:T(4,128)(2,1)}, u32[]{:S(2)}) copy-start(bf16[96,4,256]{2,1,0:T(4,128)(2,1)} %param.12) | copy-start | bytes 589828

commit v11 on v9

--- a/solution.py
+++ b/solution.py
@@ -97,25 +97,25 @@
 
 
 def _assemble(x, got, width):
-    rows = x.shape[1]
+    rows = x.shape[0]
     piece = dict(zip(_DIRS, got))
     hi_r, lo_r = slice(rows - width, rows), slice(0, width)
-    above = piece[(-1, 0)][:, hi_r, :]
-    below = piece[(1, 0)][:, lo_r, :]
+    above = piece[(-1, 0)][hi_r]
+    below = piece[(1, 0)][lo_r]
     lw = piece[(0, -1)].shape[2]
     left = piece[(0, -1)][:, :, lw - width : lw]
     right = piece[(0, 1)][:, :, 0:width]
-    top_left = piece[(-1, -1)][:, hi_r, lw - width : lw]
-    top_right = piece[(-1, 1)][:, hi_r, 0:width]
-    bottom_left = piece[(1, -1)][:, lo_r, lw - width : lw]
-    bottom_right = piece[(1, 1)][:, lo_r, 0:width]
+    top_left = piece[(-1, -1)][hi_r, :, lw - width : lw]
+    top_right = piece[(-1, 1)][hi_r, :, 0:width]
+    bottom_left = piece[(1, -1)][lo_r, :, lw - width : lw]
+    bottom_right = piece[(1, 1)][lo_r, :, 0:width]
     return jnp.concatenate(
         [
             jnp.concatenate([top_left, above, top_right], axis=2),
             jnp.concatenate([left, x, right], axis=2),
             jnp.concatenate([bottom_left, below, bottom_right], axis=2),
         ],
-        axis=1,
+        axis=0,
     )
 
 
@@ -160,9 +160,9 @@
 
 
 def _dw(padded, kernel, row_count, col_count, flip):
-    channels = padded.shape[0]
+    channels = padded.shape[1]
     wide = -(-padded.shape[2] // LANES) * LANES
-    x = jnp.transpose(padded, (1, 0, 2)).astype(jnp.float32)
+    x = padded.astype(jnp.float32)
     x = jnp.pad(x, ((0, 0), (0, 0), (0, wide - padded.shape[2])))
     taps = kernel.reshape(channels, 49)
     cb = 8
@@ -226,8 +226,9 @@
     channels, row_count, col_count = image.shape
     panel_rows = w_expand.shape[0] // lax.axis_size("filt")
     tok_count = row_count * col_count
-    padded = padded_2(image, (("space", 1), ("filt", 2)), 3, 1)
-    conv = depthwise(padded, kernel, row_count, col_count)
+    padded_rows = padded_2(jnp.transpose(image, (1, 0, 2)), (("space", 1), ("filt", 2)), 3, 1)
+    conv = depthwise(padded_rows, kernel, row_count, col_count)
+    padded = jnp.transpose(padded_rows, (1, 0, 2))
     conv = conv + dw_bias[:, None, None]
     flat = conv.reshape(channels, tok_count)
     average = jnp.mean(flat, axis=0, keepdims=True)
@@ -308,8 +309,9 @@
             g_rbias,
         ]
     )
-    panel, small, got = grad_reduce(panels, small, convolution_gradient)
-    padded_grad = _assemble(convolution_gradient, got, 3)
+    grad_rows = jnp.transpose(convolution_gradient, (1, 0, 2))
+    panel, small, got = grad_reduce(panels, small, grad_rows)
+    padded_grad = _assemble(grad_rows, got, 3)
     back = conv_back(padded_grad, kernel, row_count, col_count)
     image_grad = (cotangent.astype(jnp.float32) + back).astype(jnp.bfloat16)
     total = jnp.concatenate([panel, small])

time: 150 us -> 158 us (1.053)
  local copies, waits for them, and re-layouts: 25.3 us -> 30.8 us
    slice x12, local copies, waits for them, and re-layouts: 0.43 us -> 9.41 us  [the longest x2 2.01 us: _assemble(): top_left = piece[-1, -1][hi_r, :, lw - width:lw]]
    pallas_call x16 -> x0, local copies, waits for them, and re-layouts: 6.65 us -> none  [the longest x8 4.66 us: padded_2(): pl.pallas_call(functools.partial(halo_kernel, ns, nf, x.shape[2]), out_sh...]
    slice x2, local copies, waits for them, and re-layouts: 0.18 us -> 1.96 us  [_assemble(): left = piece[0, -1][:, :, lw - width:lw]]
    unnamed x46 -> x36, local copies, waits for them, and re-layouts: 3.77 us -> 4.43 us
where the time goes in v11:
time: 158 us; the launch traced here: 155 us
  Pallas kernels  102 us (65%)
  local copies, waits for them, and re-layouts  30.8 us (19%)
  other arithmetic  13.3 us (8%)
  matrix products  7.42 us (5%)
    pallas_call x1, Pallas kernels, grad_reduce(): pl.pallas_call(functools.partial(reduce_kernel, nfilt, nspace, pr, sr, x....  63.2 us
    pallas_call x1, Pallas kernels, padded_2(): pl.pallas_call(functools.partial(halo_kernel, ns, nf, x.shape[2]), out_sh...  26.1 us
    pallas_call x2, Pallas kernels, _dw(): pl.pallas_call(functools.partial(dw_kernel, flip, cb), out_shape=jax.Shap...  13.1 us
    unnamed x36, local copies, waits for them, and re-layouts  4.43 us
    slice x28, local copies, waits for them, and re-layouts, kernel_terms(): total = total + corr[:, row:row + ksize, row]  4.22 us
    dot_general x7, matrix products, kernel_terms(): jnp.einsum('crj,cij->cri', padded[:, :, shift_col:shift_col + col_count],...  3.99 us

profile of v11, /device:TPU:56, one launch (start us, length us, event | category | flops | bytes accessed | tf_op | source)
XLA Modules:
  0.0 154.9 jit_solution(9553932320354835025)
XLA Ops:
  0.7 1.2 fusion.43
  1.8 0.7 convert_element_type.59
  2.5 0.8 reshape.128
  3.3 0.7 copy.60.k_ref
  4.0 1.6 %copy.134 = bf16[96,4,256]{2,0,1:T(8,128)(2,1)} copy(bf16[96,4,256]{2,1,0:T(4,128)(2,1)} %param.11) | data formatting | bytes 393216 | tf_op args[0]
  5.6 1.0 copy.111
  6.6 1.0 convert_bitcast_fusion
  7.6 26.1 %shard_map.194 = (bf16[4,96,256]{2,1,0:T(8,128)(2,1)}, bf16[4,96,256]{2,1,0:T(8,128)(2,1)}, bf16[4,96,128]{2,1,0:T(8,128)(2,1)}, bf16[4,96,128]{2,1,0:T(8,128)(2...) custom-call(bf16[4,96,256]{2,1,0:T(8,128)(2,1)} %bitcast.102), custom_call_target="tpu_custom_call" | custom-call | tf_op jit(solution)/shard_map/pallas_call | solution.py:126
  33.7 1.0 slice.207
  34.7 0.9 slice.209
  35.6 1.0 slice.212
  36.6 0.9 slice.214
  37.5 1.0 slice.210
  38.5 0.9 slice.208
  39.4 0.9 slice.213
  40.3 1.3 fusion.77
  41.7 0.5 maximum_maximum_fusion
  42.1 1.3 pad_convert_fusion.x_ref
  43.4 6.5 %shard_map.195 = f32[4,96,256]{2,1,0:T(8,128)} custom-call(f32[10,96,384]{2,1,0:T(8,128)} %pad_convert_fusion.x_ref, f32[96,49]{1,0:T(8,128)} %copy.60.k_ref), custom_call_target="tpu_custom_call" | custom-call | tf_op jit(solution)/shard_map/pallas_call | solution.py:169
  49.9 1.1 bitcast_reduce_fusion
  51.1 1.1 fusion.47
  52.2 1.1 add_bitcast_fusion
  53.4 0.6 fusion.9
  54.2 0.5 multiply_reduce_fusion
  54.7 1.0 convert_reduce_fusion
  55.7 0.4 fusion.50
  56.4 0.8 reshape.130
  57.2 0.4 fusion.51
  57.6 0.5 fusion.45
  58.4 0.2 convert_reduce_fusion.1
  59.0 0.7 copy.133
  59.7 2.0 %fusion.52 = (bf16[96,10,256]{2,0,1:T(8,128)(2,1)S(1)}, bf16[96,10,256]{2,0,1:T(8,128)(2,1)}, bf16[96,10,256]{2,0,1:T(8,128)(2,1)}, bf16[96,10,256]{2,0,1:T(8,12...) fusion(bf16[96,10,262]{2,0,1:T(8,128)(2,1)S(1)} %fusion.77), kind=kLoop, calls=%fused_computation.98 | loop fusion | bytes 6881280 | tf_op jit(solution)/shard_map/slice | solution.py:192
  61.7 0.4 fusion.20
  62.1 0.4 fusion.53
  62.8 1.5 fusion.22
  64.3 0.4 fusion.54
  65.0 0.4 fusion.24
  65.4 0.4 fusion.55
  66.1 0.4 fusion.26
  66.6 0.4 fusion.56
  67.3 0.4 fusion.28
  67.7 0.4 fusion.57
  68.4 0.4 fusion.30
  68.8 0.4 fusion.32
  69.3 0.4 fusion.59
  69.7 0.4 fusion.58
  70.8 0.2 copy.101
  71.3 0.7 pad_maximum_fusion.buf_ref
  72.0 63.2 %shard_map.196 = (f32[200,128]{1,0:T(8,128)}, bf16[4,96,256]{2,1,0:T(8,128)(2,1)}, bf16[4,96,256]{2,1,0:T(8,128)(2,1)}, bf16[4,96,128]{2,1,0:T(8,128)(2,1)}, bf1...) custom-call(f32[656,128]{1,0:T(8,128)} %pad_maximum_fusion.buf_ref, ...), custom_call_target="tpu_custom_call" | custom-call | bytes 209715200 | tf_op jit(solution)/shard_map/pallas_call | solution.py:473
  135.3 1.0 slice.250
  136.3 0.7 slice_bitcast_fusion.1
  137.1 0.9 slice_bitcast_fusion
  138.0 0.6 fusion.60
  138.7 0.7 slice.270
  139.4 0.7 slice.267
  140.1 0.9 slice.252
  141.0 1.0 slice.255
  142.0 0.9 slice.257
  142.9 1.0 slice.253
  144.1 0.8 copy.105
  144.9 1.6 %fusion.38.x_ref = f32[10,96,384]{2,1,0:T(8,128)} fusion(bf16[3,96,3]{2,1,0:T(8,128)(2,1)S(1)} %slice.257, bf16[3,96,256]{2,1,0:T(8,128)(2,1)S(1)} %slice.256, bf16[3,96,3]{2,1,0:T(8,128)(2,1)S(1)} %slice.255, bf16[4,96,3]{2,1,0:T(8,128)(2,1)S(1)} %bitcast.121, bf16[3,96,3]{2,1,0:T(8,128)(2,1)S(1)} %slice.252, bf16[4,96,256]{2,1,0:T(8,128)(2,1)S(1)} %bitcast.106, ...), kind=kLoop, calls=%fused_computation.45 | loop fusion | flops 10321920 | bytes 1977600 | tf_op jit(solution)/shard_map/jit(_pad)/pad | solution.py:166
  146.5 6.5 %shard_map.197 = f32[4,96,256]{2,1,0:T(8,128)} custom-call(f32[10,96,384]{2,1,0:T(8,128)} %fusion.38.x_ref, f32[96,49]{1,0:T(8,128)} %copy.60.k_ref), custom_call_target="tpu_custom_call" | custom-call | tf_op jit(solution)/shard_map/pallas_call | solution.py:169
  153.0 1.0 fusion.44
  154.1 0.8 copy.104
  (89 shorter events, 4.2 us)
Async XLA Ops:
  0.6 52.8 %copy-start = (bf16[384,96]{0,1:T(8,128)(2,1)S(1)}, bf16[384,96]{0,1:T(8,128)(2,1)}, u32[]{:S(2)}) copy-start(bf16[384,96]{0,1:T(8,128)(2,1)} %param.17) | copy-start | bytes 221188
  6.6 33.7 %copy-start.1 = (bf16[96,4,256]{2,0,1:T(8,128)(2,1)S(1)}, bf16[96,4,256]{2,0,1:T(8,128)(2,1)}, u32[]{:S(2)}) copy-start(bf16[96,4,256]{2,0,1:T(8,128)(2,1)} %copy.134) | copy-start | bytes 589828
  34.7 7.0 %copy-start.5 = (bf16[4,96,128]{2,1,0:T(8,128)(2,1)S(1)}, bf16[4,96,128]{2,1,0:T(8,128)(2,1)}, u32[]{:S(2)}) copy-start(bf16[4,96,128]{2,1,0:T(8,128)(2,1)} %get-tuple-element.32) | copy-start | bytes 294916
  43.4 6.5 %copy-start.11 = (f32[96]{0:T(128)S(1)}, f32[96]{0:T(128)}, u32[]{:S(2)}) copy-start(f32[96]{0:T(128)} %param.14) | copy-start | bytes 1156
  49.9 3.5 %copy-start.10 = (f32[96]{0:T(128)S(1)}, f32[96]{0:T(128)}, u32[]{:S(2)}) copy-start(f32[96]{0:T(128)} %param.15) | copy-start | bytes 1156
  49.9 3.5 %copy-start.13 = (f32[96]{0:T(128)S(1)}, f32[96]{0:T(128)}, u32[]{:S(2)}) copy-start(f32[96]{0:T(128)} %param.16) | copy-start | bytes 1156
  53.3 0.9 copy-start.9
  53.3 0.9 copy-start.12
  53.4 0.9 copy-start.14
  62.1 2.9 %copy-start.4 = (bf16[96,10,256]{2,0,1:T(8,128)(2,1)S(1)}, bf16[96,10,256]{2,0,1:T(8,128)(2,1)}, u32[]{:S(2)}) copy-start(bf16[96,10,256]{2,0,1:T(8,128)(2,1)} %get-tuple-element.85) | copy-start | bytes 1474564
  135.2 8.6 %copy-start.7 = (bf16[4,96,256]{2,1,0:T(8,128)(2,1)S(1)}, bf16[4,96,256]{2,1,0:T(8,128)(2,1)}, u32[]{:S(2)}) copy-start(bf16[4,96,256]{2,1,0:T(8,128)(2,1)} %get-tuple-element.37) | copy-start | bytes 589828
  135.3 8.7 %copy-start.6 = (bf16[4,96,256]{2,1,0:T(8,128)(2,1)S(1)}, bf16[4,96,256]{2,1,0:T(8,128)(2,1)}, u32[]{:S(2)}) copy-start(bf16[4,96,256]{2,1,0:T(8,128)(2,1)} %get-tuple-element.42) | copy-start | bytes 589828
  135.3 9.7 %copy-start.2 = (bf16[12,4,8,256]{3,2,0,1:T(8,128)(2,1)S(1)}, bf16[12,4,8,256]{3,2,0,1:T(8,128)(2,1)}, u32[]{:S(2)}) copy-start(bf16[12,4,8,256]{3,2,0,1:T(8,128)(2,1)} %copy.133) | copy-start | bytes 589828
  135.3 9.7 %copy-start.8 = (bf16[4,96,128]{2,1,0:T(8,128)(2,1)S(1)}, bf16[4,96,128]{2,1,0:T(8,128)(2,1)}, u32[]{:S(2)}) copy-start(bf16[4,96,128]{2,1,0:T(8,128)(2,1)} %get-tuple-element.40) | copy-start | bytes 294916
  146.5 6.5 %copy-start.3 = (bf16[96,4,256]{2,1,0:T(4,128)(2,1)S(1)}, bf16[96,4,256]{2,1,0:T(4,128)(2,1)}, u32[]{:S(2)}) copy-start(bf16[96,4,256]{2,1,0:T(4,128)(2,1)} %param.12) | copy-start | bytes 589828

commit v12 on v9

--- a/solution.py
+++ b/solution.py
@@ -138,7 +138,7 @@
 
 
 def dw_kernel(flip, cb, x_ref, k_ref, o_ref):
-    rows, channels, cols = o_ref.shape
+    channels, rows, cols = o_ref.shape
     wide = x_ref.shape[2]
 
     def block(i, carry):
@@ -153,7 +153,8 @@
                 r0 = 6 - shift_row if flip else shift_row
                 kv = k_ref[ch, pl.ds(shift_row * 7 + shift_col, 1)]
                 acc = acc + kv[None] * xb[r0 : r0 + rows]
-        o_ref[:, ch, :] = acc
+        for r in range(rows):
+            o_ref[ch, r, :] = acc[r]
         return carry
 
     lax.fori_loop(0, channels // cb, block, 0)
@@ -168,11 +169,11 @@
     cb = 8
     out = pl.pallas_call(
         functools.partial(dw_kernel, flip, cb),
-        out_shape=jax.ShapeDtypeStruct((row_count, channels, col_count), jnp.float32),
+        out_shape=jax.ShapeDtypeStruct((channels, row_count, col_count), jnp.float32),
         in_specs=[pl.BlockSpec(memory_space=pltpu.VMEM)] * 2,
         out_specs=pl.BlockSpec(memory_space=pltpu.VMEM),
     )(x, taps)
-    return jnp.transpose(out, (1, 0, 2))
+    return out
 
 
 def depthwise(padded, kernel, row_count, col_count):

time: 150 us -> 150 us (level)
    unnamed x4 -> x2, other arithmetic: 2.06 us -> 0.02 us
    unnamed x46 -> x51, local copies, waits for them, and re-layouts: 3.77 us -> 4 us
where the time goes in v12:
time: 150 us; the launch traced here: 148 us
  Pallas kernels  103 us (69%)
  local copies, waits for them, and re-layouts  25.8 us (17%)
  other arithmetic  11.5 us (8%)
  matrix products  6.38 us (4%)
    pallas_call x1, Pallas kernels, grad_reduce(): pl.pallas_call(functools.partial(reduce_kernel, nfilt, nspace, pr, sr, x....  63.2 us
    pallas_call x1, Pallas kernels, padded_2(): pl.pallas_call(functools.partial(halo_kernel, ns, nf, x.shape[2]), out_sh...  26.1 us
    pallas_call x2, Pallas kernels, _dw(): pl.pallas_call(functools.partial(dw_kernel, flip, cb), out_shape=jax.Shap...  13.4 us
    pallas_call x8, local copies, waits for them, and re-layouts, padded_2(): pl.pallas_call(functools.partial(halo_kernel, ns, nf, x.shape[2]), out_sh...  4.66 us
    slice x28, local copies, waits for them, and re-layouts, kernel_terms(): total = total + corr[:, row:row + ksize, row]  4.22 us
    unnamed x51, local copies, waits for them, and re-layouts  4 us

profile of v12, /device:TPU:56, one launch (start us, length us, event | category | flops | bytes accessed | tf_op | source)
XLA Modules:
  0.0 147.6 jit_solution(7712189294308985339)
XLA Ops:
  0.7 2.4 %multiply_reduce_fusion = f32[96]{0:T(128)S(1)} fusion(f32[96]{0:T(128)} %param.21, bf16[96,4,256]{2,1,0:T(4,128)(2,1)} %param.12), kind=kLoop, calls=%fused_computation.39 | loop fusion | flops 294816 | bytes 197376 | tf_op jit(solution)/shard_map/reduce_sum | solution.py:263
  3.0 0.7 convert_element_type.66
  3.7 0.8 reshape.128
  4.5 0.7 copy.95.k_ref
  5.2 0.9 copy.91
  6.1 1.0 copy.152
  7.1 1.0 copy.148
  8.1 26.1 %shard_map.194 = (bf16[96,4,256]{2,1,0:T(4,128)(2,1)}, bf16[96,4,256]{2,1,0:T(4,128)(2,1)}, bf16[96,4,128]{2,1,0:T(4,128)(2,1)}, bf16[96,4,128]{2,1,0:T(4,128)(2...) custom-call(bf16[96,4,256]{2,1,0:T(4,128)(2,1)} %x_ref.1), custom_call_target="tpu_custom_call" | custom-call | tf_op jit(solution)/shard_map/pallas_call | solution.py:126
  34.2 1.0 copy.86
  35.2 0.9 copy.88
  36.1 0.9 copy.89
  37.2 0.9 copy.90
  38.1 0.9 copy.92
  39.2 0.5 fusion.56
  39.7 0.5 maximum_maximum_fusion
  40.2 1.2 pad_convert_fusion.1.x_ref
  41.4 6.7 %shard_map.195 = f32[96,4,256]{2,1,0:T(4,128)} custom-call(f32[10,96,384]{2,1,0:T(8,128)} %pad_convert_fusion.1.x_ref, f32[96,49]{1,0:T(8,128)} %copy.95.k_ref), custom_call_target="tpu_custom_call" | custom-call | tf_op jit(solution)/shard_map/pallas_call | solution.py:170
  48.1 1.2 fusion.30
  49.3 0.2 multiply_reduce_fusion.3
  49.6 0.6 fusion.9
  50.3 0.2 copy-done.16
  50.4 0.5 multiply_reduce_fusion.1
  50.9 1.0 convert_reduce_fusion
  51.9 0.4 fusion.28
  52.3 0.2 reshape.131
  52.6 0.8 reshape.130
  53.4 0.4 fusion.29
  53.8 0.5 fusion.25
  54.3 0.2 reshape.132
  54.7 0.2 convert_reduce_fusion.1
  55.0 0.1 reshape.134
  55.1 0.1 reshape.135.x_ref
  55.3 2.3 %fusion.31 = (bf16[96,10,256]{2,0,1:T(8,128)(2,1)S(1)}, bf16[96,10,256]{2,0,1:T(8,128)(2,1)}, bf16[96,10,256]{2,0,1:T(8,128)(2,1)}, bf16[96,10,256]{2,0,1:T(8,12...) fusion(bf16[96,10,262]{2,0,1:T(8,128)(2,1)S(1)} %maximum_maximum_fusion), kind=kLoop, calls=%fused_computation.75 | loop fusion | bytes 6881280 | tf_op jit(solution)/shard_map/slice | solution.py:193
  57.5 0.4 fusion.11
  58.0 0.4 fusion.32
  58.7 0.4 fusion.13
  59.1 0.4 fusion.33
  59.8 0.4 fusion.15
  60.3 0.4 fusion.34
  61.0 0.4 fusion.17
  61.4 0.4 fusion.35
  62.1 0.4 fusion.19
  62.6 0.4 fusion.36
  63.3 0.4 fusion.21
  63.7 0.4 fusion.37
  64.4 0.4 fusion.23
  64.9 0.4 fusion.38
  65.6 0.2 copy.133
  65.9 0.2 reshape.136
  66.2 0.7 pad_maximum_fusion.buf_ref
  66.9 63.2 %shard_map.196 = (f32[200,128]{1,0:T(8,128)}, bf16[96,4,256]{2,1,0:T(4,128)(2,1)}, bf16[96,4,256]{2,1,0:T(4,128)(2,1)}, bf16[96,4,128]{2,1,0:T(4,128)(2,1)}, bf1...) custom-call(f32[656,128]{1,0:T(8,128)} %pad_maximum_fusion.buf_ref, ...), custom_call_target="tpu_custom_call" | custom-call | bytes 209715200 | tf_op jit(solution)/shard_map/pallas_call | solution.py:472
  130.2 1.0 copy.134
  131.2 0.7 slice_bitcast_fusion.1
  132.0 0.9 slice_bitcast_fusion
  133.0 0.6 fusion.39
  133.6 0.7 slice.270
  134.3 0.7 slice.267
  135.0 0.9 copy.136
  136.4 0.5 maximum_bitcast_fusion
  136.9 0.2 reshape.140
  137.1 0.8 copy.144
  137.9 1.2 pad_convert_fusion.x_ref
  139.1 6.7 %shard_map.197 = f32[96,4,256]{2,1,0:T(4,128)} custom-call(f32[10,96,384]{2,1,0:T(8,128)} %pad_convert_fusion.x_ref, f32[96,49]{1,0:T(8,128)} %copy.95.k_ref), custom_call_target="tpu_custom_call" | custom-call | tf_op jit(solution)/shard_map/pallas_call | solution.py:170
  145.8 1.8 %add_convert_fusion = bf16[96,4,256]{2,1,0:T(4,128)(2,1)} fusion(f32[96,4,256]{2,1,0:T(4,128)} %shard_map.197, bf16[96,4,256]{2,1,0:T(4,128)(2,1)S(1)} %copy-done.1), kind=kLoop, calls=%fused_computation.38 | loop fusion | flops 294912 | bytes 786432 | tf_op jit(solution)/shard_map/convert_element_type | solution.py:315
  (117 shorter events, 3.9 us)
Async XLA Ops:
  0.6 48.9 %copy-start = (bf16[384,96]{0,1:T(8,128)(2,1)S(1)}, bf16[384,96]{0,1:T(8,128)(2,1)}, u32[]{:S(2)}) copy-start(bf16[384,96]{0,1:T(8,128)(2,1)} %param.17) | copy-start | bytes 221188
  34.1 4.9 %copy-start.15 = (bf16[96,4,128]{2,1,0:T(4,128)(2,1)S(1)}, bf16[96,4,128]{2,1,0:T(4,128)(2,1)}, u32[]{:S(2)}) copy-start(bf16[96,4,128]{2,1,0:T(4,128)(2,1)} %get-tuple-element.35) | copy-start | bytes 294916
  34.1 5.0 %copy-start.10 = (bf16[96,4,256]{2,1,0:T(4,128)(2,1)S(1)}, bf16[96,4,256]{2,1,0:T(4,128)(2,1)}, u32[]{:S(2)}) copy-start(bf16[96,4,256]{2,1,0:T(4,128)(2,1)} %get-tuple-element.29) | copy-start | bytes 589828
  34.2 5.0 %copy-start.9 = (bf16[96,4,256]{2,1,0:T(4,128)(2,1)S(1)}, bf16[96,4,256]{2,1,0:T(4,128)(2,1)}, u32[]{:S(2)}) copy-start(bf16[96,4,256]{2,1,0:T(4,128)(2,1)} %get-tuple-element.34) | copy-start | bytes 589828
  41.4 6.7 %copy-start.20 = (f32[96]{0:T(128)S(1)}, f32[96]{0:T(128)}, u32[]{:S(2)}) copy-start(f32[96]{0:T(128)} %param.14) | copy-start | bytes 1156
  48.1 1.5 %copy-start.17 = (f32[96]{0:T(128)S(1)}, f32[96]{0:T(128)}, u32[]{:S(2)}) copy-start(f32[96]{0:T(128)} %param.15) | copy-start | bytes 1156
  48.1 1.5 %copy-start.19 = (f32[96]{0:T(128)S(1)}, f32[96]{0:T(128)}, u32[]{:S(2)}) copy-start(f32[96]{0:T(128)} %param.16) | copy-start | bytes 1156
  49.6 0.9 copy-start.16
  49.6 0.9 copy-start.18
  49.6 0.9 copy-start.21
  55.2 9.2 %copy-start.2 = (bf16[96,4,256]{2,1,0:T(4,128)(2,1)}, bf16[96,4,256]{2,1,0:T(4,128)(2,1)S(1)}, u32[]{:S(2)}) copy-start(bf16[96,4,256]{2,1,0:T(4,128)(2,1)S(1)} %reshape.135.x_ref) | copy-start | bytes 589828
  57.5 1.1 copy-start.6
  58.0 1.9 %copy-start.5 = (bf16[96,10,256]{2,0,1:T(8,128)(2,1)S(1)}, bf16[96,10,256]{2,0,1:T(8,128)(2,1)}, u32[]{:S(2)}) copy-start(bf16[96,10,256]{2,0,1:T(8,128)(2,1)} %get-tuple-element.76) | copy-start | bytes 1474564
  59.1 1.9 %copy-start.4 = (bf16[96,10,256]{2,0,1:T(8,128)(2,1)S(1)}, bf16[96,10,256]{2,0,1:T(8,128)(2,1)}, u32[]{:S(2)}) copy-start(bf16[96,10,256]{2,0,1:T(8,128)(2,1)} %get-tuple-element.77) | copy-start | bytes 1474564
  60.3 1.9 %copy-start.3 = (bf16[96,10,256]{2,0,1:T(8,128)(2,1)S(1)}, bf16[96,10,256]{2,0,1:T(8,128)(2,1)}, u32[]{:S(2)}) copy-start(bf16[96,10,256]{2,0,1:T(8,128)(2,1)} %get-tuple-element.78) | copy-start | bytes 1474564
  130.1 5.8 %copy-start.14 = (bf16[96,4,128]{2,1,0:T(4,128)(2,1)S(1)}, bf16[96,4,128]{2,1,0:T(4,128)(2,1)}, u32[]{:S(2)}) copy-start(bf16[96,4,128]{2,1,0:T(4,128)(2,1)} %get-tuple-element.39) | copy-start | bytes 294916
  130.1 6.0 %copy-start.13 = (bf16[96,4,128]{2,1,0:T(4,128)(2,1)S(1)}, bf16[96,4,128]{2,1,0:T(4,128)(2,1)}, u32[]{:S(2)}) copy-start(bf16[96,4,128]{2,1,0:T(4,128)(2,1)} %get-tuple-element.40) | copy-start | bytes 294916
  130.1 6.0 %copy-start.12 = (bf16[96,4,128]{2,1,0:T(4,128)(2,1)S(1)}, bf16[96,4,128]{2,1,0:T(4,128)(2,1)}, u32[]{:S(2)}) copy-start(bf16[96,4,128]{2,1,0:T(4,128)(2,1)} %get-tuple-element.41) | copy-start | bytes 294916
  130.1 6.1 %copy-start.11 = (bf16[96,4,128]{2,1,0:T(4,128)(2,1)S(1)}, bf16[96,4,128]{2,1,0:T(4,128)(2,1)}, u32[]{:S(2)}) copy-start(bf16[96,4,128]{2,1,0:T(4,128)(2,1)} %get-tuple-element.43) | copy-start | bytes 294916
  130.2 6.2 %copy-start.8 = (bf16[96,4,256]{2,1,0:T(4,128)(2,1)S(1)}, bf16[96,4,256]{2,1,0:T(4,128)(2,1)}, u32[]{:S(2)}) copy-start(bf16[96,4,256]{2,1,0:T(4,128)(2,1)} %get-tuple-element.37) | copy-start | bytes 589828
  132.9 3.5 %copy-start.7 = (bf16[96,4,256]{2,1,0:T(4,128)(2,1)S(1)}, bf16[96,4,256]{2,1,0:T(4,128)(2,1)}, u32[]{:S(2)}) copy-start(bf16[96,4,256]{2,1,0:T(4,128)(2,1)} %get-tuple-element.42) | copy-start | bytes 589828
  139.1 6.7 %copy-start.1 = (bf16[96,4,256]{2,1,0:T(4,128)(2,1)S(1)}, bf16[96,4,256]{2,1,0:T(4,128)(2,1)}, u32[]{:S(2)}) copy-start(bf16[96,4,256]{2,1,0:T(4,128)(2,1)} %param.12) | copy-start | bytes 589828

commit v13 on v12

--- a/solution.py
+++ b/solution.py
@@ -137,7 +137,9 @@
     return _assemble(x, got, width)
 
 
-def dw_kernel(flip, cb, x_ref, k_ref, o_ref):
+def dw_kernel(flip, cb, x_ref, k_ref, *rest):
+    cot_ref = rest[0] if len(rest) > 1 else None
+    o_ref = rest[-1]
     channels, rows, cols = o_ref.shape
     wide = x_ref.shape[2]
 
@@ -154,13 +156,16 @@
                 kv = k_ref[ch, pl.ds(shift_row * 7 + shift_col, 1)]
                 acc = acc + kv[None] * xb[r0 : r0 + rows]
         for r in range(rows):
-            o_ref[ch, r, :] = acc[r]
+            if cot_ref is None:
+                o_ref[ch, r, :] = acc[r]
+            else:
+                o_ref[ch, r, :] = (cot_ref[ch, r, :].astype(jnp.float32) + acc[r]).astype(o_ref.dtype)
         return carry
 
     lax.fori_loop(0, channels // cb, block, 0)
 
 
-def _dw(padded, kernel, row_count, col_count, flip):
+def _dw(padded, kernel, row_count, col_count, flip, cot=None):
     channels = padded.shape[0]
     wide = -(-padded.shape[2] // LANES) * LANES
     x = jnp.transpose(padded, (1, 0, 2)).astype(jnp.float32)
@@ -169,10 +174,12 @@
     cb = 8
     out = pl.pallas_call(
         functools.partial(dw_kernel, flip, cb),
-        out_shape=jax.ShapeDtypeStruct((channels, row_count, col_count), jnp.float32),
-        in_specs=[pl.BlockSpec(memory_space=pltpu.VMEM)] * 2,
+        out_shape=jax.ShapeDtypeStruct(
+            (channels, row_count, col_count), jnp.float32 if cot is None else cot.dtype
+        ),
+        in_specs=[pl.BlockSpec(memory_space=pltpu.VMEM)] * (2 if cot is None else 3),
         out_specs=pl.BlockSpec(memory_space=pltpu.VMEM),
-    )(x, taps)
+    )(x, taps, *([] if cot is None else [cot]))
     return out
 
 
@@ -180,8 +187,8 @@
     return _dw(padded, kernel, row_count, col_count, False)
 
 
-def conv_back(padded, kernel, row_count, col_count):
-    return _dw(padded, kernel, row_count, col_count, True)
+def conv_back(padded, kernel, row_count, col_count, cot):
+    return _dw(padded, kernel, row_count, col_count, True, cot)
 
 
 def kernel_terms(padded, convolution_gradient, row_count, col_count):
@@ -311,8 +318,7 @@
     )
     panel, small, got = grad_reduce(panels, small, convolution_gradient)
     padded_grad = _assemble(convolution_gradient, got, 3)
-    back = conv_back(padded_grad, kernel, row_count, col_count)
-    image_grad = (cotangent.astype(jnp.float32) + back).astype(jnp.bfloat16)
+    image_grad = conv_back(padded_grad, kernel, row_count, col_count, cotangent)
     total = jnp.concatenate([panel, small])
     total = total * factor
     cut = [panel_rows * channels, panel_rows * channels, panel_rows]

time: 150 us -> 148 us (0.987)
  other arithmetic: 11.5 us -> 9.7 us
    convert_element_type x1 -> x0, other arithmetic: 1.79 us -> none  [shards(): image_grad = (cotangent.astype(jnp.float32) + back).astype(jnp.bfloat16)]
    unnamed x51 -> x49, local copies, waits for them, and re-layouts: 4 us -> 4 us
where the time goes in v13:
time: 148 us; the launch traced here: 146 us
  Pallas kernels  103 us (70%)
  local copies, waits for them, and re-layouts  25.8 us (17%)
  other arithmetic  9.7 us (7%)
  matrix products  6.38 us (4%)
    pallas_call x1, Pallas kernels, grad_reduce(): pl.pallas_call(functools.partial(reduce_kernel, nfilt, nspace, pr, sr, x....  63.2 us
    pallas_call x1, Pallas kernels, padded_2(): pl.pallas_call(functools.partial(halo_kernel, ns, nf, x.shape[2]), out_sh...  26.1 us
    pallas_call x2, Pallas kernels, _dw(): pl.pallas_call(functools.partial(dw_kernel, flip, cb), out_shape=jax.Shap...  13.5 us
    pallas_call x8, local copies, waits for them, and re-layouts, padded_2(): pl.pallas_call(functools.partial(halo_kernel, ns, nf, x.shape[2]), out_sh...  4.66 us
    slice x28, local copies, waits for them, and re-layouts, kernel_terms(): total = total + corr[:, row:row + ksize, row]  4.22 us
    unnamed x49, local copies, waits for them, and re-layouts  4 us

profile of v13, /device:TPU:56, one launch (start us, length us, event | category | flops | bytes accessed | tf_op | source)
XLA Modules:
  0.0 145.9 jit_solution(2004907690474087404)
XLA Ops:
  0.7 2.4 %multiply_reduce_fusion = f32[96]{0:T(128)S(1)} fusion(f32[96]{0:T(128)} %param.21, bf16[96,4,256]{2,1,0:T(4,128)(2,1)} %rest_0_.1), kind=kLoop, calls=%fused_computation.38 | loop fusion | flops 294816 | bytes 197376 | tf_op jit(solution)/shard_map/reduce_sum | solution.py:270
  3.0 0.7 convert_element_type.62
  3.7 0.8 reshape.128
  4.5 0.7 copy.95.k_ref
  5.2 0.9 copy.91
  6.1 1.0 copy.152
  7.1 1.0 copy.148
  8.1 26.1 %shard_map.194 = (bf16[96,4,256]{2,1,0:T(4,128)(2,1)}, bf16[96,4,256]{2,1,0:T(4,128)(2,1)}, bf16[96,4,128]{2,1,0:T(4,128)(2,1)}, bf16[96,4,128]{2,1,0:T(4,128)(2...) custom-call(bf16[96,4,256]{2,1,0:T(4,128)(2,1)} %x_ref.1), custom_call_target="tpu_custom_call" | custom-call | tf_op jit(solution)/shard_map/pallas_call | solution.py:126
  34.2 1.0 copy.86
  35.2 0.9 copy.88
  36.2 0.9 copy.89
  37.2 0.9 copy.90
  38.1 0.9 copy.92
  39.3 0.5 fusion.56
  39.7 0.5 maximum_maximum_fusion
  40.2 1.2 pad_convert_fusion.1.x_ref
  41.4 6.7 %shard_map.195 = f32[96,4,256]{2,1,0:T(4,128)} custom-call(f32[10,96,384]{2,1,0:T(8,128)} %pad_convert_fusion.1.x_ref, f32[96,49]{1,0:T(8,128)} %copy.95.k_ref), custom_call_target="tpu_custom_call" | custom-call | tf_op jit(solution)/shard_map/pallas_call | solution.py:175
  48.1 1.2 fusion.30
  49.3 0.2 multiply_reduce_fusion.3
  49.6 0.6 fusion.9
  50.3 0.2 copy-done.15
  50.4 0.5 multiply_reduce_fusion.1
  50.9 0.9 convert_reduce_fusion
  51.9 0.4 fusion.28
  52.3 0.2 reshape.131
  52.6 0.8 reshape.130
  53.4 0.4 fusion.29
  53.8 0.5 fusion.25
  54.3 0.2 reshape.132
  54.5 0.1 reduce_sum.97
  54.7 0.2 convert_reduce_fusion.1
  55.0 0.1 reshape.134
  55.1 0.1 reshape.135.x_ref
  55.3 2.3 %fusion.31 = (bf16[96,10,256]{2,0,1:T(8,128)(2,1)S(1)}, bf16[96,10,256]{2,0,1:T(8,128)(2,1)}, bf16[96,10,256]{2,0,1:T(8,128)(2,1)}, bf16[96,10,256]{2,0,1:T(8,12...) fusion(bf16[96,10,262]{2,0,1:T(8,128)(2,1)S(1)} %maximum_maximum_fusion), kind=kLoop, calls=%fused_computation.74 | loop fusion | bytes 6881280 | tf_op jit(solution)/shard_map/slice | solution.py:200
  57.5 0.4 fusion.11
  58.0 0.4 fusion.32
  58.7 0.4 fusion.13
  59.1 0.4 fusion.33
  59.8 0.4 fusion.15
  60.3 0.4 fusion.34
  61.0 0.4 fusion.17
  61.4 0.4 fusion.35
  62.1 0.4 fusion.19
  62.6 0.4 fusion.36
  63.3 0.4 fusion.21
  63.7 0.4 fusion.37
  64.4 0.4 fusion.23
  64.9 0.4 fusion.38
  65.6 0.2 copy.133
  65.9 0.2 reshape.136
  66.2 0.7 pad_maximum_fusion.buf_ref
  66.9 63.2 %shard_map.196 = (f32[200,128]{1,0:T(8,128)}, bf16[96,4,256]{2,1,0:T(4,128)(2,1)}, bf16[96,4,256]{2,1,0:T(4,128)(2,1)}, bf16[96,4,128]{2,1,0:T(4,128)(2,1)}, bf1...) custom-call(f32[656,128]{1,0:T(8,128)} %pad_maximum_fusion.buf_ref, ...), custom_call_target="tpu_custom_call" | custom-call | bytes 209715200 | tf_op jit(solution)/shard_map/pallas_call | solution.py:478
  130.2 1.0 copy.134
  131.3 0.7 slice_bitcast_fusion.1
  132.0 0.9 slice_bitcast_fusion
  133.0 0.6 fusion.39
  133.7 0.7 slice.270
  134.4 0.7 slice.267
  135.0 0.9 copy.136
  136.4 0.5 maximum_bitcast_fusion
  136.9 0.2 reshape.140
  137.1 0.8 copy.144
  137.9 1.2 pad_convert_fusion.x_ref
  139.1 6.8 %shard_map.197 = bf16[96,4,256]{2,1,0:T(4,128)(2,1)} custom-call(f32[10,96,384]{2,1,0:T(8,128)} %pad_convert_fusion.x_ref, f32[96,49]{1,0:T(8,128)} %copy.95.k_ref, bf16[96,4,256]{2,1,0:T(4,128)(2,1)} %rest_0_.1), custom_call_target="tpu_custom_call" | custom-call | tf_op jit(solution)/shard_map/pallas_call | solution.py:175
  (114 shorter events, 3.8 us)
Async XLA Ops:
  0.6 48.9 %copy-start = (bf16[384,96]{0,1:T(8,128)(2,1)S(1)}, bf16[384,96]{0,1:T(8,128)(2,1)}, u32[]{:S(2)}) copy-start(bf16[384,96]{0,1:T(8,128)(2,1)} %param.17) | copy-start | bytes 221188
  34.1 4.9 %copy-start.14 = (bf16[96,4,128]{2,1,0:T(4,128)(2,1)S(1)}, bf16[96,4,128]{2,1,0:T(4,128)(2,1)}, u32[]{:S(2)}) copy-start(bf16[96,4,128]{2,1,0:T(4,128)(2,1)} %get-tuple-element.35) | copy-start | bytes 294916
  34.1 5.0 %copy-start.9 = (bf16[96,4,256]{2,1,0:T(4,128)(2,1)S(1)}, bf16[96,4,256]{2,1,0:T(4,128)(2,1)}, u32[]{:S(2)}) copy-start(bf16[96,4,256]{2,1,0:T(4,128)(2,1)} %get-tuple-element.29) | copy-start | bytes 589828
  34.2 5.0 %copy-start.8 = (bf16[96,4,256]{2,1,0:T(4,128)(2,1)S(1)}, bf16[96,4,256]{2,1,0:T(4,128)(2,1)}, u32[]{:S(2)}) copy-start(bf16[96,4,256]{2,1,0:T(4,128)(2,1)} %get-tuple-element.34) | copy-start | bytes 589828
  41.4 6.7 %copy-start.19 = (f32[96]{0:T(128)S(1)}, f32[96]{0:T(128)}, u32[]{:S(2)}) copy-start(f32[96]{0:T(128)} %param.14) | copy-start | bytes 1156
  48.1 1.5 %copy-start.16 = (f32[96]{0:T(128)S(1)}, f32[96]{0:T(128)}, u32[]{:S(2)}) copy-start(f32[96]{0:T(128)} %param.15) | copy-start | bytes 1156
  48.1 1.5 %copy-start.18 = (f32[96]{0:T(128)S(1)}, f32[96]{0:T(128)}, u32[]{:S(2)}) copy-start(f32[96]{0:T(128)} %param.16) | copy-start | bytes 1156
  49.6 0.9 copy-start.15
  49.6 0.9 copy-start.17
  49.6 0.9 copy-start.20
  55.2 9.2 %copy-start.1 = (bf16[96,4,256]{2,1,0:T(4,128)(2,1)}, bf16[96,4,256]{2,1,0:T(4,128)(2,1)S(1)}, u32[]{:S(2)}) copy-start(bf16[96,4,256]{2,1,0:T(4,128)(2,1)S(1)} %reshape.135.x_ref) | copy-start | bytes 589828
  57.5 1.1 copy-start.5
  58.0 1.9 %copy-start.4 = (bf16[96,10,256]{2,0,1:T(8,128)(2,1)S(1)}, bf16[96,10,256]{2,0,1:T(8,128)(2,1)}, u32[]{:S(2)}) copy-start(bf16[96,10,256]{2,0,1:T(8,128)(2,1)} %get-tuple-element.76) | copy-start | bytes 1474564
  59.1 1.9 %copy-start.3 = (bf16[96,10,256]{2,0,1:T(8,128)(2,1)S(1)}, bf16[96,10,256]{2,0,1:T(8,128)(2,1)}, u32[]{:S(2)}) copy-start(bf16[96,10,256]{2,0,1:T(8,128)(2,1)} %get-tuple-element.77) | copy-start | bytes 1474564
  60.3 1.9 %copy-start.2 = (bf16[96,10,256]{2,0,1:T(8,128)(2,1)S(1)}, bf16[96,10,256]{2,0,1:T(8,128)(2,1)}, u32[]{:S(2)}) copy-start(bf16[96,10,256]{2,0,1:T(8,128)(2,1)} %get-tuple-element.78) | copy-start | bytes 1474564
  130.1 5.8 %copy-start.13 = (bf16[96,4,128]{2,1,0:T(4,128)(2,1)S(1)}, bf16[96,4,128]{2,1,0:T(4,128)(2,1)}, u32[]{:S(2)}) copy-start(bf16[96,4,128]{2,1,0:T(4,128)(2,1)} %get-tuple-element.39) | copy-start | bytes 294916
  130.1 6.0 %copy-start.12 = (bf16[96,4,128]{2,1,0:T(4,128)(2,1)S(1)}, bf16[96,4,128]{2,1,0:T(4,128)(2,1)}, u32[]{:S(2)}) copy-start(bf16[96,4,128]{2,1,0:T(4,128)(2,1)} %get-tuple-element.40) | copy-start | bytes 294916
  130.1 6.0 %copy-start.11 = (bf16[96,4,128]{2,1,0:T(4,128)(2,1)S(1)}, bf16[96,4,128]{2,1,0:T(4,128)(2,1)}, u32[]{:S(2)}) copy-start(bf16[96,4,128]{2,1,0:T(4,128)(2,1)} %get-tuple-element.41) | copy-start | bytes 294916
  130.2 6.1 %copy-start.10 = (bf16[96,4,128]{2,1,0:T(4,128)(2,1)S(1)}, bf16[96,4,128]{2,1,0:T(4,128)(2,1)}, u32[]{:S(2)}) copy-start(bf16[96,4,128]{2,1,0:T(4,128)(2,1)} %get-tuple-element.43) | copy-start | bytes 294916
  130.2 6.2 %copy-start.7 = (bf16[96,4,256]{2,1,0:T(4,128)(2,1)S(1)}, bf16[96,4,256]{2,1,0:T(4,128)(2,1)}, u32[]{:S(2)}) copy-start(bf16[96,4,256]{2,1,0:T(4,128)(2,1)} %get-tuple-element.37) | copy-start | bytes 589828
  132.9 3.5 %copy-start.6 = (bf16[96,4,256]{2,1,0:T(4,128)(2,1)S(1)}, bf16[96,4,256]{2,1,0:T(4,128)(2,1)}, u32[]{:S(2)}) copy-start(bf16[96,4,256]{2,1,0:T(4,128)(2,1)} %get-tuple-element.42) | copy-start | bytes 589828

commit v14 on v13

--- a/solution.py
+++ b/solution.py
@@ -145,7 +145,7 @@
 
     def block(i, carry):
         ch = pl.ds(pl.multiple_of(i * cb, cb), cb)
-        x = x_ref[:, ch, :]
+        x = x_ref[:, ch, :].astype(jnp.float32)
         acc = jnp.zeros((rows, cb, cols), jnp.float32)
         for shift_col in range(7):
             c0 = 6 - shift_col if flip else shift_col
@@ -168,7 +168,7 @@
 def _dw(padded, kernel, row_count, col_count, flip, cot=None):
     channels = padded.shape[0]
     wide = -(-padded.shape[2] // LANES) * LANES
-    x = jnp.transpose(padded, (1, 0, 2)).astype(jnp.float32)
+    x = jnp.transpose(padded, (1, 0, 2))
     x = jnp.pad(x, ((0, 0), (0, 0), (0, wide - padded.shape[2])))
     taps = kernel.reshape(channels, 49)
     cb = 8

time: 148 us -> 145 us (0.980)
  Pallas kernels: 103 us -> 100 us
  other arithmetic: 9.7 us -> 7.18 us
  local copies, waits for them, and re-layouts: 25.8 us -> 27.7 us
    pallas_call x2, Pallas kernels: 13.5 us -> 10.8 us  [_dw(): pl.pallas_call(functools.partial(dw_kernel, flip, cb), out_shape=jax.Shap...]
    pad x2 -> x0, other arithmetic: 2.5 us -> none  [_dw(): x = jnp.pad(x, ((0, 0), (0, 0), (0, wide - padded.shape[2])))]
    pad x0 -> x2, local copies, waits for them, and re-layouts: none -> 1.91 us  [_dw(): x = jnp.pad(x, ((0, 0), (0, 0), (0, wide - padded.shape[2])))]
where the time goes in v14:
time: 145 us; the launch traced here: 143 us
  Pallas kernels  100 us (69%)
  local copies, waits for them, and re-layouts  27.7 us (19%)
  other arithmetic  7.18 us (5%)
  matrix products  6.39 us (4%)
    pallas_call x1, Pallas kernels, grad_reduce(): pl.pallas_call(functools.partial(reduce_kernel, nfilt, nspace, pr, sr, x....  63.2 us
    pallas_call x1, Pallas kernels, padded_2(): pl.pallas_call(functools.partial(halo_kernel, ns, nf, x.shape[2]), out_sh...  26.1 us
    pallas_call x2, Pallas kernels, _dw(): pl.pallas_call(functools.partial(dw_kernel, flip, cb), out_shape=jax.Shap...  10.8 us
    pallas_call x8, local copies, waits for them, and re-layouts, padded_2(): pl.pallas_call(functools.partial(halo_kernel, ns, nf, x.shape[2]), out_sh...  4.66 us
    slice x28, local copies, waits for them, and re-layouts, kernel_terms(): total = total + corr[:, row:row + ksize, row]  4.22 us
    unnamed x49, local copies, waits for them, and re-layouts  4 us
    dot_general x7, matrix products, kernel_terms(): jnp.einsum('crj,cij->cri', padded[:, :, shift_col:shift_col + col_count],...  2.95 us

profile of v14, /device:TPU:56, one launch (start us, length us, event | category | flops | bytes accessed | tf_op | source)
XLA Modules:
  0.0 142.7 jit_solution(10971801363966585425)
XLA Ops:
  0.7 2.4 %multiply_reduce_fusion = f32[96]{0:T(128)S(1)} fusion(f32[96]{0:T(128)} %param.21, bf16[96,4,256]{2,1,0:T(4,128)(2,1)} %rest_0_.1), kind=kLoop, calls=%fused_computation.36 | loop fusion | flops 294816 | bytes 197376 | tf_op jit(solution)/shard_map/reduce_sum | solution.py:270
  3.0 0.7 convert_element_type.53
  3.7 0.8 reshape.128
  4.5 0.7 copy.95.k_ref
  5.2 0.9 copy.91
  6.1 1.0 copy.152
  7.1 1.0 copy.148
  8.1 26.1 %shard_map.194 = (bf16[96,4,256]{2,1,0:T(4,128)(2,1)}, bf16[96,4,256]{2,1,0:T(4,128)(2,1)}, bf16[96,4,128]{2,1,0:T(4,128)(2,1)}, bf16[96,4,128]{2,1,0:T(4,128)(2...) custom-call(bf16[96,4,256]{2,1,0:T(4,128)(2,1)} %x_ref.1), custom_call_target="tpu_custom_call" | custom-call | tf_op jit(solution)/shard_map/pallas_call | solution.py:126
  34.2 1.0 copy.86
  35.2 0.9 copy.88
  36.2 0.9 copy.89
  37.2 0.9 copy.90
  38.1 0.9 copy.92
  39.3 0.5 fusion.56
  39.7 0.5 maximum_maximum_fusion
  40.2 1.0 pad.15.x_ref
  41.1 5.3 %shard_map.195 = f32[96,4,256]{2,1,0:T(4,128)} custom-call(bf16[10,96,384]{2,1,0:T(8,128)(2,1)} %pad.15.x_ref, f32[96,49]{1,0:T(8,128)} %copy.95.k_ref), custom_call_target="tpu_custom_call" | custom-call | tf_op jit(solution)/shard_map/pallas_call | solution.py:175
  46.4 1.2 fusion.30
  47.6 0.2 multiply_reduce_fusion.3
  47.9 0.6 fusion.9
  48.6 0.2 copy-done.15
  48.8 0.5 multiply_reduce_fusion.1
  49.2 1.0 convert_reduce_fusion
  50.2 0.4 fusion.28
  50.7 0.2 reshape.131
  50.9 0.8 reshape.130
  51.7 0.4 fusion.29
  52.2 0.5 fusion.25
  52.7 0.2 reshape.132
  52.9 0.1 reduce_sum.97
  53.0 0.2 convert_reduce_fusion.1
  53.3 0.1 reshape.134
  53.4 0.1 reshape.135.x_ref
  53.6 2.3 %fusion.31 = (bf16[96,10,256]{2,0,1:T(8,128)(2,1)S(1)}, bf16[96,10,256]{2,0,1:T(8,128)(2,1)}, bf16[96,10,256]{2,0,1:T(8,128)(2,1)}, bf16[96,10,256]{2,0,1:T(8,12...) fusion(bf16[96,10,262]{2,0,1:T(8,128)(2,1)S(1)} %maximum_maximum_fusion), kind=kLoop, calls=%fused_computation.72 | loop fusion | bytes 6881280 | tf_op jit(solution)/shard_map/slice | solution.py:200
  55.9 0.4 fusion.11
  56.3 0.4 fusion.32
  57.0 0.4 fusion.13
  57.4 0.4 fusion.33
  58.2 0.4 fusion.15
  58.6 0.4 fusion.34
  59.3 0.4 fusion.17
  59.7 0.4 fusion.35
  60.5 0.4 fusion.19
  60.9 0.4 fusion.36
  61.6 0.4 fusion.21
  62.0 0.4 fusion.37
  62.8 0.4 fusion.23
  63.2 0.4 fusion.38
  64.0 0.2 copy.133
  64.2 0.2 reshape.136
  64.5 0.7 pad_maximum_fusion.buf_ref
  65.2 63.2 %shard_map.196 = (f32[200,128]{1,0:T(8,128)}, bf16[96,4,256]{2,1,0:T(4,128)(2,1)}, bf16[96,4,256]{2,1,0:T(4,128)(2,1)}, bf16[96,4,128]{2,1,0:T(4,128)(2,1)}, bf1...) custom-call(f32[656,128]{1,0:T(8,128)} %pad_maximum_fusion.buf_ref, ...), custom_call_target="tpu_custom_call" | custom-call | bytes 209715200 | tf_op jit(solution)/shard_map/pallas_call | solution.py:478
  128.5 1.0 copy.134
  129.6 0.7 slice_bitcast_fusion.1
  130.3 0.9 slice_bitcast_fusion
  131.3 0.6 fusion.39
  132.0 0.7 slice.270
  132.7 0.7 slice.267
  133.4 0.9 copy.136
  134.8 0.5 maximum_bitcast_fusion
  135.2 1.0 pad.18.x_ref
  136.2 5.5 %shard_map.197 = bf16[96,4,256]{2,1,0:T(4,128)(2,1)} custom-call(bf16[10,96,384]{2,1,0:T(8,128)(2,1)} %pad.18.x_ref, f32[96,49]{1,0:T(8,128)} %copy.95.k_ref, bf16[96,4,256]{2,1,0:T(4,128)(2,1)} %rest_0_.1), custom_call_target="tpu_custom_call" | custom-call | tf_op jit(solution)/shard_map/pallas_call | solution.py:175
  141.7 0.2 reshape.140
  141.9 0.8 copy.144
  (114 shorter events, 3.8 us)
Async XLA Ops:
  0.6 47.3 %copy-start = (bf16[384,96]{0,1:T(8,128)(2,1)S(1)}, bf16[384,96]{0,1:T(8,128)(2,1)}, u32[]{:S(2)}) copy-start(bf16[384,96]{0,1:T(8,128)(2,1)} %param.17) | copy-start | bytes 221188
  34.1 4.9 %copy-start.14 = (bf16[96,4,128]{2,1,0:T(4,128)(2,1)S(1)}, bf16[96,4,128]{2,1,0:T(4,128)(2,1)}, u32[]{:S(2)}) copy-start(bf16[96,4,128]{2,1,0:T(4,128)(2,1)} %get-tuple-element.35) | copy-start | bytes 294916
  34.1 5.0 %copy-start.9 = (bf16[96,4,256]{2,1,0:T(4,128)(2,1)S(1)}, bf16[96,4,256]{2,1,0:T(4,128)(2,1)}, u32[]{:S(2)}) copy-start(bf16[96,4,256]{2,1,0:T(4,128)(2,1)} %get-tuple-element.29) | copy-start | bytes 589828
  34.2 5.0 %copy-start.8 = (bf16[96,4,256]{2,1,0:T(4,128)(2,1)S(1)}, bf16[96,4,256]{2,1,0:T(4,128)(2,1)}, u32[]{:S(2)}) copy-start(bf16[96,4,256]{2,1,0:T(4,128)(2,1)} %get-tuple-element.34) | copy-start | bytes 589828
  40.2 6.3 %copy-start.19 = (f32[96]{0:T(128)S(1)}, f32[96]{0:T(128)}, u32[]{:S(2)}) copy-start(f32[96]{0:T(128)} %param.14) | copy-start | bytes 1156
  41.1 6.8 %copy-start.16 = (f32[96]{0:T(128)S(1)}, f32[96]{0:T(128)}, u32[]{:S(2)}) copy-start(f32[96]{0:T(128)} %param.15) | copy-start | bytes 1156
  41.1 6.8 %copy-start.18 = (f32[96]{0:T(128)S(1)}, f32[96]{0:T(128)}, u32[]{:S(2)}) copy-start(f32[96]{0:T(128)} %param.16) | copy-start | bytes 1156
  47.9 0.9 copy-start.15
  47.9 0.9 copy-start.17
  47.9 0.9 copy-start.20
  53.6 9.2 %copy-start.1 = (bf16[96,4,256]{2,1,0:T(4,128)(2,1)}, bf16[96,4,256]{2,1,0:T(4,128)(2,1)S(1)}, u32[]{:S(2)}) copy-start(bf16[96,4,256]{2,1,0:T(4,128)(2,1)S(1)} %reshape.135.x_ref) | copy-start | bytes 589828
  55.9 1.1 copy-start.5
  56.3 1.9 %copy-start.4 = (bf16[96,10,256]{2,0,1:T(8,128)(2,1)S(1)}, bf16[96,10,256]{2,0,1:T(8,128)(2,1)}, u32[]{:S(2)}) copy-start(bf16[96,10,256]{2,0,1:T(8,128)(2,1)} %get-tuple-element.76) | copy-start | bytes 1474564
  57.4 1.9 %copy-start.3 = (bf16[96,10,256]{2,0,1:T(8,128)(2,1)S(1)}, bf16[96,10,256]{2,0,1:T(8,128)(2,1)}, u32[]{:S(2)}) copy-start(bf16[96,10,256]{2,0,1:T(8,128)(2,1)} %get-tuple-element.77) | copy-start | bytes 1474564
  58.6 1.9 %copy-start.2 = (bf16[96,10,256]{2,0,1:T(8,128)(2,1)S(1)}, bf16[96,10,256]{2,0,1:T(8,128)(2,1)}, u32[]{:S(2)}) copy-start(bf16[96,10,256]{2,0,1:T(8,128)(2,1)} %get-tuple-element.78) | copy-start | bytes 1474564
  128.4 5.8 %copy-start.13 = (bf16[96,4,128]{2,1,0:T(4,128)(2,1)S(1)}, bf16[96,4,128]{2,1,0:T(4,128)(2,1)}, u32[]{:S(2)}) copy-start(bf16[96,4,128]{2,1,0:T(4,128)(2,1)} %get-tuple-element.39) | copy-start | bytes 294916
  128.5 6.0 %copy-start.12 = (bf16[96,4,128]{2,1,0:T(4,128)(2,1)S(1)}, bf16[96,4,128]{2,1,0:T(4,128)(2,1)}, u32[]{:S(2)}) copy-start(bf16[96,4,128]{2,1,0:T(4,128)(2,1)} %get-tuple-element.40) | copy-start | bytes 294916
  128.5 6.0 %copy-start.11 = (bf16[96,4,128]{2,1,0:T(4,128)(2,1)S(1)}, bf16[96,4,128]{2,1,0:T(4,128)(2,1)}, u32[]{:S(2)}) copy-start(bf16[96,4,128]{2,1,0:T(4,128)(2,1)} %get-tuple-element.41) | copy-start | bytes 294916
  128.5 6.1 %copy-start.10 = (bf16[96,4,128]{2,1,0:T(4,128)(2,1)S(1)}, bf16[96,4,128]{2,1,0:T(4,128)(2,1)}, u32[]{:S(2)}) copy-start(bf16[96,4,128]{2,1,0:T(4,128)(2,1)} %get-tuple-element.43) | copy-start | bytes 294916
  128.5 6.2 %copy-start.7 = (bf16[96,4,256]{2,1,0:T(4,128)(2,1)S(1)}, bf16[96,4,256]{2,1,0:T(4,128)(2,1)}, u32[]{:S(2)}) copy-start(bf16[96,4,256]{2,1,0:T(4,128)(2,1)} %get-tuple-element.37) | copy-start | bytes 589828
  131.2 3.5 %copy-start.6 = (bf16[96,4,256]{2,1,0:T(4,128)(2,1)S(1)}, bf16[96,4,256]{2,1,0:T(4,128)(2,1)}, u32[]{:S(2)}) copy-start(bf16[96,4,256]{2,1,0:T(4,128)(2,1)} %get-tuple-element.42) | copy-start | bytes 589828

commit v15 on v14

--- a/solution.py
+++ b/solution.py
@@ -171,7 +171,7 @@
     x = jnp.transpose(padded, (1, 0, 2))
     x = jnp.pad(x, ((0, 0), (0, 0), (0, wide - padded.shape[2])))
     taps = kernel.reshape(channels, 49)
-    cb = 8
+    cb = 16
     out = pl.pallas_call(
         functools.partial(dw_kernel, flip, cb),
         out_shape=jax.ShapeDtypeStruct(

time: 145 us -> 144 us (level)
  no operation moved by 1% of the time
where the time goes in v15:
time: 144 us; the launch traced here: 142 us
  Pallas kernels  99.1 us (69%)
  local copies, waits for them, and re-layouts  27.7 us (19%)
  other arithmetic  7.18 us (5%)
  matrix products  6.38 us (4%)
    pallas_call x1, Pallas kernels, grad_reduce(): pl.pallas_call(functools.partial(reduce_kernel, nfilt, nspace, pr, sr, x....  63.2 us
    pallas_call x1, Pallas kernels, padded_2(): pl.pallas_call(functools.partial(halo_kernel, ns, nf, x.shape[2]), out_sh...  26.1 us
    pallas_call x2, Pallas kernels, _dw(): pl.pallas_call(functools.partial(dw_kernel, flip, cb), out_shape=jax.Shap...  9.82 us
    pallas_call x8, local copies, waits for them, and re-layouts, padded_2(): pl.pallas_call(functools.partial(halo_kernel, ns, nf, x.shape[2]), out_sh...  4.66 us
    slice x28, local copies, waits for them, and re-layouts, kernel_terms(): total = total + corr[:, row:row + ksize, row]  4.22 us
    unnamed x49, local copies, waits for them, and re-layouts  4 us
    dot_general x7, matrix products, kernel_terms(): jnp.einsum('crj,cij->cri', padded[:, :, shift_col:shift_col + col_count],...  2.95 us

profile of v15, /device:TPU:56, one launch (start us, length us, event | category | flops | bytes accessed | tf_op | source)
XLA Modules:
  0.0 141.7 jit_solution(13418634578155885027)
XLA Ops:
  0.7 2.4 %multiply_reduce_fusion = f32[96]{0:T(128)S(1)} fusion(f32[96]{0:T(128)} %param.21, bf16[96,4,256]{2,1,0:T(4,128)(2,1)} %rest_0_.1), kind=kLoop, calls=%fused_computation.36 | loop fusion | flops 294816 | bytes 197376 | tf_op jit(solution)/shard_map/reduce_sum | solution.py:270
  3.0 0.7 convert_element_type.53
  3.7 0.8 reshape.128
  4.5 0.7 copy.95.k_ref
  5.2 0.9 copy.91
  6.1 1.0 copy.152
  7.1 1.0 copy.148
  8.1 26.1 %shard_map.194 = (bf16[96,4,256]{2,1,0:T(4,128)(2,1)}, bf16[96,4,256]{2,1,0:T(4,128)(2,1)}, bf16[96,4,128]{2,1,0:T(4,128)(2,1)}, bf16[96,4,128]{2,1,0:T(4,128)(2...) custom-call(bf16[96,4,256]{2,1,0:T(4,128)(2,1)} %x_ref.1), custom_call_target="tpu_custom_call" | custom-call | tf_op jit(solution)/shard_map/pallas_call | solution.py:126
  34.2 1.0 copy.86
  35.2 0.9 copy.88
  36.2 0.9 copy.89
  37.2 0.9 copy.90
  38.1 0.9 copy.92
  39.3 0.5 fusion.56
  39.7 0.5 maximum_maximum_fusion
  40.2 1.0 pad.15.x_ref
  41.1 4.8 %shard_map.195 = f32[96,4,256]{2,1,0:T(4,128)} custom-call(bf16[10,96,384]{2,1,0:T(8,128)(2,1)} %pad.15.x_ref, f32[96,49]{1,0:T(8,128)} %copy.95.k_ref), custom_call_target="tpu_custom_call" | custom-call | tf_op jit(solution)/shard_map/pallas_call | solution.py:175
  45.9 1.2 fusion.30
  47.1 0.2 multiply_reduce_fusion.3
  47.4 0.6 fusion.9
  48.1 0.2 copy-done.15
  48.2 0.5 multiply_reduce_fusion.1
  48.7 0.9 convert_reduce_fusion
  49.7 0.4 fusion.28
  50.1 0.2 reshape.131
  50.4 0.8 reshape.130
  51.2 0.4 fusion.29
  51.6 0.5 fusion.25
  52.1 0.2 reshape.132
  52.3 0.1 reduce_sum.97
  52.5 0.2 convert_reduce_fusion.1
  52.8 0.1 reshape.134
  52.9 0.1 reshape.135.x_ref
  53.1 2.3 %fusion.31 = (bf16[96,10,256]{2,0,1:T(8,128)(2,1)S(1)}, bf16[96,10,256]{2,0,1:T(8,128)(2,1)}, bf16[96,10,256]{2,0,1:T(8,128)(2,1)}, bf16[96,10,256]{2,0,1:T(8,12...) fusion(bf16[96,10,262]{2,0,1:T(8,128)(2,1)S(1)} %maximum_maximum_fusion), kind=kLoop, calls=%fused_computation.72 | loop fusion | bytes 6881280 | tf_op jit(solution)/shard_map/slice | solution.py:200
  55.3 0.4 fusion.11
  55.8 0.4 fusion.32
  56.5 0.4 fusion.13
  56.9 0.4 fusion.33
  57.6 0.4 fusion.15
  58.1 0.4 fusion.34
  58.8 0.4 fusion.17
  59.2 0.4 fusion.35
  59.9 0.4 fusion.19
  60.4 0.4 fusion.36
  61.1 0.4 fusion.21
  61.5 0.4 fusion.37
  62.2 0.4 fusion.23
  62.7 0.4 fusion.38
  63.4 0.2 copy.133
  63.7 0.2 reshape.136
  64.0 0.7 pad_maximum_fusion.buf_ref
  64.7 63.2 %shard_map.196 = (f32[200,128]{1,0:T(8,128)}, bf16[96,4,256]{2,1,0:T(4,128)(2,1)}, bf16[96,4,256]{2,1,0:T(4,128)(2,1)}, bf16[96,4,128]{2,1,0:T(4,128)(2,1)}, bf1...) custom-call(f32[656,128]{1,0:T(8,128)} %pad_maximum_fusion.buf_ref, ...), custom_call_target="tpu_custom_call" | custom-call | bytes 209715200 | tf_op jit(solution)/shard_map/pallas_call | solution.py:478
  128.0 1.0 copy.134
  129.1 0.7 slice_bitcast_fusion.1
  129.8 0.9 slice_bitcast_fusion
  130.8 0.6 fusion.39
  131.5 0.7 slice.270
  132.2 0.7 slice.267
  132.9 0.9 copy.136
  134.2 0.5 maximum_bitcast_fusion
  134.7 1.0 pad.18.x_ref
  135.7 5.0 %shard_map.197 = bf16[96,4,256]{2,1,0:T(4,128)(2,1)} custom-call(bf16[10,96,384]{2,1,0:T(8,128)(2,1)} %pad.18.x_ref, f32[96,49]{1,0:T(8,128)} %copy.95.k_ref, bf16[96,4,256]{2,1,0:T(4,128)(2,1)} %rest_0_.1), custom_call_target="tpu_custom_call" | custom-call | tf_op jit(solution)/shard_map/pallas_call | solution.py:175
  140.7 0.2 reshape.140
  140.9 0.8 copy.144
  (114 shorter events, 3.8 us)
Async XLA Ops:
  0.6 46.8 %copy-start = (bf16[384,96]{0,1:T(8,128)(2,1)S(1)}, bf16[384,96]{0,1:T(8,128)(2,1)}, u32[]{:S(2)}) copy-start(bf16[384,96]{0,1:T(8,128)(2,1)} %param.17) | copy-start | bytes 221188
  34.1 4.9 %copy-start.14 = (bf16[96,4,128]{2,1,0:T(4,128)(2,1)S(1)}, bf16[96,4,128]{2,1,0:T(4,128)(2,1)}, u32[]{:S(2)}) copy-start(bf16[96,4,128]{2,1,0:T(4,128)(2,1)} %get-tuple-element.35) | copy-start | bytes 294916
  34.1 5.0 %copy-start.9 = (bf16[96,4,256]{2,1,0:T(4,128)(2,1)S(1)}, bf16[96,4,256]{2,1,0:T(4,128)(2,1)}, u32[]{:S(2)}) copy-start(bf16[96,4,256]{2,1,0:T(4,128)(2,1)} %get-tuple-element.29) | copy-start | bytes 589828
  34.2 5.0 %copy-start.8 = (bf16[96,4,256]{2,1,0:T(4,128)(2,1)S(1)}, bf16[96,4,256]{2,1,0:T(4,128)(2,1)}, u32[]{:S(2)}) copy-start(bf16[96,4,256]{2,1,0:T(4,128)(2,1)} %get-tuple-element.34) | copy-start | bytes 589828
  40.2 5.8 %copy-start.19 = (f32[96]{0:T(128)S(1)}, f32[96]{0:T(128)}, u32[]{:S(2)}) copy-start(f32[96]{0:T(128)} %param.14) | copy-start | bytes 1156
  41.1 6.3 %copy-start.16 = (f32[96]{0:T(128)S(1)}, f32[96]{0:T(128)}, u32[]{:S(2)}) copy-start(f32[96]{0:T(128)} %param.15) | copy-start | bytes 1156
  41.1 6.3 %copy-start.18 = (f32[96]{0:T(128)S(1)}, f32[96]{0:T(128)}, u32[]{:S(2)}) copy-start(f32[96]{0:T(128)} %param.16) | copy-start | bytes 1156
  47.4 0.9 copy-start.15
  47.4 0.9 copy-start.17
  47.4 0.9 copy-start.20
  53.0 9.2 %copy-start.1 = (bf16[96,4,256]{2,1,0:T(4,128)(2,1)}, bf16[96,4,256]{2,1,0:T(4,128)(2,1)S(1)}, u32[]{:S(2)}) copy-start(bf16[96,4,256]{2,1,0:T(4,128)(2,1)S(1)} %reshape.135.x_ref) | copy-start | bytes 589828
  55.3 1.1 copy-start.5
  55.8 1.9 %copy-start.4 = (bf16[96,10,256]{2,0,1:T(8,128)(2,1)S(1)}, bf16[96,10,256]{2,0,1:T(8,128)(2,1)}, u32[]{:S(2)}) copy-start(bf16[96,10,256]{2,0,1:T(8,128)(2,1)} %get-tuple-element.76) | copy-start | bytes 1474564
  56.9 1.9 %copy-start.3 = (bf16[96,10,256]{2,0,1:T(8,128)(2,1)S(1)}, bf16[96,10,256]{2,0,1:T(8,128)(2,1)}, u32[]{:S(2)}) copy-start(bf16[96,10,256]{2,0,1:T(8,128)(2,1)} %get-tuple-element.77) | copy-start | bytes 1474564
  58.1 1.9 %copy-start.2 = (bf16[96,10,256]{2,0,1:T(8,128)(2,1)S(1)}, bf16[96,10,256]{2,0,1:T(8,128)(2,1)}, u32[]{:S(2)}) copy-start(bf16[96,10,256]{2,0,1:T(8,128)(2,1)} %get-tuple-element.78) | copy-start | bytes 1474564
  127.9 5.8 %copy-start.13 = (bf16[96,4,128]{2,1,0:T(4,128)(2,1)S(1)}, bf16[96,4,128]{2,1,0:T(4,128)(2,1)}, u32[]{:S(2)}) copy-start(bf16[96,4,128]{2,1,0:T(4,128)(2,1)} %get-tuple-element.39) | copy-start | bytes 294916
  127.9 6.0 %copy-start.12 = (bf16[96,4,128]{2,1,0:T(4,128)(2,1)S(1)}, bf16[96,4,128]{2,1,0:T(4,128)(2,1)}, u32[]{:S(2)}) copy-start(bf16[96,4,128]{2,1,0:T(4,128)(2,1)} %get-tuple-element.40) | copy-start | bytes 294916
  128.0 6.0 %copy-start.11 = (bf16[96,4,128]{2,1,0:T(4,128)(2,1)S(1)}, bf16[96,4,128]{2,1,0:T(4,128)(2,1)}, u32[]{:S(2)}) copy-start(bf16[96,4,128]{2,1,0:T(4,128)(2,1)} %get-tuple-element.41) | copy-start | bytes 294916
  128.0 6.1 %copy-start.10 = (bf16[96,4,128]{2,1,0:T(4,128)(2,1)S(1)}, bf16[96,4,128]{2,1,0:T(4,128)(2,1)}, u32[]{:S(2)}) copy-start(bf16[96,4,128]{2,1,0:T(4,128)(2,1)} %get-tuple-element.43) | copy-start | bytes 294916
  128.0 6.2 %copy-start.7 = (bf16[96,4,256]{2,1,0:T(4,128)(2,1)S(1)}, bf16[96,4,256]{2,1,0:T(4,128)(2,1)}, u32[]{:S(2)}) copy-start(bf16[96,4,256]{2,1,0:T(4,128)(2,1)} %get-tuple-element.37) | copy-start | bytes 589828
  130.7 3.5 %copy-start.6 = (bf16[96,4,256]{2,1,0:T(4,128)(2,1)S(1)}, bf16[96,4,256]{2,1,0:T(4,128)(2,1)}, u32[]{:S(2)}) copy-start(bf16[96,4,256]{2,1,0:T(4,128)(2,1)} %get-tuple-element.42) | copy-start | bytes 589828
